TPU v7x, 32 devices: a whole 2x2x4 slice. The times are simulated.
32 devices in a mesh: group: 4 (over y, x), delay: 8 (over z, core).
Axes of the slice: x: 2, y: 2, z: 4, core: 2. Of those that a mesh axis runs over, the one named last changes fastest.
Arguments:
- retarded: bfloat16 [8, 16, 3, 256, 256], P('delay', 'group'), may hold values from -0.0625 to 0.0625
- block_row: int32 [8, 16, 3], P('delay', 'group'), may hold values from 0 to 3, as said below
- block_count: int32 [8, 16], P('delay', 'group'), may hold values from 1 to 3, as said below
- send_pick: int32 [8, 4, 4], P('delay'), may hold values from 0 to 3
- history: bfloat16 [8, 4096, 128], P('delay', 'group'), may hold values from -6 to 6
- incident: bfloat16 [4, 4096, 128], P(None, 'group'), may hold values from -6 to 6
- self_block: bfloat16 [4096, 1024], P('group'), may hold values from -0.1875 to 0.1875
- sheet_diag: float32 [4096], P('group'), may hold values from 1 to 1.6
Outputs:
- currents: bfloat16 [4, 4096, 128], P(None, 'group')
Inputs may be any that keep to these rules, and one draw needn't show every extreme that they name: `block_row`: the live list places of one section, reading group and source group name distinct row blocks. `block_count`: list places at or beyond the count are ignored.
All inputs are finite; a program needn't handle non-finite values.
Results may differ from a plain program's by a relative error of at most 0.0085.
Values may be sent and summed in bfloat16 or wider, within the bound.
No kernel may reach another device: no remote copies, remote signals or barrier semaphores. Data moves between devices by JAX's collectives and lax.ppermute only.
A program may use at most 128 MiB of HBM per device.

v0:
```python
import jax
import jax.numpy as jnp
from jax import lax
from jax.sharding import PartitionSpec as P

STEPS = 4
ITERS = 3


def passed_along(block, axis, distance):
    devices = range(lax.axis_size(axis))
    route = [(i - distance, i) for i in devices if i - distance in devices]
    return lax.ppermute(block, axis, route)


def local(retarded, block_row, block_count, send_pick, history, incident, self_block, sheet_diag):
    group_index = lax.axis_index("group")
    delay_index = lax.axis_index("delay")
    weights = retarded[0]
    row_list = block_row[0]
    live_count = block_count[0]
    picks = send_pick[0]
    history_now = history[0]
    group_rows, columns = history_now.shape
    block_size = weights.shape[-1]
    group_blocks = group_rows // block_size
    list_depth = weights.shape[1]
    block_ids = jnp.arange(group_blocks, dtype=jnp.int32)
    places = jnp.arange(list_depth, dtype=jnp.int32)
    select = (
        (row_list[:, :, None] == block_ids[None, None, :])
        & (places[None, :, None] < live_count[:, None, None])
    ).astype(jnp.float32)
    send_row = lax.dynamic_index_in_dim(picks, group_index, 0, keepdims=False)
    diagonal = sheet_diag[:, None]
    results = []
    for time_step in range(STEPS):
        onehot = (send_row[:, None] == block_ids[None, :]).astype(jnp.bfloat16)
        stacked = jnp.einsum(
            "rb,bic->ric",
            onehot,
            history_now.reshape(group_blocks, block_size, columns),
            preferred_element_type=jnp.float32,
        ).astype(jnp.bfloat16)
        blocks = lax.all_to_all(stacked, "group", split_axis=0, concat_axis=0, tiled=True)
        terms = jnp.einsum("hlij,hjc->hlic", weights, blocks, preferred_element_type=jnp.float32)
        summed = jnp.einsum("hlr,hlic->ric", select, terms, precision=lax.Precision.HIGHEST)
        partial_value = summed.reshape(group_blocks * block_size, blocks.shape[-1])
        total_field = lax.psum(partial_value, "delay")
        driving = incident[time_step].astype(jnp.float32) - total_field
        iterate = driving / diagonal
        for sweep in range(ITERS):
            coupled = jnp.dot(
                self_block, iterate.astype(jnp.bfloat16), preferred_element_type=jnp.float32
            )
            iterate = (driving - coupled) / diagonal
        current = iterate.astype(jnp.bfloat16)
        results.append(current)
        if time_step + 1 < STEPS:
            shifted = passed_along(history_now, "delay", 1)
            history_now = jnp.where(delay_index == 0, current, shifted)
    return jnp.stack(results)


def solution(mesh):
    placed = (
        P("delay", "group", None, None, None),
        P("delay", "group", None),
        P("delay", "group"),
        P("delay", None, None),
        P("delay", "group", None),
        P(None, "group", None),
        P("group", None),
        P("group"),
    )
    return jax.shard_map(
        local, mesh=mesh, in_specs=placed, out_specs=P(None, "group", None), check_vma=False
    )
```

profile of v0, /device:TPU:0, one launch (start us, length us, event | category | flops | bytes accessed | tf_op | source)
XLA Modules:
  0.0 326.2 jit_solution(5447998018532186903)
XLA Ops:
  9.4 5.2 %all-to-all-start = ((bf16[4,256,128]{2,1,0:T(8,128)(2,1)}), bf16[4,256,128]{2,1,0:T(8,128)(2,1)S(1)}, u32[]{:S(2)}, u32[]{:S(2)}) async-start(bf16[4,256,128]{2,1,0:T(8,128)(2,1)} %copy.92), calls=%async_computation | async-start | bytes 524288 | tf_op jit(solution)/shard_map/all_to_all | solution.py:45
  16.0 4.0 %all-to-all-done = bf16[4,256,128]{2,1,0:T(8,128)(2,1)S(1)} async-done(((bf16[4,256,128]{2,1,0:T(8,128)(2,1)}), bf16[4,256,128]{2,1,0:T(8,128)(2,1)S(1)}, u32[]{:S(2)}, u32[]{:S(2)}) %all-to-all-start) | async-done | bytes 262176 | tf_op jit(solution)/shard_map/all_to_all | solution.py:45
  20.0 3.2 fusion.17
  23.2 2.6 copy.36
  25.8 3.0 fusion.19
  30.1 2.0 collective-permute-start
  34.2 52.4 %all-reduce.5.cloned.1.call-done = f32[1024,128]{0,1:T(8,128)} async-done(((f32[1024,128]{0,1:T(8,128)}), f32[1024,128]{0,1:T(8,128)}) %all-reduce.5.cloned.1.call-update) | async-done | bytes 524304 | tf_op jit(solution)/shard_map/psum | solution.py:49
  86.6 4.0 %fusion.56 = bf16[1024,128]{0,1:T(8,128)(2,1)} fusion(bf16[1024,1024]{1,0:T(8,128)(2,1)S(1)} %copy-done, f32[1024,128]{0,1:T(8,128)} %all-reduce.5.cloned.1.call-done, bf16[1,1024,128]{1,2,0:T(8,128)(2,1)} %copy.63, f32[1024]{0:T(1024)S(1)} %copy-done.10), kind=kOutput, calls=%fused_computation.66 | convolution fusion | flops 538705920 | bytes 3149824 | tf_op jit(solution)/shard_map/dot_general | solution.py:53
  90.6 2.8 broadcast_select_fusion.2
  95.2 9.3 %all_to_all.20 = bf16[4,256,128]{2,1,0:T(8,128)(2,1)S(1)} all-to-all(bf16[4,256,128]{2,1,0:T(8,128)(2,1)S(1)} %copy.91), channel_id=1, replica_groups=mesh['group'=4,'delay'=8] {'group'}, dimensions={0} | all-to-all | bytes 524288 | tf_op jit(solution)/shard_map/all_to_all | solution.py:45
  105.1 2.6 fusion.6
  108.9 2.0 collective-permute-start.1
  110.9 51.9 %all-reduce.7.cloned.1.call-done = f32[1024,128]{0,1:T(8,128)} async-done(((f32[1024,128]{0,1:T(8,128)}), f32[1024,128]{0,1:T(8,128)}) %all-reduce.7.cloned.1.call-update) | async-done | bytes 524304 | tf_op jit(solution)/shard_map/psum | solution.py:49
  162.8 3.0 fusion.53
  170.4 9.2 %all_to_all.21 = bf16[4,256,128]{2,1,0:T(8,128)(2,1)S(1)} all-to-all(bf16[4,256,128]{2,1,0:T(8,128)(2,1)S(1)} %copy.90), channel_id=1, replica_groups=mesh['group'=4,'delay'=8] {'group'}, dimensions={0} | all-to-all | bytes 524288 | tf_op jit(solution)/shard_map/all_to_all | solution.py:45
  180.2 2.6 fusion.3
  183.9 2.0 collective-permute-start.2
  185.9 52.8 %all-reduce.9.cloned.1.call-done = f32[1024,128]{0,1:T(8,128)} async-done(((f32[1024,128]{0,1:T(8,128)}), f32[1024,128]{0,1:T(8,128)}) %all-reduce.9.cloned.1.call-update) | async-done | bytes 524304 | tf_op jit(solution)/shard_map/psum | solution.py:49
  238.7 3.7 %fusion.50 = bf16[1024,128]{0,1:T(8,128)(2,1)} fusion(bf16[1024,1024]{1,0:T(8,128)(2,1)S(1)} %copy-done, f32[1024,128]{0,1:T(8,128)} %all-reduce.9.cloned.1.call-done, bf16[1,1024,128]{1,2,0:T(8,128)(2,1)S(1)} %copy.65, f32[1024]{0:T(1024)S(1)} %copy-done.10), kind=kOutput, calls=%fused_computation.60 | convolution fusion | flops 538705920 | bytes 3149824 | tf_op jit(solution)/shard_map/dot_general | solution.py:53
  242.5 2.0 fusion.49
  245.3 9.3 %all_to_all.22 = bf16[4,256,128]{2,1,0:T(8,128)(2,1)S(1)} all-to-all(bf16[4,256,128]{2,1,0:T(8,128)(2,1)S(1)} %copy.89), channel_id=1, replica_groups=mesh['group'=4,'delay'=8] {'group'}, dimensions={0} | all-to-all | bytes 524288 | tf_op jit(solution)/shard_map/all_to_all | solution.py:45
  255.3 2.6 fusion
  259.0 55.1 %all-reduce.11.cloned.1.call-done = f32[1024,128]{0,1:T(8,128)} async-done(((f32[1024,128]{0,1:T(8,128)}), f32[1024,128]{0,1:T(8,128)}) %all-reduce.11.cloned.1.call-update) | async-done | bytes 524304 | tf_op jit(solution)/shard_map/psum | solution.py:49
  314.1 3.0 fusion.47
  (70 shorter events, 22.3 us)
Async XLA Ops:
  6.5 80.0 %copy-start = (bf16[1024,1024]{1,0:T(8,128)(2,1)S(1)}, bf16[1024,1024]{1,0:T(8,128)(2,1)}, u32[]{:S(2)}) copy-start(bf16[1024,1024]{1,0:T(8,128)(2,1)} %param.14) | copy-start | bytes 6291460
  9.4 10.6 %all-to-all-start = ((bf16[4,256,128]{2,1,0:T(8,128)(2,1)}), bf16[4,256,128]{2,1,0:T(8,128)(2,1)S(1)}, u32[]{:S(2)}, u32[]{:S(2)}) async-start(bf16[4,256,128]{2,1,0:T(8,128)(2,1)} %copy.92), calls=%async_computation | async-start | bytes 524288 | tf_op jit(solution)/shard_map/all_to_all | solution.py:45
  14.6 72.0 %all-reduce.5.cloned.1.call-start = ((), (), s32[]{:S(2)}) async-start(), calls=%async_computation.4 | async-start | bytes 1048576 | tf_op jit(solution)/shard_map/psum | solution.py:49
  25.8 4.1 %copy-start.6 = (bf16[1,1024,128]{2,1,0:T(8,128)(2,1)S(1)}, bf16[1,1024,128]{2,1,0:T(8,128)(2,1)}, u32[]{:S(2)}) copy-start(bf16[1,1024,128]{2,1,0:T(8,128)(2,1)} %param.12) | copy-start | bytes 786436
  29.8 56.8 %copy-start.10 = (f32[1024]{0:T(1024)S(1)}, f32[1024]{0:T(1024)}, u32[]{:S(2)}) copy-start(f32[1024]{0:T(1024)} %param.15) | copy-start | bytes 12292
  29.8 132.9 %all-reduce.7.cloned.1.call-start = ((), (), s32[]{:S(2)}) async-start(), calls=%async_computation.5 | async-start | bytes 1048576 | tf_op jit(solution)/shard_map/psum | solution.py:49
  30.1 60.5 %collective-permute-start = (bf16[1024,128]{0,1:T(8,128)(2,1)S(1)}, bf16[1024,128]{0,1:T(8,128)(2,1)}, u32[]{:S(2)}, u32[]{:S(2)}) collective-permute-start(bf16[1024,128]{0,1:T(8,128)(2,1)S(1)} %bitcast.276), channel_id=1, source_target_pairs={{0,1},{1,2},{2,3},{3,4},{4,5},{5,6},{6,7},{8,9},{9,10},{10,11},{11... | collective-permute-start | bytes 786440 | tf_op jit(solution)/shard_map/ppermute | solution.py:13
  34.2 56.4 %copy-start.7 = (bf16[1,1024,128]{1,2,0:T(8,128)(2,1)S(1)}, bf16[1,1024,128]{1,2,0:T(8,128)(2,1)}, u32[]{:S(2)}) copy-start(bf16[1,1024,128]{1,2,0:T(8,128)(2,1)} %copy.63) | copy-start | bytes 786436
  94.7 9.7 %copy-start.1 = (bf16[1,4,3,256,256]{4,3,2,1,0:T(8,128)(2,1)S(1)}, bf16[1,4,3,256,256]{4,3,2,1,0:T(8,128)(2,1)}, u32[]{:S(2)}) copy-start(bf16[1,4,3,256,256]{4,3,2,1,0:T(8,128)(2,1)} %param.8) | copy-start | bytes 4718596
  108.7 130.1 %all-reduce.9.cloned.1.call-start = ((), (), s32[]{:S(2)}) async-start(), calls=%async_computation.6 | async-start | bytes 1048576 | tf_op jit(solution)/shard_map/psum | solution.py:49
  108.9 58.9 %collective-permute-start.1 = (bf16[1024,128]{0,1:T(8,128)(2,1)}, bf16[1024,128]{0,1:T(8,128)(2,1)}, u32[]{:S(2)}, u32[]{:S(2)}) collective-permute-start(bf16[1024,128]{0,1:T(8,128)(2,1)} %get-tuple-element.9), channel_id=1, source_target_pairs={{0,1},{1,2},{2,3},{3,4},{4,5},{5,6},{6,7},{8,9},{9,10},{10,11},{11... | collective-permute-start | bytes 786440 | tf_op jit(solution)/shard_map/ppermute | solution.py:13
  168.9 10.6 %copy-start.2 = (bf16[1,4,3,256,256]{4,3,2,1,0:T(8,128)(2,1)S(1)}, bf16[1,4,3,256,256]{4,3,2,1,0:T(8,128)(2,1)}, u32[]{:S(2)}) copy-start(bf16[1,4,3,256,256]{4,3,2,1,0:T(8,128)(2,1)} %param.8) | copy-start | bytes 4718596
  183.7 130.4 %all-reduce.11.cloned.1.call-start = ((), (), s32[]{:S(2)}) async-start(), calls=%async_computation.7 | async-start | bytes 1048576 | tf_op jit(solution)/shard_map/psum | solution.py:49
  183.9 60.5 %collective-permute-start.2 = (bf16[1024,128]{0,1:T(8,128)(2,1)S(1)}, bf16[1024,128]{0,1:T(8,128)(2,1)}, u32[]{:S(2)}, u32[]{:S(2)}) collective-permute-start(bf16[1024,128]{0,1:T(8,128)(2,1)S(1)} %broadcast_select_fusion.1), channel_id=1, source_target_pairs={{0,1},{1,2},{2,3},{3,4},{4,5},{5,6},{6,7},{8,9},{9,10},{10,11},{11... | collective-permute-start | bytes 786440 | tf_op jit(solution)/shard_map/ppermute | solution.py:13
  244.4 10.9 %copy-start.4 = (bf16[1024,128]{0,1:T(8,128)(2,1)}, bf16[1024,128]{0,1:T(8,128)(2,1)S(1)}, u32[]{:S(2)}) copy-start(bf16[1024,128]{0,1:T(8,128)(2,1)S(1)} %fusion.49) | copy-start | bytes 786436
  244.9 9.7 %copy-start.3 = (bf16[1,4,3,256,256]{4,3,2,1,0:T(8,128)(2,1)S(1)}, bf16[1,4,3,256,256]{4,3,2,1,0:T(8,128)(2,1)}, u32[]{:S(2)}) copy-start(bf16[1,4,3,256,256]{4,3,2,1,0:T(8,128)(2,1)} %param.8) | copy-start | bytes 4718596
  314.1 3.1 copy-start.9
  317.2 1.0 copy-start.5
  317.2 1.0 copy-start.8
Sparse Core Ops, SparseCore 0:
  30.0 56.5 all-reduce.4
  108.8 53.9 all-reduce.6
  183.8 54.8 all-reduce.8
  258.9 55.0 all-reduce.10
where the time goes:
time: 327 us; the launch traced here: 326 us
  waiting for transfers between devices  216 us (66%)
  matrix products  40.7 us (12%)
  blocking collectives  27.8 us (9%)
  local copies, waits for them, and re-layouts  15.7 us (5%)
  between operations  13.4 us (4%)
  starting transfers between devices  11.3 us (3%)
    psum x4, waiting for transfers between devices, local(): total_field = lax.psum(partial_value, 'delay')  212 us
    all_to_all x3, blocking collectives, local(): lax.all_to_all(stacked, 'group', split_axis=0, concat_axis=0, tiled=True)  27.8 us
    dot_general x8, matrix products, local(): jnp.dot(self_block, iterate.astype(jnp.bfloat16), preferred_element_type=...  21.3 us
    dot_general x4, matrix products, local(): jnp.einsum('hlr,hlic->ric', select, terms, precision=lax.Precision.HIGHEST)  10.8 us
  transfers between devices with their start and end apart: 8, of which 5 were waited for; matrix products, arithmetic and copies ran while one was open for 6% of the time, Pallas kernels for 0%

commit v1 on v0

v1 whole, which is shorter than its diff:
```python
import functools

import jax
import jax.numpy as jnp
from jax import lax
from jax.experimental import pallas as pl
from jax.experimental.pallas import tpu as pltpu
from jax.sharding import PartitionSpec as P

STEPS = 4

F32 = jnp.float32
BF16 = jnp.bfloat16
VMEM = pl.BlockSpec(memory_space=pltpu.VMEM)
SMEM = pl.BlockSpec(memory_space=pltpu.SMEM)


def peer_of(group, hop, groups):
    return group ^ hop if groups & (groups - 1) == 0 else (group + hop) % groups


def source_of(group, hop, groups):
    return group ^ hop if groups & (groups - 1) == 0 else (group - hop) % groups


def call(kernel, out_shape, scalars, arrays, scratch=()):
    return pl.pallas_call(
        kernel,
        out_shape=out_shape,
        in_specs=[SMEM] * len(scalars) + [VMEM] * len(arrays),
        out_specs=jax.tree.map(lambda _: VMEM, out_shape),
        scratch_shapes=list(scratch),
    )(*scalars, *arrays)


def dot(a, b):
    return jnp.dot(a, b, preferred_element_type=F32)


def pick_kernel(groups, block, parts, place, picks, *refs):
    sources, outs = refs[:parts], refs[parts:]
    me = place[0]
    for hop in range(groups):
        start = pl.multiple_of(picks[me, peer_of(me, hop, groups)] * block, block)
        for part in range(parts):
            outs[hop][part * block : (part + 1) * block, :] = sources[part][pl.ds(start, block), :]


def dense_kernel(groups, block, depth, place, rows, counts, weights, dense):
    me = place[0]
    dense[...] = jnp.zeros_like(dense)
    for hop in range(groups):
        source = source_of(me, hop, groups)
        for entry in range(depth):

            @pl.when(entry < counts[0, source])
            def _():
                start = pl.multiple_of(rows[source, entry] * block, block)
                dense[pl.ds(start, block), hop * block : (hop + 1) * block] = weights[source, entry]


def sheet_kernel(self_block, column, row, dense, sheet, moved):
    scaled = self_block[...].astype(F32) * column[...]
    first = scaled.astype(BF16)
    second = dot(first, first)
    total = second - scaled
    third = dot(second.astype(BF16), first)
    sheet[...] = ((total - third) * row[...]).astype(BF16)
    width = sheet.shape[1]
    for start in range(0, dense.shape[1], width):
        size = min(width, dense.shape[1] - start)
        part = dense[:, start : start + size]
        moved[:, start : start + size] = (dot(sheet[...], part) + part.astype(F32) * column[...]).astype(BF16)


def product(matrix, blocks, part, block):
    total = None
    for hop, ref in enumerate(blocks):
        term = dot(matrix[:, hop * block : (hop + 1) * block], ref[part * block : (part + 1) * block, :])
        total = term if total is None else total + term
    return total


def term_kernel(groups, block, parts, matrix, *refs):
    blocks, out = refs[:groups], refs[groups]
    rows = matrix.shape[0]
    for part in range(parts):
        out[part * rows : (part + 1) * rows, :] = product(matrix, blocks, part, block).astype(out.dtype)


def driven_kernel(steps, sheet, column, incident, out):
    for step in range(1, steps):
        field = incident[step]
        out[step - 1] = field.astype(F32) * column[...] + dot(sheet[...], field)


def emit(groups, block, place, picks, current, passed, now, sends):
    @pl.when(place[1] == 0)
    def _():
        now[...] = current

    if passed is not None:

        @pl.when(place[1] != 0)
        def _():
            now[...] = passed

    else:

        @pl.when(place[1] != 0)
        def _():
            now[...] = jnp.zeros_like(now)

    me = place[0]
    for hop in range(len(sends)):
        start = pl.multiple_of(picks[me, peer_of(me, hop, groups)] * block, block)
        sends[hop][...] = now[pl.ds(start, block), :]


def first_kernel(groups, block, fields, place, picks, sheet, column, incident, *refs):
    terms, now, sends = refs[:fields], refs[fields], refs[fields + 1 :]
    total = terms[0][...].astype(F32)
    for ref in terms[1:]:
        total = total + ref[...].astype(F32)
    driving = incident[0].astype(F32) - total
    current = driving * column[...] + dot(sheet[...], driving.astype(BF16))
    emit(groups, block, place, picks, current.astype(BF16), None, now, sends)


def next_kernel(groups, block, fields, shifts, matrix_here, place, picks, driven, own, *refs):
    refs = list(refs)
    take = lambda count: [refs.pop(0) for _ in range(count)]
    blocks = take(groups) if matrix_here else []
    terms, passed = take(fields), take(shifts)
    now, sends = refs[0], refs[1:]
    value = driven[...] - (product(own, blocks, 0, block) if matrix_here else own[...])
    for ref in terms:
        value = value - ref[...].astype(F32)
    shifted = None
    for ref in passed:
        shifted = ref[...] if shifted is None else shifted + ref[...]
    emit(groups, block, place, picks, value.astype(BF16), shifted, now, sends)


def both_kernel(groups, block, matrix, *refs):
    blocks, wide, narrow = refs[:groups], refs[groups], refs[groups + 1]
    total = product(matrix, blocks, 0, block)
    wide[...] = total
    narrow[...] = total.astype(BF16)


def local(retarded, block_row, block_count, send_pick, history, incident, self_block, sheet_diag):
    groups = lax.axis_size("group")
    delays = lax.axis_size("delay")
    chips = delays // 2
    group_index = lax.axis_index("group")
    delay_index = lax.axis_index("delay")
    place = jnp.stack([group_index, delay_index]).astype(jnp.int32)
    weights = retarded[0]
    depth, block = weights.shape[1], weights.shape[-1]
    rows, columns = history.shape[1:]
    picks = send_pick[0]
    inverse = 1.0 / sheet_diag
    column, row = inverse[:, None], inverse[None, :]
    shape = jax.ShapeDtypeStruct
    piece = lambda parts=1: shape((parts * block, columns), BF16)

    def along(array, pairs):
        return lax.ppermute(array, "delay", pairs)

    def exchange(sends):
        return [sends[0]] + [
            lax.ppermute(sends[hop], "group", [(g, peer_of(g, hop, groups)) for g in range(groups)])
            for hop in range(1, groups)
        ]

    def picked(arrays):
        parts = len(arrays)
        return call(
            functools.partial(pick_kernel, groups, block, parts),
            [piece(parts)] * groups, (place, picks), arrays,
        )

    def plus(a, b):
        return (a.astype(F32) + b.astype(F32)).astype(BF16)

    def chip_sum(term):
        return plus(term, along(term, [(2 * z + 1, 2 * z) for z in range(chips)]))

    def chip_tree(term):
        stride = 1
        while stride < chips:
            pairs = [(2 * z, 2 * (z - stride)) for z in range(stride, chips, 2 * stride)]
            term = plus(term, along(term, pairs))
            stride *= 2
        return term

    def spread(current):
        return [along(current, [(0, 2 * z)]) for z in range(1, chips)]

    blocks = exchange(picked([history[0]]))
    shifted = []
    moving = history[0]
    for _ in range(1, STEPS):
        moving = along(moving, [(d, d + 1) for d in range(delays - 1)])
        shifted.append(moving)
    dense = call(
        functools.partial(dense_kernel, groups, block, depth),
        shape((rows, groups * block), BF16),
        (place, block_row[0], block_count), (weights,),
    )
    term = call(
        functools.partial(term_kernel, groups, block, 1), shape((rows, columns), BF16), (), (dense, *blocks)
    )
    chip = chip_sum(term)
    fields = [chip] + [along(chip, [(2 * z, 0)]) for z in range(1, chips)]

    sheet, matrix = call(
        sheet_kernel,
        (shape((rows, rows), BF16), shape((rows, groups * block), BF16)),
        (), (self_block, column, row, dense),
    )
    driven = call(
        functools.partial(driven_kernel, STEPS), shape((STEPS - 1, rows, columns), F32), (), (sheet, column, incident)
    )

    later = []
    for parts in ((shifted[0],), tuple(shifted[1:])):
        blocks = exchange(picked(list(parts)))
        term = call(
            functools.partial(term_kernel, groups, block, len(parts)),
            shape((len(parts) * rows, columns), BF16), (), (matrix, *blocks),
        )
        total = chip_tree(chip_sum(term))
        later += [total[k * rows : (k + 1) * rows] for k in range(len(parts))]

    whole = shape((rows, columns), BF16)
    outs = [whole] + [piece()] * groups
    current, *sends = call(
        functools.partial(first_kernel, groups, block, len(fields)),
        outs, (place, picks), (sheet, column, incident, *fields),
    )
    found = [current]
    near = along(current, [(0, 1)])
    spreads = [spread(current)]
    blocks = exchange(sends)
    current, *sends = call(
        functools.partial(next_kernel, groups, block, 1, 2, True),
        outs, (place, picks), (driven[0], matrix, *blocks, later[0], near, spreads[0][0]),
    )
    found.append(current)
    near = along(current, [(0, 1)])
    spreads.append(spread(current))

    blocks = exchange(sends)
    wide, narrow = call(
        functools.partial(both_kernel, groups, block), (shape((rows, columns), F32), whole), (), (matrix, *blocks)
    )
    from_next = along(narrow, [(1, 0)])
    from_second = along(narrow, [(2, 0)])
    current, *sends = call(
        functools.partial(next_kernel, groups, block, 2, 1, False),
        outs, (place, picks), (driven[1], wide, later[1], from_next, near),
    )
    found.append(current)
    spreads.append(spread(current))

    blocks = exchange(sends)
    wide, narrow = call(
        functools.partial(both_kernel, groups, block), (shape((rows, columns), F32), whole), (), (matrix, *blocks)
    )
    from_next = along(narrow, [(1, 0)])
    (current,) = call(
        functools.partial(next_kernel, groups, block, 3, 0, False),
        [whole], (place, picks), (driven[2], wide, later[2], from_next, from_second),
    )
    found.append(current)
    spreads.append(spread(current))

    results = []
    for current, copies in zip(found, spreads):
        far = functools.reduce(lambda a, b: a + b, copies)
        held = jnp.where(delay_index == 0, current, far)
        partner = along(held, [(2 * z, 2 * z + 1) for z in range(chips)])
        results.append(jnp.where(delay_index % 2 == 0, held, partner))
    return jnp.stack(results)


def solution(mesh):
    placed = (
        P("delay", "group", None, None, None),
        P("delay", "group", None),
        P("delay", "group"),
        P("delay", None, None),
        P("delay", "group", None),
        P(None, "group", None),
        P("group", None),
        P("group"),
    )
    return jax.shard_map(
        local, mesh=mesh, in_specs=placed, out_specs=P(None, "group", None), check_vma=False
    )
```

time: 327 us -> 181 us (0.55)
  waiting for transfers between devices: 216 us -> 19.2 us
  starting transfers between devices: 11.3 us -> 89.5 us
  Pallas kernels: 0 us -> 52.8 us
  matrix products: 40.7 us -> 0 us
  blocking collectives: 27.8 us -> 0 us
  between operations: 13.4 us -> 0.92 us
  other arithmetic: 0.87 us -> 6.09 us
  local copies, waits for them, and re-layouts: 15.7 us -> 11.3 us
    psum x4 -> x0, waiting for transfers between devices: 212 us -> none  [local(): total_field = lax.psum(partial_value, 'delay')]
    ppermute x3 -> x52, starting transfers between devices: 6.02 us -> 89.5 us  [the longest x34 67.5 us: along(): return lax.ppermute(array, 'delay', pairs)]
    pallas_call x0 -> x15, Pallas kernels: none -> 52.8 us  [call(): pl.pallas_call(kernel, out_shape=out_shape, in_specs=[SMEM] * len(scalars...]
    dot_general x20 -> x0, matrix products: 40.7 us -> none  [the longest x8 21.3 us: local(): jnp.dot(self_block, iterate.astype(jnp.bfloat16), preferred_element_type=...]
    all_to_all x3 -> x0, blocking collectives: 27.8 us -> none  [local(): lax.all_to_all(stacked, 'group', split_axis=0, concat_axis=0, tiled=True)]
    ppermute x3 -> x52, waiting for transfers between devices: 0.01 us -> 19.2 us  [the longest x34 17.1 us: along(): return lax.ppermute(array, 'delay', pairs)]
    all_to_all x1 -> x0, starting transfers between devices: 5.19 us -> none  [local(): lax.all_to_all(stacked, 'group', split_axis=0, concat_axis=0, tiled=True)]
    all_to_all x1 -> x0, waiting for transfers between devices: 4.03 us -> none  [local(): lax.all_to_all(stacked, 'group', split_axis=0, concat_axis=0, tiled=True)]
  transfers between devices with their start and end apart: 8 -> 52, of which waited for: 5 -> 12; matrix products, arithmetic and copies ran while one was open for 6% -> 5% of each run, Pallas kernels for 0% -> 28%
where the time goes in v1:
time: 181 us; the launch traced here: 180 us
  starting transfers between devices  89.5 us (49%)
  Pallas kernels  52.8 us (29%)
  waiting for transfers between devices  19.2 us (11%)
  local copies, waits for them, and re-layouts  11.3 us (6%)
  other arithmetic  6.09 us (3%)
    ppermute x34, starting transfers between devices, along(): return lax.ppermute(array, 'delay', pairs)  67.5 us
    pallas_call x15, Pallas kernels, call(): pl.pallas_call(kernel, out_shape=out_shape, in_specs=[SMEM] * len(scalars...  52.8 us
    ppermute x18, starting transfers between devices, exchange(): lax.ppermute(sends[hop], 'group', [(g, peer_of(g, hop, groups)) for g in...  22 us
    ppermute x34, waiting for transfers between devices, along(): return lax.ppermute(array, 'delay', pairs)  17.1 us
    unnamed x83, local copies, waits for them, and re-layouts  8.33 us
  transfers between devices with their start and end apart: 52, of which 12 were waited for; matrix products, arithmetic and copies ran while one was open for 5% of the time, Pallas kernels for 28%

profile of v1, /device:TPU:0, one launch (start us, length us, event | category | flops | bytes accessed | tf_op | source)
XLA Modules:
  0.0 179.9 jit_solution(17184292274693324667)
XLA Ops:
  0.0 2.4 %collective-permute-start.14 = (bf16[1024,128]{1,0:T(8,128)(2,1)}, bf16[1024,128]{1,0:T(8,128)(2,1)S(1)}, u32[]{:S(2)}, u32[]{:S(2)}) collective-permute-start(bf16[1024,128]{1,0:T(8,128)(2,1)} %bitcast.23), channel_id=1, source_target_pairs={{0,1},{1,2},{2,3},{3,4},{4,5},{5,6},{6,7},{8,9},{9,10},{10,11},{11... | collective-permute-start | bytes 786440 | tf_op jit(solution)/shard_map/ppermute | solution.py:169
  3.8 6.8 %collective-permute-start.29 = (bf16[1024,128]{1,0:T(8,128)(2,1)S(1)}, bf16[1024,128]{1,0:T(8,128)(2,1)S(1)}, u32[]{:S(2)}, u32[]{:S(2)}) collective-permute-start(bf16[1024,128]{1,0:T(8,128)(2,1)S(1)} %collective-permute-done.14.refs_0_), channel_id=1, source_target_pairs={{0,1},{1,2},{2,3},{3,4},{4,5},{5,6},{6,7},{8,9},{9,10},{10,11},{11... | collective-permute-start | bytes 786440 | tf_op jit(solution)/shard_map/ppermute | solution.py:169
  11.7 6.4 %collective-permute-start.30 = (bf16[1024,128]{1,0:T(8,128)(2,1)S(1)}, bf16[1024,128]{1,0:T(8,128)(2,1)S(1)}, u32[]{:S(2)}, u32[]{:S(2)}) collective-permute-start(bf16[1024,128]{1,0:T(8,128)(2,1)S(1)} %collective-permute-done.29.refs_0_), channel_id=1, source_target_pairs={{0,1},{1,2},{2,3},{3,4},{4,5},{5,6},{6,7},{8,9},{9,10},{10,11},{11... | collective-permute-start | bytes 786440 | tf_op jit(solution)/shard_map/ppermute | solution.py:169
  20.0 1.9 %shard_map.92 = (bf16[512,128]{1,0:T(8,128)(2,1)}, bf16[512,128]{1,0:T(8,128)(2,1)}, bf16[512,128]{1,0:T(8,128)(2,1)}, bf16[512,128]{1,0:T(8,128)(2,1)}) custom-call(s32[2]{0:T(128)} %pad_add_fusion.place, s32[4,4]{1,0:T(4,128)} %bitcast.25, bf16[1024,128]{1,0:T(8,128)(2,1)} %copy-done.15, bf16[1024,128]{1,0:T(8,128)(2,1)} %copy-done.16), custom_call_target="tpu_custom_call" | custom-call | tf_op jit(solution)/shard_map/pallas_call | solution.py:27
  33.7 3.1 %shard_map.82.dense.matrix = bf16[1024,1024]{1,0:T(8,128)(2,1)} custom-call(s32[2]{0:T(128)} %pad_add_fusion.place, s32[4,3]{1,0:T(4,128)} %bitcast.34, s32[1,4]{1,0:T(1,128)} %counts.1, bf16[4,3,256,256]{3,2,1,0:T(8,128)(2,1)} %bitcast.22), custom_call_target="tpu_custom_call" | custom-call | tf_op jit(solution)/shard_map/pallas_call | solution.py:27
  36.7 10.5 %shard_map.83 = (bf16[1024,1024]{1,0:T(8,128)(2,1)}, bf16[1024,1024]{1,0:T(8,128)(2,1)}) custom-call(bf16[1024,1024]{1,0:T(8,128)(2,1)} %self_block.1, f32[1024,1]{1,0:T(8,128)} %copy.11.column, f32[1,1024]{1,0:T(1,128)} %bitcast.33, bf16[1024,1024]{1,0:T(8,128)(2,1)} %shard_map.82.dense.matrix), custom_call_target="tpu_custom_call" | custom-call | tf_op jit(solution)/shard_map/pallas_call | solution.py:27
  48.0 3.8 %shard_map.93 = bf16[2048,128]{1,0:T(8,128)(2,1)} custom-call(bf16[1024,1024]{1,0:T(8,128)(2,1)} %get-tuple-element.44.matrix.own, bf16[512,128]{1,0:T(8,128)(2,1)} %get-tuple-element.59.refs_0_, bf16[512,128]{1,0:T(8,128)(2,1)} %copy-done.20, bf16[512,128]{1,0:T(8,128)(2,1)} %copy-done.21, bf16[512,128]{1,0:T(8,128)(2,1)} %copy-done.22), custom_call_target="tpu_custom_call" | custom-call | tf_op jit(solution)/shard_map/pallas_call | solution.py:27
  53.8 3.1 %shard_map.85 = bf16[1024,128]{1,0:T(8,128)(2,1)} custom-call(bf16[1024,1024]{1,0:T(8,128)(2,1)} %shard_map.82.dense.matrix, bf16[256,128]{1,0:T(8,128)(2,1)} %get-tuple-element.39.refs_0_, bf16[256,128]{1,0:T(8,128)(2,1)} %copy-done.26, bf16[256,128]{1,0:T(8,128)(2,1)} %copy-done.27, bf16[256,128]{1,0:T(8,128)(2,1)} %copy-done.28), custom_call_target="tpu_custom_call" | custom-call | tf_op jit(solution)/shard_map/pallas_call | solution.py:27
  69.1 3.1 %shard_map.89 = bf16[1024,128]{1,0:T(8,128)(2,1)} custom-call(bf16[1024,1024]{1,0:T(8,128)(2,1)} %get-tuple-element.44.matrix.own, bf16[256,128]{1,0:T(8,128)(2,1)} %get-tuple-element.49.refs_0_, bf16[256,128]{1,0:T(8,128)(2,1)} %copy-done.32, bf16[256,128]{1,0:T(8,128)(2,1)} %copy-done.33, bf16[256,128]{1,0:T(8,128)(2,1)} %copy-done.35), custom_call_target="tpu_custom_call" | custom-call | tf_op jit(solution)/shard_map/pallas_call | solution.py:27
  78.3 5.0 %shard_map.87 = f32[3,1024,128]{2,1,0:T(8,128)} custom-call(bf16[1024,1024]{1,0:T(8,128)(2,1)} %get-tuple-element.38.sheet, f32[1024,1]{1,0:T(8,128)} %copy.11.column, bf16[4,1024,128]{2,1,0:T(8,128)(2,1)} %incident.3), custom_call_target="tpu_custom_call" | custom-call | tf_op jit(solution)/shard_map/pallas_call | solution.py:27
  84.8 3.9 %shard_map.86 = (bf16[1024,128]{1,0:T(8,128)(2,1)}, bf16[256,128]{1,0:T(8,128)(2,1)}, bf16[256,128]{1,0:T(8,128)(2,1)}, bf16[256,128]{1,0:T(8,128)(2,1)}, bf16[256,128]{1,0:T(8,128)(2,1)}) custom-call(s32[2]{0:T(128)} %pad_add_fusion.place, s32[4,4]{1,0:T(4,128)} %bitcast.28, bf16[1024,1024]{1,0:T(8,128)(2,1)} %get-tuple-element.38.sheet, ...), custom_call_target="tpu_custom_call" | custom-call | tf_op jit(solution)/shard_map/pallas_call | solution.py:27
  88.7 9.2 %collective-permute-start.7 = (bf16[1024,128]{1,0:T(8,128)(2,1)}, bf16[1024,128]{1,0:T(8,128)(2,1)S(1)}, u32[]{:S(2)}, u32[]{:S(2)}) collective-permute-start(bf16[1024,128]{1,0:T(8,128)(2,1)} %get-tuple-element.43), channel_id=1, source_target_pairs={{0,2},{8,10},{16,18},{24,26}} | collective-permute-start | bytes 786440 | tf_op jit(solution)/shard_map/ppermute | solution.py:169
  105.8 3.5 %collective-permute-done.20 = bf16[1024,128]{1,0:T(8,128)(2,1)S(1)} collective-permute-done((bf16[1024,128]{1,0:T(8,128)(2,1)S(1)}, bf16[1024,128]{1,0:T(8,128)(2,1)S(1)}, u32[]{:S(2)}, u32[]{:S(2)}) %collective-permute-start.20) | collective-permute-done | bytes 262176 | tf_op jit(solution)/shard_map/ppermute | solution.py:169
  109.3 2.4 %collective-permute-start.13 = (bf16[256,128]{1,0:T(8,128)(2,1)S(1)}, bf16[256,128]{1,0:T(8,128)(2,1)S(1)}, u32[]{:S(2)}, u32[]{:S(2)}) collective-permute-start(bf16[256,128]{1,0:T(8,128)(2,1)S(1)} %copy-done.39), channel_id=1, source_target_pairs={{0,24},{8,16},{16,8},{24,0},{1,25},{9,17},{17,9},{25,1},{2,26},{10... | collective-permute-start | bytes 196616 | tf_op jit(solution)/shard_map/ppermute | solution.py:173
  112.4 2.0 %collective-permute-done.13.refs_3_ = bf16[256,128]{1,0:T(8,128)(2,1)S(1)} collective-permute-done((bf16[256,128]{1,0:T(8,128)(2,1)S(1)}, bf16[256,128]{1,0:T(8,128)(2,1)S(1)}, u32[]{:S(2)}, u32[]{:S(2)}) %collective-permute-start.13) | collective-permute-done | bytes 65568 | tf_op jit(solution)/shard_map/ppermute | solution.py:173
  115.3 3.6 %shard_map.90 = (bf16[1024,128]{1,0:T(8,128)(2,1)}, bf16[256,128]{1,0:T(8,128)(2,1)}, bf16[256,128]{1,0:T(8,128)(2,1)}, bf16[256,128]{1,0:T(8,128)(2,1)}, bf16[256,128]{1,0:T(8,128)(2,1)}) custom-call(s32[2]{0:T(128)} %pad_add_fusion.place, s32[4,4]{1,0:T(4,128)} %bitcast.29, f32[1024,128]{1,0:T(8,128)} %get-tuple-element.71.driven, ...), custom_call_target="tpu_custom_call" | custom-call | tf_op jit(solution)/shard_map/pallas_call | solution.py:27
  122.4 2.7 %collective-permute-start.8 = (bf16[1024,128]{1,0:T(8,128)(2,1)S(1)}, bf16[1024,128]{1,0:T(8,128)(2,1)S(1)}, u32[]{:S(2)}, u32[]{:S(2)}) collective-permute-start(bf16[1024,128]{1,0:T(8,128)(2,1)S(1)} %copy-done.7), channel_id=1, source_target_pairs={{0,4},{8,12},{16,20},{24,28}} | collective-permute-start | bytes 786440 | tf_op jit(solution)/shard_map/ppermute | solution.py:169
  128.4 3.3 %shard_map.91 = (f32[1024,128]{1,0:T(8,128)}, bf16[1024,128]{1,0:T(8,128)(2,1)}) custom-call(bf16[1024,1024]{1,0:T(8,128)(2,1)} %get-tuple-element.44.matrix.own, bf16[256,128]{1,0:T(8,128)(2,1)} %get-tuple-element.54.refs_0_, bf16[256,128]{1,0:T(8,128)(2,1)} %copy-done.34, bf16[256,128]{1,0:T(8,128)(2,1)} %copy-done.36, bf16[256,128]{1,0:T(8,128)(2,1)} %copy-done.37), custom_call_target="tpu_custom_call" | custom-call | tf_op jit(solution)/shard_map/pallas_call | solution.py:27
  136.1 2.5 %shard_map.94 = (bf16[1024,128]{1,0:T(8,128)(2,1)}, bf16[256,128]{1,0:T(8,128)(2,1)}, bf16[256,128]{1,0:T(8,128)(2,1)}, bf16[256,128]{1,0:T(8,128)(2,1)}, bf16[256,128]{1,0:T(8,128)(2,1)}) custom-call(s32[2]{0:T(128)} %pad_add_fusion.place, s32[4,4]{1,0:T(4,128)} %bitcast.30, f32[1024,128]{1,0:T(8,128)} %get-tuple-element.73.driven, ...), custom_call_target="tpu_custom_call" | custom-call | tf_op jit(solution)/shard_map/pallas_call | solution.py:27
  146.8 3.2 %shard_map.95 = (f32[1024,128]{1,0:T(8,128)}, bf16[1024,128]{1,0:T(8,128)(2,1)}) custom-call(bf16[1024,1024]{1,0:T(8,128)(2,1)} %get-tuple-element.44.matrix.own, bf16[256,128]{1,0:T(8,128)(2,1)} %get-tuple-element.65.refs_0_, bf16[256,128]{1,0:T(8,128)(2,1)} %copy-done.29, bf16[256,128]{1,0:T(8,128)(2,1)} %copy-done.30, bf16[256,128]{1,0:T(8,128)(2,1)} %copy-done.31), custom_call_target="tpu_custom_call" | custom-call | tf_op jit(solution)/shard_map/pallas_call | solution.py:27
  154.0 2.7 %collective-permute-start.39 = (bf16[1024,128]{1,0:T(8,128)(2,1)S(1)}, bf16[1024,128]{1,0:T(8,128)(2,1)S(1)}, u32[]{:S(2)}, u32[]{:S(2)}) collective-permute-start(bf16[1024,128]{1,0:T(8,128)(2,1)S(1)} %copy-done.8), channel_id=1, source_target_pairs={{0,2},{8,10},{16,18},{24,26}} | collective-permute-start | bytes 786440 | tf_op jit(solution)/shard_map/ppermute | solution.py:169
  159.4 2.4 %shard_map.96 = bf16[1024,128]{1,0:T(8,128)(2,1)} custom-call(s32[2]{0:T(128)} %pad_add_fusion.place, s32[4,4]{1,0:T(4,128)} %bitcast.31, f32[1024,128]{1,0:T(8,128)} %get-tuple-element.72.driven, f32[1024,128]{1,0:T(8,128)} %get-tuple-element.69.own, bf16[1024,128]{1,0:T(8,128)(2,1)} %get-tuple-element.74.refs_0_, bf16[1024,128]{1,0:T(8,128)(2,1)} %copy-done.19, ...), custom_call_target="tpu_custom_call" | custom-call | tf_op jit(solution)/shard_map/pallas_call | solution.py:27
  170.7 2.8 %collective-permute-done.49 = bf16[1024,128]{1,0:T(8,128)(2,1)S(1)} collective-permute-done((bf16[1024,128]{1,0:T(8,128)(2,1)}, bf16[1024,128]{1,0:T(8,128)(2,1)S(1)}, u32[]{:S(2)}, u32[]{:S(2)}) %collective-permute-start.49) | collective-permute-done | bytes 262176 | tf_op jit(solution)/shard_map/ppermute | solution.py:169
  173.5 2.8 %collective-permute-done.50 = bf16[1024,128]{1,0:T(8,128)(2,1)S(1)} collective-permute-done((bf16[1024,128]{1,0:T(8,128)(2,1)}, bf16[1024,128]{1,0:T(8,128)(2,1)S(1)}, u32[]{:S(2)}, u32[]{:S(2)}) %collective-permute-start.50) | collective-permute-done | bytes 262176 | tf_op jit(solution)/shard_map/ppermute | solution.py:169
  (199 shorter events, 85.8 us)
Async XLA Ops:
  25.1 28.0 %collective-permute-start = (bf16[256,128]{1,0:T(8,128)(2,1)}, bf16[256,128]{1,0:T(8,128)(2,1)S(1)}, u32[]{:S(2)}, u32[]{:S(2)}) collective-permute-start(bf16[256,128]{1,0:T(8,128)(2,1)} %get-tuple-element.40), channel_id=1, source_target_pairs={{0,8},{8,0},{16,24},{24,16},{1,9},{9,1},{17,25},{25,17},{2,10},{10... | collective-permute-start | bytes 196616 | tf_op jit(solution)/shard_map/ppermute | solution.py:173
  25.6 27.5 %collective-permute-start.1 = (bf16[256,128]{1,0:T(8,128)(2,1)}, bf16[256,128]{1,0:T(8,128)(2,1)S(1)}, u32[]{:S(2)}, u32[]{:S(2)}) collective-permute-start(bf16[256,128]{1,0:T(8,128)(2,1)} %get-tuple-element.41), channel_id=1, source_target_pairs={{0,16},{8,24},{16,0},{24,8},{1,17},{9,25},{17,1},{25,9},{2,18},{10... | collective-permute-start | bytes 196616 | tf_op jit(solution)/shard_map/ppermute | solution.py:173
  27.2 26.0 %collective-permute-start.2 = (bf16[256,128]{1,0:T(8,128)(2,1)}, bf16[256,128]{1,0:T(8,128)(2,1)S(1)}, u32[]{:S(2)}, u32[]{:S(2)}) collective-permute-start(bf16[256,128]{1,0:T(8,128)(2,1)} %get-tuple-element.42), channel_id=1, source_target_pairs={{0,24},{8,16},{16,8},{24,0},{1,25},{9,17},{17,9},{25,1},{2,26},{10... | collective-permute-start | bytes 196616 | tf_op jit(solution)/shard_map/ppermute | solution.py:173
  28.6 18.7 %collective-permute-start.32 = (bf16[512,128]{1,0:T(8,128)(2,1)}, bf16[512,128]{1,0:T(8,128)(2,1)S(1)}, u32[]{:S(2)}, u32[]{:S(2)}) collective-permute-start(bf16[512,128]{1,0:T(8,128)(2,1)} %get-tuple-element.61), channel_id=1, source_target_pairs={{0,16},{8,24},{16,0},{24,8},{1,17},{9,25},{17,1},{25,9},{2,18},{10... | collective-permute-start | bytes 393224 | tf_op jit(solution)/shard_map/ppermute | solution.py:173
  30.1 17.1 %collective-permute-start.33 = (bf16[512,128]{1,0:T(8,128)(2,1)}, bf16[512,128]{1,0:T(8,128)(2,1)S(1)}, u32[]{:S(2)}, u32[]{:S(2)}) collective-permute-start(bf16[512,128]{1,0:T(8,128)(2,1)} %get-tuple-element.62), channel_id=1, source_target_pairs={{0,24},{8,16},{16,8},{24,0},{1,25},{9,17},{17,9},{25,1},{2,26},{10... | collective-permute-start | bytes 393224 | tf_op jit(solution)/shard_map/ppermute | solution.py:173
  51.8 21.7 %collective-permute-start.34 = (bf16[2048,128]{1,0:T(8,128)(2,1)}, bf16[2048,128]{1,0:T(8,128)(2,1)S(1)}, u32[]{:S(2)}, u32[]{:S(2)}) collective-permute-start(bf16[2048,128]{1,0:T(8,128)(2,1)} %shard_map.93), channel_id=1, source_target_pairs={{1,0},{3,2},{5,4},{7,6},{9,8},{11,10},{13,12},{15,14},{17,16},{19,... | collective-permute-start | bytes 1572872 | tf_op jit(solution)/shard_map/ppermute | solution.py:169
  64.5 18.7 %collective-permute-start.4 = (bf16[1024,128]{1,0:T(8,128)(2,1)S(1)}, bf16[1024,128]{1,0:T(8,128)(2,1)S(1)}, u32[]{:S(2)}, u32[]{:S(2)}) collective-permute-start(bf16[1024,128]{1,0:T(8,128)(2,1)S(1)} %add_convert_fusion.6.refs_0_), channel_id=1, source_target_pairs={{2,0},{10,8},{18,16},{26,24}} | collective-permute-start | bytes 786440 | tf_op jit(solution)/shard_map/ppermute | solution.py:169
  65.9 17.4 %collective-permute-start.5 = (bf16[1024,128]{1,0:T(8,128)(2,1)S(1)}, bf16[1024,128]{1,0:T(8,128)(2,1)S(1)}, u32[]{:S(2)}, u32[]{:S(2)}) collective-permute-start(bf16[1024,128]{1,0:T(8,128)(2,1)S(1)} %add_convert_fusion.6.refs_0_), channel_id=1, source_target_pairs={{4,0},{12,8},{20,16},{28,24}} | collective-permute-start | bytes 786440 | tf_op jit(solution)/shard_map/ppermute | solution.py:169
  67.2 16.1 %collective-permute-start.6 = (bf16[1024,128]{1,0:T(8,128)(2,1)S(1)}, bf16[1024,128]{1,0:T(8,128)(2,1)S(1)}, u32[]{:S(2)}, u32[]{:S(2)}) collective-permute-start(bf16[1024,128]{1,0:T(8,128)(2,1)S(1)} %add_convert_fusion.6.refs_0_), channel_id=1, source_target_pairs={{6,0},{14,8},{22,16},{30,24}} | collective-permute-start | bytes 786440 | tf_op jit(solution)/shard_map/ppermute | solution.py:169
  73.7 27.9 %collective-permute-start.35 = (bf16[2048,128]{1,0:T(8,128)(2,1)S(1)}, bf16[2048,128]{1,0:T(8,128)(2,1)S(1)}, u32[]{:S(2)}, u32[]{:S(2)}) collective-permute-start(bf16[2048,128]{1,0:T(8,128)(2,1)S(1)} %add_convert_fusion.2), channel_id=1, source_target_pairs={{2,0},{6,4},{10,8},{14,12},{18,16},{22,20},{26,24},{30,28}} | collective-permute-start | bytes 1572872 | tf_op jit(solution)/shard_map/ppermute | solution.py:169
  77.0 22.9 %collective-permute-start.19 = (bf16[1024,128]{1,0:T(8,128)(2,1)S(1)}, bf16[1024,128]{1,0:T(8,128)(2,1)S(1)}, u32[]{:S(2)}, u32[]{:S(2)}) collective-permute-start(bf16[1024,128]{1,0:T(8,128)(2,1)S(1)} %add_convert_fusion.5), channel_id=1, source_target_pairs={{2,0},{6,4},{10,8},{14,12},{18,16},{22,20},{26,24},{30,28}} | collective-permute-start | bytes 786440 | tf_op jit(solution)/shard_map/ppermute | solution.py:169
  88.7 25.7 %collective-permute-start.7 = (bf16[1024,128]{1,0:T(8,128)(2,1)}, bf16[1024,128]{1,0:T(8,128)(2,1)S(1)}, u32[]{:S(2)}, u32[]{:S(2)}) collective-permute-start(bf16[1024,128]{1,0:T(8,128)(2,1)} %get-tuple-element.43), channel_id=1, source_target_pairs={{0,2},{8,10},{16,18},{24,26}} | collective-permute-start | bytes 786440 | tf_op jit(solution)/shard_map/ppermute | solution.py:169
  97.9 16.5 %collective-permute-start.21 = (bf16[1024,128]{1,0:T(8,128)(2,1)}, bf16[1024,128]{1,0:T(8,128)(2,1)S(1)}, u32[]{:S(2)}, u32[]{:S(2)}) collective-permute-start(bf16[1024,128]{1,0:T(8,128)(2,1)} %get-tuple-element.43), channel_id=1, source_target_pairs={{0,1},{8,9},{16,17},{24,25}} | collective-permute-start | bytes 786440 | tf_op jit(solution)/shard_map/ppermute | solution.py:169
  101.7 31.3 %collective-permute-start.36 = (bf16[2048,128]{1,0:T(8,128)(2,1)S(1)}, bf16[2048,128]{1,0:T(8,128)(2,1)S(1)}, u32[]{:S(2)}, u32[]{:S(2)}) collective-permute-start(bf16[2048,128]{1,0:T(8,128)(2,1)S(1)} %add_convert_fusion.1), channel_id=1, source_target_pairs={{4,0},{12,8},{20,16},{28,24}} | collective-permute-start | bytes 1572872 | tf_op jit(solution)/shard_map/ppermute | solution.py:169
  122.4 19.7 %collective-permute-start.8 = (bf16[1024,128]{1,0:T(8,128)(2,1)S(1)}, bf16[1024,128]{1,0:T(8,128)(2,1)S(1)}, u32[]{:S(2)}, u32[]{:S(2)}) collective-permute-start(bf16[1024,128]{1,0:T(8,128)(2,1)S(1)} %copy-done.7), channel_id=1, source_target_pairs={{0,4},{8,12},{16,20},{24,28}} | collective-permute-start | bytes 786440 | tf_op jit(solution)/shard_map/ppermute | solution.py:169
  125.1 17.0 %collective-permute-start.9 = (bf16[1024,128]{1,0:T(8,128)(2,1)S(1)}, bf16[1024,128]{1,0:T(8,128)(2,1)S(1)}, u32[]{:S(2)}, u32[]{:S(2)}) collective-permute-start(bf16[1024,128]{1,0:T(8,128)(2,1)S(1)} %copy-done.7), channel_id=1, source_target_pairs={{0,6},{8,14},{16,22},{24,30}} | collective-permute-start | bytes 786440 | tf_op jit(solution)/shard_map/ppermute | solution.py:169
  142.2 10.5 %collective-permute-start.10 = (bf16[1024,128]{1,0:T(8,128)(2,1)S(1)}, bf16[1024,128]{1,0:T(8,128)(2,1)S(1)}, u32[]{:S(2)}, u32[]{:S(2)}) collective-permute-start(bf16[1024,128]{1,0:T(8,128)(2,1)S(1)} %add_select_fusion.3), channel_id=1, source_target_pairs={{0,1},{2,3},{4,5},{6,7},{8,9},{10,11},{12,13},{14,15},{16,17},{18,... | collective-permute-start | bytes 786440 | tf_op jit(solution)/shard_map/ppermute | solution.py:169
  143.5 10.5 %collective-permute-start.22 = (bf16[1024,128]{1,0:T(8,128)(2,1)S(1)}, bf16[1024,128]{1,0:T(8,128)(2,1)S(1)}, u32[]{:S(2)}, u32[]{:S(2)}) collective-permute-start(bf16[1024,128]{1,0:T(8,128)(2,1)S(1)} %copy-done.6), channel_id=1, source_target_pairs={{0,2},{8,10},{16,18},{24,26}} | collective-permute-start | bytes 786440 | tf_op jit(solution)/shard_map/ppermute | solution.py:169
  144.8 11.9 %collective-permute-start.47 = (bf16[1024,128]{1,0:T(8,128)(2,1)}, bf16[1024,128]{1,0:T(8,128)(2,1)S(1)}, u32[]{:S(2)}, u32[]{:S(2)}) collective-permute-start(bf16[1024,128]{1,0:T(8,128)(2,1)} %get-tuple-element.63), channel_id=1, source_target_pairs={{2,0},{10,8},{18,16},{26,24}} | collective-permute-start | bytes 786440 | tf_op jit(solution)/shard_map/ppermute | solution.py:169
  151.3 10.5 %collective-permute-start.23 = (bf16[1024,128]{1,0:T(8,128)(2,1)S(1)}, bf16[1024,128]{1,0:T(8,128)(2,1)S(1)}, u32[]{:S(2)}, u32[]{:S(2)}) collective-permute-start(bf16[1024,128]{1,0:T(8,128)(2,1)S(1)} %copy-done.6), channel_id=1, source_target_pairs={{0,4},{8,12},{16,20},{24,28}} | collective-permute-start | bytes 786440 | tf_op jit(solution)/shard_map/ppermute | solution.py:169
  152.7 10.7 %collective-permute-start.24 = (bf16[1024,128]{1,0:T(8,128)(2,1)S(1)}, bf16[1024,128]{1,0:T(8,128)(2,1)S(1)}, u32[]{:S(2)}, u32[]{:S(2)}) collective-permute-start(bf16[1024,128]{1,0:T(8,128)(2,1)S(1)} %copy-done.6), channel_id=1, source_target_pairs={{0,6},{8,14},{16,22},{24,30}} | collective-permute-start | bytes 786440 | tf_op jit(solution)/shard_map/ppermute | solution.py:169
  154.0 10.7 %collective-permute-start.39 = (bf16[1024,128]{1,0:T(8,128)(2,1)S(1)}, bf16[1024,128]{1,0:T(8,128)(2,1)S(1)}, u32[]{:S(2)}, u32[]{:S(2)}) collective-permute-start(bf16[1024,128]{1,0:T(8,128)(2,1)S(1)} %copy-done.8), channel_id=1, source_target_pairs={{0,2},{8,10},{16,18},{24,26}} | collective-permute-start | bytes 786440 | tf_op jit(solution)/shard_map/ppermute | solution.py:169
  164.6 11.6 %collective-permute-start.50 = (bf16[1024,128]{1,0:T(8,128)(2,1)}, bf16[1024,128]{1,0:T(8,128)(2,1)S(1)}, u32[]{:S(2)}, u32[]{:S(2)}) collective-permute-start(bf16[1024,128]{1,0:T(8,128)(2,1)} %shard_map.96), channel_id=1, source_target_pairs={{0,6},{8,14},{16,22},{24,30}} | collective-permute-start | bytes 786440 | tf_op jit(solution)/shard_map/ppermute | solution.py:169
  166.3 11.4 %collective-permute-start.25 = (bf16[1024,128]{1,0:T(8,128)(2,1)S(1)}, bf16[1024,128]{1,0:T(8,128)(2,1)S(1)}, u32[]{:S(2)}, u32[]{:S(2)}) collective-permute-start(bf16[1024,128]{1,0:T(8,128)(2,1)S(1)} %add_select_fusion.2), channel_id=1, source_target_pairs={{0,1},{2,3},{4,5},{6,7},{8,9},{10,11},{12,13},{14,15},{16,17},{18,... | collective-permute-start | bytes 786440 | tf_op jit(solution)/shard_map/ppermute | solution.py:169
  (69 other events, 412.1 us)

commit v2 on v1

v2 whole, which is shorter than its diff:
```python
import functools

import jax
import jax.numpy as jnp
from jax import lax
from jax.experimental import pallas as pl
from jax.experimental.pallas import tpu as pltpu
from jax.sharding import PartitionSpec as P

STEPS = 4

F32 = jnp.float32
BF16 = jnp.bfloat16
VMEM = pl.BlockSpec(memory_space=pltpu.VMEM)
SMEM = pl.BlockSpec(memory_space=pltpu.SMEM)


def peer_of(group, hop, groups):
    return group ^ hop if groups & (groups - 1) == 0 else (group + hop) % groups


def source_of(group, hop, groups):
    return group ^ hop if groups & (groups - 1) == 0 else (group - hop) % groups


def call(kernel, out_shape, scalars, arrays, spare=2):
    held = sum(a.size * a.dtype.itemsize for a in (*arrays, *jax.tree.leaves(out_shape)))
    return pl.pallas_call(
        kernel,
        out_shape=out_shape,
        in_specs=[SMEM] * len(scalars) + [VMEM] * len(arrays),
        out_specs=jax.tree.map(lambda _: VMEM, out_shape),
        compiler_params=pltpu.CompilerParams(vmem_limit_bytes=held + spare * (1 << 20)),
    )(*scalars, *arrays)


def dot(a, b):
    return jnp.dot(a, b, preferred_element_type=F32)


def pick_kernel(groups, block, parts, picks, *refs):
    sources, outs = refs[:parts], refs[parts:]
    for hop in range(groups):
        start = pl.multiple_of(picks[hop] * block, block)
        for part in range(parts):
            outs[hop][part * block : (part + 1) * block, :] = sources[part][pl.ds(start, block), :]


def dense_kernel(groups, block, depth, place, rows, counts, weights, dense):
    me = place[0]
    dense[...] = jnp.zeros_like(dense)
    for hop in range(groups):
        source = source_of(me, hop, groups)
        for entry in range(depth):

            @pl.when(entry < counts[0, source])
            def _():
                start = pl.multiple_of(rows[source, entry] * block, block)
                dense[pl.ds(start, block), hop * block : (hop + 1) * block] = weights[source, entry]


def sheet_kernel(self_block, column, row, dense, sheet, moved):
    scaled = self_block[...].astype(F32) * column[...]
    first = scaled.astype(BF16)
    second = dot(first, first)
    total = second - scaled
    third = dot(second.astype(BF16), first)
    sheet[...] = ((total - third) * row[...]).astype(BF16)
    width = sheet.shape[1]
    for start in range(0, dense.shape[1], width):
        size = min(width, dense.shape[1] - start)
        part = dense[:, start : start + size]
        moved[:, start : start + size] = (dot(sheet[...], part) + part.astype(F32) * column[...]).astype(BF16)


def product(matrix, blocks, part, block):
    total = None
    for hop, ref in enumerate(blocks):
        term = dot(matrix[:, hop * block : (hop + 1) * block], ref[part * block : (part + 1) * block, :])
        total = term if total is None else total + term
    return total


def term_kernel(groups, block, parts, matrix, *refs):
    blocks, out = refs[:groups], refs[groups]
    rows = matrix.shape[0]
    for part in range(parts):
        out[part * rows : (part + 1) * rows, :] = product(matrix, blocks, part, block).astype(out.dtype)


def driven_kernel(steps, sheet, column, incident, out):
    for step in range(1, steps):
        field = incident[step]
        out[step - 1] = field.astype(F32) * column[...] + dot(sheet[...], field)


def emit(block, sends, parts, picks, current):
    hops = len(sends)
    for part in range(parts):
        for hop in range(hops):
            start = pl.multiple_of(picks[part, hop] * block, block)
            sends[hop][part * block : (part + 1) * block, :] = current[pl.ds(start, block), :]


def first_kernel(groups, block, fields, picks, sheet, column, incident, *refs):
    terms, now, sends = refs[:fields], refs[fields], refs[fields + 1 :]
    total = terms[0][...].astype(F32)
    for ref in terms[1:]:
        total = total + ref[...].astype(F32)
    driving = incident[0].astype(F32) - total
    current = driving * column[...] + dot(sheet[...], driving.astype(BF16))
    now[...] = current.astype(BF16)
    emit(block, sends, 2, picks, now)


def next_kernel(groups, block, step, place, picks, driven, matrix, aside, *refs):
    refs = list(refs)
    take = lambda count: [refs.pop(0) for _ in range(count)]
    blocks = take(groups)
    older = take(groups) if step > 1 else None
    terms = take(1 if step < 3 else 2)
    passed = take(1) if step == 1 else None
    now = take(1)[0]
    if step == 2:
        own = take(1)[0]
    sends = refs
    near = product(matrix, blocks, 0, block)
    value = driven[step - 1] - near
    if step == 2:
        own[...] = near.astype(BF16)
    if step > 1:
        value = value - product(aside, older, 1, block)
    for ref in terms:
        value = value - ref[...].astype(F32)
    now[...] = value.astype(BF16)
    if sends:
        emit(block, sends, 2 if step == 1 else 1, picks, now)
    if passed is not None:

        @pl.when(place[1] == 2)
        def _():
            emit(block, sends, 1, picks, passed[0])


def local(retarded, block_row, block_count, send_pick, history, incident, self_block, sheet_diag):
    groups = lax.axis_size("group")
    delays = lax.axis_size("delay")
    chips = delays // 2
    group_index = lax.axis_index("group")
    delay_index = lax.axis_index("delay")
    place = jnp.stack([group_index, delay_index]).astype(jnp.int32)
    weights = retarded[0]
    depth, block = weights.shape[1], weights.shape[-1]
    rows, columns = history.shape[1:]
    inverse = 1.0 / sheet_diag
    column, row = inverse[:, None], inverse[None, :]
    shape = jax.ShapeDtypeStruct
    piece = lambda parts=1: shape((parts * block, columns), BF16)

    def along(array, pairs):
        return lax.ppermute(array, "delay", pairs)

    def swap(array):
        return along(array, [(d, d ^ 1) for d in range(delays)])

    def exchange(sends):
        return [sends[0]] + [
            lax.ppermute(sends[hop], "group", [(g, peer_of(g, hop, groups)) for g in range(groups)])
            for hop in range(1, groups)
        ]

    hops = jnp.stack([peer_of(group_index, hop, groups) for hop in range(groups)])
    mine = lax.dynamic_index_in_dim(send_pick[0], group_index, 0, keepdims=False)[hops]
    picks = jnp.stack([mine, swap(mine)])

    def picked(arrays):
        parts = len(arrays)
        return call(
            functools.partial(pick_kernel, groups, block, parts),
            [piece(parts)] * groups, (mine,), arrays,
        )

    def plus(a, b):
        return (a.astype(F32) + b.astype(F32)).astype(BF16)

    def chip_sum(term):
        return plus(term, swap(term))

    def chip_tree(term):
        stride = 1
        while stride < chips:
            pairs = [(2 * z, 2 * (z - stride)) for z in range(stride, chips, 2 * stride)]
            term = plus(term, along(term, pairs))
            stride *= 2
        return term

    def spread_tree(array):
        stride = 1
        while stride < chips:
            stride *= 2
        held = array
        z = delay_index // 2
        while stride > 1:
            stride //= 2
            pairs = [(2 * c, 2 * (c + stride)) for c in range(0, chips, 2 * stride) if c + stride < chips]
            got = along(held, pairs)
            held = jnp.where(z % (2 * stride) == stride, got, held)
        return held

    sends = picked([history[0]])
    blocks = exchange(sends)
    shifted = []
    moving, _ = lax.optimization_barrier((history[0], sends[0]))
    for _ in range(1, STEPS):
        moving = along(moving, [(d, d + 1) for d in range(delays - 1)])
        shifted.append(moving)
    dense = call(
        functools.partial(dense_kernel, groups, block, depth),
        shape((rows, groups * block), BF16),
        (place, block_row[0], block_count), (weights,),
    )
    term = call(
        functools.partial(term_kernel, groups, block, 1), shape((rows, columns), BF16), (), (dense, *blocks)
    )
    chip = chip_sum(term)
    fields = [chip] + [along(chip, [(2 * z, 0)]) for z in range(1, chips)]

    sheet, matrix = call(
        sheet_kernel,
        (shape((rows, rows), BF16), shape((rows, groups * block), BF16)),
        (), (self_block, column, row, dense), 8,
    )
    aside = swap(matrix)
    driven = call(
        functools.partial(driven_kernel, STEPS), shape((STEPS - 1, rows, columns), F32), (), (sheet, column, incident)
    )

    later = []
    for parts in ((shifted[0],), tuple(shifted[1:])):
        blocks = exchange(picked(list(parts)))
        term = call(
            functools.partial(term_kernel, groups, block, len(parts)),
            shape((len(parts) * rows, columns), BF16), (), (matrix, *blocks),
        )
        total = chip_tree(chip_sum(term))
        later += [total[k * rows : (k + 1) * rows] for k in range(len(parts))]

    whole = shape((rows, columns), BF16)
    current, *sends = call(
        functools.partial(first_kernel, groups, block, len(fields)),
        [whole] + [piece(2)] * groups, (picks,), (sheet, column, incident, *fields),
    )
    found = [current]
    second = along(current, [(0, 2)])
    older = exchange(sends)
    current, *sends = call(
        functools.partial(next_kernel, groups, block, 1),
        [whole] + [piece(2)] * groups, (place, picks), (driven, matrix, aside, *older, later[0], second),
    )
    found.append(current)
    pair = spread_tree(jnp.concatenate(found))
    blocks = exchange(sends)
    current, own, *sends = call(
        functools.partial(next_kernel, groups, block, 2),
        [whole, whole] + [piece()] * groups, (place, picks), (driven, matrix, aside, *blocks, *older, later[1]),
    )
    found.append(current)
    third = spread_tree(current)
    older = blocks
    from_second = along(own, [(2, 0)])
    blocks = exchange(sends)
    (current,) = call(
        functools.partial(next_kernel, groups, block, 3),
        [whole], (place, picks), (driven, matrix, aside, *blocks, *older, later[2], from_second),
    )
    copies = [along(current, [(0, 2 * z)]) for z in range(1, chips)]
    early = jnp.concatenate([pair, third])
    early = jnp.where(delay_index % 2 == 0, early, swap(early))
    far = functools.reduce(lambda a, b: a + b, copies)
    held = jnp.where(delay_index == 0, current, far)
    last = jnp.where(delay_index % 2 == 0, held, swap(held))
    return jnp.concatenate([early, last]).reshape(STEPS, rows, columns)


def solution(mesh):
    placed = (
        P("delay", "group", None, None, None),
        P("delay", "group", None),
        P("delay", "group"),
        P("delay", None, None),
        P("delay", "group", None),
        P(None, "group", None),
        P("group", None),
        P("group"),
    )
    return jax.shard_map(
        local, mesh=mesh, in_specs=placed, out_specs=P(None, "group", None), check_vma=False
    )
```

time: 181 us -> 169 us (0.934)
  waiting for transfers between devices: 19.2 us -> 47.3 us
  Pallas kernels: 52.8 us -> 25.6 us
  starting transfers between devices: 89.5 us -> 67.4 us
  other arithmetic: 6.09 us -> 11.4 us
  local copies, waits for them, and re-layouts: 11.3 us -> 15.8 us
    pallas_call x15 -> x13, Pallas kernels: 52.8 us -> 25.6 us  [call(): pl.pallas_call(kernel, out_shape=out_shape, in_specs=[SMEM] * len(scalars...]
    ppermute x34 -> x26, starting transfers between devices: 67.5 us -> 48.1 us  [along(): return lax.ppermute(array, 'delay', pairs)]
    ppermute x18, waiting for transfers between devices: 2.06 us -> 16.2 us  [exchange(): lax.ppermute(sends[hop], 'group', [(g, peer_of(g, hop, groups)) for g in...]
    ppermute x34 -> x26, waiting for transfers between devices: 17.1 us -> 31.1 us  [along(): return lax.ppermute(array, 'delay', pairs)]
    unnamed x83 -> x56, local copies, waits for them, and re-layouts: 8.33 us -> 14.8 us
    select_n x0 -> x7, other arithmetic: none -> 4.01 us  [the longest x4 3.7 us: spread_tree(): held = jnp.where(z % (2 * stride) == stride, got, held)]
    ppermute x18, starting transfers between devices: 22 us -> 19.4 us  [exchange(): lax.ppermute(sends[hop], 'group', [(g, peer_of(g, hop, groups)) for g in...]
  transfers between devices with their start and end apart: 52 -> 44, of which waited for: 12 -> 19; matrix products, arithmetic and copies ran while one was open for 5% -> 7% of each run, Pallas kernels for 28% -> 13%
where the time goes in v2:
time: 169 us; the launch traced here: 168 us
  starting transfers between devices  67.4 us (40%)
  waiting for transfers between devices  47.3 us (28%)
  Pallas kernels  25.6 us (15%)
  local copies, waits for them, and re-layouts  15.8 us (9%)
  other arithmetic  11.4 us (7%)
    ppermute x26, starting transfers between devices, along(): return lax.ppermute(array, 'delay', pairs)  48.1 us
    ppermute x26, waiting for transfers between devices, along(): return lax.ppermute(array, 'delay', pairs)  31.1 us
    pallas_call x13, Pallas kernels, call(): pl.pallas_call(kernel, out_shape=out_shape, in_specs=[SMEM] * len(scalars...  25.6 us
    ppermute x18, starting transfers between devices, exchange(): lax.ppermute(sends[hop], 'group', [(g, peer_of(g, hop, groups)) for g in...  19.4 us
    ppermute x18, waiting for transfers between devices, exchange(): lax.ppermute(sends[hop], 'group', [(g, peer_of(g, hop, groups)) for g in...  16.2 us
    unnamed x56, local copies, waits for them, and re-layouts  14.8 us
    convert_element_type x7, other arithmetic, plus(): return (a.astype(F32) + b.astype(F32)).astype(BF16)  4.44 us
    select_n x4, other arithmetic, spread_tree(): held = jnp.where(z % (2 * stride) == stride, got, held)  3.7 us
  transfers between devices with their start and end apart: 44, of which 19 were waited for; matrix products, arithmetic and copies ran while one was open for 7% of the time, Pallas kernels for 13%

profile of v2, /device:TPU:0, one launch (start us, length us, event | category | flops | bytes accessed | tf_op | source)
XLA Modules:
  0.0 168.0 jit_solution(17832287361503803881)
XLA Ops:
  3.5 2.4 %collective-permute-start.12 = (bf16[1024,128]{1,0:T(8,128)(2,1)S(1)}, bf16[1024,128]{1,0:T(8,128)(2,1)S(1)}, u32[]{:S(2)}, u32[]{:S(2)}) collective-permute-start(bf16[1024,128]{1,0:T(8,128)(2,1)S(1)} %bitcast.20), channel_id=1, source_target_pairs={{0,1},{1,2},{2,3},{3,4},{4,5},{5,6},{6,7},{8,9},{9,10},{10,11},{11... | collective-permute-start | bytes 786440 | tf_op jit(solution)/shard_map/ppermute | solution.py:161
  7.0 6.7 %collective-permute-start.25 = (bf16[1024,128]{1,0:T(8,128)(2,1)S(1)}, bf16[1024,128]{1,0:T(8,128)(2,1)S(1)}, u32[]{:S(2)}, u32[]{:S(2)}) collective-permute-start(bf16[1024,128]{1,0:T(8,128)(2,1)S(1)} %collective-permute-done.12.refs_0_), channel_id=1, source_target_pairs={{0,1},{1,2},{2,3},{3,4},{4,5},{5,6},{6,7},{8,9},{9,10},{10,11},{11... | collective-permute-start | bytes 786440 | tf_op jit(solution)/shard_map/ppermute | solution.py:161
  14.9 6.5 %collective-permute-start.26 = (bf16[1024,128]{1,0:T(8,128)(2,1)S(1)}, bf16[1024,128]{1,0:T(8,128)(2,1)S(1)}, u32[]{:S(2)}, u32[]{:S(2)}) collective-permute-start(bf16[1024,128]{1,0:T(8,128)(2,1)S(1)} %collective-permute-done.25.refs_0_), channel_id=1, source_target_pairs={{0,1},{1,2},{2,3},{3,4},{4,5},{5,6},{6,7},{8,9},{9,10},{10,11},{11... | collective-permute-start | bytes 786440 | tf_op jit(solution)/shard_map/ppermute | solution.py:161
  30.9 6.9 %shard_map.83 = (bf16[1024,1024]{1,0:T(8,128)(2,1)S(1)}, bf16[1024,1024]{1,0:T(8,128)(2,1)S(1)}) custom-call(bf16[1024,1024]{1,0:T(8,128)(2,1)S(1)} %copy-done.9, f32[1024,1]{1,0:T(8,128)S(1)} %copy.11.column, f32[1,1024]{1,0:T(1,128)S(1)} %bitcast.22, bf16[1024,1024]{1,0:T(8,128)(2,1)S(1)} %shard_map.82.dense.matrix), custom_call_target="tpu_custom_call" | custom-call | tf_op jit(solution)/shard_map/pallas_call | solution.py:28
  39.1 3.9 %collective-permute-start.30 = (bf16[2048,128]{1,0:T(8,128)(2,1)S(1)}, bf16[2048,128]{1,0:T(8,128)(2,1)S(1)}, u32[]{:S(2)}, u32[]{:S(2)}) collective-permute-start(bf16[2048,128]{1,0:T(8,128)(2,1)S(1)} %shard_map.92), channel_id=1, source_target_pairs={{0,1},{1,0},{2,3},{3,2},{4,5},{5,4},{6,7},{7,6},{8,9},{9,8},{10,11... | collective-permute-start | bytes 1572872 | tf_op jit(solution)/shard_map/ppermute | solution.py:161
  60.5 10.4 %collective-permute-done.17 = bf16[1024,128]{1,0:T(8,128)(2,1)S(1)} collective-permute-done((bf16[1024,128]{1,0:T(8,128)(2,1)S(1)}, bf16[1024,128]{1,0:T(8,128)(2,1)S(1)}, u32[]{:S(2)}, u32[]{:S(2)}) %collective-permute-start.17) | collective-permute-done | bytes 262176 | tf_op jit(solution)/shard_map/ppermute | solution.py:161
  78.3 2.0 %collective-permute-done.6.refs_2_ = bf16[1024,128]{1,0:T(8,128)(2,1)S(1)} collective-permute-done((bf16[1024,128]{1,0:T(8,128)(2,1)S(1)}, bf16[1024,128]{1,0:T(8,128)(2,1)S(1)}, u32[]{:S(2)}, u32[]{:S(2)}) %collective-permute-start.6) | collective-permute-done | bytes 262176 | tf_op jit(solution)/shard_map/ppermute | solution.py:161
  80.2 11.1 %collective-permute-done.5.refs_1_ = bf16[1024,128]{1,0:T(8,128)(2,1)S(1)} collective-permute-done((bf16[1024,128]{1,0:T(8,128)(2,1)S(1)}, bf16[1024,128]{1,0:T(8,128)(2,1)S(1)}, u32[]{:S(2)}, u32[]{:S(2)}) %collective-permute-start.5) | collective-permute-done | bytes 262176 | tf_op jit(solution)/shard_map/ppermute | solution.py:161
  91.4 2.0 %shard_map.86 = (bf16[1024,128]{1,0:T(8,128)(2,1)S(1)}, bf16[512,128]{1,0:T(8,128)(2,1)S(1)}, bf16[512,128]{1,0:T(8,128)(2,1)}, bf16[512,128]{1,0:T(8,128)(2,1)S(1)}, bf16[512,128]{1,0:T(8,128)(2,1)S(1)}) custom-call(s32[2,4]{1,0:T(2,128)S(1)} %pad_add_fusion.picks, bf16[1024,1024]{1,0:T(8,128)(2,1)S(1)} %get-tuple-element.36.sheet, ...), custom_call_target="tpu_custom_call" | custom-call | tf_op jit(solution)/shard_map/pallas_call | solution.py:28
  98.2 1.8 %shard_map.87.driven = f32[3,1024,128]{2,1,0:T(8,128)S(1)} custom-call(bf16[1024,1024]{1,0:T(8,128)(2,1)S(1)} %copy-done.6, f32[1024,1]{1,0:T(8,128)S(1)} %copy.11.column, bf16[4,1024,128]{2,1,0:T(8,128)(2,1)S(1)} %copy-done.8), custom_call_target="tpu_custom_call" | custom-call | tf_op jit(solution)/shard_map/pallas_call | solution.py:28
  103.5 2.1 %collective-permute-start.11 = (bf16[512,128]{1,0:T(8,128)(2,1)S(1)}, bf16[512,128]{1,0:T(8,128)(2,1)S(1)}, u32[]{:S(2)}, u32[]{:S(2)}) collective-permute-start(bf16[512,128]{1,0:T(8,128)(2,1)S(1)} %get-tuple-element.46), channel_id=1, source_target_pairs={{0,24},{8,16},{16,8},{24,0},{1,25},{9,17},{17,9},{25,1},{2,26},{10... | collective-permute-start | bytes 393224 | tf_op jit(solution)/shard_map/ppermute | solution.py:168
  107.7 1.9 %collective-permute-done.11.refs_3_.refs_7_ = bf16[512,128]{1,0:T(8,128)(2,1)S(1)} collective-permute-done((bf16[512,128]{1,0:T(8,128)(2,1)S(1)}, bf16[512,128]{1,0:T(8,128)(2,1)S(1)}, u32[]{:S(2)}, u32[]{:S(2)}) %collective-permute-start.11) | collective-permute-done | bytes 131104 | tf_op jit(solution)/shard_map/ppermute | solution.py:168
  111.0 2.4 %shard_map.90 = (bf16[1024,128]{1,0:T(8,128)(2,1)S(1)}, bf16[512,128]{1,0:T(8,128)(2,1)S(1)}, bf16[512,128]{1,0:T(8,128)(2,1)S(1)}, bf16[512,128]{1,0:T(8,128)(2,1)S(1)}, bf16[512,128]{1,0:T(8,128)(2,1)S(1)}) custom-call(s32[2]{0:T(128)S(1)} %pad_add_fusion.1.place, s32[2,4]{1,0:T(2,128)S(1)} %pad_add_fusion.picks, f32[3,1024,128]{2,1,0:T(8,128)S(1)} %copy-done.2, ...), custom_call_target="tpu_custom_call" | custom-call | tf_op jit(solution)/shard_map/pallas_call | solution.py:28
  113.4 2.0 %collective-permute-start.22 = (bf16[512,128]{1,0:T(8,128)(2,1)S(1)}, bf16[512,128]{1,0:T(8,128)(2,1)S(1)}, u32[]{:S(2)}, u32[]{:S(2)}) collective-permute-start(bf16[512,128]{1,0:T(8,128)(2,1)S(1)} %get-tuple-element.54), channel_id=1, source_target_pairs={{0,8},{8,0},{16,24},{24,16},{1,9},{9,1},{17,25},{25,17},{2,10},{10... | collective-permute-start | bytes 393224 | tf_op jit(solution)/shard_map/ppermute | solution.py:168
  120.4 2.0 %collective-permute-done.24.refs_3_.refs_7_ = bf16[512,128]{1,0:T(8,128)(2,1)S(1)} collective-permute-done((bf16[512,128]{1,0:T(8,128)(2,1)S(1)}, bf16[512,128]{1,0:T(8,128)(2,1)S(1)}, u32[]{:S(2)}, u32[]{:S(2)}) %collective-permute-start.24) | collective-permute-done | bytes 131104 | tf_op jit(solution)/shard_map/ppermute | solution.py:168
  122.4 3.6 %shard_map.93 = (bf16[1024,128]{1,0:T(8,128)(2,1)S(1)}, bf16[1024,128]{1,0:T(8,128)(2,1)}, bf16[256,128]{1,0:T(8,128)(2,1)S(1)}, bf16[256,128]{1,0:T(8,128)(2,1)...) custom-call(s32[2]{0:T(128)S(1)} %pad_add_fusion.1.place, s32[2,4]{1,0:T(2,128)S(1)} %pad_add_fusion.picks, ...), custom_call_target="tpu_custom_call" | custom-call | tf_op jit(solution)/shard_map/pallas_call | solution.py:28
  129.5 4.7 %collective-permute-start.21 = (bf16[2048,128]{1,0:T(8,128)(2,1)}, bf16[2048,128]{1,0:T(8,128)(2,1)}, u32[]{:S(2)}, u32[]{:S(2)}) collective-permute-start(bf16[2048,128]{1,0:T(8,128)(2,1)} %broadcast_select_fusion.1), channel_id=1, source_target_pairs={{0,2},{4,6},{8,10},{12,14},{16,18},{20,22},{24,26},{28,30}} | collective-permute-start | bytes 1572872 | tf_op jit(solution)/shard_map/ppermute | solution.py:161
  135.0 2.0 %collective-permute-start.34 = (bf16[1024,128]{1,0:T(8,128)(2,1)}, bf16[1024,128]{1,0:T(8,128)(2,1)}, u32[]{:S(2)}, u32[]{:S(2)}) collective-permute-start(bf16[1024,128]{1,0:T(8,128)(2,1)} %broadcast_select_fusion.4), channel_id=1, source_target_pairs={{0,2},{4,6},{8,10},{12,14},{16,18},{20,22},{24,26},{28,30}} | collective-permute-start | bytes 786440 | tf_op jit(solution)/shard_map/ppermute | solution.py:161
  138.0 3.3 %collective-permute-done.36.refs_1_ = bf16[256,128]{1,0:T(8,128)(2,1)S(1)} collective-permute-done((bf16[256,128]{1,0:T(8,128)(2,1)S(1)}, bf16[256,128]{1,0:T(8,128)(2,1)S(1)}, u32[]{:S(2)}, u32[]{:S(2)}) %collective-permute-start.36) | collective-permute-done | bytes 65568 | tf_op jit(solution)/shard_map/ppermute | solution.py:168
  142.5 4.1 %collective-permute-done.38.refs_3_ = bf16[256,128]{1,0:T(8,128)(2,1)S(1)} collective-permute-done((bf16[256,128]{1,0:T(8,128)(2,1)}, bf16[256,128]{1,0:T(8,128)(2,1)S(1)}, u32[]{:S(2)}, u32[]{:S(2)}) %collective-permute-start.38) | collective-permute-done | bytes 65568 | tf_op jit(solution)/shard_map/ppermute | solution.py:168
  150.3 2.9 %shard_map.94 = bf16[1024,128]{1,0:T(8,128)(2,1)S(1)} custom-call(s32[2]{0:T(128)S(1)} %pad_add_fusion.1.place, s32[2,4]{1,0:T(2,128)S(1)} %pad_add_fusion.picks, f32[3,1024,128]{2,1,0:T(8,128)S(1)} %copy-done.4, bf16[1024,1024]{1,0:T(8,128)(2,1)S(1)} %get-tuple-element.42.matrix, bf16[1024,1024]{1,0:T(8,128)(2,1)} %collective-permute-done.8.aside, ...), custom_call_target="tpu_custom_call" | custom-call | tf_op jit(solution)/shard_map/pallas_call | solution.py:28
  154.5 2.9 %collective-permute-start.41 = (bf16[1024,128]{1,0:T(8,128)(2,1)S(1)}, bf16[1024,128]{1,0:T(8,128)(2,1)S(1)}, u32[]{:S(2)}, u32[]{:S(2)}) collective-permute-start(bf16[1024,128]{1,0:T(8,128)(2,1)S(1)} %shard_map.94), channel_id=1, source_target_pairs={{0,4},{8,12},{16,20},{24,28}} | collective-permute-start | bytes 786440 | tf_op jit(solution)/shard_map/ppermute | solution.py:161
  157.5 2.0 %collective-permute-start.40 = (bf16[1024,128]{1,0:T(8,128)(2,1)S(1)}, bf16[1024,128]{1,0:T(8,128)(2,1)}, u32[]{:S(2)}, u32[]{:S(2)}) collective-permute-start(bf16[1024,128]{1,0:T(8,128)(2,1)S(1)} %shard_map.94), channel_id=1, source_target_pairs={{0,2},{8,10},{16,18},{24,26}} | collective-permute-start | bytes 786440 | tf_op jit(solution)/shard_map/ppermute | solution.py:161
  161.8 2.4 %collective-permute-done.40 = bf16[1024,128]{1,0:T(8,128)(2,1)} collective-permute-done((bf16[1024,128]{1,0:T(8,128)(2,1)S(1)}, bf16[1024,128]{1,0:T(8,128)(2,1)}, u32[]{:S(2)}, u32[]{:S(2)}) %collective-permute-start.40) | collective-permute-done | bytes 262176 | tf_op jit(solution)/shard_map/ppermute | solution.py:161
  (159 shorter events, 75.3 us)
Async XLA Ops:
  7.0 7.9 %collective-permute-start.25 = (bf16[1024,128]{1,0:T(8,128)(2,1)S(1)}, bf16[1024,128]{1,0:T(8,128)(2,1)S(1)}, u32[]{:S(2)}, u32[]{:S(2)}) collective-permute-start(bf16[1024,128]{1,0:T(8,128)(2,1)S(1)} %collective-permute-done.12.refs_0_), channel_id=1, source_target_pairs={{0,1},{1,2},{2,3},{3,4},{4,5},{5,6},{6,7},{8,9},{9,10},{10,11},{11... | collective-permute-start | bytes 786440 | tf_op jit(solution)/shard_map/ppermute | solution.py:161
  14.9 7.7 %collective-permute-start.26 = (bf16[1024,128]{1,0:T(8,128)(2,1)S(1)}, bf16[1024,128]{1,0:T(8,128)(2,1)S(1)}, u32[]{:S(2)}, u32[]{:S(2)}) collective-permute-start(bf16[1024,128]{1,0:T(8,128)(2,1)S(1)} %collective-permute-done.25.refs_0_), channel_id=1, source_target_pairs={{0,1},{1,2},{2,3},{3,4},{4,5},{5,6},{6,7},{8,9},{9,10},{10,11},{11... | collective-permute-start | bytes 786440 | tf_op jit(solution)/shard_map/ppermute | solution.py:161
  23.9 13.9 %collective-permute-start.27 = (bf16[512,128]{1,0:T(8,128)(2,1)}, bf16[512,128]{1,0:T(8,128)(2,1)S(1)}, u32[]{:S(2)}, u32[]{:S(2)}) collective-permute-start(bf16[512,128]{1,0:T(8,128)(2,1)} %get-tuple-element.58), channel_id=1, source_target_pairs={{0,8},{8,0},{16,24},{24,16},{1,9},{9,1},{17,25},{25,17},{2,10},{10... | collective-permute-start | bytes 393224 | tf_op jit(solution)/shard_map/ppermute | solution.py:168
  25.4 12.5 %collective-permute-start.28 = (bf16[512,128]{1,0:T(8,128)(2,1)}, bf16[512,128]{1,0:T(8,128)(2,1)S(1)}, u32[]{:S(2)}, u32[]{:S(2)}) collective-permute-start(bf16[512,128]{1,0:T(8,128)(2,1)} %get-tuple-element.59), channel_id=1, source_target_pairs={{0,16},{8,24},{16,0},{24,8},{1,17},{9,25},{17,1},{25,9},{2,18},{10... | collective-permute-start | bytes 393224 | tf_op jit(solution)/shard_map/ppermute | solution.py:168
  26.9 11.0 %collective-permute-start.29 = (bf16[512,128]{1,0:T(8,128)(2,1)}, bf16[512,128]{1,0:T(8,128)(2,1)S(1)}, u32[]{:S(2)}, u32[]{:S(2)}) collective-permute-start(bf16[512,128]{1,0:T(8,128)(2,1)} %get-tuple-element.60), channel_id=1, source_target_pairs={{0,24},{8,16},{16,8},{24,0},{1,25},{9,17},{17,9},{25,1},{2,26},{10... | collective-permute-start | bytes 393224 | tf_op jit(solution)/shard_map/ppermute | solution.py:168
  39.1 16.9 %collective-permute-start.30 = (bf16[2048,128]{1,0:T(8,128)(2,1)S(1)}, bf16[2048,128]{1,0:T(8,128)(2,1)S(1)}, u32[]{:S(2)}, u32[]{:S(2)}) collective-permute-start(bf16[2048,128]{1,0:T(8,128)(2,1)S(1)} %shard_map.92), channel_id=1, source_target_pairs={{0,1},{1,0},{2,3},{3,2},{4,5},{5,4},{6,7},{7,6},{8,9},{9,8},{10,11... | collective-permute-start | bytes 1572872 | tf_op jit(solution)/shard_map/ppermute | solution.py:161
  51.4 58.2 %collective-permute-start.8 = (bf16[1024,1024]{1,0:T(8,128)(2,1)S(1)}, bf16[1024,1024]{1,0:T(8,128)(2,1)}, u32[]{:S(2)}, u32[]{:S(2)}) collective-permute-start(bf16[1024,1024]{1,0:T(8,128)(2,1)S(1)} %get-tuple-element.42.matrix), channel_id=1, source_target_pairs={{0,1},{1,0},{2,3},{3,2},{4,5},{5,4},{6,7},{7,6},{8,9},{9,8},{10,11... | collective-permute-start | bytes 6291464 | tf_op jit(solution)/shard_map/ppermute | solution.py:161
  52.1 7.0 %collective-permute-start.4 = (bf16[1024,128]{1,0:T(8,128)(2,1)S(1)}, bf16[1024,128]{1,0:T(8,128)(2,1)S(1)}, u32[]{:S(2)}, u32[]{:S(2)}) collective-permute-start(bf16[1024,128]{1,0:T(8,128)(2,1)S(1)} %shard_map.85), channel_id=1, source_target_pairs={{0,1},{1,0},{2,3},{3,2},{4,5},{5,4},{6,7},{7,6},{8,9},{9,8},{10,11... | collective-permute-start | bytes 786440 | tf_op jit(solution)/shard_map/ppermute | solution.py:161
  56.2 18.1 %collective-permute-start.31 = (bf16[2048,128]{1,0:T(8,128)(2,1)S(1)}, bf16[2048,128]{1,0:T(8,128)(2,1)S(1)}, u32[]{:S(2)}, u32[]{:S(2)}) collective-permute-start(bf16[2048,128]{1,0:T(8,128)(2,1)S(1)} %add_convert_fusion.2), channel_id=1, source_target_pairs={{2,0},{6,4},{10,8},{14,12},{18,16},{22,20},{26,24},{30,28}} | collective-permute-start | bytes 1572872 | tf_op jit(solution)/shard_map/ppermute | solution.py:161
  57.7 13.2 %collective-permute-start.17 = (bf16[1024,128]{1,0:T(8,128)(2,1)S(1)}, bf16[1024,128]{1,0:T(8,128)(2,1)S(1)}, u32[]{:S(2)}, u32[]{:S(2)}) collective-permute-start(bf16[1024,128]{1,0:T(8,128)(2,1)S(1)} %add_convert_fusion.5), channel_id=1, source_target_pairs={{2,0},{6,4},{10,8},{14,12},{18,16},{22,20},{26,24},{30,28}} | collective-permute-start | bytes 786440 | tf_op jit(solution)/shard_map/ppermute | solution.py:161
  59.0 13.9 %collective-permute-start = (s32[4]{0:T(128)S(1)}, s32[4]{0:T(128)S(1)}, u32[]{:S(2)}, u32[]{:S(2)}) collective-permute-start(s32[4]{0:T(128)S(1)} %gather_fusion), channel_id=1, source_target_pairs={{0,1},{1,0},{2,3},{3,2},{4,5},{5,4},{6,7},{7,6},{8,9},{9,8},{10,11... | collective-permute-start | bytes 56 | tf_op jit(solution)/shard_map/ppermute | solution.py:161
  59.2 17.6 %collective-permute-start.7 = (bf16[1024,128]{1,0:T(8,128)(2,1)S(1)}, bf16[1024,128]{1,0:T(8,128)(2,1)S(1)}, u32[]{:S(2)}, u32[]{:S(2)}) collective-permute-start(bf16[1024,128]{1,0:T(8,128)(2,1)S(1)} %add_convert_fusion.6.refs_0_), channel_id=1, source_target_pairs={{6,0},{14,8},{22,16},{30,24}} | collective-permute-start | bytes 786440 | tf_op jit(solution)/shard_map/ppermute | solution.py:161
  70.9 9.3 %collective-permute-start.6 = (bf16[1024,128]{1,0:T(8,128)(2,1)S(1)}, bf16[1024,128]{1,0:T(8,128)(2,1)S(1)}, u32[]{:S(2)}, u32[]{:S(2)}) collective-permute-start(bf16[1024,128]{1,0:T(8,128)(2,1)S(1)} %add_convert_fusion.6.refs_0_), channel_id=1, source_target_pairs={{4,0},{12,8},{20,16},{28,24}} | collective-permute-start | bytes 786440 | tf_op jit(solution)/shard_map/ppermute | solution.py:161
  73.0 18.4 %collective-permute-start.5 = (bf16[1024,128]{1,0:T(8,128)(2,1)S(1)}, bf16[1024,128]{1,0:T(8,128)(2,1)S(1)}, u32[]{:S(2)}, u32[]{:S(2)}) collective-permute-start(bf16[1024,128]{1,0:T(8,128)(2,1)S(1)} %add_convert_fusion.6.refs_0_), channel_id=1, source_target_pairs={{2,0},{10,8},{18,16},{26,24}} | collective-permute-start | bytes 786440 | tf_op jit(solution)/shard_map/ppermute | solution.py:161
  74.3 29.3 %collective-permute-start.18 = (bf16[1024,128]{1,0:T(8,128)(2,1)}, bf16[1024,128]{1,0:T(8,128)(2,1)}, u32[]{:S(2)}, u32[]{:S(2)}) collective-permute-start(bf16[1024,128]{1,0:T(8,128)(2,1)} %add_convert_fusion.4), channel_id=1, source_target_pairs={{4,0},{12,8},{20,16},{28,24}} | collective-permute-start | bytes 786440 | tf_op jit(solution)/shard_map/ppermute | solution.py:161
  76.8 41.6 %collective-permute-start.32 = (bf16[2048,128]{1,0:T(8,128)(2,1)}, bf16[2048,128]{1,0:T(8,128)(2,1)}, u32[]{:S(2)}, u32[]{:S(2)}) collective-permute-start(bf16[2048,128]{1,0:T(8,128)(2,1)} %add_convert_fusion.1), channel_id=1, source_target_pairs={{4,0},{12,8},{20,16},{28,24}} | collective-permute-start | bytes 1572872 | tf_op jit(solution)/shard_map/ppermute | solution.py:161
  94.8 7.9 %collective-permute-start.9 = (bf16[512,128]{1,0:T(8,128)(2,1)}, bf16[512,128]{1,0:T(8,128)(2,1)S(1)}, u32[]{:S(2)}, u32[]{:S(2)}) collective-permute-start(bf16[512,128]{1,0:T(8,128)(2,1)} %get-tuple-element.44), channel_id=1, source_target_pairs={{0,8},{8,0},{16,24},{24,16},{1,9},{9,1},{17,25},{25,17},{2,10},{10... | collective-permute-start | bytes 393224 | tf_op jit(solution)/shard_map/ppermute | solution.py:168
  101.1 8.5 %collective-permute-start.19 = (bf16[1024,128]{1,0:T(8,128)(2,1)S(1)}, bf16[1024,128]{1,0:T(8,128)(2,1)S(1)}, u32[]{:S(2)}, u32[]{:S(2)}) collective-permute-start(bf16[1024,128]{1,0:T(8,128)(2,1)S(1)} %copy-done.13), channel_id=1, source_target_pairs={{0,2},{8,10},{16,18},{24,26}} | collective-permute-start | bytes 786440 | tf_op jit(solution)/shard_map/ppermute | solution.py:161
  117.0 11.6 %collective-permute-start.20 = (bf16[2048,128]{1,0:T(8,128)(2,1)S(1)}, bf16[2048,128]{1,0:T(8,128)(2,1)S(1)}, u32[]{:S(2)}, u32[]{:S(2)}) collective-permute-start(bf16[2048,128]{1,0:T(8,128)(2,1)S(1)} %constant_dynamic-update-slice_fusion), channel_id=1, source_target_pairs={{0,4},{8,12},{16,20},{24,28}} | collective-permute-start | bytes 1572872 | tf_op jit(solution)/shard_map/ppermute | solution.py:161
  126.0 21.2 %collective-permute-start.39 = (bf16[1024,128]{1,0:T(8,128)(2,1)}, bf16[1024,128]{1,0:T(8,128)(2,1)S(1)}, u32[]{:S(2)}, u32[]{:S(2)}) collective-permute-start(bf16[1024,128]{1,0:T(8,128)(2,1)} %get-tuple-element.66), channel_id=1, source_target_pairs={{2,0},{10,8},{18,16},{26,24}} | collective-permute-start | bytes 786440 | tf_op jit(solution)/shard_map/ppermute | solution.py:161
  129.5 31.0 %collective-permute-start.21 = (bf16[2048,128]{1,0:T(8,128)(2,1)}, bf16[2048,128]{1,0:T(8,128)(2,1)}, u32[]{:S(2)}, u32[]{:S(2)}) collective-permute-start(bf16[2048,128]{1,0:T(8,128)(2,1)} %broadcast_select_fusion.1), channel_id=1, source_target_pairs={{0,2},{4,6},{8,10},{12,14},{16,18},{20,22},{24,26},{28,30}} | collective-permute-start | bytes 1572872 | tf_op jit(solution)/shard_map/ppermute | solution.py:161
  135.0 24.5 %collective-permute-start.34 = (bf16[1024,128]{1,0:T(8,128)(2,1)}, bf16[1024,128]{1,0:T(8,128)(2,1)}, u32[]{:S(2)}, u32[]{:S(2)}) collective-permute-start(bf16[1024,128]{1,0:T(8,128)(2,1)} %broadcast_select_fusion.4), channel_id=1, source_target_pairs={{0,2},{4,6},{8,10},{12,14},{16,18},{20,22},{24,26},{28,30}} | collective-permute-start | bytes 786440 | tf_op jit(solution)/shard_map/ppermute | solution.py:161
  153.2 8.5 %collective-permute-start.42 = (bf16[1024,128]{1,0:T(8,128)(2,1)S(1)}, bf16[1024,128]{1,0:T(8,128)(2,1)S(1)}, u32[]{:S(2)}, u32[]{:S(2)}) collective-permute-start(bf16[1024,128]{1,0:T(8,128)(2,1)S(1)} %shard_map.94), channel_id=1, source_target_pairs={{0,6},{8,14},{16,22},{24,30}} | collective-permute-start | bytes 786440 | tf_op jit(solution)/shard_map/ppermute | solution.py:161
  154.5 7.2 %collective-permute-start.41 = (bf16[1024,128]{1,0:T(8,128)(2,1)S(1)}, bf16[1024,128]{1,0:T(8,128)(2,1)S(1)}, u32[]{:S(2)}, u32[]{:S(2)}) collective-permute-start(bf16[1024,128]{1,0:T(8,128)(2,1)S(1)} %shard_map.94), channel_id=1, source_target_pairs={{0,4},{8,12},{16,20},{24,28}} | collective-permute-start | bytes 786440 | tf_op jit(solution)/shard_map/ppermute | solution.py:161
  (47 other events, 322.1 us)

commit v3 on v2

v3 whole, which is shorter than its diff:
```python
import functools

import jax
import jax.numpy as jnp
from jax import lax
from jax.experimental import pallas as pl
from jax.experimental.pallas import tpu as pltpu
from jax.sharding import PartitionSpec as P


STEPS = 4

F32 = jnp.float32
BF16 = jnp.bfloat16
VMEM = pl.BlockSpec(memory_space=pltpu.VMEM)
SMEM = pl.BlockSpec(memory_space=pltpu.SMEM)


def peer_of(group, hop, groups):
    return group ^ hop if groups & (groups - 1) == 0 else (group + hop) % groups


def source_of(group, hop, groups):
    return group ^ hop if groups & (groups - 1) == 0 else (group - hop) % groups


def call(kernel, out_shape, scalars, arrays, spare=2):
    held = sum(a.size * a.dtype.itemsize for a in (*arrays, *jax.tree.leaves(out_shape)))
    return pl.pallas_call(
        kernel,
        out_shape=out_shape,
        in_specs=[SMEM] * len(scalars) + [VMEM] * len(arrays),
        out_specs=jax.tree.map(lambda _: VMEM, out_shape),
        compiler_params=pltpu.CompilerParams(vmem_limit_bytes=held + spare * (1 << 20)),
    )(*scalars, *arrays)


def dot(a, b):
    return jnp.dot(a, b, preferred_element_type=F32)


def dense_kernel(groups, block, depth, place, rows, counts, weights, dense):
    me = place[0]
    dense[...] = jnp.zeros_like(dense)
    for hop in range(groups):
        source = source_of(me, hop, groups)
        for entry in range(depth):

            @pl.when(entry < counts[0, source])
            def _():
                start = pl.multiple_of(rows[source, entry] * block, block)
                dense[pl.ds(start, block), hop * block : (hop + 1) * block] = weights[source, entry]


def sheet_kernel(self_block, column, row, sheet):
    scaled = self_block[...].astype(F32) * column[...]
    first = scaled.astype(BF16)
    second = dot(first, first)
    total = second - scaled
    third = dot(second.astype(BF16), first)
    sheet[...] = ((total - third) * row[...]).astype(BF16)


def product(matrix, blocks, part, block):
    total = None
    for hop, ref in enumerate(blocks):
        term = dot(matrix[:, hop * block : (hop + 1) * block], ref[part * block : (part + 1) * block, :])
        total = term if total is None else total + term
    return total


def emit(block, sends, part, sources, picks, row):
    for hop, out in enumerate(sends):
        start = pl.multiple_of(picks[row, hop] * block, block)
        out[part * block : (part + 1) * block, :] = sources[pl.ds(start, block), :]


def pick_kernel(block, parts, picks, *refs):
    sources, sends = refs[:parts], refs[parts:]
    for part, source in enumerate(sources):
        for hop, out in enumerate(sends):
            start = pl.multiple_of(picks[hop] * block, block)
            out[part * block : (part + 1) * block, :] = source[pl.ds(start, block), :]


def early_kernel(groups, block, place, matrix, *refs):
    blocks, outs = refs[:groups], refs[groups:]
    for part, out in enumerate(outs):

        @pl.when(place[1] >= part)
        def _():
            out[...] = product(matrix, blocks, part, block).astype(BF16)

        @pl.when(place[1] < part)
        def _():
            out[...] = jnp.zeros_like(out)


def near_kernel(groups, block, place, matrix, aside, *refs):
    blocks, refs = refs[:groups], refs[groups:]
    older, refs = (refs[:groups], refs[groups:]) if len(refs) > 2 else (None, refs)
    wide, narrow = refs
    total = product(matrix, blocks, 0, block)
    narrow[...] = jnp.where(place[1] >= 2, total, 0.0).astype(BF16)
    if older is not None:
        total = total + product(aside, older, 1, block)
    wide[...] = total


def step_kernel(block, step, fields, place, picks, sheet, column, incident, *refs):
    refs = list(refs)
    take = lambda count: [refs.pop(0) for _ in range(count)]
    terms = take(fields)
    wide = take(1)[0] if step > 0 else None
    history = take(1)[0] if step < 2 else None
    passed = take(1)[0] if step == 1 else None
    now, sends = refs[0], refs[1:]
    driving = incident[step].astype(F32)
    for ref in terms:
        driving = driving - ref[...].astype(F32)
    if wide is not None:
        driving = driving - wide[...]
    current = driving * column[...] + dot(sheet[...], driving.astype(BF16))
    now[...] = current.astype(BF16)
    if history is None:
        emit(block, sends, 0, now, picks, 0)
        return

    @pl.when(place[1] == 0)
    def _():
        emit(block, sends, 0, now, picks, 0)
        emit(block, sends, 1, now, picks, 1)

    inner = place[1] == 2 if passed is not None else False

    @pl.when((place[1] != 0) & jnp.logical_not(inner))
    def _():
        emit(block, sends, 0, history, picks, 0)
        emit(block, sends, 1, history, picks, 0)

    if passed is not None:

        @pl.when(inner)
        def _():
            emit(block, sends, 0, passed, picks, 0)
            emit(block, sends, 1, passed, picks, 0)


def last_kernel(groups, block, step, fields, sheet, column, incident, matrix, aside, *refs):
    blocks, older = refs[:groups], refs[groups : 2 * groups]
    terms, now = refs[2 * groups : 2 * groups + fields], refs[-1]
    driving = incident[step].astype(F32)
    for ref in terms:
        driving = driving - ref[...].astype(F32)
    driving = driving - product(matrix, blocks, 0, block) - product(aside, older, 1, block)
    now[...] = (driving * column[...] + dot(sheet[...], driving.astype(BF16))).astype(BF16)


def local(retarded, block_row, block_count, send_pick, history, incident, self_block, sheet_diag):
    groups = lax.axis_size("group")
    delays = lax.axis_size("delay")
    chips = delays // 2
    group_index = lax.axis_index("group")
    delay_index = lax.axis_index("delay")
    weights = retarded[0]
    depth, block = weights.shape[1], weights.shape[-1]
    rows, columns = history.shape[1:]
    shape = jax.ShapeDtypeStruct
    piece = lambda parts=1: shape((parts * block, columns), BF16)
    whole = shape((rows, columns), BF16)

    def along(array, pairs):
        return lax.ppermute(array, "delay", pairs)

    def swap(array):
        return along(array, [(d, d ^ 1) for d in range(delays)])

    def shift(array):
        return along(array, [(d, (d + 1) % delays) for d in range(delays)])

    def exchange(sends):
        return [sends[0]] + [
            lax.ppermute(sends[hop], "group", [(g, peer_of(g, hop, groups)) for g in range(groups)])
            for hop in range(1, groups)
        ]

    def plus(a, b):
        return (a.astype(F32) + b.astype(F32)).astype(BF16)

    def gathered(term):
        chip = plus(term, swap(term))
        return [chip] + [along(chip, [(2 * z, 0)]) for z in range(1, chips)]

    def spread_tree(array):
        stride = 1
        while stride < chips:
            stride *= 2
        held = array
        z = delay_index // 2
        while stride > 1:
            stride //= 2
            pairs = [(2 * c, 2 * (c + stride)) for c in range(0, chips, 2 * stride) if c + stride < chips]
            got = along(held, pairs)
            held = jnp.where(z % (2 * stride) == stride, got, held)
        return held

    earlier = shift(history[0])
    place = jnp.stack([group_index, delay_index]).astype(jnp.int32)
    hops = jnp.stack([peer_of(group_index, hop, groups) for hop in range(groups)])
    mine = lax.dynamic_index_in_dim(send_pick[0], group_index, 0, keepdims=False)[hops]
    inverse = 1.0 / sheet_diag
    column, row = inverse[:, None], inverse[None, :]
    dense = call(
        functools.partial(dense_kernel, groups, block, depth),
        shape((rows, groups * block), BF16),
        (place, block_row[0], block_count), (weights,),
    )
    sheet = call(sheet_kernel, shape((rows, rows), BF16), (), (self_block, column, row), 8 + 12)

    sends = call(
        functools.partial(pick_kernel, block, 2), [piece(2)] * groups, (mine,), (history[0], earlier)
    )
    blocks = exchange(sends)
    earlier = shift(earlier)
    terms = call(
        functools.partial(early_kernel, groups, block), [whole, whole], (place,), (dense, *blocks)
    )
    picks = jnp.stack([mine, swap(mine)])
    fields = gathered(terms[0])
    later = gathered(terms[1])
    oldest = shift(earlier)
    aside = swap(dense)

    law = (sheet, column, incident)
    current, *sends = call(
        functools.partial(step_kernel, block, 0, chips),
        [whole] + [piece(2)] * groups, (place, picks), (*law, *fields, earlier),
    )
    found = [current]
    older = exchange(sends)
    second = along(current, [(0, 2)])
    wide, narrow = call(
        functools.partial(near_kernel, groups, block),
        [shape((rows, columns), F32), whole], (place,), (dense, aside, *older),
    )
    fields = gathered(narrow)
    current, *sends = call(
        functools.partial(step_kernel, block, 1, chips),
        [whole] + [piece(2)] * groups, (place, picks), (*law, *later, wide, oldest, second),
    )
    found.append(current)
    blocks = exchange(sends)
    pair = spread_tree(jnp.concatenate(found))
    wide, narrow = call(
        functools.partial(near_kernel, groups, block),
        [shape((rows, columns), F32), whole], (place,), (dense, aside, *blocks, *older),
    )
    later = gathered(narrow)
    current, *sends = call(
        functools.partial(step_kernel, block, 2, chips),
        [whole] + [piece()] * groups, (place, picks), (*law, *fields, wide),
    )
    found.append(current)
    older = blocks
    blocks = exchange(sends)
    third = spread_tree(current)
    current = call(
        functools.partial(last_kernel, groups, block, 3, chips),
        whole, (), (*law, dense, aside, *blocks, *older, *later),
    )
    copies = [along(current, [(0, 2 * z)]) for z in range(1, chips)]
    early = jnp.concatenate([pair, third])
    early = jnp.where(delay_index % 2 == 0, early, swap(early))
    far = functools.reduce(lambda a, b: a + b, copies)
    held = jnp.where(delay_index == 0, current, far)
    last = jnp.where(delay_index % 2 == 0, held, swap(held))
    return jnp.concatenate([early, last]).reshape(STEPS, rows, columns)


def solution(mesh):
    placed = (
        P("delay", "group", None, None, None),
        P("delay", "group", None),
        P("delay", "group"),
        P("delay", None, None),
        P("delay", "group", None),
        P(None, "group", None),
        P("group", None),
        P("group"),
    )

    return jax.shard_map(local, mesh=mesh, in_specs=placed, out_specs=P(None, "group", None), check_vma=False)
```

time: 169 us -> 151 us (0.89)
  starting transfers between devices: 67.4 us -> 57.6 us
  waiting for transfers between devices: 47.3 us -> 37.8 us
  local copies, waits for them, and re-layouts: 15.8 us -> 22 us
  Pallas kernels: 25.6 us -> 22.1 us
  other arithmetic: 11.4 us -> 9.5 us
    ppermute x18 -> x12, waiting for transfers between devices: 16.2 us -> 7.58 us  [exchange(): lax.ppermute(sends[hop], 'group', [(g, peer_of(g, hop, groups)) for g in...]
    unnamed x56 -> x54, local copies, waits for them, and re-layouts: 14.8 us -> 20.4 us
    ppermute x26 -> x31, starting transfers between devices: 48.1 us -> 42.7 us  [along(): return lax.ppermute(array, 'delay', pairs)]
    ppermute x18 -> x12, starting transfers between devices: 19.4 us -> 15 us  [exchange(): lax.ppermute(sends[hop], 'group', [(g, peer_of(g, hop, groups)) for g in...]
    pallas_call x13 -> x10, Pallas kernels: 25.6 us -> 22.1 us  [call(): pl.pallas_call(kernel, out_shape=out_shape, in_specs=[SMEM] * len(scalars...]
    convert_element_type x7 -> x4, other arithmetic: 4.44 us -> 2.26 us  [plus(): return (a.astype(F32) + b.astype(F32)).astype(BF16)]
    ppermute x26 -> x31, waiting for transfers between devices: 31.1 us -> 30.2 us  [along(): return lax.ppermute(array, 'delay', pairs)]
  transfers between devices with their start and end apart: 44 -> 43, of which waited for: 19 -> 15; matrix products, arithmetic and copies ran while one was open for 7% -> 7% of each run, Pallas kernels for 13% -> 14%
where the time goes in v3:
time: 151 us; the launch traced here: 150 us
  starting transfers between devices  57.6 us (38%)
  waiting for transfers between devices  37.8 us (25%)
  Pallas kernels  22.1 us (15%)
  local copies, waits for them, and re-layouts  22 us (15%)
  other arithmetic  9.5 us (6%)
    ppermute x31, starting transfers between devices, along(): return lax.ppermute(array, 'delay', pairs)  42.7 us
    ppermute x31, waiting for transfers between devices, along(): return lax.ppermute(array, 'delay', pairs)  30.2 us
    pallas_call x10, Pallas kernels, call(): pl.pallas_call(kernel, out_shape=out_shape, in_specs=[SMEM] * len(scalars...  22.1 us
    unnamed x54, local copies, waits for them, and re-layouts  20.4 us
    ppermute x12, starting transfers between devices, exchange(): lax.ppermute(sends[hop], 'group', [(g, peer_of(g, hop, groups)) for g in...  15 us
    ppermute x12, waiting for transfers between devices, exchange(): lax.ppermute(sends[hop], 'group', [(g, peer_of(g, hop, groups)) for g in...  7.58 us
    select_n x4, other arithmetic, spread_tree(): held = jnp.where(z % (2 * stride) == stride, got, held)  4.72 us
  transfers between devices with their start and end apart: 43, of which 15 were waited for; matrix products, arithmetic and copies ran while one was open for 7% of the time, Pallas kernels for 14%

profile of v3, /device:TPU:0, one launch (start us, length us, event | category | flops | bytes accessed | tf_op | source)
XLA Modules:
  0.0 149.5 jit_solution(18062288592087342388)
XLA Ops:
  5.2 8.0 %collective-permute-done.1.refs_1_ = bf16[1024,128]{1,0:T(8,128)(2,1)S(1)} collective-permute-done((bf16[1024,128]{1,0:T(8,128)(2,1)S(1)}, bf16[1024,128]{1,0:T(8,128)(2,1)S(1)}, u32[]{:S(2)}, u32[]{:S(2)}) %collective-permute-start.1) | collective-permute-done | bytes 262176 | tf_op jit(solution)/shard_map/ppermute | solution.py:173
  20.3 2.4 %collective-permute-done.4.refs_3_ = bf16[512,128]{1,0:T(8,128)(2,1)S(1)} collective-permute-done((bf16[512,128]{1,0:T(8,128)(2,1)S(1)}, bf16[512,128]{1,0:T(8,128)(2,1)S(1)}, u32[]{:S(2)}, u32[]{:S(2)}) %collective-permute-start.4) | collective-permute-done | bytes 131104 | tf_op jit(solution)/shard_map/ppermute | solution.py:183
  28.3 3.5 %collective-permute-done.9.refs_4_ = bf16[1024,128]{1,0:T(8,128)(2,1)S(1)} collective-permute-done((bf16[1024,128]{1,0:T(8,128)(2,1)S(1)}, bf16[1024,128]{1,0:T(8,128)(2,1)S(1)}, u32[]{:S(2)}, u32[]{:S(2)}) %collective-permute-start.9) | collective-permute-done | bytes 262176 | tf_op jit(solution)/shard_map/ppermute | solution.py:173
  34.9 4.6 %shard_map.82.sheet = bf16[1024,1024]{1,0:T(8,128)(2,1)S(1)} custom-call(bf16[1024,1024]{1,0:T(8,128)(2,1)S(1)} %copy-done.7, f32[1024,1]{1,0:T(8,128)S(1)} %copy.10.column, f32[1,1024]{1,0:T(1,128)S(1)} %bitcast.22), custom_call_target="tpu_custom_call" | custom-call | tf_op jit(solution)/shard_map/pallas_call | solution.py:29
  39.6 2.3 %collective-permute-done.8.refs_3_ = bf16[1024,128]{1,0:T(8,128)(2,1)} collective-permute-done((bf16[1024,128]{1,0:T(8,128)(2,1)S(1)}, bf16[1024,128]{1,0:T(8,128)(2,1)}, u32[]{:S(2)}, u32[]{:S(2)}) %collective-permute-start.8) | collective-permute-done | bytes 262176 | tf_op jit(solution)/shard_map/ppermute | solution.py:173
  41.9 1.9 %shard_map.86 = (bf16[1024,128]{1,0:T(8,128)(2,1)S(1)}, bf16[512,128]{1,0:T(8,128)(2,1)S(1)}, bf16[512,128]{1,0:T(8,128)(2,1)S(1)}, bf16[512,128]{1,0:T(8,128)(2,1)S(1)}, bf16[512,128]{1,0:T(8,128)(2,1)S(1)}) custom-call(s32[2]{0:T(128)S(1)} %pad_add_fusion.1.place, s32[2,4]{1,0:T(2,128)S(1)} %pad_add_fusion.picks, bf16[1024,1024]{1,0:T(8,128)(2,1)S(1)} %shard_map.82.sheet, ...), custom_call_target="tpu_custom_call" | custom-call | tf_op jit(solution)/shard_map/pallas_call | solution.py:29
  45.0 2.5 %collective-permute-start.17 = (bf16[512,128]{1,0:T(8,128)(2,1)S(1)}, bf16[512,128]{1,0:T(8,128)(2,1)S(1)}, u32[]{:S(2)}, u32[]{:S(2)}) collective-permute-start(bf16[512,128]{1,0:T(8,128)(2,1)S(1)} %get-tuple-element.40), channel_id=1, source_target_pairs={{0,24},{8,16},{16,8},{24,0},{1,25},{9,17},{17,9},{25,1},{2,26},{10... | collective-permute-start | bytes 393224 | tf_op jit(solution)/shard_map/ppermute | solution.py:183
  52.8 3.3 %collective-permute-start.19 = (bf16[1024,128]{1,0:T(8,128)(2,1)S(1)}, bf16[1024,128]{1,0:T(8,128)(2,1)S(1)}, u32[]{:S(2)}, u32[]{:S(2)}) collective-permute-start(bf16[1024,128]{1,0:T(8,128)(2,1)S(1)} %get-tuple-element.35), channel_id=1, source_target_pairs={{0,2},{8,10},{16,18},{24,26}} | collective-permute-start | bytes 786440 | tf_op jit(solution)/shard_map/ppermute | solution.py:173
  56.2 2.3 %shard_map.87 = (f32[1024,128]{1,0:T(8,128)S(1)}, bf16[1024,128]{1,0:T(8,128)(2,1)S(1)}) custom-call(s32[2]{0:T(128)S(1)} %pad_add_fusion.1.place, bf16[1024,1024]{1,0:T(8,128)(2,1)S(1)} %shard_map.83.matrix, bf16[1024,1024]{1,0:T(8,128)(2,1)} %collective-permute-done.14.aside, bf16[512,128]{1,0:T(8,128)(2,1)S(1)} %get-tuple-element.37.refs_0_.refs_4_, ...), custom_call_target="tpu_custom_call" | custom-call | tf_op jit(solution)/shard_map/pallas_call | solution.py:29
  59.3 3.5 %collective-permute-done.11.refs_1_ = bf16[1024,128]{1,0:T(8,128)(2,1)S(1)} collective-permute-done((bf16[1024,128]{1,0:T(8,128)(2,1)S(1)}, bf16[1024,128]{1,0:T(8,128)(2,1)S(1)}, u32[]{:S(2)}, u32[]{:S(2)}) %collective-permute-start.11) | collective-permute-done | bytes 262176 | tf_op jit(solution)/shard_map/ppermute | solution.py:173
  66.0 1.8 %collective-permute-start.28 = (bf16[512,128]{1,0:T(8,128)(2,1)S(1)}, bf16[512,128]{1,0:T(8,128)(2,1)S(1)}, u32[]{:S(2)}, u32[]{:S(2)}) collective-permute-start(bf16[512,128]{1,0:T(8,128)(2,1)S(1)} %get-tuple-element.47), channel_id=1, source_target_pairs={{0,24},{8,16},{16,8},{24,0},{1,25},{9,17},{17,9},{25,1},{2,26},{10... | collective-permute-start | bytes 393224 | tf_op jit(solution)/shard_map/ppermute | solution.py:183
  68.5 2.1 %collective-permute-start.20 = (bf16[2048,128]{1,0:T(8,128)(2,1)}, bf16[2048,128]{1,0:T(8,128)(2,1)}, u32[]{:S(2)}, u32[]{:S(2)}) collective-permute-start(bf16[2048,128]{1,0:T(8,128)(2,1)} %constant_dynamic-update-slice_fusion), channel_id=1, source_target_pairs={{0,4},{8,12},{16,20},{24,28}} | collective-permute-start | bytes 1572872 | tf_op jit(solution)/shard_map/ppermute | solution.py:173
  71.8 3.6 %shard_map.89 = (f32[1024,128]{1,0:T(8,128)S(1)}, bf16[1024,128]{1,0:T(8,128)(2,1)}) custom-call(s32[2]{0:T(128)S(1)} %pad_add_fusion.1.place, bf16[1024,1024]{1,0:T(8,128)(2,1)S(1)} %shard_map.83.matrix, bf16[1024,1024]{1,0:T(8,128)(2,1)} %collective-permute-done.14.aside, bf16[512,128]{1,0:T(8,128)(2,1)S(1)} %get-tuple-element.44.refs_0_.refs_4_, ...), custom_call_target="tpu_custom_call" | custom-call | tf_op jit(solution)/shard_map/pallas_call | solution.py:29
  82.7 7.6 %collective-permute-done.23.refs_1_ = bf16[1024,128]{1,0:T(8,128)(2,1)} collective-permute-done((bf16[1024,128]{1,0:T(8,128)(2,1)S(1)}, bf16[1024,128]{1,0:T(8,128)(2,1)}, u32[]{:S(2)}, u32[]{:S(2)}) %collective-permute-start.23) | collective-permute-done | bytes 262176 | tf_op jit(solution)/shard_map/ppermute | solution.py:173
  95.5 1.9 %shard_map.90 = (bf16[1024,128]{1,0:T(8,128)(2,1)S(1)}, bf16[256,128]{1,0:T(8,128)(2,1)S(1)}, bf16[256,128]{1,0:T(8,128)(2,1)S(1)}, bf16[256,128]{1,0:T(8,128)(2,1)S(1)}, bf16[256,128]{1,0:T(8,128)(2,1)S(1)}) custom-call(s32[2]{0:T(128)S(1)} %pad_add_fusion.1.place, s32[2,4]{1,0:T(2,128)S(1)} %pad_add_fusion.picks, bf16[1024,1024]{1,0:T(8,128)(2,1)S(1)} %copy-done.2, ...), custom_call_target="tpu_custom_call" | custom-call | tf_op jit(solution)/shard_map/pallas_call | solution.py:29
  98.0 6.3 %collective-permute-start.29 = (bf16[1024,128]{1,0:T(8,128)(2,1)S(1)}, bf16[1024,128]{1,0:T(8,128)(2,1)S(1)}, u32[]{:S(2)}, u32[]{:S(2)}) collective-permute-start(bf16[1024,128]{1,0:T(8,128)(2,1)S(1)} %get-tuple-element.49), channel_id=1, source_target_pairs={{0,4},{8,12},{16,20},{24,28}} | collective-permute-start | bytes 786440 | tf_op jit(solution)/shard_map/ppermute | solution.py:173
  106.8 1.9 %broadcast_select_fusion.1 = bf16[2048,128]{1,0:T(8,128)(2,1)} fusion(bf16[2048,128]{1,0:T(8,128)(2,1)} %collective-permute-done.20, bf16[2048,128]{1,0:T(8,128)(2,1)} %constant_dynamic-update-slice_fusion, pred[]{:T(512)S(6)} %eq.24), kind=kLoop, calls=%fused_computation.8 | loop fusion | flops 262144 | bytes 1572865 | tf_op jit(solution)/shard_map/jit(_where)/select_n | solution.py:204
  110.6 1.9 %collective-permute-start.34 = (bf16[256,128]{1,0:T(8,128)(2,1)S(1)}, bf16[256,128]{1,0:T(8,128)(2,1)S(1)}, u32[]{:S(2)}, u32[]{:S(2)}) collective-permute-start(bf16[256,128]{1,0:T(8,128)(2,1)S(1)} %get-tuple-element.53), channel_id=1, source_target_pairs={{0,24},{8,16},{16,8},{24,0},{1,25},{9,17},{17,9},{25,1},{2,26},{10... | collective-permute-start | bytes 196616 | tf_op jit(solution)/shard_map/ppermute | solution.py:183
  112.5 2.1 %collective-permute-start.21 = (bf16[2048,128]{1,0:T(8,128)(2,1)}, bf16[2048,128]{1,0:T(8,128)(2,1)}, u32[]{:S(2)}, u32[]{:S(2)}) collective-permute-start(bf16[2048,128]{1,0:T(8,128)(2,1)} %broadcast_select_fusion.1), channel_id=1, source_target_pairs={{0,2},{4,6},{8,10},{12,14},{16,18},{20,22},{24,26},{28,30}} | collective-permute-start | bytes 1572872 | tf_op jit(solution)/shard_map/ppermute | solution.py:173
  116.5 2.0 %collective-permute-start.30 = (bf16[1024,128]{1,0:T(8,128)(2,1)}, bf16[1024,128]{1,0:T(8,128)(2,1)}, u32[]{:S(2)}, u32[]{:S(2)}) collective-permute-start(bf16[1024,128]{1,0:T(8,128)(2,1)} %broadcast_select_fusion.4), channel_id=1, source_target_pairs={{0,2},{4,6},{8,10},{12,14},{16,18},{20,22},{24,26},{28,30}} | collective-permute-start | bytes 786440 | tf_op jit(solution)/shard_map/ppermute | solution.py:173
  128.1 3.5 %shard_map.91 = bf16[1024,128]{1,0:T(8,128)(2,1)S(1)} custom-call(bf16[1024,1024]{1,0:T(8,128)(2,1)S(1)} %copy-done.3, f32[1024,1]{1,0:T(8,128)S(1)} %copy.10.column, bf16[4,1024,128]{2,1,0:T(8,128)(2,1)S(1)} %copy-done.6, bf16[1024,1024]{1,0:T(8,128)(2,1)S(1)} %shard_map.83.matrix, bf16[1024,1024]{1,0:T(8,128)(2,1)} %collective-permute-done.14.aside, ...), custom_call_target="tpu_custom_call" | custom-call | tf_op jit(solution)/shard_map/pallas_call | solution.py:29
  132.9 6.0 %collective-permute-start.40 = (bf16[1024,128]{1,0:T(8,128)(2,1)S(1)}, bf16[1024,128]{1,0:T(8,128)(2,1)S(1)}, u32[]{:S(2)}, u32[]{:S(2)}) collective-permute-start(bf16[1024,128]{1,0:T(8,128)(2,1)S(1)} %shard_map.91), channel_id=1, source_target_pairs={{0,4},{8,12},{16,20},{24,28}} | collective-permute-start | bytes 786440 | tf_op jit(solution)/shard_map/ppermute | solution.py:173
  139.0 2.0 %collective-permute-start.41 = (bf16[1024,128]{1,0:T(8,128)(2,1)S(1)}, bf16[1024,128]{1,0:T(8,128)(2,1)}, u32[]{:S(2)}, u32[]{:S(2)}) collective-permute-start(bf16[1024,128]{1,0:T(8,128)(2,1)S(1)} %shard_map.91), channel_id=1, source_target_pairs={{0,6},{8,14},{16,22},{24,30}} | collective-permute-start | bytes 786440 | tf_op jit(solution)/shard_map/ppermute | solution.py:173
  143.2 2.4 %collective-permute-done.41 = bf16[1024,128]{1,0:T(8,128)(2,1)} collective-permute-done((bf16[1024,128]{1,0:T(8,128)(2,1)S(1)}, bf16[1024,128]{1,0:T(8,128)(2,1)}, u32[]{:S(2)}, u32[]{:S(2)}) %collective-permute-start.41) | collective-permute-done | bytes 262176 | tf_op jit(solution)/shard_map/ppermute | solution.py:173
  (148 shorter events, 69.4 us)
Async XLA Ops:
  3.8 49.0 %collective-permute-start.14 = (bf16[1024,1024]{1,0:T(8,128)(2,1)S(1)}, bf16[1024,1024]{1,0:T(8,128)(2,1)}, u32[]{:S(2)}, u32[]{:S(2)}) collective-permute-start(bf16[1024,1024]{1,0:T(8,128)(2,1)S(1)} %shard_map.83.matrix), channel_id=1, source_target_pairs={{0,1},{1,0},{2,3},{3,2},{4,5},{5,4},{6,7},{7,6},{8,9},{9,8},{10,11... | collective-permute-start | bytes 6291464 | tf_op jit(solution)/shard_map/ppermute | solution.py:173
  4.4 8.8 %collective-permute-start.1 = (bf16[1024,128]{1,0:T(8,128)(2,1)S(1)}, bf16[1024,128]{1,0:T(8,128)(2,1)S(1)}, u32[]{:S(2)}, u32[]{:S(2)}) collective-permute-start(bf16[1024,128]{1,0:T(8,128)(2,1)S(1)} %bitcast.19), channel_id=1, source_target_pairs={{0,1},{1,2},{2,3},{3,4},{4,5},{5,6},{6,7},{7,0},{8,9},{9,10},{10,1... | collective-permute-start | bytes 786440 | tf_op jit(solution)/shard_map/ppermute | solution.py:173
  24.9 20.0 %collective-permute-start.10 = (bf16[1024,128]{1,0:T(8,128)(2,1)S(1)}, bf16[1024,128]{1,0:T(8,128)(2,1)}, u32[]{:S(2)}, u32[]{:S(2)}) collective-permute-start(bf16[1024,128]{1,0:T(8,128)(2,1)S(1)} %get-tuple-element.36), channel_id=1, source_target_pairs={{0,1},{1,0},{2,3},{3,2},{4,5},{5,4},{6,7},{7,6},{8,9},{9,8},{10,11... | collective-permute-start | bytes 786440 | tf_op jit(solution)/shard_map/ppermute | solution.py:173
  25.7 13.9 %collective-permute-start.6 = (bf16[1024,128]{1,0:T(8,128)(2,1)S(1)}, bf16[1024,128]{1,0:T(8,128)(2,1)}, u32[]{:S(2)}, u32[]{:S(2)}) collective-permute-start(bf16[1024,128]{1,0:T(8,128)(2,1)S(1)} %add_convert_fusion.3.refs_0_), channel_id=1, source_target_pairs={{2,0},{10,8},{18,16},{26,24}} | collective-permute-start | bytes 786440 | tf_op jit(solution)/shard_map/ppermute | solution.py:173
  27.0 12.7 %collective-permute-start.7 = (bf16[1024,128]{1,0:T(8,128)(2,1)S(1)}, bf16[1024,128]{1,0:T(8,128)(2,1)}, u32[]{:S(2)}, u32[]{:S(2)}) collective-permute-start(bf16[1024,128]{1,0:T(8,128)(2,1)S(1)} %add_convert_fusion.3.refs_0_), channel_id=1, source_target_pairs={{4,0},{12,8},{20,16},{28,24}} | collective-permute-start | bytes 786440 | tf_op jit(solution)/shard_map/ppermute | solution.py:173
  31.8 10.2 %collective-permute-start.8 = (bf16[1024,128]{1,0:T(8,128)(2,1)S(1)}, bf16[1024,128]{1,0:T(8,128)(2,1)}, u32[]{:S(2)}, u32[]{:S(2)}) collective-permute-start(bf16[1024,128]{1,0:T(8,128)(2,1)S(1)} %add_convert_fusion.3.refs_0_), channel_id=1, source_target_pairs={{6,0},{14,8},{22,16},{30,24}} | collective-permute-start | bytes 786440 | tf_op jit(solution)/shard_map/ppermute | solution.py:173
  39.6 18.9 %collective-permute-start.18 = (bf16[1024,128]{1,0:T(8,128)(2,1)S(1)}, bf16[1024,128]{1,0:T(8,128)(2,1)S(1)}, u32[]{:S(2)}, u32[]{:S(2)}) collective-permute-start(bf16[1024,128]{1,0:T(8,128)(2,1)S(1)} %collective-permute-done.9.refs_4_), channel_id=1, source_target_pairs={{0,1},{1,2},{2,3},{3,4},{4,5},{5,6},{6,7},{7,0},{8,9},{9,10},{10,1... | collective-permute-start | bytes 786440 | tf_op jit(solution)/shard_map/ppermute | solution.py:173
  48.9 13.9 %collective-permute-start.11 = (bf16[1024,128]{1,0:T(8,128)(2,1)S(1)}, bf16[1024,128]{1,0:T(8,128)(2,1)S(1)}, u32[]{:S(2)}, u32[]{:S(2)}) collective-permute-start(bf16[1024,128]{1,0:T(8,128)(2,1)S(1)} %add_convert_fusion.2.refs_0_), channel_id=1, source_target_pairs={{2,0},{10,8},{18,16},{26,24}} | collective-permute-start | bytes 786440 | tf_op jit(solution)/shard_map/ppermute | solution.py:173
  50.2 12.6 %collective-permute-start.12 = (bf16[1024,128]{1,0:T(8,128)(2,1)S(1)}, bf16[1024,128]{1,0:T(8,128)(2,1)S(1)}, u32[]{:S(2)}, u32[]{:S(2)}) collective-permute-start(bf16[1024,128]{1,0:T(8,128)(2,1)S(1)} %add_convert_fusion.2.refs_0_), channel_id=1, source_target_pairs={{4,0},{12,8},{20,16},{28,24}} | collective-permute-start | bytes 786440 | tf_op jit(solution)/shard_map/ppermute | solution.py:173
  51.5 11.3 %collective-permute-start.13 = (bf16[1024,128]{1,0:T(8,128)(2,1)S(1)}, bf16[1024,128]{1,0:T(8,128)(2,1)S(1)}, u32[]{:S(2)}, u32[]{:S(2)}) collective-permute-start(bf16[1024,128]{1,0:T(8,128)(2,1)S(1)} %add_convert_fusion.2.refs_0_), channel_id=1, source_target_pairs={{6,0},{14,8},{22,16},{30,24}} | collective-permute-start | bytes 786440 | tf_op jit(solution)/shard_map/ppermute | solution.py:173
  52.8 10.0 %collective-permute-start.19 = (bf16[1024,128]{1,0:T(8,128)(2,1)S(1)}, bf16[1024,128]{1,0:T(8,128)(2,1)S(1)}, u32[]{:S(2)}, u32[]{:S(2)}) collective-permute-start(bf16[1024,128]{1,0:T(8,128)(2,1)S(1)} %get-tuple-element.35), channel_id=1, source_target_pairs={{0,2},{8,10},{16,18},{24,26}} | collective-permute-start | bytes 786440 | tf_op jit(solution)/shard_map/ppermute | solution.py:173
  58.5 17.7 %collective-permute-start.22 = (bf16[1024,128]{1,0:T(8,128)(2,1)S(1)}, bf16[1024,128]{1,0:T(8,128)(2,1)S(1)}, u32[]{:S(2)}, u32[]{:S(2)}) collective-permute-start(bf16[1024,128]{1,0:T(8,128)(2,1)S(1)} %get-tuple-element.43), channel_id=1, source_target_pairs={{0,1},{1,0},{2,3},{3,2},{4,5},{5,4},{6,7},{7,6},{8,9},{9,8},{10,11... | collective-permute-start | bytes 786440 | tf_op jit(solution)/shard_map/ppermute | solution.py:173
  68.5 36.8 %collective-permute-start.20 = (bf16[2048,128]{1,0:T(8,128)(2,1)}, bf16[2048,128]{1,0:T(8,128)(2,1)}, u32[]{:S(2)}, u32[]{:S(2)}) collective-permute-start(bf16[2048,128]{1,0:T(8,128)(2,1)} %constant_dynamic-update-slice_fusion), channel_id=1, source_target_pairs={{0,4},{8,12},{16,20},{24,28}} | collective-permute-start | bytes 1572872 | tf_op jit(solution)/shard_map/ppermute | solution.py:173
  76.3 14.0 %collective-permute-start.23 = (bf16[1024,128]{1,0:T(8,128)(2,1)S(1)}, bf16[1024,128]{1,0:T(8,128)(2,1)}, u32[]{:S(2)}, u32[]{:S(2)}) collective-permute-start(bf16[1024,128]{1,0:T(8,128)(2,1)S(1)} %add_convert_fusion.1.refs_0_), channel_id=1, source_target_pairs={{2,0},{10,8},{18,16},{26,24}} | collective-permute-start | bytes 786440 | tf_op jit(solution)/shard_map/ppermute | solution.py:173
  77.6 14.0 %collective-permute-start.24 = (bf16[1024,128]{1,0:T(8,128)(2,1)S(1)}, bf16[1024,128]{1,0:T(8,128)(2,1)}, u32[]{:S(2)}, u32[]{:S(2)}) collective-permute-start(bf16[1024,128]{1,0:T(8,128)(2,1)S(1)} %add_convert_fusion.1.refs_0_), channel_id=1, source_target_pairs={{4,0},{12,8},{20,16},{28,24}} | collective-permute-start | bytes 786440 | tf_op jit(solution)/shard_map/ppermute | solution.py:173
  78.9 12.7 %collective-permute-start.25 = (bf16[1024,128]{1,0:T(8,128)(2,1)S(1)}, bf16[1024,128]{1,0:T(8,128)(2,1)}, u32[]{:S(2)}, u32[]{:S(2)}) collective-permute-start(bf16[1024,128]{1,0:T(8,128)(2,1)S(1)} %add_convert_fusion.1.refs_0_), channel_id=1, source_target_pairs={{6,0},{14,8},{22,16},{30,24}} | collective-permute-start | bytes 786440 | tf_op jit(solution)/shard_map/ppermute | solution.py:173
  81.4 37.1 %collective-permute-start.36 = (bf16[1024,128]{1,0:T(8,128)(2,1)S(1)}, bf16[1024,128]{1,0:T(8,128)(2,1)}, u32[]{:S(2)}, u32[]{:S(2)}) collective-permute-start(bf16[1024,128]{1,0:T(8,128)(2,1)S(1)} %add_convert_fusion.refs_8_), channel_id=1, source_target_pairs={{2,0},{10,8},{18,16},{26,24}} | collective-permute-start | bytes 786440 | tf_op jit(solution)/shard_map/ppermute | solution.py:173
  90.3 28.2 %collective-permute-start.37 = (bf16[1024,128]{1,0:T(8,128)(2,1)S(1)}, bf16[1024,128]{1,0:T(8,128)(2,1)}, u32[]{:S(2)}, u32[]{:S(2)}) collective-permute-start(bf16[1024,128]{1,0:T(8,128)(2,1)S(1)} %add_convert_fusion.refs_8_), channel_id=1, source_target_pairs={{4,0},{12,8},{20,16},{28,24}} | collective-permute-start | bytes 786440 | tf_op jit(solution)/shard_map/ppermute | solution.py:173
  98.0 14.5 %collective-permute-start.29 = (bf16[1024,128]{1,0:T(8,128)(2,1)S(1)}, bf16[1024,128]{1,0:T(8,128)(2,1)S(1)}, u32[]{:S(2)}, u32[]{:S(2)}) collective-permute-start(bf16[1024,128]{1,0:T(8,128)(2,1)S(1)} %get-tuple-element.49), channel_id=1, source_target_pairs={{0,4},{8,12},{16,20},{24,28}} | collective-permute-start | bytes 786440 | tf_op jit(solution)/shard_map/ppermute | solution.py:173
  109.3 10.1 %collective-permute-start.38 = (bf16[1024,128]{1,0:T(8,128)(2,1)S(1)}, bf16[1024,128]{1,0:T(8,128)(2,1)S(1)}, u32[]{:S(2)}, u32[]{:S(2)}) collective-permute-start(bf16[1024,128]{1,0:T(8,128)(2,1)S(1)} %add_convert_fusion.refs_8_), channel_id=1, source_target_pairs={{6,0},{14,8},{22,16},{30,24}} | collective-permute-start | bytes 786440 | tf_op jit(solution)/shard_map/ppermute | solution.py:173
  112.5 29.5 %collective-permute-start.21 = (bf16[2048,128]{1,0:T(8,128)(2,1)}, bf16[2048,128]{1,0:T(8,128)(2,1)}, u32[]{:S(2)}, u32[]{:S(2)}) collective-permute-start(bf16[2048,128]{1,0:T(8,128)(2,1)} %broadcast_select_fusion.1), channel_id=1, source_target_pairs={{0,2},{4,6},{8,10},{12,14},{16,18},{20,22},{24,26},{28,30}} | collective-permute-start | bytes 1572872 | tf_op jit(solution)/shard_map/ppermute | solution.py:173
  116.5 24.5 %collective-permute-start.30 = (bf16[1024,128]{1,0:T(8,128)(2,1)}, bf16[1024,128]{1,0:T(8,128)(2,1)}, u32[]{:S(2)}, u32[]{:S(2)}) collective-permute-start(bf16[1024,128]{1,0:T(8,128)(2,1)} %broadcast_select_fusion.4), channel_id=1, source_target_pairs={{0,2},{4,6},{8,10},{12,14},{16,18},{20,22},{24,26},{28,30}} | collective-permute-start | bytes 786440 | tf_op jit(solution)/shard_map/ppermute | solution.py:173
  131.6 11.6 %collective-permute-start.39 = (bf16[1024,128]{1,0:T(8,128)(2,1)S(1)}, bf16[1024,128]{1,0:T(8,128)(2,1)S(1)}, u32[]{:S(2)}, u32[]{:S(2)}) collective-permute-start(bf16[1024,128]{1,0:T(8,128)(2,1)S(1)} %shard_map.91), channel_id=1, source_target_pairs={{0,2},{8,10},{16,18},{24,26}} | collective-permute-start | bytes 786440 | tf_op jit(solution)/shard_map/ppermute | solution.py:173
  132.9 10.3 %collective-permute-start.40 = (bf16[1024,128]{1,0:T(8,128)(2,1)S(1)}, bf16[1024,128]{1,0:T(8,128)(2,1)S(1)}, u32[]{:S(2)}, u32[]{:S(2)}) collective-permute-start(bf16[1024,128]{1,0:T(8,128)(2,1)S(1)} %shard_map.91), channel_id=1, source_target_pairs={{0,4},{8,12},{16,20},{24,28}} | collective-permute-start | bytes 786440 | tf_op jit(solution)/shard_map/ppermute | solution.py:173
  (45 other events, 186.1 us)

commit v4 on v3

v4 whole, which is shorter than its diff:
```python
import functools

import jax
import jax.numpy as jnp
from jax import lax
from jax.experimental import pallas as pl
from jax.experimental.pallas import tpu as pltpu
from jax.sharding import PartitionSpec as P


STEPS = 4

F32 = jnp.float32
BF16 = jnp.bfloat16
VMEM = pl.BlockSpec(memory_space=pltpu.VMEM)
SMEM = pl.BlockSpec(memory_space=pltpu.SMEM)


def peer_of(group, hop, groups):
    return group ^ hop if groups & (groups - 1) == 0 else (group + hop) % groups


def source_of(group, hop, groups):
    return group ^ hop if groups & (groups - 1) == 0 else (group - hop) % groups


def call(kernel, out_shape, scalars, arrays, spare=2):
    held = sum(a.size * a.dtype.itemsize for a in (*arrays, *jax.tree.leaves(out_shape)))
    return pl.pallas_call(
        kernel,
        out_shape=out_shape,
        in_specs=[SMEM] * len(scalars) + [VMEM] * len(arrays),
        out_specs=jax.tree.map(lambda _: VMEM, out_shape),
        compiler_params=pltpu.CompilerParams(vmem_limit_bytes=held + spare * (1 << 20)),
    )(*scalars, *arrays)


def dot(a, b):
    return jnp.dot(a, b, preferred_element_type=F32)


def dense_kernel(groups, block, depth, rows, counts, weights, dense):
    me = lax.axis_index("group")
    dense[...] = jnp.zeros_like(dense)
    for hop in range(groups):
        source = source_of(me, hop, groups)
        for entry in range(depth):

            @pl.when(entry < counts[0, source])
            def _():
                start = pl.multiple_of(rows[0, source, entry] * block, block)
                dense[pl.ds(start, block), hop * block : (hop + 1) * block] = weights[source, entry]


def sheet_kernel(self_block, column, row, sheet):
    scaled = self_block[...].astype(F32) * column[...]
    first = scaled.astype(BF16)
    second = dot(first, first)
    total = second - scaled
    third = dot(second.astype(BF16), first)
    sheet[...] = ((total - third) * row[...]).astype(BF16)


def product(matrix, blocks, part, block):
    total = None
    for hop, ref in enumerate(blocks):
        term = dot(matrix[:, hop * block : (hop + 1) * block], ref[part * block : (part + 1) * block, :])
        total = term if total is None else total + term
    return total


def emit(groups, block, sends, part, source, table):
    me = lax.axis_index("group")
    for hop, out in enumerate(sends):
        start = pl.multiple_of(table[0, me, peer_of(me, hop, groups)] * block, block)
        out[part * block : (part + 1) * block, :] = source[pl.ds(start, block), :]


def pick_kernel(groups, block, table, first, second, *sends):
    emit(groups, block, sends, 0, first, table)
    emit(groups, block, sends, 1, second, table)


def early_kernel(groups, block, matrix, *refs):
    blocks, outs = refs[:groups], refs[groups:]
    delay = lax.axis_index("delay")
    for part, out in enumerate(outs):

        @pl.when(delay >= part)
        def _():
            out[...] = product(matrix, blocks, part, block).astype(BF16)

        @pl.when(delay < part)
        def _():
            out[...] = jnp.zeros_like(out)


def plus_kernel(first, second, out):
    out[...] = (first[...].astype(F32) + second[...].astype(F32)).astype(BF16)


def near_kernel(groups, block, matrix, aside, *refs):
    blocks, refs = refs[:groups], refs[groups:]
    older, refs = (refs[:groups], refs[groups:]) if len(refs) > 2 else (None, refs)
    wide, narrow = refs
    total = product(matrix, blocks, 0, block)
    narrow[...] = jnp.where(lax.axis_index("delay") >= 2, total, 0.0).astype(BF16)
    if older is not None:
        total = total + product(aside, older, 1, block)
    wide[...] = total


def law_of(driving, sheet, column):
    return (driving * column[...] + dot(sheet[...], driving.astype(BF16))).astype(BF16)


def driving_of(incident, step, terms):
    driving = incident[step].astype(F32)
    for ref in terms:
        driving = driving - ref[...].astype(F32)
    return driving


def step_kernel(groups, block, step, fields, table, other, sheet, column, incident, *refs):
    terms, refs = refs[:fields], refs[fields:]
    delay = lax.axis_index("delay")
    history = passed = second = None
    if step < 2:
        history, refs = refs[0], refs[1:]
    if step == 1:
        second, refs = refs[0], refs[1:]
    if step > 0:
        passed, refs = refs[0], refs[1:]
    carry, sends = refs[0], refs[1:]
    current = law_of(driving_of(incident, step, terms), sheet, column)
    if step > 0:

        @pl.when(delay == 0)
        def _():
            carry[...] = current

        @pl.when(delay != 0)
        def _():
            carry[...] = passed[...]

    else:
        carry[...] = current
    if step == 2:
        emit(groups, block, sends, 0, carry, table)
        return

    @pl.when(delay == 0)
    def _():
        emit(groups, block, sends, 0, carry, table)
        emit(groups, block, sends, 1, carry, other)

    @pl.when((delay != 0) if step == 0 else (delay != 0) & (delay != 2))
    def _():
        emit(groups, block, sends, 0, history, table)
        emit(groups, block, sends, 1, history, table)

    if step == 1:

        @pl.when(delay == 2)
        def _():
            emit(groups, block, sends, 0, second, table)
            emit(groups, block, sends, 1, second, table)


def last_kernel(groups, block, step, sheet, column, incident, matrix, aside, *refs):
    blocks, older, refs = refs[:groups], refs[groups : 2 * groups], refs[2 * groups :]
    terms, passed, carry = refs[:-2], refs[-2], refs[-1]
    delay = lax.axis_index("delay")
    driving = driving_of(incident, step, terms)
    driving = driving - product(matrix, blocks, 0, block) - product(aside, older, 1, block)
    current = law_of(driving, sheet, column)

    @pl.when(delay == 0)
    def _():
        carry[...] = current

    @pl.when(delay != 0)
    def _():
        carry[...] = passed[...]


def choose_kernel(plan, *refs):
    sources, out = refs[:-1], refs[-1]
    rows = sources[0].shape[0]
    chip = lax.axis_index("delay") // 2
    for z, chosen in enumerate(plan):

        @pl.when(chip == z)
        def _():
            for place, index in enumerate(chosen):
                out[place * rows : (place + 1) * rows, :] = sources[index][...]


def out_kernel(early, early_other, late, late_other, out, sems):
    split = early.shape[0]

    def write(first, second):
        copies = (
            pltpu.make_async_copy(first, out.at[:split], sems.at[0]),
            pltpu.make_async_copy(second, out.at[split:], sems.at[1]),
        )
        for copy in copies:
            copy.start()
        for copy in copies:
            copy.wait()

    odd = lax.axis_index("delay") % 2

    @pl.when(odd == 0)
    def _():
        write(early, late)

    @pl.when(odd == 1)
    def _():
        write(early_other, late_other)


def local(retarded, block_row, block_count, send_pick, history, incident, self_block, sheet_diag):
    groups = lax.axis_size("group")
    delays = lax.axis_size("delay")
    chips = delays // 2
    weights = retarded[0]
    depth, block = weights.shape[1], weights.shape[-1]
    rows, columns = history.shape[1:]
    shape = jax.ShapeDtypeStruct
    piece = lambda parts=1: shape((parts * block, columns), BF16)
    whole = shape((rows, columns), BF16)
    wide_whole = shape((rows, columns), F32)
    bind = functools.partial

    def along(array, pairs):
        return lax.ppermute(array, "delay", pairs)

    def swap(array):
        return along(array, [(d, d ^ 1) for d in range(delays)])

    def shift(array, by=1):
        return along(array, [(d, (d + by) % delays) for d in range(delays)])

    def exchange(sends):
        return [sends[0]] + [
            lax.ppermute(sends[hop], "group", [(g, peer_of(g, hop, groups)) for g in range(groups)])
            for hop in range(1, groups)
        ]

    def gathered(term):
        other = swap(term)
        chip = call(plus_kernel, whole, (), (term, other))
        return [chip] + [along(chip, [(2 * z, 0)]) for z in range(1, chips)]

    earlier = shift(history[0])
    other = swap(send_pick)
    inverse = 1.0 / sheet_diag
    column, row = inverse[:, None], inverse[None, :]
    dense = call(
        bind(dense_kernel, groups, block, depth),
        shape((rows, groups * block), BF16), (block_row, block_count), (weights,),
    )
    sheet = call(sheet_kernel, shape((rows, rows), BF16), (), (self_block, column, row), 20)

    sends = call(
        bind(pick_kernel, groups, block), [piece(2)] * groups, (send_pick,), (history[0], earlier)
    )
    blocks = exchange(sends)
    earlier = shift(earlier)
    terms = call(bind(early_kernel, groups, block), [whole, whole], (), (dense, *blocks))
    fields = gathered(terms[0])
    later = gathered(terms[1])
    oldest = shift(earlier)
    aside = swap(dense)

    law = (sheet, column, incident)
    tables = (send_pick, other)
    found, slots = [], []

    def stepped(step, fields, extra, parts):
        carry, *sends = call(
            bind(step_kernel, groups, block, step, len(fields)),
            [whole] + [piece(parts)] * groups, tables, (*law, *fields, *extra),
        )
        found.append(carry)
        return sends

    def rotate(array):
        slots.append(shift(array, 2))

    sends = stepped(0, fields, (earlier,), 2)
    older = exchange(sends)
    rotate(found[0])
    wide, narrow = call(
        bind(near_kernel, groups, block), [wide_whole, whole], (), (dense, aside, *older)
    )
    fields = gathered(narrow)
    sends = stepped(1, (*later, wide), (oldest, slots[0], slots[-1]), 2)
    blocks = exchange(sends)
    rotate(found[1])
    wide, narrow = call(
        bind(near_kernel, groups, block), [wide_whole, whole], (), (dense, aside, *blocks, *older)
    )
    later = gathered(narrow)
    sends = stepped(2, (*fields, wide), (slots[-1],), 1)
    older = blocks
    blocks = exchange(sends)
    rotate(found[2])
    carry = call(
        bind(last_kernel, groups, block, 3),
        whole, (), (*law, dense, aside, *blocks, *older, *later, slots[-1]),
    )
    found.append(carry)
    heads = [z for z in range(STEPS) if z < chips]
    finals = [
        along(carry, [(2 * z, 2 * (z + k)) for z in heads if z + k < chips]) for k in range(1, chips)
    ]

    def origin(step, z):
        beyond = z - (STEPS - 1 - step)
        if z == 0:
            return found[step]
        return finals[beyond - 1] if beyond > 0 else slots[step + z - 1]

    def chosen(steps):
        sources, plan = [], []
        for z in range(chips):
            plan.append([])
            for step in steps:
                array = origin(step, z)
                known = [k for k, source in enumerate(sources) if source is array]
                if not known:
                    sources.append(array)
                plan[-1].append(known[0] if known else len(sources) - 1)
        return call(
            bind(choose_kernel, plan), shape((len(steps) * rows, columns), BF16), (), sources
        )

    ready = [s for s in range(STEPS) if chips - 1 <= STEPS - 1 - s] or [0]
    early = chosen(ready)
    early_other = swap(early)
    late = chosen([s for s in range(STEPS) if s not in ready])
    late_other = swap(late)
    out = pl.pallas_call(
        out_kernel,
        out_shape=shape((STEPS * rows, columns), BF16),
        in_specs=[VMEM] * 4,
        out_specs=pl.BlockSpec(memory_space=pl.ANY),
        scratch_shapes=[pltpu.SemaphoreType.DMA((2,))],
        compiler_params=pltpu.CompilerParams(vmem_limit_bytes=4 << 20),
    )(early, early_other, late, late_other)
    return out.reshape(STEPS, rows, columns)


def solution(mesh):
    placed = (
        P("delay", "group", None, None, None),
        P("delay", "group", None),
        P("delay", "group"),
        P("delay", None, None),
        P("delay", "group", None),
        P(None, "group", None),
        P("group", None),
        P("group"),
    )

    return jax.shard_map(local, mesh=mesh, in_specs=placed, out_specs=P(None, "group", None), check_vma=False)
```

time: 151 us -> 146 us (0.967)
  waiting for transfers between devices: 37.8 us -> 71.2 us
  local copies, waits for them, and re-layouts: 22 us -> 4.67 us
  starting transfers between devices: 57.6 us -> 44.2 us
  other arithmetic: 9.5 us -> 0.01 us
    ppermute x31 -> x29, waiting for transfers between devices: 30.2 us -> 50.8 us  [along(): return lax.ppermute(array, 'delay', pairs)]
    unnamed x54 -> x15, local copies, waits for them, and re-layouts: 20.4 us -> 4.45 us
    ppermute x31 -> x29, starting transfers between devices: 42.7 us -> 29.4 us  [along(): return lax.ppermute(array, 'delay', pairs)]
    ppermute x12, waiting for transfers between devices: 7.58 us -> 20.4 us  [exchange(): lax.ppermute(sends[hop], 'group', [(g, peer_of(g, hop, groups)) for g in...]
    select_n x8 -> x0, other arithmetic: 6.04 us -> none  [the longest x4 4.72 us: spread_tree(): held = jnp.where(z % (2 * stride) == stride, got, held)]
    convert_element_type x4 -> x0, other arithmetic: 2.26 us -> none  [plus(): return (a.astype(F32) + b.astype(F32)).astype(BF16)]
    pallas_call x10 -> x16, Pallas kernels: 22.1 us -> 21.6 us  [call(): pl.pallas_call(kernel, out_shape=out_shape, in_specs=[SMEM] * len(scalars...]
  transfers between devices with their start and end apart: 43 -> 41, of which waited for: 15 -> 21; matrix products, arithmetic and copies ran while one was open for 7% -> 0% of each run, Pallas kernels for 14% -> 12%
where the time goes in v4:
time: 146 us; the launch traced here: 143 us
  waiting for transfers between devices  71.2 us (49%)
  starting transfers between devices  44.2 us (30%)
  Pallas kernels  22.6 us (15%)
  local copies, waits for them, and re-layouts  4.67 us (3%)
    ppermute x29, waiting for transfers between devices, along(): return lax.ppermute(array, 'delay', pairs)  50.8 us
    ppermute x29, starting transfers between devices, along(): return lax.ppermute(array, 'delay', pairs)  29.4 us
    pallas_call x16, Pallas kernels, call(): pl.pallas_call(kernel, out_shape=out_shape, in_specs=[SMEM] * len(scalars...  21.6 us
    ppermute x12, waiting for transfers between devices, exchange(): lax.ppermute(sends[hop], 'group', [(g, peer_of(g, hop, groups)) for g in...  20.4 us
    ppermute x12, starting transfers between devices, exchange(): lax.ppermute(sends[hop], 'group', [(g, peer_of(g, hop, groups)) for g in...  14.8 us
    unnamed x15, local copies, waits for them, and re-layouts  4.45 us
  transfers between devices with their start and end apart: 41, of which 21 were waited for; matrix products, arithmetic and copies ran while one was open for 0% of the time, Pallas kernels for 12%

profile of v4, /device:TPU:0, one launch (start us, length us, event | category | flops | bytes accessed | tf_op | source)
XLA Modules:
  0.0 143.3 jit_solution(11049614717128695815)
XLA Ops:
  4.4 8.7 %collective-permute-done.1.second = bf16[1024,128]{1,0:T(8,128)(2,1)S(1)} collective-permute-done((bf16[1024,128]{1,0:T(8,128)(2,1)S(1)}, bf16[1024,128]{1,0:T(8,128)(2,1)S(1)}, u32[]{:S(2)}, u32[]{:S(2)}) %collective-permute-start.1) | collective-permute-done | bytes 262176 | tf_op jit(solution)/shard_map/ppermute | solution.py:237
  17.2 1.7 %collective-permute-done.2.refs_1_ = bf16[512,128]{1,0:T(8,128)(2,1)S(1)} collective-permute-done((bf16[512,128]{1,0:T(8,128)(2,1)S(1)}, bf16[512,128]{1,0:T(8,128)(2,1)S(1)}, u32[]{:S(2)}, u32[]{:S(2)}) %collective-permute-start.2) | collective-permute-done | bytes 131104 | tf_op jit(solution)/shard_map/ppermute | solution.py:247
  20.2 2.4 %collective-permute-done.4.refs_3_ = bf16[512,128]{1,0:T(8,128)(2,1)S(1)} collective-permute-done((bf16[512,128]{1,0:T(8,128)(2,1)S(1)}, bf16[512,128]{1,0:T(8,128)(2,1)S(1)}, u32[]{:S(2)}, u32[]{:S(2)}) %collective-permute-start.4) | collective-permute-done | bytes 131104 | tf_op jit(solution)/shard_map/ppermute | solution.py:247
  29.0 2.2 %collective-permute-done.9.refs_4_ = bf16[1024,128]{1,0:T(8,128)(2,1)S(1)} collective-permute-done((bf16[1024,128]{1,0:T(8,128)(2,1)S(1)}, bf16[1024,128]{1,0:T(8,128)(2,1)S(1)}, u32[]{:S(2)}, u32[]{:S(2)}) %collective-permute-start.9) | collective-permute-done | bytes 262176 | tf_op jit(solution)/shard_map/ppermute | solution.py:237
  31.4 1.6 %copy-done.1 = bf16[1024,1024]{1,0:T(8,128)(2,1)S(1)} copy-done((bf16[1024,1024]{1,0:T(8,128)(2,1)S(1)}, bf16[1024,1024]{1,0:T(8,128)(2,1)}, u32[]{:S(2)}) %copy-start.1) | copy-done | bytes 2097176
  33.0 4.6 %shard_map.82.sheet = bf16[1024,1024]{1,0:T(8,128)(2,1)S(1)} custom-call(bf16[1024,1024]{1,0:T(8,128)(2,1)S(1)} %copy-done.1, f32[1024,1]{1,0:T(8,128)S(1)} %copy.10.column, f32[1,1024]{1,0:T(1,128)S(1)} %bitcast.9), custom_call_target="tpu_custom_call" | custom-call | tf_op jit(solution)/shard_map/pallas_call | solution.py:29
  37.7 2.0 %collective-permute-done.6.refs_1_ = bf16[1024,128]{1,0:T(8,128)(2,1)} collective-permute-done((bf16[1024,128]{1,0:T(8,128)(2,1)S(1)}, bf16[1024,128]{1,0:T(8,128)(2,1)}, u32[]{:S(2)}, u32[]{:S(2)}) %collective-permute-start.6) | collective-permute-done | bytes 262176 | tf_op jit(solution)/shard_map/ppermute | solution.py:237
  39.7 2.0 %shard_map.87 = (bf16[1024,128]{1,0:T(8,128)(2,1)S(1)}, bf16[512,128]{1,0:T(8,128)(2,1)S(1)}, bf16[512,128]{1,0:T(8,128)(2,1)S(1)}, bf16[512,128]{1,0:T(8,128)(2,1)S(1)}, bf16[512,128]{1,0:T(8,128)(2,1)S(1)}) custom-call(s32[1,4,4]{2,1,0:T(4,128)S(1)} %copy-done.4, s32[1,4,4]{2,1,0:T(4,128)S(1)} %collective-permute-done.other, ...), custom_call_target="tpu_custom_call" | custom-call | tf_op jit(solution)/shard_map/pallas_call | solution.py:29
  42.7 2.5 %collective-permute-start.18 = (bf16[512,128]{1,0:T(8,128)(2,1)S(1)}, bf16[512,128]{1,0:T(8,128)(2,1)S(1)}, u32[]{:S(2)}, u32[]{:S(2)}) collective-permute-start(bf16[512,128]{1,0:T(8,128)(2,1)S(1)} %get-tuple-element.40), channel_id=1, source_target_pairs={{0,24},{8,16},{16,8},{24,0},{1,25},{9,17},{17,9},{25,1},{2,26},{10... | collective-permute-start | bytes 393224 | tf_op jit(solution)/shard_map/ppermute | solution.py:247
  52.5 2.3 %shard_map.89 = (f32[1024,128]{1,0:T(8,128)S(1)}, bf16[1024,128]{1,0:T(8,128)(2,1)S(1)}) custom-call(bf16[1024,1024]{1,0:T(8,128)(2,1)S(1)} %shard_map.83.matrix, bf16[1024,1024]{1,0:T(8,128)(2,1)} %collective-permute-done.15.aside, bf16[512,128]{1,0:T(8,128)(2,1)S(1)} %get-tuple-element.37.refs_0_.refs_4_, ...), custom_call_target="tpu_custom_call" | custom-call | tf_op jit(solution)/shard_map/pallas_call | solution.py:29
  54.9 12.0 %collective-permute-done.12.refs_1_ = bf16[1024,128]{1,0:T(8,128)(2,1)S(1)} collective-permute-done((bf16[1024,128]{1,0:T(8,128)(2,1)S(1)}, bf16[1024,128]{1,0:T(8,128)(2,1)S(1)}, u32[]{:S(2)}, u32[]{:S(2)}) %collective-permute-start.12) | collective-permute-done | bytes 262176 | tf_op jit(solution)/shard_map/ppermute | solution.py:237
  70.1 1.8 %collective-permute-start.27 = (bf16[512,128]{1,0:T(8,128)(2,1)S(1)}, bf16[512,128]{1,0:T(8,128)(2,1)S(1)}, u32[]{:S(2)}, u32[]{:S(2)}) collective-permute-start(bf16[512,128]{1,0:T(8,128)(2,1)S(1)} %get-tuple-element.47), channel_id=1, source_target_pairs={{0,24},{8,16},{16,8},{24,0},{1,25},{9,17},{17,9},{25,1},{2,26},{10... | collective-permute-start | bytes 393224 | tf_op jit(solution)/shard_map/ppermute | solution.py:247
  76.0 2.8 %shard_map.92 = (f32[1024,128]{1,0:T(8,128)S(1)}, bf16[1024,128]{1,0:T(8,128)(2,1)S(1)}) custom-call(bf16[1024,1024]{1,0:T(8,128)(2,1)S(1)} %shard_map.83.matrix, bf16[1024,1024]{1,0:T(8,128)(2,1)} %collective-permute-done.15.aside, bf16[512,128]{1,0:T(8,128)(2,1)S(1)} %get-tuple-element.44.refs_0_.refs_4_, ...), custom_call_target="tpu_custom_call" | custom-call | tf_op jit(solution)/shard_map/pallas_call | solution.py:29
  84.4 5.3 %collective-permute-done.20.refs_5_.refs_2_.refs_3_ = bf16[1024,128]{1,0:T(8,128)(2,1)S(1)} collective-permute-done((bf16[1024,128]{1,0:T(8,128)(2,1)S(1)}, bf16[1024,128]{1,0:T(8,128)(2,1)S(1)}, u32[]{:S(2)}, u32[]{:S(2)}) %collective-permute-start.20) | collective-permute-done | bytes 262176 | tf_op jit(solution)/shard_map/ppermute | solution.py:237
  90.9 12.6 %collective-permute-done.22.refs_1_ = bf16[1024,128]{1,0:T(8,128)(2,1)S(1)} collective-permute-done((bf16[1024,128]{1,0:T(8,128)(2,1)S(1)}, bf16[1024,128]{1,0:T(8,128)(2,1)S(1)}, u32[]{:S(2)}, u32[]{:S(2)}) %collective-permute-start.22) | collective-permute-done | bytes 262176 | tf_op jit(solution)/shard_map/ppermute | solution.py:237
  107.4 3.5 %collective-permute-done.30.refs_1_ = bf16[256,128]{1,0:T(8,128)(2,1)S(1)} collective-permute-done((bf16[256,128]{1,0:T(8,128)(2,1)S(1)}, bf16[256,128]{1,0:T(8,128)(2,1)S(1)}, u32[]{:S(2)}, u32[]{:S(2)}) %collective-permute-start.30) | collective-permute-done | bytes 65568 | tf_op jit(solution)/shard_map/ppermute | solution.py:247
  112.3 2.8 %collective-permute-done.31.refs_2_ = bf16[256,128]{1,0:T(8,128)(2,1)S(1)} collective-permute-done((bf16[256,128]{1,0:T(8,128)(2,1)S(1)}, bf16[256,128]{1,0:T(8,128)(2,1)S(1)}, u32[]{:S(2)}, u32[]{:S(2)}) %collective-permute-start.31) | collective-permute-done | bytes 65568 | tf_op jit(solution)/shard_map/ppermute | solution.py:247
  115.1 1.8 %collective-permute-start.32 = (bf16[256,128]{1,0:T(8,128)(2,1)S(1)}, bf16[256,128]{1,0:T(8,128)(2,1)S(1)}, u32[]{:S(2)}, u32[]{:S(2)}) collective-permute-start(bf16[256,128]{1,0:T(8,128)(2,1)S(1)} %get-tuple-element.53), channel_id=1, source_target_pairs={{0,24},{8,16},{16,8},{24,0},{1,25},{9,17},{17,9},{25,1},{2,26},{10... | collective-permute-start | bytes 196616 | tf_op jit(solution)/shard_map/ppermute | solution.py:247
  116.9 3.4 %collective-permute-done.32.refs_3_ = bf16[256,128]{1,0:T(8,128)(2,1)S(1)} collective-permute-done((bf16[256,128]{1,0:T(8,128)(2,1)S(1)}, bf16[256,128]{1,0:T(8,128)(2,1)S(1)}, u32[]{:S(2)}, u32[]{:S(2)}) %collective-permute-start.32) | collective-permute-done | bytes 65568 | tf_op jit(solution)/shard_map/ppermute | solution.py:247
  120.3 3.4 %shard_map.96.refs_2_ = bf16[1024,128]{1,0:T(8,128)(2,1)S(1)} custom-call(bf16[1024,1024]{1,0:T(8,128)(2,1)S(1)} %shard_map.82.sheet, f32[1024,1]{1,0:T(8,128)S(1)} %copy.10.column, bf16[4,1024,128]{2,1,0:T(8,128)(2,1)S(1)} %copy-done, bf16[1024,1024]{1,0:T(8,128)(2,1)S(1)} %shard_map.83.matrix, bf16[1024,1024]{1,0:T(8,128)(2,1)} %collective-permute-done.15.aside, ...), custom_call_target="tpu_custom_call" | custom-call | tf_op jit(solution)/shard_map/pallas_call | solution.py:29
  125.1 7.5 %collective-permute-start.38 = (bf16[1024,128]{1,0:T(8,128)(2,1)S(1)}, bf16[1024,128]{1,0:T(8,128)(2,1)S(1)}, u32[]{:S(2)}, u32[]{:S(2)}) collective-permute-start(bf16[1024,128]{1,0:T(8,128)(2,1)S(1)} %shard_map.96.refs_2_), channel_id=1, source_target_pairs={{0,4},{2,6},{8,12},{10,14},{16,20},{18,22},{24,28},{26,30}} | collective-permute-start | bytes 786440 | tf_op jit(solution)/shard_map/ppermute | solution.py:237
  133.9 2.6 %collective-permute-done.38.refs_6_ = bf16[1024,128]{1,0:T(8,128)(2,1)S(1)} collective-permute-done((bf16[1024,128]{1,0:T(8,128)(2,1)S(1)}, bf16[1024,128]{1,0:T(8,128)(2,1)S(1)}, u32[]{:S(2)}, u32[]{:S(2)}) %collective-permute-start.38) | collective-permute-done | bytes 262176 | tf_op jit(solution)/shard_map/ppermute | solution.py:237
  136.5 2.8 %collective-permute-done.39.refs_7_ = bf16[1024,128]{1,0:T(8,128)(2,1)S(1)} collective-permute-done((bf16[1024,128]{1,0:T(8,128)(2,1)S(1)}, bf16[1024,128]{1,0:T(8,128)(2,1)S(1)}, u32[]{:S(2)}, u32[]{:S(2)}) %collective-permute-start.39) | collective-permute-done | bytes 262176 | tf_op jit(solution)/shard_map/ppermute | solution.py:237
  140.1 2.0 %collective-permute-done.29.early_other = bf16[1024,128]{1,0:T(8,128)(2,1)S(1)} collective-permute-done((bf16[1024,128]{1,0:T(8,128)(2,1)S(1)}, bf16[1024,128]{1,0:T(8,128)(2,1)S(1)}, u32[]{:S(2)}, u32[]{:S(2)}) %collective-permute-start.29) | collective-permute-done | bytes 262176 | tf_op jit(solution)/shard_map/ppermute | solution.py:237
  (92 shorter events, 48.6 us)
Async XLA Ops:
  3.7 47.6 %collective-permute-start.15 = (bf16[1024,1024]{1,0:T(8,128)(2,1)S(1)}, bf16[1024,1024]{1,0:T(8,128)(2,1)}, u32[]{:S(2)}, u32[]{:S(2)}) collective-permute-start(bf16[1024,1024]{1,0:T(8,128)(2,1)S(1)} %shard_map.83.matrix), channel_id=1, source_target_pairs={{0,1},{1,0},{2,3},{3,2},{4,5},{5,4},{6,7},{7,6},{8,9},{9,8},{10,11... | collective-permute-start | bytes 6291464 | tf_op jit(solution)/shard_map/ppermute | solution.py:237
  4.3 8.8 %collective-permute-start.1 = (bf16[1024,128]{1,0:T(8,128)(2,1)S(1)}, bf16[1024,128]{1,0:T(8,128)(2,1)S(1)}, u32[]{:S(2)}, u32[]{:S(2)}) collective-permute-start(bf16[1024,128]{1,0:T(8,128)(2,1)S(1)} %bitcast.6), channel_id=1, source_target_pairs={{0,1},{1,2},{2,3},{3,4},{4,5},{5,6},{6,7},{7,0},{8,9},{9,10},{10,1... | collective-permute-start | bytes 786440 | tf_op jit(solution)/shard_map/ppermute | solution.py:237
  23.5 7.7 %collective-permute-start.9 = (bf16[1024,128]{1,0:T(8,128)(2,1)S(1)}, bf16[1024,128]{1,0:T(8,128)(2,1)S(1)}, u32[]{:S(2)}, u32[]{:S(2)}) collective-permute-start(bf16[1024,128]{1,0:T(8,128)(2,1)S(1)} %collective-permute-done.1.second), channel_id=1, source_target_pairs={{0,1},{1,2},{2,3},{3,4},{4,5},{5,6},{6,7},{7,0},{8,9},{9,10},{10,1... | collective-permute-start | bytes 786440 | tf_op jit(solution)/shard_map/ppermute | solution.py:237
  25.1 14.6 %collective-permute-start.6 = (bf16[1024,128]{1,0:T(8,128)(2,1)S(1)}, bf16[1024,128]{1,0:T(8,128)(2,1)}, u32[]{:S(2)}, u32[]{:S(2)}) collective-permute-start(bf16[1024,128]{1,0:T(8,128)(2,1)S(1)} %shard_map.86.refs_0_), channel_id=1, source_target_pairs={{2,0},{10,8},{18,16},{26,24}} | collective-permute-start | bytes 786440 | tf_op jit(solution)/shard_map/ppermute | solution.py:237
  26.4 13.3 %collective-permute-start.7 = (bf16[1024,128]{1,0:T(8,128)(2,1)S(1)}, bf16[1024,128]{1,0:T(8,128)(2,1)}, u32[]{:S(2)}, u32[]{:S(2)}) collective-permute-start(bf16[1024,128]{1,0:T(8,128)(2,1)S(1)} %shard_map.86.refs_0_), channel_id=1, source_target_pairs={{4,0},{12,8},{20,16},{28,24}} | collective-permute-start | bytes 786440 | tf_op jit(solution)/shard_map/ppermute | solution.py:237
  27.7 12.0 %collective-permute-start.8 = (bf16[1024,128]{1,0:T(8,128)(2,1)S(1)}, bf16[1024,128]{1,0:T(8,128)(2,1)}, u32[]{:S(2)}, u32[]{:S(2)}) collective-permute-start(bf16[1024,128]{1,0:T(8,128)(2,1)S(1)} %shard_map.86.refs_0_), channel_id=1, source_target_pairs={{6,0},{14,8},{22,16},{30,24}} | collective-permute-start | bytes 786440 | tf_op jit(solution)/shard_map/ppermute | solution.py:237
  31.2 14.0 %collective-permute-start.11 = (bf16[1024,128]{1,0:T(8,128)(2,1)S(1)}, bf16[1024,128]{1,0:T(8,128)(2,1)}, u32[]{:S(2)}, u32[]{:S(2)}) collective-permute-start(bf16[1024,128]{1,0:T(8,128)(2,1)S(1)} %get-tuple-element.36.first), channel_id=1, source_target_pairs={{0,1},{1,0},{2,3},{3,2},{4,5},{5,4},{6,7},{7,6},{8,9},{9,8},{10,11... | collective-permute-start | bytes 786440 | tf_op jit(solution)/shard_map/ppermute | solution.py:237
  42.7 7.3 %collective-permute-start.18 = (bf16[512,128]{1,0:T(8,128)(2,1)S(1)}, bf16[512,128]{1,0:T(8,128)(2,1)S(1)}, u32[]{:S(2)}, u32[]{:S(2)}) collective-permute-start(bf16[512,128]{1,0:T(8,128)(2,1)S(1)} %get-tuple-element.40), channel_id=1, source_target_pairs={{0,24},{8,16},{16,8},{24,0},{1,25},{9,17},{17,9},{25,1},{2,26},{10... | collective-permute-start | bytes 393224 | tf_op jit(solution)/shard_map/ppermute | solution.py:247
  45.2 9.6 %collective-permute-start.19 = (bf16[1024,128]{1,0:T(8,128)(2,1)S(1)}, bf16[1024,128]{1,0:T(8,128)(2,1)S(1)}, u32[]{:S(2)}, u32[]{:S(2)}) collective-permute-start(bf16[1024,128]{1,0:T(8,128)(2,1)S(1)} %collective-permute-done.9.refs_4_), channel_id=1, source_target_pairs={{0,1},{1,2},{2,3},{3,4},{4,5},{5,6},{6,7},{7,0},{8,9},{9,10},{10,1... | collective-permute-start | bytes 786440 | tf_op jit(solution)/shard_map/ppermute | solution.py:237
  47.1 19.8 %collective-permute-start.12 = (bf16[1024,128]{1,0:T(8,128)(2,1)S(1)}, bf16[1024,128]{1,0:T(8,128)(2,1)S(1)}, u32[]{:S(2)}, u32[]{:S(2)}) collective-permute-start(bf16[1024,128]{1,0:T(8,128)(2,1)S(1)} %shard_map.88.refs_0_), channel_id=1, source_target_pairs={{2,0},{10,8},{18,16},{26,24}} | collective-permute-start | bytes 786440 | tf_op jit(solution)/shard_map/ppermute | solution.py:237
  48.8 18.1 %collective-permute-start.13 = (bf16[1024,128]{1,0:T(8,128)(2,1)S(1)}, bf16[1024,128]{1,0:T(8,128)(2,1)S(1)}, u32[]{:S(2)}, u32[]{:S(2)}) collective-permute-start(bf16[1024,128]{1,0:T(8,128)(2,1)S(1)} %shard_map.88.refs_0_), channel_id=1, source_target_pairs={{4,0},{12,8},{20,16},{28,24}} | collective-permute-start | bytes 786440 | tf_op jit(solution)/shard_map/ppermute | solution.py:237
  50.1 16.8 %collective-permute-start.14 = (bf16[1024,128]{1,0:T(8,128)(2,1)S(1)}, bf16[1024,128]{1,0:T(8,128)(2,1)S(1)}, u32[]{:S(2)}, u32[]{:S(2)}) collective-permute-start(bf16[1024,128]{1,0:T(8,128)(2,1)S(1)} %shard_map.88.refs_0_), channel_id=1, source_target_pairs={{6,0},{14,8},{22,16},{30,24}} | collective-permute-start | bytes 786440 | tf_op jit(solution)/shard_map/ppermute | solution.py:237
  51.4 15.5 %collective-permute-start.10 = (bf16[1024,128]{1,0:T(8,128)(2,1)S(1)}, bf16[1024,128]{1,0:T(8,128)(2,1)S(1)}, u32[]{:S(2)}, u32[]{:S(2)}) collective-permute-start(bf16[1024,128]{1,0:T(8,128)(2,1)S(1)} %get-tuple-element.35.refs_0_), channel_id=1, source_target_pairs={{0,2},{1,3},{2,4},{3,5},{4,6},{5,7},{6,0},{7,1},{8,10},{9,11},{10,... | collective-permute-start | bytes 786440 | tf_op jit(solution)/shard_map/ppermute | solution.py:237
  54.8 24.2 %collective-permute-start.21 = (bf16[1024,128]{1,0:T(8,128)(2,1)S(1)}, bf16[1024,128]{1,0:T(8,128)(2,1)S(1)}, u32[]{:S(2)}, u32[]{:S(2)}) collective-permute-start(bf16[1024,128]{1,0:T(8,128)(2,1)S(1)} %get-tuple-element.43.first), channel_id=1, source_target_pairs={{0,1},{1,0},{2,3},{3,2},{4,5},{5,4},{6,7},{7,6},{8,9},{9,8},{10,11... | collective-permute-start | bytes 786440 | tf_op jit(solution)/shard_map/ppermute | solution.py:237
  78.9 10.7 %collective-permute-start.20 = (bf16[1024,128]{1,0:T(8,128)(2,1)S(1)}, bf16[1024,128]{1,0:T(8,128)(2,1)S(1)}, u32[]{:S(2)}, u32[]{:S(2)}) collective-permute-start(bf16[1024,128]{1,0:T(8,128)(2,1)S(1)} %get-tuple-element.42.refs_0_), channel_id=1, source_target_pairs={{0,2},{1,3},{2,4},{3,5},{4,6},{5,7},{6,0},{7,1},{8,10},{9,11},{10,... | collective-permute-start | bytes 786440 | tf_op jit(solution)/shard_map/ppermute | solution.py:237
  79.1 24.4 %collective-permute-start.22 = (bf16[1024,128]{1,0:T(8,128)(2,1)S(1)}, bf16[1024,128]{1,0:T(8,128)(2,1)S(1)}, u32[]{:S(2)}, u32[]{:S(2)}) collective-permute-start(bf16[1024,128]{1,0:T(8,128)(2,1)S(1)} %shard_map.91.refs_0_), channel_id=1, source_target_pairs={{2,0},{10,8},{18,16},{26,24}} | collective-permute-start | bytes 786440 | tf_op jit(solution)/shard_map/ppermute | solution.py:237
  80.4 24.4 %collective-permute-start.23 = (bf16[1024,128]{1,0:T(8,128)(2,1)S(1)}, bf16[1024,128]{1,0:T(8,128)(2,1)S(1)}, u32[]{:S(2)}, u32[]{:S(2)}) collective-permute-start(bf16[1024,128]{1,0:T(8,128)(2,1)S(1)} %shard_map.91.refs_0_), channel_id=1, source_target_pairs={{4,0},{12,8},{20,16},{28,24}} | collective-permute-start | bytes 786440 | tf_op jit(solution)/shard_map/ppermute | solution.py:237
  81.7 23.1 %collective-permute-start.24 = (bf16[1024,128]{1,0:T(8,128)(2,1)S(1)}, bf16[1024,128]{1,0:T(8,128)(2,1)S(1)}, u32[]{:S(2)}, u32[]{:S(2)}) collective-permute-start(bf16[1024,128]{1,0:T(8,128)(2,1)S(1)} %shard_map.91.refs_0_), channel_id=1, source_target_pairs={{6,0},{14,8},{22,16},{30,24}} | collective-permute-start | bytes 786440 | tf_op jit(solution)/shard_map/ppermute | solution.py:237
  83.1 37.2 %collective-permute-start.34 = (bf16[1024,128]{1,0:T(8,128)(2,1)S(1)}, bf16[1024,128]{1,0:T(8,128)(2,1)S(1)}, u32[]{:S(2)}, u32[]{:S(2)}) collective-permute-start(bf16[1024,128]{1,0:T(8,128)(2,1)S(1)} %shard_map.95.refs_8_), channel_id=1, source_target_pairs={{2,0},{10,8},{18,16},{26,24}} | collective-permute-start | bytes 786440 | tf_op jit(solution)/shard_map/ppermute | solution.py:237
  89.6 30.6 %collective-permute-start.35 = (bf16[1024,128]{1,0:T(8,128)(2,1)S(1)}, bf16[1024,128]{1,0:T(8,128)(2,1)S(1)}, u32[]{:S(2)}, u32[]{:S(2)}) collective-permute-start(bf16[1024,128]{1,0:T(8,128)(2,1)S(1)} %shard_map.95.refs_8_), channel_id=1, source_target_pairs={{4,0},{12,8},{20,16},{28,24}} | collective-permute-start | bytes 786440 | tf_op jit(solution)/shard_map/ppermute | solution.py:237
  103.5 16.8 %collective-permute-start.36 = (bf16[1024,128]{1,0:T(8,128)(2,1)S(1)}, bf16[1024,128]{1,0:T(8,128)(2,1)S(1)}, u32[]{:S(2)}, u32[]{:S(2)}) collective-permute-start(bf16[1024,128]{1,0:T(8,128)(2,1)S(1)} %shard_map.95.refs_8_), channel_id=1, source_target_pairs={{6,0},{14,8},{22,16},{30,24}} | collective-permute-start | bytes 786440 | tf_op jit(solution)/shard_map/ppermute | solution.py:237
  106.3 14.0 %collective-permute-start.28 = (bf16[1024,128]{1,0:T(8,128)(2,1)S(1)}, bf16[1024,128]{1,0:T(8,128)(2,1)S(1)}, u32[]{:S(2)}, u32[]{:S(2)}) collective-permute-start(bf16[1024,128]{1,0:T(8,128)(2,1)S(1)} %get-tuple-element.49.refs_1_), channel_id=1, source_target_pairs={{0,2},{1,3},{2,4},{3,5},{4,6},{5,7},{6,0},{7,1},{8,10},{9,11},{10,... | collective-permute-start | bytes 786440 | tf_op jit(solution)/shard_map/ppermute | solution.py:237
  123.7 10.2 %collective-permute-start.37 = (bf16[1024,128]{1,0:T(8,128)(2,1)S(1)}, bf16[1024,128]{1,0:T(8,128)(2,1)S(1)}, u32[]{:S(2)}, u32[]{:S(2)}) collective-permute-start(bf16[1024,128]{1,0:T(8,128)(2,1)S(1)} %shard_map.96.refs_2_), channel_id=1, source_target_pairs={{0,2},{2,4},{4,6},{8,10},{10,12},{12,14},{16,18},{18,20},{20,22},{... | collective-permute-start | bytes 786440 | tf_op jit(solution)/shard_map/ppermute | solution.py:237
  125.1 11.5 %collective-permute-start.38 = (bf16[1024,128]{1,0:T(8,128)(2,1)S(1)}, bf16[1024,128]{1,0:T(8,128)(2,1)S(1)}, u32[]{:S(2)}, u32[]{:S(2)}) collective-permute-start(bf16[1024,128]{1,0:T(8,128)(2,1)S(1)} %shard_map.96.refs_2_), channel_id=1, source_target_pairs={{0,4},{2,6},{8,12},{10,14},{16,20},{18,22},{24,28},{26,30}} | collective-permute-start | bytes 786440 | tf_op jit(solution)/shard_map/ppermute | solution.py:237
  (24 other events, 131.4 us)

commit v5 on v4

--- a/solution.py
+++ b/solution.py
@@ -242,6 +242,9 @@
     def shift(array, by=1):
         return along(array, [(d, (d + by) % delays) for d in range(delays)])
 
+    def onward(array, by=1):
+        return along(array, [(d, d + by) for d in range(0, delays - by, by)])
+
     def exchange(sends):
         return [sends[0]] + [
             lax.ppermute(sends[hop], "group", [(g, peer_of(g, hop, groups)) for g in range(groups)])
@@ -254,12 +257,12 @@
         return [chip] + [along(chip, [(2 * z, 0)]) for z in range(1, chips)]
 
     earlier = shift(history[0])
-    other = swap(send_pick)
     inverse = 1.0 / sheet_diag
     column, row = inverse[:, None], inverse[None, :]
+    listed = jnp.clip(block_row, 0, rows // block - 1)
     dense = call(
         bind(dense_kernel, groups, block, depth),
-        shape((rows, groups * block), BF16), (block_row, block_count), (weights,),
+        shape((rows, groups * block), BF16), (listed, block_count), (weights,),
     )
     sheet = call(sheet_kernel, shape((rows, rows), BF16), (), (self_block, column, row), 20)
 
@@ -268,10 +271,11 @@
     )
     blocks = exchange(sends)
     earlier = shift(earlier)
+    other = swap(send_pick)
     terms = call(bind(early_kernel, groups, block), [whole, whole], (), (dense, *blocks))
     fields = gathered(terms[0])
     later = gathered(terms[1])
-    oldest = shift(earlier)
+    oldest = onward(earlier)
     aside = swap(dense)
 
     law = (sheet, column, incident)
@@ -287,7 +291,7 @@
         return sends
 
     def rotate(array):
-        slots.append(shift(array, 2))
+        slots.append(onward(array, 2))
 
     sends = stepped(0, fields, (earlier,), 2)
     older = exchange(sends)
@@ -307,18 +311,20 @@
     older = blocks
     blocks = exchange(sends)
     rotate(found[2])
+    rotate(slots[-1])
     carry = call(
         bind(last_kernel, groups, block, 3),
         whole, (), (*law, dense, aside, *blocks, *older, *later, slots[-1]),
     )
     found.append(carry)
-    heads = [z for z in range(STEPS) if z < chips]
+    reach = [STEPS - step for step in range(STEPS - 1)] + [0]
+    heads = [z for z in reach if z < chips]
     finals = [
         along(carry, [(2 * z, 2 * (z + k)) for z in heads if z + k < chips]) for k in range(1, chips)
     ]
 
     def origin(step, z):
-        beyond = z - (STEPS - 1 - step)
+        beyond = z - reach[step]
         if z == 0:
             return found[step]
         return finals[beyond - 1] if beyond > 0 else slots[step + z - 1]
@@ -337,7 +343,7 @@
             bind(choose_kernel, plan), shape((len(steps) * rows, columns), BF16), (), sources
         )
 
-    ready = [s for s in range(STEPS) if chips - 1 <= STEPS - 1 - s] or [0]
+    ready = [s for s in range(STEPS) if chips - 1 <= reach[s]] or [0]
     early = chosen(ready)
     early_other = swap(early)
     late = chosen([s for s in range(STEPS) if s not in ready])

time: 146 us -> 127 us (0.87); the launches traced: 143 us -> 127 us
  waiting for transfers between devices: 71.2 us -> 44.5 us
  starting transfers between devices: 44.2 us -> 54.2 us
    ppermute x29 -> x30, waiting for transfers between devices: 50.8 us -> 25.6 us  [along(): return lax.ppermute(array, 'delay', pairs)]
    ppermute x29 -> x30, starting transfers between devices: 29.4 us -> 38.9 us  [along(): return lax.ppermute(array, 'delay', pairs)]
    ppermute x12, waiting for transfers between devices: 20.4 us -> 18.9 us  [exchange(): lax.ppermute(sends[hop], 'group', [(g, peer_of(g, hop, groups)) for g in...]
  transfers between devices with their start and end apart: 41 -> 42, of which waited for: 21 -> 17; matrix products, arithmetic and copies ran while one was open for 0% -> 0% of each run, Pallas kernels for 12% -> 14%
where the time goes in v5:
time: 127 us
  starting transfers between devices  54.2 us (43%)
  waiting for transfers between devices  44.5 us (35%)
  Pallas kernels  22.6 us (18%)
  local copies, waits for them, and re-layouts  4.67 us (4%)
    ppermute x30, starting transfers between devices, along(): return lax.ppermute(array, 'delay', pairs)  38.9 us
    ppermute x30, waiting for transfers between devices, along(): return lax.ppermute(array, 'delay', pairs)  25.6 us
    pallas_call x16, Pallas kernels, call(): pl.pallas_call(kernel, out_shape=out_shape, in_specs=[SMEM] * len(scalars...  21.6 us
    ppermute x12, waiting for transfers between devices, exchange(): lax.ppermute(sends[hop], 'group', [(g, peer_of(g, hop, groups)) for g in...  18.9 us
    ppermute x12, starting transfers between devices, exchange(): lax.ppermute(sends[hop], 'group', [(g, peer_of(g, hop, groups)) for g in...  15.3 us
    unnamed x15, local copies, waits for them, and re-layouts  4.45 us
  transfers between devices with their start and end apart: 42, of which 17 were waited for; matrix products, arithmetic and copies ran while one was open for 0% of the time, Pallas kernels for 14%

profile of v5, /device:TPU:0, one launch (start us, length us, event | category | flops | bytes accessed | tf_op | source)
XLA Modules:
  0.0 126.7 jit_solution(10236333123320930550)
XLA Ops:
  4.4 8.7 %collective-permute-done.1.second = bf16[1024,128]{1,0:T(8,128)(2,1)S(1)} collective-permute-done((bf16[1024,128]{1,0:T(8,128)(2,1)S(1)}, bf16[1024,128]{1,0:T(8,128)(2,1)S(1)}, u32[]{:S(2)}, u32[]{:S(2)}) %collective-permute-start.1) | collective-permute-done | bytes 262176 | tf_op jit(solution)/shard_map/ppermute | solution.py:237
  20.2 2.4 %collective-permute-done.4.refs_3_ = bf16[512,128]{1,0:T(8,128)(2,1)S(1)} collective-permute-done((bf16[512,128]{1,0:T(8,128)(2,1)S(1)}, bf16[512,128]{1,0:T(8,128)(2,1)S(1)}, u32[]{:S(2)}, u32[]{:S(2)}) %collective-permute-start.4) | collective-permute-done | bytes 131104 | tf_op jit(solution)/shard_map/ppermute | solution.py:250
  29.0 2.2 %collective-permute-done.9.refs_4_ = bf16[1024,128]{1,0:T(8,128)(2,1)S(1)} collective-permute-done((bf16[1024,128]{1,0:T(8,128)(2,1)S(1)}, bf16[1024,128]{1,0:T(8,128)(2,1)S(1)}, u32[]{:S(2)}, u32[]{:S(2)}) %collective-permute-start.9) | collective-permute-done | bytes 262176 | tf_op jit(solution)/shard_map/ppermute | solution.py:237
  33.0 4.6 %shard_map.82.sheet = bf16[1024,1024]{1,0:T(8,128)(2,1)S(1)} custom-call(bf16[1024,1024]{1,0:T(8,128)(2,1)S(1)} %copy-done.1, f32[1024,1]{1,0:T(8,128)S(1)} %copy.10.column, f32[1,1024]{1,0:T(1,128)S(1)} %bitcast.9), custom_call_target="tpu_custom_call" | custom-call | tf_op jit(solution)/shard_map/pallas_call | solution.py:29
  37.7 2.0 %collective-permute-done.6.refs_1_ = bf16[1024,128]{1,0:T(8,128)(2,1)} collective-permute-done((bf16[1024,128]{1,0:T(8,128)(2,1)S(1)}, bf16[1024,128]{1,0:T(8,128)(2,1)}, u32[]{:S(2)}, u32[]{:S(2)}) %collective-permute-start.6) | collective-permute-done | bytes 262176 | tf_op jit(solution)/shard_map/ppermute | solution.py:237
  39.7 2.0 %shard_map.87 = (bf16[1024,128]{1,0:T(8,128)(2,1)S(1)}, bf16[512,128]{1,0:T(8,128)(2,1)S(1)}, bf16[512,128]{1,0:T(8,128)(2,1)S(1)}, bf16[512,128]{1,0:T(8,128)(2,1)S(1)}, bf16[512,128]{1,0:T(8,128)(2,1)S(1)}) custom-call(s32[1,4,4]{2,1,0:T(4,128)S(1)} %copy-done.4, s32[1,4,4]{2,1,0:T(4,128)S(1)} %collective-permute-done.other, ...), custom_call_target="tpu_custom_call" | custom-call | tf_op jit(solution)/shard_map/pallas_call | solution.py:29
  42.8 2.5 %collective-permute-start.17 = (bf16[512,128]{1,0:T(8,128)(2,1)S(1)}, bf16[512,128]{1,0:T(8,128)(2,1)S(1)}, u32[]{:S(2)}, u32[]{:S(2)}) collective-permute-start(bf16[512,128]{1,0:T(8,128)(2,1)S(1)} %get-tuple-element.40), channel_id=1, source_target_pairs={{0,24},{8,16},{16,8},{24,0},{1,25},{9,17},{17,9},{25,1},{2,26},{10... | collective-permute-start | bytes 393224 | tf_op jit(solution)/shard_map/ppermute | solution.py:250
  51.5 3.3 %collective-permute-start.19 = (bf16[1024,128]{1,0:T(8,128)(2,1)S(1)}, bf16[1024,128]{1,0:T(8,128)(2,1)S(1)}, u32[]{:S(2)}, u32[]{:S(2)}) collective-permute-start(bf16[1024,128]{1,0:T(8,128)(2,1)S(1)} %get-tuple-element.35.refs_0_), channel_id=1, source_target_pairs={{0,2},{2,4},{4,6},{8,10},{10,12},{12,14},{16,18},{18,20},{20,22},{... | collective-permute-start | bytes 786440 | tf_op jit(solution)/shard_map/ppermute | solution.py:237
  54.8 2.3 %shard_map.89 = (f32[1024,128]{1,0:T(8,128)S(1)}, bf16[1024,128]{1,0:T(8,128)(2,1)S(1)}) custom-call(bf16[1024,1024]{1,0:T(8,128)(2,1)S(1)} %shard_map.83.matrix, bf16[1024,1024]{1,0:T(8,128)(2,1)} %collective-permute-done.14.aside, bf16[512,128]{1,0:T(8,128)(2,1)S(1)} %get-tuple-element.37.refs_0_.refs_4_, ...), custom_call_target="tpu_custom_call" | custom-call | tf_op jit(solution)/shard_map/pallas_call | solution.py:29
  57.2 4.2 %collective-permute-done.11.refs_1_ = bf16[1024,128]{1,0:T(8,128)(2,1)S(1)} collective-permute-done((bf16[1024,128]{1,0:T(8,128)(2,1)S(1)}, bf16[1024,128]{1,0:T(8,128)(2,1)S(1)}, u32[]{:S(2)}, u32[]{:S(2)}) %collective-permute-start.11) | collective-permute-done | bytes 262176 | tf_op jit(solution)/shard_map/ppermute | solution.py:237
  72.2 4.2 %collective-permute-done.27.refs_3_.refs_7_ = bf16[512,128]{1,0:T(8,128)(2,1)S(1)} collective-permute-done((bf16[512,128]{1,0:T(8,128)(2,1)S(1)}, bf16[512,128]{1,0:T(8,128)(2,1)S(1)}, u32[]{:S(2)}, u32[]{:S(2)}) %collective-permute-start.27) | collective-permute-done | bytes 131104 | tf_op jit(solution)/shard_map/ppermute | solution.py:250
  76.4 2.8 %shard_map.92 = (f32[1024,128]{1,0:T(8,128)S(1)}, bf16[1024,128]{1,0:T(8,128)(2,1)S(1)}) custom-call(bf16[1024,1024]{1,0:T(8,128)(2,1)S(1)} %shard_map.83.matrix, bf16[1024,1024]{1,0:T(8,128)(2,1)} %collective-permute-done.14.aside, bf16[512,128]{1,0:T(8,128)(2,1)S(1)} %get-tuple-element.44.refs_0_.refs_4_, ...), custom_call_target="tpu_custom_call" | custom-call | tf_op jit(solution)/shard_map/pallas_call | solution.py:29
  81.6 2.3 %collective-permute-start.28 = (bf16[1024,128]{1,0:T(8,128)(2,1)S(1)}, bf16[1024,128]{1,0:T(8,128)(2,1)S(1)}, u32[]{:S(2)}, u32[]{:S(2)}) collective-permute-start(bf16[1024,128]{1,0:T(8,128)(2,1)S(1)} %get-tuple-element.49.refs_0_), channel_id=1, source_target_pairs={{0,2},{2,4},{4,6},{8,10},{10,12},{12,14},{16,18},{18,20},{20,22},{... | collective-permute-start | bytes 786440 | tf_op jit(solution)/shard_map/ppermute | solution.py:237
  87.9 4.4 %collective-permute-start.29 = (bf16[1024,128]{1,0:T(8,128)(2,1)S(1)}, bf16[1024,128]{1,0:T(8,128)(2,1)S(1)}, u32[]{:S(2)}, u32[]{:S(2)}) collective-permute-start(bf16[1024,128]{1,0:T(8,128)(2,1)S(1)} %collective-permute-done.28.refs_4_.refs_2_), channel_id=1, source_target_pairs={{0,2},{2,4},{4,6},{8,10},{10,12},{12,14},{16,18},{18,20},{20,22},{... | collective-permute-start | bytes 786440 | tf_op jit(solution)/shard_map/ppermute | solution.py:237
  93.4 3.3 %collective-permute-done.31.refs_1_ = bf16[256,128]{1,0:T(8,128)(2,1)S(1)} collective-permute-done((bf16[256,128]{1,0:T(8,128)(2,1)S(1)}, bf16[256,128]{1,0:T(8,128)(2,1)S(1)}, u32[]{:S(2)}, u32[]{:S(2)}) %collective-permute-start.31) | collective-permute-done | bytes 65568 | tf_op jit(solution)/shard_map/ppermute | solution.py:250
  96.6 1.9 %collective-permute-start.32 = (bf16[256,128]{1,0:T(8,128)(2,1)S(1)}, bf16[256,128]{1,0:T(8,128)(2,1)S(1)}, u32[]{:S(2)}, u32[]{:S(2)}) collective-permute-start(bf16[256,128]{1,0:T(8,128)(2,1)S(1)} %get-tuple-element.52), channel_id=1, source_target_pairs={{0,16},{8,24},{16,0},{24,8},{1,17},{9,25},{17,1},{25,9},{2,18},{10... | collective-permute-start | bytes 196616 | tf_op jit(solution)/shard_map/ppermute | solution.py:250
  98.6 2.4 %collective-permute-done.32.refs_2_ = bf16[256,128]{1,0:T(8,128)(2,1)S(1)} collective-permute-done((bf16[256,128]{1,0:T(8,128)(2,1)S(1)}, bf16[256,128]{1,0:T(8,128)(2,1)S(1)}, u32[]{:S(2)}, u32[]{:S(2)}) %collective-permute-start.32) | collective-permute-done | bytes 65568 | tf_op jit(solution)/shard_map/ppermute | solution.py:250
  100.9 1.9 %collective-permute-start.33 = (bf16[256,128]{1,0:T(8,128)(2,1)S(1)}, bf16[256,128]{1,0:T(8,128)(2,1)S(1)}, u32[]{:S(2)}, u32[]{:S(2)}) collective-permute-start(bf16[256,128]{1,0:T(8,128)(2,1)S(1)} %get-tuple-element.53), channel_id=1, source_target_pairs={{0,24},{8,16},{16,8},{24,0},{1,25},{9,17},{17,9},{25,1},{2,26},{10... | collective-permute-start | bytes 196616 | tf_op jit(solution)/shard_map/ppermute | solution.py:250
  102.8 3.2 %collective-permute-done.33.refs_3_ = bf16[256,128]{1,0:T(8,128)(2,1)S(1)} collective-permute-done((bf16[256,128]{1,0:T(8,128)(2,1)S(1)}, bf16[256,128]{1,0:T(8,128)(2,1)S(1)}, u32[]{:S(2)}, u32[]{:S(2)}) %collective-permute-start.33) | collective-permute-done | bytes 65568 | tf_op jit(solution)/shard_map/ppermute | solution.py:250
  106.1 3.4 %shard_map.96.refs_1_ = bf16[1024,128]{1,0:T(8,128)(2,1)S(1)} custom-call(bf16[1024,1024]{1,0:T(8,128)(2,1)S(1)} %shard_map.82.sheet, f32[1024,1]{1,0:T(8,128)S(1)} %copy.10.column, bf16[4,1024,128]{2,1,0:T(8,128)(2,1)S(1)} %copy-done, bf16[1024,1024]{1,0:T(8,128)(2,1)S(1)} %shard_map.83.matrix, bf16[1024,1024]{1,0:T(8,128)(2,1)} %collective-permute-done.14.aside, ...), custom_call_target="tpu_custom_call" | custom-call | tf_op jit(solution)/shard_map/pallas_call | solution.py:29
  109.5 4.0 %collective-permute-start.38 = (bf16[1024,128]{1,0:T(8,128)(2,1)S(1)}, bf16[1024,128]{1,0:T(8,128)(2,1)S(1)}, u32[]{:S(2)}, u32[]{:S(2)}) collective-permute-start(bf16[1024,128]{1,0:T(8,128)(2,1)S(1)} %shard_map.96.refs_1_), channel_id=1, source_target_pairs={{4,6},{0,2},{12,14},{8,10},{20,22},{16,18},{28,30},{24,26}} | collective-permute-start | bytes 786440 | tf_op jit(solution)/shard_map/ppermute | solution.py:237
  113.5 3.3 %collective-permute-start.39 = (bf16[1024,128]{1,0:T(8,128)(2,1)S(1)}, bf16[1024,128]{1,0:T(8,128)(2,1)S(1)}, u32[]{:S(2)}, u32[]{:S(2)}) collective-permute-start(bf16[1024,128]{1,0:T(8,128)(2,1)S(1)} %shard_map.96.refs_1_), channel_id=1, source_target_pairs={{0,4},{8,12},{16,20},{24,28}} | collective-permute-start | bytes 786440 | tf_op jit(solution)/shard_map/ppermute | solution.py:237
  118.3 2.4 %collective-permute-done.39.refs_5_ = bf16[1024,128]{1,0:T(8,128)(2,1)S(1)} collective-permute-done((bf16[1024,128]{1,0:T(8,128)(2,1)S(1)}, bf16[1024,128]{1,0:T(8,128)(2,1)S(1)}, u32[]{:S(2)}, u32[]{:S(2)}) %collective-permute-start.39) | collective-permute-done | bytes 262176 | tf_op jit(solution)/shard_map/ppermute | solution.py:237
  120.7 2.8 %collective-permute-done.40.refs_6_ = bf16[1024,128]{1,0:T(8,128)(2,1)S(1)} collective-permute-done((bf16[1024,128]{1,0:T(8,128)(2,1)S(1)}, bf16[1024,128]{1,0:T(8,128)(2,1)S(1)}, u32[]{:S(2)}, u32[]{:S(2)}) %collective-permute-start.40) | collective-permute-done | bytes 262176 | tf_op jit(solution)/shard_map/ppermute | solution.py:237
  (95 shorter events, 49.4 us)
Async XLA Ops:
  3.7 47.7 %collective-permute-start.14 = (bf16[1024,1024]{1,0:T(8,128)(2,1)S(1)}, bf16[1024,1024]{1,0:T(8,128)(2,1)}, u32[]{:S(2)}, u32[]{:S(2)}) collective-permute-start(bf16[1024,1024]{1,0:T(8,128)(2,1)S(1)} %shard_map.83.matrix), channel_id=1, source_target_pairs={{0,1},{1,0},{2,3},{3,2},{4,5},{5,4},{6,7},{7,6},{8,9},{9,8},{10,11... | collective-permute-start | bytes 6291464 | tf_op jit(solution)/shard_map/ppermute | solution.py:237
  4.3 8.8 %collective-permute-start.1 = (bf16[1024,128]{1,0:T(8,128)(2,1)S(1)}, bf16[1024,128]{1,0:T(8,128)(2,1)S(1)}, u32[]{:S(2)}, u32[]{:S(2)}) collective-permute-start(bf16[1024,128]{1,0:T(8,128)(2,1)S(1)} %bitcast.6), channel_id=1, source_target_pairs={{0,1},{1,2},{2,3},{3,4},{4,5},{5,6},{6,7},{7,0},{8,9},{9,10},{10,1... | collective-permute-start | bytes 786440 | tf_op jit(solution)/shard_map/ppermute | solution.py:237
  23.5 7.7 %collective-permute-start.9 = (bf16[1024,128]{1,0:T(8,128)(2,1)S(1)}, bf16[1024,128]{1,0:T(8,128)(2,1)S(1)}, u32[]{:S(2)}, u32[]{:S(2)}) collective-permute-start(bf16[1024,128]{1,0:T(8,128)(2,1)S(1)} %collective-permute-done.1.second), channel_id=1, source_target_pairs={{0,1},{1,2},{2,3},{3,4},{4,5},{5,6},{6,7},{7,0},{8,9},{9,10},{10,1... | collective-permute-start | bytes 786440 | tf_op jit(solution)/shard_map/ppermute | solution.py:237
  25.1 14.6 %collective-permute-start.6 = (bf16[1024,128]{1,0:T(8,128)(2,1)S(1)}, bf16[1024,128]{1,0:T(8,128)(2,1)}, u32[]{:S(2)}, u32[]{:S(2)}) collective-permute-start(bf16[1024,128]{1,0:T(8,128)(2,1)S(1)} %shard_map.86.refs_0_), channel_id=1, source_target_pairs={{2,0},{10,8},{18,16},{26,24}} | collective-permute-start | bytes 786440 | tf_op jit(solution)/shard_map/ppermute | solution.py:237
  26.4 13.3 %collective-permute-start.7 = (bf16[1024,128]{1,0:T(8,128)(2,1)S(1)}, bf16[1024,128]{1,0:T(8,128)(2,1)}, u32[]{:S(2)}, u32[]{:S(2)}) collective-permute-start(bf16[1024,128]{1,0:T(8,128)(2,1)S(1)} %shard_map.86.refs_0_), channel_id=1, source_target_pairs={{4,0},{12,8},{20,16},{28,24}} | collective-permute-start | bytes 786440 | tf_op jit(solution)/shard_map/ppermute | solution.py:237
  27.7 12.0 %collective-permute-start.8 = (bf16[1024,128]{1,0:T(8,128)(2,1)S(1)}, bf16[1024,128]{1,0:T(8,128)(2,1)}, u32[]{:S(2)}, u32[]{:S(2)}) collective-permute-start(bf16[1024,128]{1,0:T(8,128)(2,1)S(1)} %shard_map.86.refs_0_), channel_id=1, source_target_pairs={{6,0},{14,8},{22,16},{30,24}} | collective-permute-start | bytes 786440 | tf_op jit(solution)/shard_map/ppermute | solution.py:237
  31.2 14.0 %collective-permute-start.10 = (bf16[1024,128]{1,0:T(8,128)(2,1)S(1)}, bf16[1024,128]{1,0:T(8,128)(2,1)}, u32[]{:S(2)}, u32[]{:S(2)}) collective-permute-start(bf16[1024,128]{1,0:T(8,128)(2,1)S(1)} %get-tuple-element.36.first), channel_id=1, source_target_pairs={{0,1},{1,0},{2,3},{3,2},{4,5},{5,4},{6,7},{7,6},{8,9},{9,8},{10,11... | collective-permute-start | bytes 786440 | tf_op jit(solution)/shard_map/ppermute | solution.py:237
  42.8 7.4 %collective-permute-start.17 = (bf16[512,128]{1,0:T(8,128)(2,1)S(1)}, bf16[512,128]{1,0:T(8,128)(2,1)S(1)}, u32[]{:S(2)}, u32[]{:S(2)}) collective-permute-start(bf16[512,128]{1,0:T(8,128)(2,1)S(1)} %get-tuple-element.40), channel_id=1, source_target_pairs={{0,24},{8,16},{16,8},{24,0},{1,25},{9,17},{17,9},{25,1},{2,26},{10... | collective-permute-start | bytes 393224 | tf_op jit(solution)/shard_map/ppermute | solution.py:250
  45.2 11.9 %collective-permute-start.18 = (bf16[1024,128]{1,0:T(8,128)(2,1)S(1)}, bf16[1024,128]{1,0:T(8,128)(2,1)S(1)}, u32[]{:S(2)}, u32[]{:S(2)}) collective-permute-start(bf16[1024,128]{1,0:T(8,128)(2,1)S(1)} %collective-permute-done.9.refs_4_), channel_id=1, source_target_pairs={{0,1},{1,2},{2,3},{3,4},{4,5},{5,6},{6,7},{8,9},{9,10},{10,11},{11... | collective-permute-start | bytes 786440 | tf_op jit(solution)/shard_map/ppermute | solution.py:237
  47.5 13.9 %collective-permute-start.11 = (bf16[1024,128]{1,0:T(8,128)(2,1)S(1)}, bf16[1024,128]{1,0:T(8,128)(2,1)S(1)}, u32[]{:S(2)}, u32[]{:S(2)}) collective-permute-start(bf16[1024,128]{1,0:T(8,128)(2,1)S(1)} %shard_map.88.refs_0_), channel_id=1, source_target_pairs={{2,0},{10,8},{18,16},{26,24}} | collective-permute-start | bytes 786440 | tf_op jit(solution)/shard_map/ppermute | solution.py:237
  48.8 12.6 %collective-permute-start.12 = (bf16[1024,128]{1,0:T(8,128)(2,1)S(1)}, bf16[1024,128]{1,0:T(8,128)(2,1)S(1)}, u32[]{:S(2)}, u32[]{:S(2)}) collective-permute-start(bf16[1024,128]{1,0:T(8,128)(2,1)S(1)} %shard_map.88.refs_0_), channel_id=1, source_target_pairs={{4,0},{12,8},{20,16},{28,24}} | collective-permute-start | bytes 786440 | tf_op jit(solution)/shard_map/ppermute | solution.py:237
  50.2 11.3 %collective-permute-start.13 = (bf16[1024,128]{1,0:T(8,128)(2,1)S(1)}, bf16[1024,128]{1,0:T(8,128)(2,1)S(1)}, u32[]{:S(2)}, u32[]{:S(2)}) collective-permute-start(bf16[1024,128]{1,0:T(8,128)(2,1)S(1)} %shard_map.88.refs_0_), channel_id=1, source_target_pairs={{6,0},{14,8},{22,16},{30,24}} | collective-permute-start | bytes 786440 | tf_op jit(solution)/shard_map/ppermute | solution.py:237
  51.5 10.0 %collective-permute-start.19 = (bf16[1024,128]{1,0:T(8,128)(2,1)S(1)}, bf16[1024,128]{1,0:T(8,128)(2,1)S(1)}, u32[]{:S(2)}, u32[]{:S(2)}) collective-permute-start(bf16[1024,128]{1,0:T(8,128)(2,1)S(1)} %get-tuple-element.35.refs_0_), channel_id=1, source_target_pairs={{0,2},{2,4},{4,6},{8,10},{10,12},{12,14},{16,18},{18,20},{20,22},{... | collective-permute-start | bytes 786440 | tf_op jit(solution)/shard_map/ppermute | solution.py:237
  57.1 9.0 %collective-permute-start.21 = (bf16[1024,128]{1,0:T(8,128)(2,1)S(1)}, bf16[1024,128]{1,0:T(8,128)(2,1)S(1)}, u32[]{:S(2)}, u32[]{:S(2)}) collective-permute-start(bf16[1024,128]{1,0:T(8,128)(2,1)S(1)} %get-tuple-element.43.first), channel_id=1, source_target_pairs={{0,1},{1,0},{2,3},{3,2},{4,5},{5,4},{6,7},{7,6},{8,9},{9,8},{10,11... | collective-permute-start | bytes 786440 | tf_op jit(solution)/shard_map/ppermute | solution.py:237
  64.5 14.8 %collective-permute-start.20 = (bf16[1024,128]{1,0:T(8,128)(2,1)S(1)}, bf16[1024,128]{1,0:T(8,128)(2,1)S(1)}, u32[]{:S(2)}, u32[]{:S(2)}) collective-permute-start(bf16[1024,128]{1,0:T(8,128)(2,1)S(1)} %get-tuple-element.42.refs_1_), channel_id=1, source_target_pairs={{0,2},{2,4},{4,6},{8,10},{10,12},{12,14},{16,18},{18,20},{20,22},{... | collective-permute-start | bytes 786440 | tf_op jit(solution)/shard_map/ppermute | solution.py:237
  66.2 13.9 %collective-permute-start.22 = (bf16[1024,128]{1,0:T(8,128)(2,1)S(1)}, bf16[1024,128]{1,0:T(8,128)(2,1)S(1)}, u32[]{:S(2)}, u32[]{:S(2)}) collective-permute-start(bf16[1024,128]{1,0:T(8,128)(2,1)S(1)} %shard_map.91.refs_0_), channel_id=1, source_target_pairs={{2,0},{10,8},{18,16},{26,24}} | collective-permute-start | bytes 786440 | tf_op jit(solution)/shard_map/ppermute | solution.py:237
  67.5 12.6 %collective-permute-start.23 = (bf16[1024,128]{1,0:T(8,128)(2,1)S(1)}, bf16[1024,128]{1,0:T(8,128)(2,1)S(1)}, u32[]{:S(2)}, u32[]{:S(2)}) collective-permute-start(bf16[1024,128]{1,0:T(8,128)(2,1)S(1)} %shard_map.91.refs_0_), channel_id=1, source_target_pairs={{4,0},{12,8},{20,16},{28,24}} | collective-permute-start | bytes 786440 | tf_op jit(solution)/shard_map/ppermute | solution.py:237
  69.2 10.9 %collective-permute-start.24 = (bf16[1024,128]{1,0:T(8,128)(2,1)S(1)}, bf16[1024,128]{1,0:T(8,128)(2,1)S(1)}, u32[]{:S(2)}, u32[]{:S(2)}) collective-permute-start(bf16[1024,128]{1,0:T(8,128)(2,1)S(1)} %shard_map.91.refs_0_), channel_id=1, source_target_pairs={{6,0},{14,8},{22,16},{30,24}} | collective-permute-start | bytes 786440 | tf_op jit(solution)/shard_map/ppermute | solution.py:237
  84.0 22.1 %collective-permute-start.35 = (bf16[1024,128]{1,0:T(8,128)(2,1)S(1)}, bf16[1024,128]{1,0:T(8,128)(2,1)S(1)}, u32[]{:S(2)}, u32[]{:S(2)}) collective-permute-start(bf16[1024,128]{1,0:T(8,128)(2,1)S(1)} %shard_map.95.refs_8_), channel_id=1, source_target_pairs={{2,0},{10,8},{18,16},{26,24}} | collective-permute-start | bytes 786440 | tf_op jit(solution)/shard_map/ppermute | solution.py:237
  85.3 20.8 %collective-permute-start.36 = (bf16[1024,128]{1,0:T(8,128)(2,1)S(1)}, bf16[1024,128]{1,0:T(8,128)(2,1)S(1)}, u32[]{:S(2)}, u32[]{:S(2)}) collective-permute-start(bf16[1024,128]{1,0:T(8,128)(2,1)S(1)} %shard_map.95.refs_8_), channel_id=1, source_target_pairs={{4,0},{12,8},{20,16},{28,24}} | collective-permute-start | bytes 786440 | tf_op jit(solution)/shard_map/ppermute | solution.py:237
  86.6 19.5 %collective-permute-start.37 = (bf16[1024,128]{1,0:T(8,128)(2,1)S(1)}, bf16[1024,128]{1,0:T(8,128)(2,1)S(1)}, u32[]{:S(2)}, u32[]{:S(2)}) collective-permute-start(bf16[1024,128]{1,0:T(8,128)(2,1)S(1)} %shard_map.95.refs_8_), channel_id=1, source_target_pairs={{6,0},{14,8},{22,16},{30,24}} | collective-permute-start | bytes 786440 | tf_op jit(solution)/shard_map/ppermute | solution.py:237
  87.9 18.2 %collective-permute-start.29 = (bf16[1024,128]{1,0:T(8,128)(2,1)S(1)}, bf16[1024,128]{1,0:T(8,128)(2,1)S(1)}, u32[]{:S(2)}, u32[]{:S(2)}) collective-permute-start(bf16[1024,128]{1,0:T(8,128)(2,1)S(1)} %collective-permute-done.28.refs_4_.refs_2_), channel_id=1, source_target_pairs={{0,2},{2,4},{4,6},{8,10},{10,12},{12,14},{16,18},{18,20},{20,22},{... | collective-permute-start | bytes 786440 | tf_op jit(solution)/shard_map/ppermute | solution.py:237
  109.5 8.7 %collective-permute-start.38 = (bf16[1024,128]{1,0:T(8,128)(2,1)S(1)}, bf16[1024,128]{1,0:T(8,128)(2,1)S(1)}, u32[]{:S(2)}, u32[]{:S(2)}) collective-permute-start(bf16[1024,128]{1,0:T(8,128)(2,1)S(1)} %shard_map.96.refs_1_), channel_id=1, source_target_pairs={{4,6},{0,2},{12,14},{8,10},{20,22},{16,18},{28,30},{24,26}} | collective-permute-start | bytes 786440 | tf_op jit(solution)/shard_map/ppermute | solution.py:237
  113.5 7.2 %collective-permute-start.39 = (bf16[1024,128]{1,0:T(8,128)(2,1)S(1)}, bf16[1024,128]{1,0:T(8,128)(2,1)S(1)}, u32[]{:S(2)}, u32[]{:S(2)}) collective-permute-start(bf16[1024,128]{1,0:T(8,128)(2,1)S(1)} %shard_map.96.refs_1_), channel_id=1, source_target_pairs={{0,4},{8,12},{16,20},{24,28}} | collective-permute-start | bytes 786440 | tf_op jit(solution)/shard_map/ppermute | solution.py:237
  (25 other events, 143.3 us)

commit v6 on v5

--- a/solution.py
+++ b/solution.py
@@ -76,23 +76,16 @@
         out[part * block : (part + 1) * block, :] = source[pl.ds(start, block), :]
 
 
-def pick_kernel(groups, block, table, first, second, *sends):
-    emit(groups, block, sends, 0, first, table)
-    emit(groups, block, sends, 1, second, table)
-
-
-def early_kernel(groups, block, matrix, *refs):
-    blocks, outs = refs[:groups], refs[groups:]
-    delay = lax.axis_index("delay")
-    for part, out in enumerate(outs):
-
-        @pl.when(delay >= part)
-        def _():
-            out[...] = product(matrix, blocks, part, block).astype(BF16)
-
-        @pl.when(delay < part)
-        def _():
-            out[...] = jnp.zeros_like(out)
+def pick_kernel(groups, block, table, source, *sends):
+    emit(groups, block, sends, 0, source, table)
+
+
+def term_kernel(groups, block, first, matrix, *refs):
+    blocks, out = refs[:groups], refs[groups]
+    total = product(matrix, blocks, 0, block)
+    if first > 0:
+        total = jnp.where(lax.axis_index("delay") >= first, total, 0.0)
+    out[...] = total.astype(BF16)
 
 
 def plus_kernel(first, second, out):
@@ -124,35 +117,21 @@
 def step_kernel(groups, block, step, fields, table, other, sheet, column, incident, *refs):
     terms, refs = refs[:fields], refs[fields:]
     delay = lax.axis_index("delay")
-    history = passed = second = None
+    history = second = None
     if step < 2:
         history, refs = refs[0], refs[1:]
     if step == 1:
         second, refs = refs[0], refs[1:]
-    if step > 0:
-        passed, refs = refs[0], refs[1:]
-    carry, sends = refs[0], refs[1:]
-    current = law_of(driving_of(incident, step, terms), sheet, column)
-    if step > 0:
-
-        @pl.when(delay == 0)
-        def _():
-            carry[...] = current
-
-        @pl.when(delay != 0)
-        def _():
-            carry[...] = passed[...]
-
-    else:
-        carry[...] = current
+    now, sends = refs[0], refs[1:]
+    now[...] = law_of(driving_of(incident, step, terms), sheet, column)
     if step == 2:
-        emit(groups, block, sends, 0, carry, table)
+        emit(groups, block, sends, 0, now, table)
         return
 
     @pl.when(delay == 0)
     def _():
-        emit(groups, block, sends, 0, carry, table)
-        emit(groups, block, sends, 1, carry, other)
+        emit(groups, block, sends, 0, now, table)
+        emit(groups, block, sends, 1, now, other)
 
     @pl.when((delay != 0) if step == 0 else (delay != 0) & (delay != 2))
     def _():
@@ -165,6 +144,18 @@
         def _():
             emit(groups, block, sends, 0, second, table)
             emit(groups, block, sends, 1, second, table)
+
+
+def carry_kernel(current, passed, carry):
+    delay = lax.axis_index("delay")
+
+    @pl.when(delay == 0)
+    def _():
+        carry[...] = current[...]
+
+    @pl.when(delay != 0)
+    def _():
+        carry[...] = passed[...]
 
 
 def last_kernel(groups, block, step, sheet, column, incident, matrix, aside, *refs):
@@ -257,24 +248,29 @@
         return [chip] + [along(chip, [(2 * z, 0)]) for z in range(1, chips)]
 
     earlier = shift(history[0])
-    inverse = 1.0 / sheet_diag
-    column, row = inverse[:, None], inverse[None, :]
     listed = jnp.clip(block_row, 0, rows // block - 1)
+
+    def picked(array):
+        return call(bind(pick_kernel, groups, block), [piece()] * groups, (send_pick,), (array,))
+
+    def term_of(blocks, first):
+        return call(bind(term_kernel, groups, block, first), whole, (), (dense, *blocks))
+
+    sends = picked(history[0])
+    blocks = exchange(sends)
     dense = call(
         bind(dense_kernel, groups, block, depth),
         shape((rows, groups * block), BF16), (listed, block_count), (weights,),
     )
+    fields = gathered(term_of(blocks, 0))
+    sends = picked(earlier)
+    blocks = exchange(sends)
+    earlier = onward(earlier)
+    inverse = 1.0 / sheet_diag
+    column, row = inverse[:, None], inverse[None, :]
     sheet = call(sheet_kernel, shape((rows, rows), BF16), (), (self_block, column, row), 20)
-
-    sends = call(
-        bind(pick_kernel, groups, block), [piece(2)] * groups, (send_pick,), (history[0], earlier)
-    )
-    blocks = exchange(sends)
-    earlier = shift(earlier)
+    later = gathered(term_of(blocks, 1))
     other = swap(send_pick)
-    terms = call(bind(early_kernel, groups, block), [whole, whole], (), (dense, *blocks))
-    fields = gathered(terms[0])
-    later = gathered(terms[1])
     oldest = onward(earlier)
     aside = swap(dense)
 
@@ -283,41 +279,44 @@
     found, slots = [], []
 
     def stepped(step, fields, extra, parts):
-        carry, *sends = call(
+        current, *sends = call(
             bind(step_kernel, groups, block, step, len(fields)),
             [whole] + [piece(parts)] * groups, tables, (*law, *fields, *extra),
         )
-        found.append(carry)
+        found.append(current)
         return sends
 
-    def rotate(array):
+    def pass_on():
+        array = found[-1]
+        if slots:
+            array = call(carry_kernel, whole, (), (array, slots[-1]))
         slots.append(onward(array, 2))
+
+    def near_of(blocks, older):
+        return call(
+            bind(near_kernel, groups, block), [wide_whole, whole], (), (dense, aside, *blocks, *older)
+        )
 
     sends = stepped(0, fields, (earlier,), 2)
     older = exchange(sends)
-    rotate(found[0])
-    wide, narrow = call(
-        bind(near_kernel, groups, block), [wide_whole, whole], (), (dense, aside, *older)
-    )
+    pass_on()
+    wide, narrow = near_of(older, ())
     fields = gathered(narrow)
-    sends = stepped(1, (*later, wide), (oldest, slots[0], slots[-1]), 2)
+    sends = stepped(1, (*later, wide), (oldest, slots[0]), 2)
     blocks = exchange(sends)
-    rotate(found[1])
-    wide, narrow = call(
-        bind(near_kernel, groups, block), [wide_whole, whole], (), (dense, aside, *blocks, *older)
-    )
+    pass_on()
+    wide, narrow = near_of(blocks, older)
     later = gathered(narrow)
-    sends = stepped(2, (*fields, wide), (slots[-1],), 1)
+    sends = stepped(2, (*fields, wide), (), 1)
     older = blocks
     blocks = exchange(sends)
-    rotate(found[2])
-    rotate(slots[-1])
+    pass_on()
     carry = call(
         bind(last_kernel, groups, block, 3),
         whole, (), (*law, dense, aside, *blocks, *older, *later, slots[-1]),
     )
     found.append(carry)
-    reach = [STEPS - step for step in range(STEPS - 1)] + [0]
+    reach = [STEPS - 1 - step for step in range(STEPS)]
     heads = [z for z in reach if z < chips]
     finals = [
         along(carry, [(2 * z, 2 * (z + k)) for z in heads if z + k < chips]) for k in range(1, chips)

time: 127 us -> 135 us (1.063)
  the two profiles are of different devices: /device:TPU:0 before, /device:TPU:25 now
where the time goes in v6:
time: 135 us; the launch traced here: 134 us
  starting transfers between devices  86.4 us (64%)
  Pallas kernels  23.9 us (18%)
  waiting for transfers between devices  18.7 us (14%)
  local copies, waits for them, and re-layouts  4.68 us (3%)
    ppermute x29, starting transfers between devices, along(): return lax.ppermute(array, 'delay', pairs)  71.5 us
    pallas_call x20, Pallas kernels, call(): pl.pallas_call(kernel, out_shape=out_shape, in_specs=[SMEM] * len(scalars...  22.9 us
    ppermute x15, waiting for transfers between devices, exchange(): lax.ppermute(sends[hop], 'group', [(g, peer_of(g, hop, groups)) for g in...  16.5 us
    ppermute x15, starting transfers between devices, exchange(): lax.ppermute(sends[hop], 'group', [(g, peer_of(g, hop, groups)) for g in...  15 us
    unnamed x15, local copies, waits for them, and re-layouts  4.45 us
  transfers between devices with their start and end apart: 44, of which 14 were waited for; matrix products, arithmetic and copies ran while one was open for 0% of the time, Pallas kernels for 14%

profile of v6, /device:TPU:25, one launch (start us, length us, event | category | flops | bytes accessed | tf_op | source)
XLA Modules:
  0.0 134.3 jit_solution(15487234209247455596)
XLA Ops:
  0.8 1.4 %copy-done.2 = bf16[1,4,3,256,256]{4,3,2,1,0:T(8,128)(2,1)S(1)} copy-done((bf16[1,4,3,256,256]{4,3,2,1,0:T(8,128)(2,1)S(1)}, bf16[1,4,3,256,256]{4,3,2,1,0:T(8,128)(2,1)}, u32[]{:S(2)}) %copy-start.2) | copy-done | bytes 1572888
  9.8 1.8 %collective-permute-done.3.refs_3_ = bf16[256,128]{1,0:T(8,128)(2,1)S(1)} collective-permute-done((bf16[256,128]{1,0:T(8,128)(2,1)S(1)}, bf16[256,128]{1,0:T(8,128)(2,1)S(1)}, u32[]{:S(2)}, u32[]{:S(2)}) %collective-permute-start.3) | collective-permute-done | bytes 65568 | tf_op jit(solution)/shard_map/ppermute | solution.py:241
  12.4 2.3 %collective-permute-start.4 = (bf16[1024,128]{1,0:T(8,128)(2,1)S(1)}, bf16[1024,128]{1,0:T(8,128)(2,1)S(1)}, u32[]{:S(2)}, u32[]{:S(2)}) collective-permute-start(bf16[1024,128]{1,0:T(8,128)(2,1)S(1)} %shard_map.85.first), channel_id=1, source_target_pairs={{0,1},{1,0},{2,3},{3,2},{4,5},{5,4},{6,7},{7,6},{8,9},{9,8},{10,11... | collective-permute-start | bytes 786440 | tf_op jit(solution)/shard_map/ppermute | solution.py:228
  18.3 2.2 %collective-permute-start.13 = (bf16[256,128]{1,0:T(8,128)(2,1)S(1)}, bf16[256,128]{1,0:T(8,128)(2,1)S(1)}, u32[]{:S(2)}, u32[]{:S(2)}) collective-permute-start(bf16[256,128]{1,0:T(8,128)(2,1)S(1)} %get-tuple-element.40), channel_id=1, source_target_pairs={{0,24},{8,16},{16,8},{24,0},{1,25},{9,17},{17,9},{25,1},{2,26},{10... | collective-permute-start | bytes 196616 | tf_op jit(solution)/shard_map/ppermute | solution.py:241
  26.3 3.7 %collective-permute-start.14 = (bf16[1024,128]{1,0:T(8,128)(2,1)S(1)}, bf16[1024,128]{1,0:T(8,128)(2,1)}, u32[]{:S(2)}, u32[]{:S(2)}) collective-permute-start(bf16[1024,128]{1,0:T(8,128)(2,1)S(1)} %shard_map.89.first), channel_id=1, source_target_pairs={{0,1},{1,0},{2,3},{3,2},{4,5},{5,4},{6,7},{7,6},{8,9},{9,8},{10,11... | collective-permute-start | bytes 786440 | tf_op jit(solution)/shard_map/ppermute | solution.py:228
  30.2 1.6 %copy-done.1 = bf16[1024,1024]{1,0:T(8,128)(2,1)S(1)} copy-done((bf16[1024,1024]{1,0:T(8,128)(2,1)S(1)}, bf16[1024,1024]{1,0:T(8,128)(2,1)}, u32[]{:S(2)}) %copy-start.1) | copy-done | bytes 2097176
  31.8 4.6 %shard_map.82.sheet = bf16[1024,1024]{1,0:T(8,128)(2,1)S(1)} custom-call(bf16[1024,1024]{1,0:T(8,128)(2,1)S(1)} %copy-done.1, f32[1024,1]{1,0:T(8,128)S(1)} %copy.10.column, f32[1,1024]{1,0:T(1,128)S(1)} %bitcast.9), custom_call_target="tpu_custom_call" | custom-call | tf_op jit(solution)/shard_map/pallas_call | solution.py:29
  36.4 2.0 %shard_map.87 = (bf16[1024,128]{1,0:T(8,128)(2,1)S(1)}, bf16[512,128]{1,0:T(8,128)(2,1)S(1)}, bf16[512,128]{1,0:T(8,128)(2,1)S(1)}, bf16[512,128]{1,0:T(8,128)(2,1)S(1)}, bf16[512,128]{1,0:T(8,128)(2,1)S(1)}) custom-call(s32[1,4,4]{2,1,0:T(4,128)S(1)} %copy-done.4, s32[1,4,4]{2,1,0:T(4,128)S(1)} %collective-permute-done.other, ...), custom_call_target="tpu_custom_call" | custom-call | tf_op jit(solution)/shard_map/pallas_call | solution.py:29
  47.9 2.3 %shard_map.91 = (f32[1024,128]{1,0:T(8,128)S(1)}, bf16[1024,128]{1,0:T(8,128)(2,1)S(1)}) custom-call(bf16[1024,1024]{1,0:T(8,128)(2,1)S(1)} %shard_map.83.matrix, bf16[1024,1024]{1,0:T(8,128)(2,1)} %collective-permute-done.18.aside, bf16[512,128]{1,0:T(8,128)(2,1)S(1)} %get-tuple-element.41.refs_0_.refs_4_, ...), custom_call_target="tpu_custom_call" | custom-call | tf_op jit(solution)/shard_map/pallas_call | solution.py:29
  50.2 5.7 %collective-permute-start.24 = (bf16[1024,128]{1,0:T(8,128)(2,1)S(1)}, bf16[1024,128]{1,0:T(8,128)(2,1)S(1)}, u32[]{:S(2)}, u32[]{:S(2)}) collective-permute-start(bf16[1024,128]{1,0:T(8,128)(2,1)S(1)} %get-tuple-element.47.first), channel_id=1, source_target_pairs={{0,1},{1,0},{2,3},{3,2},{4,5},{5,4},{6,7},{7,6},{8,9},{9,8},{10,11... | collective-permute-start | bytes 786440 | tf_op jit(solution)/shard_map/ppermute | solution.py:228
  56.0 1.5 %shard_map.92 = (bf16[1024,128]{1,0:T(8,128)(2,1)S(1)}, bf16[512,128]{1,0:T(8,128)(2,1)S(1)}, bf16[512,128]{1,0:T(8,128)(2,1)S(1)}, bf16[512,128]{1,0:T(8,128)(2,1)S(1)}, bf16[512,128]{1,0:T(8,128)(2,1)S(1)}) custom-call(s32[1,4,4]{2,1,0:T(4,128)S(1)} %copy-done.4, s32[1,4,4]{2,1,0:T(4,128)S(1)} %collective-permute-done.other, ...), custom_call_target="tpu_custom_call" | custom-call | tf_op jit(solution)/shard_map/pallas_call | solution.py:29
  58.3 1.8 %collective-permute-start.30 = (bf16[512,128]{1,0:T(8,128)(2,1)S(1)}, bf16[512,128]{1,0:T(8,128)(2,1)S(1)}, u32[]{:S(2)}, u32[]{:S(2)}) collective-permute-start(bf16[512,128]{1,0:T(8,128)(2,1)S(1)} %get-tuple-element.51), channel_id=1, source_target_pairs={{0,24},{8,16},{16,8},{24,0},{1,25},{9,17},{17,9},{25,1},{2,26},{10... | collective-permute-start | bytes 393224 | tf_op jit(solution)/shard_map/ppermute | solution.py:241
  61.6 2.4 %collective-permute-done.30.refs_3_.refs_7_ = bf16[512,128]{1,0:T(8,128)(2,1)S(1)} collective-permute-done((bf16[512,128]{1,0:T(8,128)(2,1)S(1)}, bf16[512,128]{1,0:T(8,128)(2,1)S(1)}, u32[]{:S(2)}, u32[]{:S(2)}) %collective-permute-start.30) | collective-permute-done | bytes 131104 | tf_op jit(solution)/shard_map/ppermute | solution.py:241
  64.0 2.8 %shard_map.95 = (f32[1024,128]{1,0:T(8,128)S(1)}, bf16[1024,128]{1,0:T(8,128)(2,1)S(1)}) custom-call(bf16[1024,1024]{1,0:T(8,128)(2,1)S(1)} %shard_map.83.matrix, bf16[1024,1024]{1,0:T(8,128)(2,1)} %collective-permute-done.18.aside, bf16[512,128]{1,0:T(8,128)(2,1)S(1)} %get-tuple-element.48.refs_0_.refs_4_, ...), custom_call_target="tpu_custom_call" | custom-call | tf_op jit(solution)/shard_map/pallas_call | solution.py:29
  66.8 2.8 %collective-permute-start.36 = (bf16[1024,128]{1,0:T(8,128)(2,1)S(1)}, bf16[1024,128]{1,0:T(8,128)(2,1)S(1)}, u32[]{:S(2)}, u32[]{:S(2)}) collective-permute-start(bf16[1024,128]{1,0:T(8,128)(2,1)S(1)} %get-tuple-element.58.first), channel_id=1, source_target_pairs={{0,1},{1,0},{2,3},{3,2},{4,5},{5,4},{6,7},{7,6},{8,9},{9,8},{10,11... | collective-permute-start | bytes 786440 | tf_op jit(solution)/shard_map/ppermute | solution.py:228
  74.8 1.4 %shard_map.96 = (bf16[1024,128]{1,0:T(8,128)(2,1)S(1)}, bf16[256,128]{1,0:T(8,128)(2,1)S(1)}, bf16[256,128]{1,0:T(8,128)(2,1)S(1)}, bf16[256,128]{1,0:T(8,128)(2,1)S(1)}, bf16[256,128]{1,0:T(8,128)(2,1)S(1)}) custom-call(s32[1,4,4]{2,1,0:T(4,128)S(1)} %copy-done.4, s32[1,4,4]{2,1,0:T(4,128)S(1)} %collective-permute-done.other, ...), custom_call_target="tpu_custom_call" | custom-call | tf_op jit(solution)/shard_map/pallas_call | solution.py:29
  77.0 1.5 %collective-permute-start.33 = (bf16[256,128]{1,0:T(8,128)(2,1)S(1)}, bf16[256,128]{1,0:T(8,128)(2,1)S(1)}, u32[]{:S(2)}, u32[]{:S(2)}) collective-permute-start(bf16[256,128]{1,0:T(8,128)(2,1)S(1)} %get-tuple-element.55), channel_id=1, source_target_pairs={{0,8},{8,0},{16,24},{24,16},{1,9},{9,1},{17,25},{25,17},{2,10},{10... | collective-permute-start | bytes 196616 | tf_op jit(solution)/shard_map/ppermute | solution.py:241
  78.5 1.7 %collective-permute-done.33.refs_1_ = bf16[256,128]{1,0:T(8,128)(2,1)S(1)} collective-permute-done((bf16[256,128]{1,0:T(8,128)(2,1)S(1)}, bf16[256,128]{1,0:T(8,128)(2,1)S(1)}, u32[]{:S(2)}, u32[]{:S(2)}) %collective-permute-start.33) | collective-permute-done | bytes 65568 | tf_op jit(solution)/shard_map/ppermute | solution.py:241
  80.9 2.4 %collective-permute-done.34.refs_2_ = bf16[256,128]{1,0:T(8,128)(2,1)S(1)} collective-permute-done((bf16[256,128]{1,0:T(8,128)(2,1)S(1)}, bf16[256,128]{1,0:T(8,128)(2,1)S(1)}, u32[]{:S(2)}, u32[]{:S(2)}) %collective-permute-start.34) | collective-permute-done | bytes 65568 | tf_op jit(solution)/shard_map/ppermute | solution.py:241
  83.3 1.9 %collective-permute-start.35 = (bf16[256,128]{1,0:T(8,128)(2,1)S(1)}, bf16[256,128]{1,0:T(8,128)(2,1)S(1)}, u32[]{:S(2)}, u32[]{:S(2)}) collective-permute-start(bf16[256,128]{1,0:T(8,128)(2,1)S(1)} %get-tuple-element.57), channel_id=1, source_target_pairs={{0,24},{8,16},{16,8},{24,0},{1,25},{9,17},{17,9},{25,1},{2,26},{10... | collective-permute-start | bytes 196616 | tf_op jit(solution)/shard_map/ppermute | solution.py:241
  85.1 2.1 %collective-permute-done.35.refs_3_ = bf16[256,128]{1,0:T(8,128)(2,1)S(1)} collective-permute-done((bf16[256,128]{1,0:T(8,128)(2,1)S(1)}, bf16[256,128]{1,0:T(8,128)(2,1)S(1)}, u32[]{:S(2)}, u32[]{:S(2)}) %collective-permute-start.35) | collective-permute-done | bytes 65568 | tf_op jit(solution)/shard_map/ppermute | solution.py:241
  87.3 3.4 %shard_map.100.refs_2_ = bf16[1024,128]{1,0:T(8,128)(2,1)S(1)} custom-call(bf16[1024,1024]{1,0:T(8,128)(2,1)S(1)} %shard_map.82.sheet, f32[1024,1]{1,0:T(8,128)S(1)} %copy.10.column, bf16[4,1024,128]{2,1,0:T(8,128)(2,1)S(1)} %copy-done, bf16[1024,1024]{1,0:T(8,128)(2,1)S(1)} %shard_map.83.matrix, bf16[1024,1024]{1,0:T(8,128)(2,1)} %collective-permute-done.18.aside, ...), custom_call_target="tpu_custom_call" | custom-call | tf_op jit(solution)/shard_map/pallas_call | solution.py:29
  92.9 38.0 %collective-permute-start.43 = (bf16[3072,128]{1,0:T(8,128)(2,1)S(1)}, bf16[3072,128]{1,0:T(8,128)(2,1)S(1)}, u32[]{:S(2)}, u32[]{:S(2)}) collective-permute-start(bf16[3072,128]{1,0:T(8,128)(2,1)S(1)} %shard_map.101.late), channel_id=1, source_target_pairs={{0,1},{1,0},{2,3},{3,2},{4,5},{5,4},{6,7},{7,6},{8,9},{9,8},{10,11... | collective-permute-start | bytes 2359304 | tf_op jit(solution)/shard_map/ppermute | solution.py:228
  131.0 2.2 %collective-permute-done.32.early_other = bf16[1024,128]{1,0:T(8,128)(2,1)S(1)} collective-permute-done((bf16[1024,128]{1,0:T(8,128)(2,1)S(1)}, bf16[1024,128]{1,0:T(8,128)(2,1)S(1)}, u32[]{:S(2)}, u32[]{:S(2)}) %collective-permute-start.32) | collective-permute-done | bytes 262176 | tf_op jit(solution)/shard_map/ppermute | solution.py:228
  (103 shorter events, 40.3 us)
Async XLA Ops:
  3.7 43.5 %collective-permute-start.18 = (bf16[1024,1024]{1,0:T(8,128)(2,1)S(1)}, bf16[1024,1024]{1,0:T(8,128)(2,1)}, u32[]{:S(2)}, u32[]{:S(2)}) collective-permute-start(bf16[1024,1024]{1,0:T(8,128)(2,1)S(1)} %shard_map.83.matrix), channel_id=1, source_target_pairs={{0,1},{1,0},{2,3},{3,2},{4,5},{5,4},{6,7},{7,6},{8,9},{9,8},{10,11... | collective-permute-start | bytes 6291464 | tf_op jit(solution)/shard_map/ppermute | solution.py:228
  4.5 10.2 %collective-permute-start.8 = (bf16[1024,128]{1,0:T(8,128)(2,1)S(1)}, bf16[1024,128]{1,0:T(8,128)(2,1)S(1)}, u32[]{:S(2)}, u32[]{:S(2)}) collective-permute-start(bf16[1024,128]{1,0:T(8,128)(2,1)S(1)} %bitcast.6), channel_id=1, source_target_pairs={{0,1},{1,2},{2,3},{3,4},{4,5},{5,6},{6,7},{7,0},{8,9},{9,10},{10,1... | collective-permute-start | bytes 786440 | tf_op jit(solution)/shard_map/ppermute | solution.py:228
  12.4 5.9 %collective-permute-start.4 = (bf16[1024,128]{1,0:T(8,128)(2,1)S(1)}, bf16[1024,128]{1,0:T(8,128)(2,1)S(1)}, u32[]{:S(2)}, u32[]{:S(2)}) collective-permute-start(bf16[1024,128]{1,0:T(8,128)(2,1)S(1)} %shard_map.85.first), channel_id=1, source_target_pairs={{0,1},{1,0},{2,3},{3,2},{4,5},{5,4},{6,7},{7,6},{8,9},{9,8},{10,11... | collective-permute-start | bytes 786440 | tf_op jit(solution)/shard_map/ppermute | solution.py:228
  14.6 11.6 %collective-permute-start.9 = (bf16[1024,128]{1,0:T(8,128)(2,1)S(1)}, bf16[1024,128]{1,0:T(8,128)(2,1)S(1)}, u32[]{:S(2)}, u32[]{:S(2)}) collective-permute-start(bf16[1024,128]{1,0:T(8,128)(2,1)S(1)} %collective-permute-done.8.source), channel_id=1, source_target_pairs={{0,1},{1,2},{2,3},{3,4},{4,5},{5,6},{6,7},{8,9},{9,10},{10,11},{11... | collective-permute-start | bytes 786440 | tf_op jit(solution)/shard_map/ppermute | solution.py:228
  18.3 5.9 %collective-permute-start.13 = (bf16[256,128]{1,0:T(8,128)(2,1)S(1)}, bf16[256,128]{1,0:T(8,128)(2,1)S(1)}, u32[]{:S(2)}, u32[]{:S(2)}) collective-permute-start(bf16[256,128]{1,0:T(8,128)(2,1)S(1)} %get-tuple-element.40), channel_id=1, source_target_pairs={{0,24},{8,16},{16,8},{24,0},{1,25},{9,17},{17,9},{25,1},{2,26},{10... | collective-permute-start | bytes 196616 | tf_op jit(solution)/shard_map/ppermute | solution.py:241
  21.4 15.0 %collective-permute-start.5 = (bf16[1024,128]{1,0:T(8,128)(2,1)S(1)}, bf16[1024,128]{1,0:T(8,128)(2,1)}, u32[]{:S(2)}, u32[]{:S(2)}) collective-permute-start(bf16[1024,128]{1,0:T(8,128)(2,1)S(1)} %shard_map.86.refs_0_), channel_id=1, source_target_pairs={{2,0},{10,8},{18,16},{26,24}} | collective-permute-start | bytes 786440 | tf_op jit(solution)/shard_map/ppermute | solution.py:228
  22.8 13.6 %collective-permute-start.6 = (bf16[1024,128]{1,0:T(8,128)(2,1)S(1)}, bf16[1024,128]{1,0:T(8,128)(2,1)}, u32[]{:S(2)}, u32[]{:S(2)}) collective-permute-start(bf16[1024,128]{1,0:T(8,128)(2,1)S(1)} %shard_map.86.refs_0_), channel_id=1, source_target_pairs={{4,0},{12,8},{20,16},{28,24}} | collective-permute-start | bytes 786440 | tf_op jit(solution)/shard_map/ppermute | solution.py:228
  24.2 12.2 %collective-permute-start.7 = (bf16[1024,128]{1,0:T(8,128)(2,1)S(1)}, bf16[1024,128]{1,0:T(8,128)(2,1)}, u32[]{:S(2)}, u32[]{:S(2)}) collective-permute-start(bf16[1024,128]{1,0:T(8,128)(2,1)S(1)} %shard_map.86.refs_0_), channel_id=1, source_target_pairs={{6,0},{14,8},{22,16},{30,24}} | collective-permute-start | bytes 786440 | tf_op jit(solution)/shard_map/ppermute | solution.py:228
  26.3 14.9 %collective-permute-start.14 = (bf16[1024,128]{1,0:T(8,128)(2,1)S(1)}, bf16[1024,128]{1,0:T(8,128)(2,1)}, u32[]{:S(2)}, u32[]{:S(2)}) collective-permute-start(bf16[1024,128]{1,0:T(8,128)(2,1)S(1)} %shard_map.89.first), channel_id=1, source_target_pairs={{0,1},{1,0},{2,3},{3,2},{4,5},{5,4},{6,7},{7,6},{8,9},{9,8},{10,11... | collective-permute-start | bytes 786440 | tf_op jit(solution)/shard_map/ppermute | solution.py:228
  39.6 5.2 %collective-permute-start.20 = (bf16[512,128]{1,0:T(8,128)(2,1)S(1)}, bf16[512,128]{1,0:T(8,128)(2,1)S(1)}, u32[]{:S(2)}, u32[]{:S(2)}) collective-permute-start(bf16[512,128]{1,0:T(8,128)(2,1)S(1)} %get-tuple-element.43), channel_id=1, source_target_pairs={{0,16},{8,24},{16,0},{24,8},{1,17},{9,25},{17,1},{25,9},{2,18},{10... | collective-permute-start | bytes 393224 | tf_op jit(solution)/shard_map/ppermute | solution.py:241
  40.3 6.3 %collective-permute-start.21 = (bf16[512,128]{1,0:T(8,128)(2,1)S(1)}, bf16[512,128]{1,0:T(8,128)(2,1)S(1)}, u32[]{:S(2)}, u32[]{:S(2)}) collective-permute-start(bf16[512,128]{1,0:T(8,128)(2,1)S(1)} %get-tuple-element.44), channel_id=1, source_target_pairs={{0,24},{8,16},{16,8},{24,0},{1,25},{9,17},{17,9},{25,1},{2,26},{10... | collective-permute-start | bytes 393224 | tf_op jit(solution)/shard_map/ppermute | solution.py:241
  41.1 9.1 %collective-permute-start.22 = (bf16[1024,128]{1,0:T(8,128)(2,1)S(1)}, bf16[1024,128]{1,0:T(8,128)(2,1)S(1)}, u32[]{:S(2)}, u32[]{:S(2)}) collective-permute-start(bf16[1024,128]{1,0:T(8,128)(2,1)S(1)} %collective-permute-done.9.refs_4_), channel_id=1, source_target_pairs={{0,1},{1,2},{2,3},{3,4},{4,5},{5,6},{6,7},{8,9},{9,10},{10,11},{11... | collective-permute-start | bytes 786440 | tf_op jit(solution)/shard_map/ppermute | solution.py:228
  43.5 12.4 %collective-permute-start.10 = (bf16[1024,128]{1,0:T(8,128)(2,1)S(1)}, bf16[1024,128]{1,0:T(8,128)(2,1)S(1)}, u32[]{:S(2)}, u32[]{:S(2)}) collective-permute-start(bf16[1024,128]{1,0:T(8,128)(2,1)S(1)} %get-tuple-element.36.refs_0_), channel_id=1, source_target_pairs={{0,2},{2,4},{4,6},{8,10},{10,12},{12,14},{16,18},{18,20},{20,22},{... | collective-permute-start | bytes 786440 | tf_op jit(solution)/shard_map/ppermute | solution.py:228
  44.8 11.2 %collective-permute-start.15 = (bf16[1024,128]{1,0:T(8,128)(2,1)S(1)}, bf16[1024,128]{1,0:T(8,128)(2,1)S(1)}, u32[]{:S(2)}, u32[]{:S(2)}) collective-permute-start(bf16[1024,128]{1,0:T(8,128)(2,1)S(1)} %shard_map.90.refs_0_), channel_id=1, source_target_pairs={{2,0},{10,8},{18,16},{26,24}} | collective-permute-start | bytes 786440 | tf_op jit(solution)/shard_map/ppermute | solution.py:228
  46.5 9.4 %collective-permute-start.16 = (bf16[1024,128]{1,0:T(8,128)(2,1)S(1)}, bf16[1024,128]{1,0:T(8,128)(2,1)S(1)}, u32[]{:S(2)}, u32[]{:S(2)}) collective-permute-start(bf16[1024,128]{1,0:T(8,128)(2,1)S(1)} %shard_map.90.refs_0_), channel_id=1, source_target_pairs={{4,0},{12,8},{20,16},{28,24}} | collective-permute-start | bytes 786440 | tf_op jit(solution)/shard_map/ppermute | solution.py:228
  47.2 8.8 %collective-permute-start.17 = (bf16[1024,128]{1,0:T(8,128)(2,1)S(1)}, bf16[1024,128]{1,0:T(8,128)(2,1)S(1)}, u32[]{:S(2)}, u32[]{:S(2)}) collective-permute-start(bf16[1024,128]{1,0:T(8,128)(2,1)S(1)} %shard_map.90.refs_0_), channel_id=1, source_target_pairs={{6,0},{14,8},{22,16},{30,24}} | collective-permute-start | bytes 786440 | tf_op jit(solution)/shard_map/ppermute | solution.py:228
  50.2 19.4 %collective-permute-start.24 = (bf16[1024,128]{1,0:T(8,128)(2,1)S(1)}, bf16[1024,128]{1,0:T(8,128)(2,1)S(1)}, u32[]{:S(2)}, u32[]{:S(2)}) collective-permute-start(bf16[1024,128]{1,0:T(8,128)(2,1)S(1)} %get-tuple-element.47.first), channel_id=1, source_target_pairs={{0,1},{1,0},{2,3},{3,2},{4,5},{5,4},{6,7},{7,6},{8,9},{9,8},{10,11... | collective-permute-start | bytes 786440 | tf_op jit(solution)/shard_map/ppermute | solution.py:228
  58.3 5.6 %collective-permute-start.30 = (bf16[512,128]{1,0:T(8,128)(2,1)S(1)}, bf16[512,128]{1,0:T(8,128)(2,1)S(1)}, u32[]{:S(2)}, u32[]{:S(2)}) collective-permute-start(bf16[512,128]{1,0:T(8,128)(2,1)S(1)} %get-tuple-element.51), channel_id=1, source_target_pairs={{0,24},{8,16},{16,8},{24,0},{1,25},{9,17},{17,9},{25,1},{2,26},{10... | collective-permute-start | bytes 393224 | tf_op jit(solution)/shard_map/ppermute | solution.py:241
  66.8 5.6 %collective-permute-start.36 = (bf16[1024,128]{1,0:T(8,128)(2,1)S(1)}, bf16[1024,128]{1,0:T(8,128)(2,1)S(1)}, u32[]{:S(2)}, u32[]{:S(2)}) collective-permute-start(bf16[1024,128]{1,0:T(8,128)(2,1)S(1)} %get-tuple-element.58.first), channel_id=1, source_target_pairs={{0,1},{1,0},{2,3},{3,2},{4,5},{5,4},{6,7},{7,6},{8,9},{9,8},{10,11... | collective-permute-start | bytes 786440 | tf_op jit(solution)/shard_map/ppermute | solution.py:228
  72.5 14.7 %collective-permute-start.37 = (bf16[1024,128]{1,0:T(8,128)(2,1)S(1)}, bf16[1024,128]{1,0:T(8,128)(2,1)S(1)}, u32[]{:S(2)}, u32[]{:S(2)}) collective-permute-start(bf16[1024,128]{1,0:T(8,128)(2,1)S(1)} %shard_map.99.refs_8_), channel_id=1, source_target_pairs={{2,0},{10,8},{18,16},{26,24}} | collective-permute-start | bytes 786440 | tf_op jit(solution)/shard_map/ppermute | solution.py:228
  73.2 14.0 %collective-permute-start.38 = (bf16[1024,128]{1,0:T(8,128)(2,1)S(1)}, bf16[1024,128]{1,0:T(8,128)(2,1)S(1)}, u32[]{:S(2)}, u32[]{:S(2)}) collective-permute-start(bf16[1024,128]{1,0:T(8,128)(2,1)S(1)} %shard_map.99.refs_8_), channel_id=1, source_target_pairs={{4,0},{12,8},{20,16},{28,24}} | collective-permute-start | bytes 786440 | tf_op jit(solution)/shard_map/ppermute | solution.py:228
  73.9 13.4 %collective-permute-start.39 = (bf16[1024,128]{1,0:T(8,128)(2,1)S(1)}, bf16[1024,128]{1,0:T(8,128)(2,1)S(1)}, u32[]{:S(2)}, u32[]{:S(2)}) collective-permute-start(bf16[1024,128]{1,0:T(8,128)(2,1)S(1)} %shard_map.99.refs_8_), channel_id=1, source_target_pairs={{6,0},{14,8},{22,16},{30,24}} | collective-permute-start | bytes 786440 | tf_op jit(solution)/shard_map/ppermute | solution.py:228
  76.3 11.0 %collective-permute-start.31 = (bf16[1024,128]{1,0:T(8,128)(2,1)S(1)}, bf16[1024,128]{1,0:T(8,128)(2,1)S(1)}, u32[]{:S(2)}, u32[]{:S(2)}) collective-permute-start(bf16[1024,128]{1,0:T(8,128)(2,1)S(1)} %shard_map.97), channel_id=1, source_target_pairs={{0,2},{2,4},{4,6},{8,10},{10,12},{12,14},{16,18},{18,20},{20,22},{... | collective-permute-start | bytes 786440 | tf_op jit(solution)/shard_map/ppermute | solution.py:228
  92.9 40.3 %collective-permute-start.43 = (bf16[3072,128]{1,0:T(8,128)(2,1)S(1)}, bf16[3072,128]{1,0:T(8,128)(2,1)S(1)}, u32[]{:S(2)}, u32[]{:S(2)}) collective-permute-start(bf16[3072,128]{1,0:T(8,128)(2,1)S(1)} %shard_map.101.late), channel_id=1, source_target_pairs={{0,1},{1,0},{2,3},{3,2},{4,5},{5,4},{6,7},{7,6},{8,9},{9,8},{10,11... | collective-permute-start | bytes 2359304 | tf_op jit(solution)/shard_map/ppermute | solution.py:228
  (27 other events, 98.3 us)

commit v7 on v6

--- a/solution.py
+++ b/solution.py
@@ -160,19 +160,10 @@
 
 def last_kernel(groups, block, step, sheet, column, incident, matrix, aside, *refs):
     blocks, older, refs = refs[:groups], refs[groups : 2 * groups], refs[2 * groups :]
-    terms, passed, carry = refs[:-2], refs[-2], refs[-1]
-    delay = lax.axis_index("delay")
+    terms, now = refs[:-1], refs[-1]
     driving = driving_of(incident, step, terms)
     driving = driving - product(matrix, blocks, 0, block) - product(aside, older, 1, block)
-    current = law_of(driving, sheet, column)
-
-    @pl.when(delay == 0)
-    def _():
-        carry[...] = current
-
-    @pl.when(delay != 0)
-    def _():
-        carry[...] = passed[...]
+    now[...] = law_of(driving, sheet, column)
 
 
 def choose_kernel(plan, *refs):
@@ -311,16 +302,19 @@
     older = blocks
     blocks = exchange(sends)
     pass_on()
-    carry = call(
-        bind(last_kernel, groups, block, 3),
-        whole, (), (*law, dense, aside, *blocks, *older, *later, slots[-1]),
+    found.append(
+        call(
+            bind(last_kernel, groups, block, 3), whole, (),
+            (*law, dense, aside, *blocks, *older, *later),
+        )
     )
-    found.append(carry)
+    carry = call(carry_kernel, whole, (), (found[-1], slots[-1]))
     reach = [STEPS - 1 - step for step in range(STEPS)]
     heads = [z for z in reach if z < chips]
-    finals = [
-        along(carry, [(2 * z, 2 * (z + k)) for z in heads if z + k < chips]) for k in range(1, chips)
-    ]
+    finals = []
+    for k in range(1, chips):
+        pairs = [(2 * z, 2 * (z + k)) for z in heads if z + k < chips]
+        finals.append(along(found[-1] if len(pairs) == 1 else carry, pairs))
 
     def origin(step, z):
         beyond = z - reach[step]

time: 135 us -> 135 us (level)
    pallas_call x20 -> x21, Pallas kernels: 22.9 us -> 22.9 us  [call(): pl.pallas_call(kernel, out_shape=out_shape, in_specs=[SMEM] * len(scalars...]
  transfers between devices with their start and end apart: 44 -> 44, of which waited for: 14 -> 14; matrix products, arithmetic and copies ran while one was open for 0% -> 0% of each run, Pallas kernels for 14% -> 16%
where the time goes in v7:
time: 135 us; the launch traced here: 134 us
  starting transfers between devices  86.2 us (64%)
  Pallas kernels  23.9 us (18%)
  waiting for transfers between devices  18.7 us (14%)
  local copies, waits for them, and re-layouts  4.68 us (3%)
    ppermute x29, starting transfers between devices, along(): return lax.ppermute(array, 'delay', pairs)  71.2 us
    pallas_call x21, Pallas kernels, call(): pl.pallas_call(kernel, out_shape=out_shape, in_specs=[SMEM] * len(scalars...  22.9 us
    ppermute x15, waiting for transfers between devices, exchange(): lax.ppermute(sends[hop], 'group', [(g, peer_of(g, hop, groups)) for g in...  16.5 us
    ppermute x15, starting transfers between devices, exchange(): lax.ppermute(sends[hop], 'group', [(g, peer_of(g, hop, groups)) for g in...  15 us
    unnamed x15, local copies, waits for them, and re-layouts  4.45 us
  transfers between devices with their start and end apart: 44, of which 14 were waited for; matrix products, arithmetic and copies ran while one was open for 0% of the time, Pallas kernels for 16%

profile of v7, /device:TPU:25, one launch (start us, length us, event | category | flops | bytes accessed | tf_op | source)
XLA Modules:
  0.0 134.1 jit_solution(14367982965162358792)
XLA Ops:
  0.8 1.4 %copy-done.2 = bf16[1,4,3,256,256]{4,3,2,1,0:T(8,128)(2,1)S(1)} copy-done((bf16[1,4,3,256,256]{4,3,2,1,0:T(8,128)(2,1)S(1)}, bf16[1,4,3,256,256]{4,3,2,1,0:T(8,128)(2,1)}, u32[]{:S(2)}) %copy-start.2) | copy-done | bytes 1572888
  9.8 1.8 %collective-permute-done.3.refs_3_ = bf16[256,128]{1,0:T(8,128)(2,1)S(1)} collective-permute-done((bf16[256,128]{1,0:T(8,128)(2,1)S(1)}, bf16[256,128]{1,0:T(8,128)(2,1)S(1)}, u32[]{:S(2)}, u32[]{:S(2)}) %collective-permute-start.3) | collective-permute-done | bytes 65568 | tf_op jit(solution)/shard_map/ppermute | solution.py:232
  12.4 2.3 %collective-permute-start.4 = (bf16[1024,128]{1,0:T(8,128)(2,1)S(1)}, bf16[1024,128]{1,0:T(8,128)(2,1)S(1)}, u32[]{:S(2)}, u32[]{:S(2)}) collective-permute-start(bf16[1024,128]{1,0:T(8,128)(2,1)S(1)} %shard_map.85.first), channel_id=1, source_target_pairs={{0,1},{1,0},{2,3},{3,2},{4,5},{5,4},{6,7},{7,6},{8,9},{9,8},{10,11... | collective-permute-start | bytes 786440 | tf_op jit(solution)/shard_map/ppermute | solution.py:219
  18.3 2.2 %collective-permute-start.13 = (bf16[256,128]{1,0:T(8,128)(2,1)S(1)}, bf16[256,128]{1,0:T(8,128)(2,1)S(1)}, u32[]{:S(2)}, u32[]{:S(2)}) collective-permute-start(bf16[256,128]{1,0:T(8,128)(2,1)S(1)} %get-tuple-element.40), channel_id=1, source_target_pairs={{0,24},{8,16},{16,8},{24,0},{1,25},{9,17},{17,9},{25,1},{2,26},{10... | collective-permute-start | bytes 196616 | tf_op jit(solution)/shard_map/ppermute | solution.py:232
  26.3 3.7 %collective-permute-start.14 = (bf16[1024,128]{1,0:T(8,128)(2,1)S(1)}, bf16[1024,128]{1,0:T(8,128)(2,1)}, u32[]{:S(2)}, u32[]{:S(2)}) collective-permute-start(bf16[1024,128]{1,0:T(8,128)(2,1)S(1)} %shard_map.89.first), channel_id=1, source_target_pairs={{0,1},{1,0},{2,3},{3,2},{4,5},{5,4},{6,7},{7,6},{8,9},{9,8},{10,11... | collective-permute-start | bytes 786440 | tf_op jit(solution)/shard_map/ppermute | solution.py:219
  30.2 1.6 %copy-done.1 = bf16[1024,1024]{1,0:T(8,128)(2,1)S(1)} copy-done((bf16[1024,1024]{1,0:T(8,128)(2,1)S(1)}, bf16[1024,1024]{1,0:T(8,128)(2,1)}, u32[]{:S(2)}) %copy-start.1) | copy-done | bytes 2097176
  31.8 4.6 %shard_map.82.sheet = bf16[1024,1024]{1,0:T(8,128)(2,1)S(1)} custom-call(bf16[1024,1024]{1,0:T(8,128)(2,1)S(1)} %copy-done.1, f32[1024,1]{1,0:T(8,128)S(1)} %copy.10.column, f32[1,1024]{1,0:T(1,128)S(1)} %bitcast.9), custom_call_target="tpu_custom_call" | custom-call | tf_op jit(solution)/shard_map/pallas_call | solution.py:29
  36.4 2.0 %shard_map.87 = (bf16[1024,128]{1,0:T(8,128)(2,1)S(1)}, bf16[512,128]{1,0:T(8,128)(2,1)S(1)}, bf16[512,128]{1,0:T(8,128)(2,1)S(1)}, bf16[512,128]{1,0:T(8,128)(2,1)S(1)}, bf16[512,128]{1,0:T(8,128)(2,1)S(1)}) custom-call(s32[1,4,4]{2,1,0:T(4,128)S(1)} %copy-done.4, s32[1,4,4]{2,1,0:T(4,128)S(1)} %collective-permute-done.other, ...), custom_call_target="tpu_custom_call" | custom-call | tf_op jit(solution)/shard_map/pallas_call | solution.py:29
  47.9 2.3 %shard_map.91 = (f32[1024,128]{1,0:T(8,128)S(1)}, bf16[1024,128]{1,0:T(8,128)(2,1)S(1)}) custom-call(bf16[1024,1024]{1,0:T(8,128)(2,1)S(1)} %shard_map.83.matrix, bf16[1024,1024]{1,0:T(8,128)(2,1)} %collective-permute-done.18.aside, bf16[512,128]{1,0:T(8,128)(2,1)S(1)} %get-tuple-element.41.refs_0_.refs_4_, ...), custom_call_target="tpu_custom_call" | custom-call | tf_op jit(solution)/shard_map/pallas_call | solution.py:29
  50.2 5.7 %collective-permute-start.24 = (bf16[1024,128]{1,0:T(8,128)(2,1)S(1)}, bf16[1024,128]{1,0:T(8,128)(2,1)S(1)}, u32[]{:S(2)}, u32[]{:S(2)}) collective-permute-start(bf16[1024,128]{1,0:T(8,128)(2,1)S(1)} %get-tuple-element.47.first), channel_id=1, source_target_pairs={{0,1},{1,0},{2,3},{3,2},{4,5},{5,4},{6,7},{7,6},{8,9},{9,8},{10,11... | collective-permute-start | bytes 786440 | tf_op jit(solution)/shard_map/ppermute | solution.py:219
  56.0 1.5 %shard_map.92 = (bf16[1024,128]{1,0:T(8,128)(2,1)S(1)}, bf16[512,128]{1,0:T(8,128)(2,1)S(1)}, bf16[512,128]{1,0:T(8,128)(2,1)S(1)}, bf16[512,128]{1,0:T(8,128)(2,1)S(1)}, bf16[512,128]{1,0:T(8,128)(2,1)S(1)}) custom-call(s32[1,4,4]{2,1,0:T(4,128)S(1)} %copy-done.4, s32[1,4,4]{2,1,0:T(4,128)S(1)} %collective-permute-done.other, ...), custom_call_target="tpu_custom_call" | custom-call | tf_op jit(solution)/shard_map/pallas_call | solution.py:29
  58.3 1.8 %collective-permute-start.30 = (bf16[512,128]{1,0:T(8,128)(2,1)S(1)}, bf16[512,128]{1,0:T(8,128)(2,1)S(1)}, u32[]{:S(2)}, u32[]{:S(2)}) collective-permute-start(bf16[512,128]{1,0:T(8,128)(2,1)S(1)} %get-tuple-element.51), channel_id=1, source_target_pairs={{0,24},{8,16},{16,8},{24,0},{1,25},{9,17},{17,9},{25,1},{2,26},{10... | collective-permute-start | bytes 393224 | tf_op jit(solution)/shard_map/ppermute | solution.py:232
  61.6 2.4 %collective-permute-done.30.refs_3_.refs_7_ = bf16[512,128]{1,0:T(8,128)(2,1)S(1)} collective-permute-done((bf16[512,128]{1,0:T(8,128)(2,1)S(1)}, bf16[512,128]{1,0:T(8,128)(2,1)S(1)}, u32[]{:S(2)}, u32[]{:S(2)}) %collective-permute-start.30) | collective-permute-done | bytes 131104 | tf_op jit(solution)/shard_map/ppermute | solution.py:232
  64.0 2.8 %shard_map.95 = (f32[1024,128]{1,0:T(8,128)S(1)}, bf16[1024,128]{1,0:T(8,128)(2,1)S(1)}) custom-call(bf16[1024,1024]{1,0:T(8,128)(2,1)S(1)} %shard_map.83.matrix, bf16[1024,1024]{1,0:T(8,128)(2,1)} %collective-permute-done.18.aside, bf16[512,128]{1,0:T(8,128)(2,1)S(1)} %get-tuple-element.48.refs_0_.refs_4_, ...), custom_call_target="tpu_custom_call" | custom-call | tf_op jit(solution)/shard_map/pallas_call | solution.py:29
  66.8 2.8 %collective-permute-start.36 = (bf16[1024,128]{1,0:T(8,128)(2,1)S(1)}, bf16[1024,128]{1,0:T(8,128)(2,1)S(1)}, u32[]{:S(2)}, u32[]{:S(2)}) collective-permute-start(bf16[1024,128]{1,0:T(8,128)(2,1)S(1)} %get-tuple-element.58.first), channel_id=1, source_target_pairs={{0,1},{1,0},{2,3},{3,2},{4,5},{5,4},{6,7},{7,6},{8,9},{9,8},{10,11... | collective-permute-start | bytes 786440 | tf_op jit(solution)/shard_map/ppermute | solution.py:219
  74.8 1.4 %shard_map.96 = (bf16[1024,128]{1,0:T(8,128)(2,1)S(1)}, bf16[256,128]{1,0:T(8,128)(2,1)S(1)}, bf16[256,128]{1,0:T(8,128)(2,1)S(1)}, bf16[256,128]{1,0:T(8,128)(2,1)S(1)}, bf16[256,128]{1,0:T(8,128)(2,1)S(1)}) custom-call(s32[1,4,4]{2,1,0:T(4,128)S(1)} %copy-done.4, s32[1,4,4]{2,1,0:T(4,128)S(1)} %collective-permute-done.other, ...), custom_call_target="tpu_custom_call" | custom-call | tf_op jit(solution)/shard_map/pallas_call | solution.py:29
  77.0 1.5 %collective-permute-start.33 = (bf16[256,128]{1,0:T(8,128)(2,1)S(1)}, bf16[256,128]{1,0:T(8,128)(2,1)S(1)}, u32[]{:S(2)}, u32[]{:S(2)}) collective-permute-start(bf16[256,128]{1,0:T(8,128)(2,1)S(1)} %get-tuple-element.55), channel_id=1, source_target_pairs={{0,8},{8,0},{16,24},{24,16},{1,9},{9,1},{17,25},{25,17},{2,10},{10... | collective-permute-start | bytes 196616 | tf_op jit(solution)/shard_map/ppermute | solution.py:232
  78.5 1.7 %collective-permute-done.33.refs_1_ = bf16[256,128]{1,0:T(8,128)(2,1)S(1)} collective-permute-done((bf16[256,128]{1,0:T(8,128)(2,1)S(1)}, bf16[256,128]{1,0:T(8,128)(2,1)S(1)}, u32[]{:S(2)}, u32[]{:S(2)}) %collective-permute-start.33) | collective-permute-done | bytes 65568 | tf_op jit(solution)/shard_map/ppermute | solution.py:232
  80.9 2.3 %collective-permute-done.34.refs_2_ = bf16[256,128]{1,0:T(8,128)(2,1)S(1)} collective-permute-done((bf16[256,128]{1,0:T(8,128)(2,1)S(1)}, bf16[256,128]{1,0:T(8,128)(2,1)S(1)}, u32[]{:S(2)}, u32[]{:S(2)}) %collective-permute-start.34) | collective-permute-done | bytes 65568 | tf_op jit(solution)/shard_map/ppermute | solution.py:232
  83.3 1.9 %collective-permute-start.35 = (bf16[256,128]{1,0:T(8,128)(2,1)S(1)}, bf16[256,128]{1,0:T(8,128)(2,1)S(1)}, u32[]{:S(2)}, u32[]{:S(2)}) collective-permute-start(bf16[256,128]{1,0:T(8,128)(2,1)S(1)} %get-tuple-element.57), channel_id=1, source_target_pairs={{0,24},{8,16},{16,8},{24,0},{1,25},{9,17},{17,9},{25,1},{2,26},{10... | collective-permute-start | bytes 196616 | tf_op jit(solution)/shard_map/ppermute | solution.py:232
  85.2 2.1 %collective-permute-done.35.refs_3_ = bf16[256,128]{1,0:T(8,128)(2,1)S(1)} collective-permute-done((bf16[256,128]{1,0:T(8,128)(2,1)S(1)}, bf16[256,128]{1,0:T(8,128)(2,1)S(1)}, u32[]{:S(2)}, u32[]{:S(2)}) %collective-permute-start.35) | collective-permute-done | bytes 65568 | tf_op jit(solution)/shard_map/ppermute | solution.py:232
  87.3 3.4 %shard_map.100.current.refs_2_ = bf16[1024,128]{1,0:T(8,128)(2,1)S(1)} custom-call(bf16[1024,1024]{1,0:T(8,128)(2,1)S(1)} %shard_map.82.sheet, f32[1024,1]{1,0:T(8,128)S(1)} %copy.10.column, bf16[4,1024,128]{2,1,0:T(8,128)(2,1)S(1)} %copy-done, bf16[1024,1024]{1,0:T(8,128)(2,1)S(1)} %shard_map.83.matrix, bf16[1024,1024]{1,0:T(8,128)(2,1)} %collective-permute-done.18.aside, ...), custom_call_target="tpu_custom_call" | custom-call | tf_op jit(solution)/shard_map/pallas_call | solution.py:29
  92.9 37.7 %collective-permute-start.43 = (bf16[3072,128]{1,0:T(8,128)(2,1)S(1)}, bf16[3072,128]{1,0:T(8,128)(2,1)S(1)}, u32[]{:S(2)}, u32[]{:S(2)}) collective-permute-start(bf16[3072,128]{1,0:T(8,128)(2,1)S(1)} %shard_map.102.late), channel_id=1, source_target_pairs={{0,1},{1,0},{2,3},{3,2},{4,5},{5,4},{6,7},{7,6},{8,9},{9,8},{10,11... | collective-permute-start | bytes 2359304 | tf_op jit(solution)/shard_map/ppermute | solution.py:219
  130.8 2.2 %collective-permute-done.32.early_other = bf16[1024,128]{1,0:T(8,128)(2,1)S(1)} collective-permute-done((bf16[1024,128]{1,0:T(8,128)(2,1)S(1)}, bf16[1024,128]{1,0:T(8,128)(2,1)S(1)}, u32[]{:S(2)}, u32[]{:S(2)}) %collective-permute-start.32) | collective-permute-done | bytes 262176 | tf_op jit(solution)/shard_map/ppermute | solution.py:219
  (104 shorter events, 40.4 us)
Async XLA Ops:
  3.7 43.5 %collective-permute-start.18 = (bf16[1024,1024]{1,0:T(8,128)(2,1)S(1)}, bf16[1024,1024]{1,0:T(8,128)(2,1)}, u32[]{:S(2)}, u32[]{:S(2)}) collective-permute-start(bf16[1024,1024]{1,0:T(8,128)(2,1)S(1)} %shard_map.83.matrix), channel_id=1, source_target_pairs={{0,1},{1,0},{2,3},{3,2},{4,5},{5,4},{6,7},{7,6},{8,9},{9,8},{10,11... | collective-permute-start | bytes 6291464 | tf_op jit(solution)/shard_map/ppermute | solution.py:219
  4.5 10.2 %collective-permute-start.8 = (bf16[1024,128]{1,0:T(8,128)(2,1)S(1)}, bf16[1024,128]{1,0:T(8,128)(2,1)S(1)}, u32[]{:S(2)}, u32[]{:S(2)}) collective-permute-start(bf16[1024,128]{1,0:T(8,128)(2,1)S(1)} %bitcast.6), channel_id=1, source_target_pairs={{0,1},{1,2},{2,3},{3,4},{4,5},{5,6},{6,7},{7,0},{8,9},{9,10},{10,1... | collective-permute-start | bytes 786440 | tf_op jit(solution)/shard_map/ppermute | solution.py:219
  12.4 5.9 %collective-permute-start.4 = (bf16[1024,128]{1,0:T(8,128)(2,1)S(1)}, bf16[1024,128]{1,0:T(8,128)(2,1)S(1)}, u32[]{:S(2)}, u32[]{:S(2)}) collective-permute-start(bf16[1024,128]{1,0:T(8,128)(2,1)S(1)} %shard_map.85.first), channel_id=1, source_target_pairs={{0,1},{1,0},{2,3},{3,2},{4,5},{5,4},{6,7},{7,6},{8,9},{9,8},{10,11... | collective-permute-start | bytes 786440 | tf_op jit(solution)/shard_map/ppermute | solution.py:219
  14.6 11.6 %collective-permute-start.9 = (bf16[1024,128]{1,0:T(8,128)(2,1)S(1)}, bf16[1024,128]{1,0:T(8,128)(2,1)S(1)}, u32[]{:S(2)}, u32[]{:S(2)}) collective-permute-start(bf16[1024,128]{1,0:T(8,128)(2,1)S(1)} %collective-permute-done.8.source), channel_id=1, source_target_pairs={{0,1},{1,2},{2,3},{3,4},{4,5},{5,6},{6,7},{8,9},{9,10},{10,11},{11... | collective-permute-start | bytes 786440 | tf_op jit(solution)/shard_map/ppermute | solution.py:219
  18.3 5.9 %collective-permute-start.13 = (bf16[256,128]{1,0:T(8,128)(2,1)S(1)}, bf16[256,128]{1,0:T(8,128)(2,1)S(1)}, u32[]{:S(2)}, u32[]{:S(2)}) collective-permute-start(bf16[256,128]{1,0:T(8,128)(2,1)S(1)} %get-tuple-element.40), channel_id=1, source_target_pairs={{0,24},{8,16},{16,8},{24,0},{1,25},{9,17},{17,9},{25,1},{2,26},{10... | collective-permute-start | bytes 196616 | tf_op jit(solution)/shard_map/ppermute | solution.py:232
  21.4 15.0 %collective-permute-start.5 = (bf16[1024,128]{1,0:T(8,128)(2,1)S(1)}, bf16[1024,128]{1,0:T(8,128)(2,1)}, u32[]{:S(2)}, u32[]{:S(2)}) collective-permute-start(bf16[1024,128]{1,0:T(8,128)(2,1)S(1)} %shard_map.86.refs_0_), channel_id=1, source_target_pairs={{2,0},{10,8},{18,16},{26,24}} | collective-permute-start | bytes 786440 | tf_op jit(solution)/shard_map/ppermute | solution.py:219
  22.8 13.6 %collective-permute-start.6 = (bf16[1024,128]{1,0:T(8,128)(2,1)S(1)}, bf16[1024,128]{1,0:T(8,128)(2,1)}, u32[]{:S(2)}, u32[]{:S(2)}) collective-permute-start(bf16[1024,128]{1,0:T(8,128)(2,1)S(1)} %shard_map.86.refs_0_), channel_id=1, source_target_pairs={{4,0},{12,8},{20,16},{28,24}} | collective-permute-start | bytes 786440 | tf_op jit(solution)/shard_map/ppermute | solution.py:219
  24.2 12.2 %collective-permute-start.7 = (bf16[1024,128]{1,0:T(8,128)(2,1)S(1)}, bf16[1024,128]{1,0:T(8,128)(2,1)}, u32[]{:S(2)}, u32[]{:S(2)}) collective-permute-start(bf16[1024,128]{1,0:T(8,128)(2,1)S(1)} %shard_map.86.refs_0_), channel_id=1, source_target_pairs={{6,0},{14,8},{22,16},{30,24}} | collective-permute-start | bytes 786440 | tf_op jit(solution)/shard_map/ppermute | solution.py:219
  26.3 14.9 %collective-permute-start.14 = (bf16[1024,128]{1,0:T(8,128)(2,1)S(1)}, bf16[1024,128]{1,0:T(8,128)(2,1)}, u32[]{:S(2)}, u32[]{:S(2)}) collective-permute-start(bf16[1024,128]{1,0:T(8,128)(2,1)S(1)} %shard_map.89.first), channel_id=1, source_target_pairs={{0,1},{1,0},{2,3},{3,2},{4,5},{5,4},{6,7},{7,6},{8,9},{9,8},{10,11... | collective-permute-start | bytes 786440 | tf_op jit(solution)/shard_map/ppermute | solution.py:219
  39.6 5.2 %collective-permute-start.20 = (bf16[512,128]{1,0:T(8,128)(2,1)S(1)}, bf16[512,128]{1,0:T(8,128)(2,1)S(1)}, u32[]{:S(2)}, u32[]{:S(2)}) collective-permute-start(bf16[512,128]{1,0:T(8,128)(2,1)S(1)} %get-tuple-element.43), channel_id=1, source_target_pairs={{0,16},{8,24},{16,0},{24,8},{1,17},{9,25},{17,1},{25,9},{2,18},{10... | collective-permute-start | bytes 393224 | tf_op jit(solution)/shard_map/ppermute | solution.py:232
  40.3 6.3 %collective-permute-start.21 = (bf16[512,128]{1,0:T(8,128)(2,1)S(1)}, bf16[512,128]{1,0:T(8,128)(2,1)S(1)}, u32[]{:S(2)}, u32[]{:S(2)}) collective-permute-start(bf16[512,128]{1,0:T(8,128)(2,1)S(1)} %get-tuple-element.44), channel_id=1, source_target_pairs={{0,24},{8,16},{16,8},{24,0},{1,25},{9,17},{17,9},{25,1},{2,26},{10... | collective-permute-start | bytes 393224 | tf_op jit(solution)/shard_map/ppermute | solution.py:232
  41.1 9.1 %collective-permute-start.22 = (bf16[1024,128]{1,0:T(8,128)(2,1)S(1)}, bf16[1024,128]{1,0:T(8,128)(2,1)S(1)}, u32[]{:S(2)}, u32[]{:S(2)}) collective-permute-start(bf16[1024,128]{1,0:T(8,128)(2,1)S(1)} %collective-permute-done.9.refs_4_), channel_id=1, source_target_pairs={{0,1},{1,2},{2,3},{3,4},{4,5},{5,6},{6,7},{8,9},{9,10},{10,11},{11... | collective-permute-start | bytes 786440 | tf_op jit(solution)/shard_map/ppermute | solution.py:219
  43.5 12.4 %collective-permute-start.10 = (bf16[1024,128]{1,0:T(8,128)(2,1)S(1)}, bf16[1024,128]{1,0:T(8,128)(2,1)S(1)}, u32[]{:S(2)}, u32[]{:S(2)}) collective-permute-start(bf16[1024,128]{1,0:T(8,128)(2,1)S(1)} %get-tuple-element.36.refs_0_), channel_id=1, source_target_pairs={{0,2},{2,4},{4,6},{8,10},{10,12},{12,14},{16,18},{18,20},{20,22},{... | collective-permute-start | bytes 786440 | tf_op jit(solution)/shard_map/ppermute | solution.py:219
  44.8 11.2 %collective-permute-start.15 = (bf16[1024,128]{1,0:T(8,128)(2,1)S(1)}, bf16[1024,128]{1,0:T(8,128)(2,1)S(1)}, u32[]{:S(2)}, u32[]{:S(2)}) collective-permute-start(bf16[1024,128]{1,0:T(8,128)(2,1)S(1)} %shard_map.90.refs_0_), channel_id=1, source_target_pairs={{2,0},{10,8},{18,16},{26,24}} | collective-permute-start | bytes 786440 | tf_op jit(solution)/shard_map/ppermute | solution.py:219
  46.5 9.4 %collective-permute-start.16 = (bf16[1024,128]{1,0:T(8,128)(2,1)S(1)}, bf16[1024,128]{1,0:T(8,128)(2,1)S(1)}, u32[]{:S(2)}, u32[]{:S(2)}) collective-permute-start(bf16[1024,128]{1,0:T(8,128)(2,1)S(1)} %shard_map.90.refs_0_), channel_id=1, source_target_pairs={{4,0},{12,8},{20,16},{28,24}} | collective-permute-start | bytes 786440 | tf_op jit(solution)/shard_map/ppermute | solution.py:219
  47.2 8.8 %collective-permute-start.17 = (bf16[1024,128]{1,0:T(8,128)(2,1)S(1)}, bf16[1024,128]{1,0:T(8,128)(2,1)S(1)}, u32[]{:S(2)}, u32[]{:S(2)}) collective-permute-start(bf16[1024,128]{1,0:T(8,128)(2,1)S(1)} %shard_map.90.refs_0_), channel_id=1, source_target_pairs={{6,0},{14,8},{22,16},{30,24}} | collective-permute-start | bytes 786440 | tf_op jit(solution)/shard_map/ppermute | solution.py:219
  50.2 19.4 %collective-permute-start.24 = (bf16[1024,128]{1,0:T(8,128)(2,1)S(1)}, bf16[1024,128]{1,0:T(8,128)(2,1)S(1)}, u32[]{:S(2)}, u32[]{:S(2)}) collective-permute-start(bf16[1024,128]{1,0:T(8,128)(2,1)S(1)} %get-tuple-element.47.first), channel_id=1, source_target_pairs={{0,1},{1,0},{2,3},{3,2},{4,5},{5,4},{6,7},{7,6},{8,9},{9,8},{10,11... | collective-permute-start | bytes 786440 | tf_op jit(solution)/shard_map/ppermute | solution.py:219
  58.3 5.6 %collective-permute-start.30 = (bf16[512,128]{1,0:T(8,128)(2,1)S(1)}, bf16[512,128]{1,0:T(8,128)(2,1)S(1)}, u32[]{:S(2)}, u32[]{:S(2)}) collective-permute-start(bf16[512,128]{1,0:T(8,128)(2,1)S(1)} %get-tuple-element.51), channel_id=1, source_target_pairs={{0,24},{8,16},{16,8},{24,0},{1,25},{9,17},{17,9},{25,1},{2,26},{10... | collective-permute-start | bytes 393224 | tf_op jit(solution)/shard_map/ppermute | solution.py:232
  66.8 5.6 %collective-permute-start.36 = (bf16[1024,128]{1,0:T(8,128)(2,1)S(1)}, bf16[1024,128]{1,0:T(8,128)(2,1)S(1)}, u32[]{:S(2)}, u32[]{:S(2)}) collective-permute-start(bf16[1024,128]{1,0:T(8,128)(2,1)S(1)} %get-tuple-element.58.first), channel_id=1, source_target_pairs={{0,1},{1,0},{2,3},{3,2},{4,5},{5,4},{6,7},{7,6},{8,9},{9,8},{10,11... | collective-permute-start | bytes 786440 | tf_op jit(solution)/shard_map/ppermute | solution.py:219
  72.6 14.7 %collective-permute-start.37 = (bf16[1024,128]{1,0:T(8,128)(2,1)S(1)}, bf16[1024,128]{1,0:T(8,128)(2,1)S(1)}, u32[]{:S(2)}, u32[]{:S(2)}) collective-permute-start(bf16[1024,128]{1,0:T(8,128)(2,1)S(1)} %shard_map.99.refs_8_), channel_id=1, source_target_pairs={{2,0},{10,8},{18,16},{26,24}} | collective-permute-start | bytes 786440 | tf_op jit(solution)/shard_map/ppermute | solution.py:219
  73.2 14.0 %collective-permute-start.38 = (bf16[1024,128]{1,0:T(8,128)(2,1)S(1)}, bf16[1024,128]{1,0:T(8,128)(2,1)S(1)}, u32[]{:S(2)}, u32[]{:S(2)}) collective-permute-start(bf16[1024,128]{1,0:T(8,128)(2,1)S(1)} %shard_map.99.refs_8_), channel_id=1, source_target_pairs={{4,0},{12,8},{20,16},{28,24}} | collective-permute-start | bytes 786440 | tf_op jit(solution)/shard_map/ppermute | solution.py:219
  73.9 13.4 %collective-permute-start.39 = (bf16[1024,128]{1,0:T(8,128)(2,1)S(1)}, bf16[1024,128]{1,0:T(8,128)(2,1)S(1)}, u32[]{:S(2)}, u32[]{:S(2)}) collective-permute-start(bf16[1024,128]{1,0:T(8,128)(2,1)S(1)} %shard_map.99.refs_8_), channel_id=1, source_target_pairs={{6,0},{14,8},{22,16},{30,24}} | collective-permute-start | bytes 786440 | tf_op jit(solution)/shard_map/ppermute | solution.py:219
  76.3 15.1 %collective-permute-start.31 = (bf16[1024,128]{1,0:T(8,128)(2,1)S(1)}, bf16[1024,128]{1,0:T(8,128)(2,1)S(1)}, u32[]{:S(2)}, u32[]{:S(2)}) collective-permute-start(bf16[1024,128]{1,0:T(8,128)(2,1)S(1)} %shard_map.97), channel_id=1, source_target_pairs={{0,2},{2,4},{4,6},{8,10},{10,12},{12,14},{16,18},{18,20},{20,22},{... | collective-permute-start | bytes 786440 | tf_op jit(solution)/shard_map/ppermute | solution.py:219
  92.9 40.0 %collective-permute-start.43 = (bf16[3072,128]{1,0:T(8,128)(2,1)S(1)}, bf16[3072,128]{1,0:T(8,128)(2,1)S(1)}, u32[]{:S(2)}, u32[]{:S(2)}) collective-permute-start(bf16[3072,128]{1,0:T(8,128)(2,1)S(1)} %shard_map.102.late), channel_id=1, source_target_pairs={{0,1},{1,0},{2,3},{3,2},{4,5},{5,4},{6,7},{7,6},{8,9},{9,8},{10,11... | collective-permute-start | bytes 2359304 | tf_op jit(solution)/shard_map/ppermute | solution.py:219
  (27 other events, 98.4 us)

commit v8 on v7

--- a/solution.py
+++ b/solution.py
@@ -88,18 +88,17 @@
     out[...] = total.astype(BF16)
 
 
-def plus_kernel(first, second, out):
-    out[...] = (first[...].astype(F32) + second[...].astype(F32)).astype(BF16)
-
-
-def near_kernel(groups, block, matrix, aside, *refs):
-    blocks, refs = refs[:groups], refs[groups:]
-    older, refs = (refs[:groups], refs[groups:]) if len(refs) > 2 else (None, refs)
-    wide, narrow = refs
+def plus_kernel(start, first, second, out):
+    total = first[...].astype(F32) + second[...].astype(F32)
+    if start > 0:
+        total = jnp.where(lax.axis_index("delay") >= start, total, 0.0)
+    out[...] = total.astype(BF16)
+
+
+def near_kernel(groups, block, first, matrix, *refs):
+    blocks, wide, narrow = refs[:groups], refs[groups], refs[groups + 1]
     total = product(matrix, blocks, 0, block)
-    narrow[...] = jnp.where(lax.axis_index("delay") >= 2, total, 0.0).astype(BF16)
-    if older is not None:
-        total = total + product(aside, older, 1, block)
+    narrow[...] = jnp.where(lax.axis_index("delay") >= first, total, 0.0).astype(BF16)
     wide[...] = total
 
 
@@ -115,14 +114,9 @@
 
 
 def step_kernel(groups, block, step, fields, table, other, sheet, column, incident, *refs):
-    terms, refs = refs[:fields], refs[fields:]
+    terms, sources, refs = refs[:fields], refs[fields:-groups - 1], refs[-groups - 1 :]
+    now, sends = refs[0], refs[1:]
     delay = lax.axis_index("delay")
-    history = second = None
-    if step < 2:
-        history, refs = refs[0], refs[1:]
-    if step == 1:
-        second, refs = refs[0], refs[1:]
-    now, sends = refs[0], refs[1:]
     now[...] = law_of(driving_of(incident, step, terms), sheet, column)
     if step == 2:
         emit(groups, block, sends, 0, now, table)
@@ -131,19 +125,17 @@
     @pl.when(delay == 0)
     def _():
         emit(groups, block, sends, 0, now, table)
-        emit(groups, block, sends, 1, now, other)
-
-    @pl.when((delay != 0) if step == 0 else (delay != 0) & (delay != 2))
-    def _():
-        emit(groups, block, sends, 0, history, table)
-        emit(groups, block, sends, 1, history, table)
-
-    if step == 1:
-
-        @pl.when(delay == 2)
-        def _():
-            emit(groups, block, sends, 0, second, table)
-            emit(groups, block, sends, 1, second, table)
+        if step == 1:
+            emit(groups, block, sends, 1, now, other)
+
+    for place, source in enumerate(sources, 1):
+        last = place == len(sources)
+
+        @pl.when((delay >= place) if last else (delay == place))
+        def _(source=source):
+            emit(groups, block, sends, 0, source, table)
+            if step == 1:
+                emit(groups, block, sends, 1, source, table)
 
 
 def carry_kernel(current, passed, carry):
@@ -233,10 +225,13 @@
             for hop in range(1, groups)
         ]
 
-    def gathered(term):
+    def gathered(term, first=0):
         other = swap(term)
-        chip = call(plus_kernel, whole, (), (term, other))
-        return [chip] + [along(chip, [(2 * z, 0)]) for z in range(1, chips)]
+        chip = call(bind(plus_kernel, first), whole, (), (term, other))
+        fields = [chip]
+        for z in range(1, chips):
+            fields.append(along(chip, [(2 * z, 0)]))
+        return fields, other
 
     earlier = shift(history[0])
     listed = jnp.clip(block_row, 0, rows // block - 1)
@@ -253,16 +248,16 @@
         bind(dense_kernel, groups, block, depth),
         shape((rows, groups * block), BF16), (listed, block_count), (weights,),
     )
-    fields = gathered(term_of(blocks, 0))
+    fields, _ = gathered(term_of(blocks, 0))
     sends = picked(earlier)
     blocks = exchange(sends)
-    earlier = onward(earlier)
+    earlier = shift(earlier)
     inverse = 1.0 / sheet_diag
     column, row = inverse[:, None], inverse[None, :]
     sheet = call(sheet_kernel, shape((rows, rows), BF16), (), (self_block, column, row), 20)
-    later = gathered(term_of(blocks, 1))
+    later, _ = gathered(term_of(blocks, 1))
     other = swap(send_pick)
-    oldest = onward(earlier)
+    oldest = shift(earlier)
     aside = swap(dense)
 
     law = (sheet, column, incident)
@@ -283,23 +278,23 @@
             array = call(carry_kernel, whole, (), (array, slots[-1]))
         slots.append(onward(array, 2))
 
-    def near_of(blocks, older):
+    def near_of(blocks, first):
         return call(
-            bind(near_kernel, groups, block), [wide_whole, whole], (), (dense, aside, *blocks, *older)
-        )
-
-    sends = stepped(0, fields, (earlier,), 2)
+            bind(near_kernel, groups, block, first), [wide_whole, whole], (), (dense, *blocks)
+        )
+
+    sends = stepped(0, fields, (earlier,), 1)
+    blocks = exchange(sends)
+    handed = swap(found[0])
+    pass_on()
+    wide, narrow = near_of(blocks, 2)
+    fields, _ = gathered(narrow)
+    sends = stepped(1, (*later, wide), (handed, slots[0], oldest), 2)
     older = exchange(sends)
     pass_on()
-    wide, narrow = near_of(older, ())
-    fields = gathered(narrow)
-    sends = stepped(1, (*later, wide), (oldest, slots[0]), 2)
-    blocks = exchange(sends)
-    pass_on()
-    wide, narrow = near_of(blocks, older)
-    later = gathered(narrow)
-    sends = stepped(2, (*fields, wide), (), 1)
-    older = blocks
+    wide, narrow = near_of(older, 1)
+    later, partner = gathered(narrow, 2)
+    sends = stepped(2, (*fields, wide, partner), (), 1)
     blocks = exchange(sends)
     pass_on()
     found.append(

time: 135 us -> 131 us (0.970)
  the two profiles are of different devices: /device:TPU:25 before, /device:TPU:0 now
where the time goes in v8:
time: 131 us; the launch traced here: 129 us
  waiting for transfers between devices  51.3 us (39%)
  starting transfers between devices  49.9 us (38%)
  Pallas kernels  20.6 us (16%)
  local copies, waits for them, and re-layouts  7 us (5%)
    ppermute x30, waiting for transfers between devices, along(): return lax.ppermute(array, 'delay', pairs)  48.5 us
    ppermute x30, starting transfers between devices, along(): return lax.ppermute(array, 'delay', pairs)  30.2 us
    ppermute x15, starting transfers between devices, exchange(): lax.ppermute(sends[hop], 'group', [(g, peer_of(g, hop, groups)) for g in...  19.7 us
    pallas_call x21, Pallas kernels, call(): pl.pallas_call(kernel, out_shape=out_shape, in_specs=[SMEM] * len(scalars...  19.6 us
    unnamed x23, local copies, waits for them, and re-layouts  6.77 us
    ppermute x15, waiting for transfers between devices, exchange(): lax.ppermute(sends[hop], 'group', [(g, peer_of(g, hop, groups)) for g in...  2.78 us
  transfers between devices with their start and end apart: 45, of which 16 were waited for; matrix products, arithmetic and copies ran while one was open for 1% of the time, Pallas kernels for 15%

profile of v8, /device:TPU:0, one launch (start us, length us, event | category | flops | bytes accessed | tf_op | source)
XLA Modules:
  0.0 129.3 jit_solution(1130509907459505680)
XLA Ops:
  2.2 3.0 %collective-permute-start.1 = (bf16[256,128]{1,0:T(8,128)(2,1)S(1)}, bf16[256,128]{1,0:T(8,128)(2,1)S(1)}, u32[]{:S(2)}, u32[]{:S(2)}) collective-permute-start(bf16[256,128]{1,0:T(8,128)(2,1)S(1)} %get-tuple-element.33), channel_id=1, source_target_pairs={{0,8},{8,0},{16,24},{24,16},{1,9},{9,1},{17,25},{25,17},{2,10},{10... | collective-permute-start | bytes 196616 | tf_op jit(solution)/shard_map/ppermute | solution.py:224
  5.3 1.5 %collective-permute-start.2 = (bf16[256,128]{1,0:T(8,128)(2,1)S(1)}, bf16[256,128]{1,0:T(8,128)(2,1)S(1)}, u32[]{:S(2)}, u32[]{:S(2)}) collective-permute-start(bf16[256,128]{1,0:T(8,128)(2,1)S(1)} %get-tuple-element.34), channel_id=1, source_target_pairs={{0,16},{8,24},{16,0},{24,8},{1,17},{9,25},{17,1},{25,9},{2,18},{10... | collective-permute-start | bytes 196616 | tf_op jit(solution)/shard_map/ppermute | solution.py:224
  13.7 5.2 %collective-permute-done.8.source = bf16[1024,128]{1,0:T(8,128)(2,1)S(1)} collective-permute-done((bf16[1024,128]{1,0:T(8,128)(2,1)S(1)}, bf16[1024,128]{1,0:T(8,128)(2,1)S(1)}, u32[]{:S(2)}, u32[]{:S(2)}) %collective-permute-start.8) | collective-permute-done | bytes 262176 | tf_op jit(solution)/shard_map/ppermute | solution.py:211
  26.6 1.5 %collective-permute-start.11 = (bf16[256,128]{1,0:T(8,128)(2,1)}, bf16[256,128]{1,0:T(8,128)(2,1)S(1)}, u32[]{:S(2)}, u32[]{:S(2)}) collective-permute-start(bf16[256,128]{1,0:T(8,128)(2,1)} %get-tuple-element.38), channel_id=1, source_target_pairs={{0,8},{8,0},{16,24},{24,16},{1,9},{9,1},{17,25},{25,17},{2,10},{10... | collective-permute-start | bytes 196616 | tf_op jit(solution)/shard_map/ppermute | solution.py:224
  28.1 6.8 %collective-permute-done.5.refs_1_ = bf16[1024,128]{1,0:T(8,128)(2,1)S(1)} collective-permute-done((bf16[1024,128]{1,0:T(8,128)(2,1)S(1)}, bf16[1024,128]{1,0:T(8,128)(2,1)S(1)}, u32[]{:S(2)}, u32[]{:S(2)}) %collective-permute-start.5) | collective-permute-done | bytes 262176 | tf_op jit(solution)/shard_map/ppermute | solution.py:211
  34.9 1.5 %collective-permute-start.12 = (bf16[256,128]{1,0:T(8,128)(2,1)}, bf16[256,128]{1,0:T(8,128)(2,1)}, u32[]{:S(2)}, u32[]{:S(2)}) collective-permute-start(bf16[256,128]{1,0:T(8,128)(2,1)} %get-tuple-element.39), channel_id=1, source_target_pairs={{0,16},{8,24},{16,0},{24,8},{1,17},{9,25},{17,1},{25,9},{2,18},{10... | collective-permute-start | bytes 196616 | tf_op jit(solution)/shard_map/ppermute | solution.py:224
  38.8 1.6 %copy-done.1 = bf16[1024,1024]{1,0:T(8,128)(2,1)S(1)} copy-done((bf16[1024,1024]{1,0:T(8,128)(2,1)S(1)}, bf16[1024,1024]{1,0:T(8,128)(2,1)}, u32[]{:S(2)}) %copy-start.1) | copy-done | bytes 2097176
  40.4 4.6 %shard_map.82.sheet = bf16[1024,1024]{1,0:T(8,128)(2,1)S(1)} custom-call(bf16[1024,1024]{1,0:T(8,128)(2,1)S(1)} %copy-done.1, f32[1024,1]{1,0:T(8,128)S(1)} %copy.10.column, f32[1,1024]{1,0:T(1,128)S(1)} %bitcast.9), custom_call_target="tpu_custom_call" | custom-call | tf_op jit(solution)/shard_map/pallas_call | solution.py:29
  45.1 1.8 %shard_map.87 = (bf16[1024,128]{1,0:T(8,128)(2,1)S(1)}, bf16[256,128]{1,0:T(8,128)(2,1)S(1)}, bf16[256,128]{1,0:T(8,128)(2,1)S(1)}, bf16[256,128]{1,0:T(8,128)(2,1)S(1)}, bf16[256,128]{1,0:T(8,128)(2,1)S(1)}) custom-call(s32[1,4,4]{2,1,0:T(4,128)S(1)} %copy-done.8, s32[1,4,4]{2,1,0:T(4,128)S(1)} %collective-permute-done.other, ...), custom_call_target="tpu_custom_call" | custom-call | tf_op jit(solution)/shard_map/pallas_call | solution.py:29
  47.5 1.5 %collective-permute-start.19 = (bf16[256,128]{1,0:T(8,128)(2,1)S(1)}, bf16[256,128]{1,0:T(8,128)(2,1)S(1)}, u32[]{:S(2)}, u32[]{:S(2)}) collective-permute-start(bf16[256,128]{1,0:T(8,128)(2,1)S(1)} %get-tuple-element.43), channel_id=1, source_target_pairs={{0,16},{8,24},{16,0},{24,8},{1,17},{9,25},{17,1},{25,9},{2,18},{10... | collective-permute-start | bytes 196616 | tf_op jit(solution)/shard_map/ppermute | solution.py:224
  50.4 1.6 %shard_map.89.first = bf16[1024,128]{1,0:T(8,128)(2,1)S(1)} custom-call(bf16[1024,1024]{1,0:T(8,128)(2,1)S(1)} %shard_map.83.matrix, bf16[256,128]{1,0:T(8,128)(2,1)S(1)} %get-tuple-element.37.refs_0_, bf16[256,128]{1,0:T(8,128)(2,1)S(1)} %collective-permute-done.11.refs_1_, bf16[256,128]{1,0:T(8,128)(2,1)} %collective-permute-done.12.refs_2_, ...), custom_call_target="tpu_custom_call" | custom-call | tf_op jit(solution)/shard_map/pallas_call | solution.py:29
  55.5 4.2 %collective-permute-done.22.refs_7_ = bf16[1024,128]{1,0:T(8,128)(2,1)S(1)} collective-permute-done((bf16[1024,128]{1,0:T(8,128)(2,1)S(1)}, bf16[1024,128]{1,0:T(8,128)(2,1)S(1)}, u32[]{:S(2)}, u32[]{:S(2)}) %collective-permute-start.22) | collective-permute-done | bytes 262176 | tf_op jit(solution)/shard_map/ppermute | solution.py:211
  65.0 8.6 %collective-permute-done.15.refs_1_ = bf16[1024,128]{1,0:T(8,128)(2,1)S(1)} collective-permute-done((bf16[1024,128]{1,0:T(8,128)(2,1)S(1)}, bf16[1024,128]{1,0:T(8,128)(2,1)S(1)}, u32[]{:S(2)}, u32[]{:S(2)}) %collective-permute-start.15) | collective-permute-done | bytes 262176 | tf_op jit(solution)/shard_map/ppermute | solution.py:211
  75.7 1.5 %collective-permute-start.29 = (bf16[512,128]{1,0:T(8,128)(2,1)S(1)}, bf16[512,128]{1,0:T(8,128)(2,1)S(1)}, u32[]{:S(2)}, u32[]{:S(2)}) collective-permute-start(bf16[512,128]{1,0:T(8,128)(2,1)S(1)} %get-tuple-element.50), channel_id=1, source_target_pairs={{0,16},{8,24},{16,0},{24,8},{1,17},{9,25},{17,1},{25,9},{2,18},{10... | collective-permute-start | bytes 393224 | tf_op jit(solution)/shard_map/ppermute | solution.py:224
  83.9 1.5 %collective-permute-start.23 = (bf16[1024,128]{1,0:T(8,128)(2,1)S(1)}, bf16[1024,128]{1,0:T(8,128)(2,1)S(1)}, u32[]{:S(2)}, u32[]{:S(2)}) collective-permute-start(bf16[1024,128]{1,0:T(8,128)(2,1)S(1)} %shard_map.93), channel_id=1, source_target_pairs={{0,2},{2,4},{4,6},{8,10},{10,12},{12,14},{16,18},{18,20},{20,22},{... | collective-permute-start | bytes 786440 | tf_op jit(solution)/shard_map/ppermute | solution.py:211
  85.4 6.7 %collective-permute-done.26.refs_2_ = bf16[1024,128]{1,0:T(8,128)(2,1)S(1)} collective-permute-done((bf16[1024,128]{1,0:T(8,128)(2,1)S(1)}, bf16[1024,128]{1,0:T(8,128)(2,1)S(1)}, u32[]{:S(2)}, u32[]{:S(2)}) %collective-permute-start.26) | collective-permute-done | bytes 262176 | tf_op jit(solution)/shard_map/ppermute | solution.py:211
  94.1 1.5 %collective-permute-start.36 = (bf16[256,128]{1,0:T(8,128)(2,1)S(1)}, bf16[256,128]{1,0:T(8,128)(2,1)S(1)}, u32[]{:S(2)}, u32[]{:S(2)}) collective-permute-start(bf16[256,128]{1,0:T(8,128)(2,1)S(1)} %get-tuple-element.57), channel_id=1, source_target_pairs={{0,16},{8,24},{16,0},{24,8},{1,17},{9,25},{17,1},{25,9},{2,18},{10... | collective-permute-start | bytes 196616 | tf_op jit(solution)/shard_map/ppermute | solution.py:224
  101.1 3.3 %collective-permute-start.32 = (bf16[1024,128]{1,0:T(8,128)(2,1)S(1)}, bf16[1024,128]{1,0:T(8,128)(2,1)S(1)}, u32[]{:S(2)}, u32[]{:S(2)}) collective-permute-start(bf16[1024,128]{1,0:T(8,128)(2,1)S(1)} %shard_map.97), channel_id=1, source_target_pairs={{0,2},{2,4},{4,6},{8,10},{10,12},{12,14},{16,18},{18,20},{20,22},{... | collective-permute-start | bytes 786440 | tf_op jit(solution)/shard_map/ppermute | solution.py:211
  104.5 6.6 %collective-permute-done.38.refs_9_ = bf16[1024,128]{1,0:T(8,128)(2,1)S(1)} collective-permute-done((bf16[1024,128]{1,0:T(8,128)(2,1)S(1)}, bf16[1024,128]{1,0:T(8,128)(2,1)S(1)}, u32[]{:S(2)}, u32[]{:S(2)}) %collective-permute-start.38) | collective-permute-done | bytes 262176 | tf_op jit(solution)/shard_map/ppermute | solution.py:211
  111.1 3.4 %shard_map.100.current.refs_2_ = bf16[1024,128]{1,0:T(8,128)(2,1)S(1)} custom-call(bf16[1024,1024]{1,0:T(8,128)(2,1)S(1)} %shard_map.82.sheet, f32[1024,1]{1,0:T(8,128)S(1)} %copy.10.column, bf16[4,1024,128]{2,1,0:T(8,128)(2,1)S(1)} %copy-done, bf16[1024,1024]{1,0:T(8,128)(2,1)S(1)} %shard_map.83.matrix, bf16[1024,1024]{1,0:T(8,128)(2,1)} %collective-permute-done.34.aside, ...), custom_call_target="tpu_custom_call" | custom-call | tf_op jit(solution)/shard_map/pallas_call | solution.py:29
  116.0 2.2 %collective-permute-start.42 = (bf16[1024,128]{1,0:T(8,128)(2,1)S(1)}, bf16[1024,128]{1,0:T(8,128)(2,1)S(1)}, u32[]{:S(2)}, u32[]{:S(2)}) collective-permute-start(bf16[1024,128]{1,0:T(8,128)(2,1)S(1)} %shard_map.101), channel_id=1, source_target_pairs={{2,6},{0,4},{10,14},{8,12},{18,22},{16,20},{26,30},{24,28}} | collective-permute-start | bytes 786440 | tf_op jit(solution)/shard_map/ppermute | solution.py:211
  119.9 2.9 %collective-permute-done.42.refs_6_ = bf16[1024,128]{1,0:T(8,128)(2,1)S(1)} collective-permute-done((bf16[1024,128]{1,0:T(8,128)(2,1)S(1)}, bf16[1024,128]{1,0:T(8,128)(2,1)S(1)}, u32[]{:S(2)}, u32[]{:S(2)}) %collective-permute-start.42) | collective-permute-done | bytes 262176 | tf_op jit(solution)/shard_map/ppermute | solution.py:211
  122.7 2.8 %collective-permute-done.43.refs_7_ = bf16[1024,128]{1,0:T(8,128)(2,1)S(1)} collective-permute-done((bf16[1024,128]{1,0:T(8,128)(2,1)S(1)}, bf16[1024,128]{1,0:T(8,128)(2,1)S(1)}, u32[]{:S(2)}, u32[]{:S(2)}) %collective-permute-start.43) | collective-permute-done | bytes 262176 | tf_op jit(solution)/shard_map/ppermute | solution.py:211
  126.3 2.0 %collective-permute-done.33.early_other = bf16[1024,128]{1,0:T(8,128)(2,1)S(1)} collective-permute-done((bf16[1024,128]{1,0:T(8,128)(2,1)S(1)}, bf16[1024,128]{1,0:T(8,128)(2,1)S(1)}, u32[]{:S(2)}, u32[]{:S(2)}) %collective-permute-start.33) | collective-permute-done | bytes 262176 | tf_op jit(solution)/shard_map/ppermute | solution.py:211
  (114 shorter events, 50.8 us)
Async XLA Ops:
  2.2 8.9 %collective-permute-start.1 = (bf16[256,128]{1,0:T(8,128)(2,1)S(1)}, bf16[256,128]{1,0:T(8,128)(2,1)S(1)}, u32[]{:S(2)}, u32[]{:S(2)}) collective-permute-start(bf16[256,128]{1,0:T(8,128)(2,1)S(1)} %get-tuple-element.33), channel_id=1, source_target_pairs={{0,8},{8,0},{16,24},{24,16},{1,9},{9,1},{17,25},{25,17},{2,10},{10... | collective-permute-start | bytes 196616 | tf_op jit(solution)/shard_map/ppermute | solution.py:224
  10.5 100.5 %collective-permute-start.34 = (bf16[1024,1024]{1,0:T(8,128)(2,1)S(1)}, bf16[1024,1024]{1,0:T(8,128)(2,1)}, u32[]{:S(2)}, u32[]{:S(2)}) collective-permute-start(bf16[1024,1024]{1,0:T(8,128)(2,1)S(1)} %shard_map.83.matrix), channel_id=1, source_target_pairs={{0,1},{1,0},{2,3},{3,2},{4,5},{5,4},{6,7},{7,6},{8,9},{9,8},{10,11... | collective-permute-start | bytes 6291464 | tf_op jit(solution)/shard_map/ppermute | solution.py:211
  10.6 8.2 %collective-permute-start.8 = (bf16[1024,128]{1,0:T(8,128)(2,1)S(1)}, bf16[1024,128]{1,0:T(8,128)(2,1)S(1)}, u32[]{:S(2)}, u32[]{:S(2)}) collective-permute-start(bf16[1024,128]{1,0:T(8,128)(2,1)S(1)} %bitcast.7), channel_id=1, source_target_pairs={{0,1},{1,2},{2,3},{3,4},{4,5},{5,6},{6,7},{7,0},{8,9},{9,10},{10,1... | collective-permute-start | bytes 786440 | tf_op jit(solution)/shard_map/ppermute | solution.py:211
  18.9 7.7 %collective-permute-start.9 = (bf16[1024,128]{1,0:T(8,128)(2,1)S(1)}, bf16[1024,128]{1,0:T(8,128)(2,1)S(1)}, u32[]{:S(2)}, u32[]{:S(2)}) collective-permute-start(bf16[1024,128]{1,0:T(8,128)(2,1)S(1)} %collective-permute-done.8.source), channel_id=1, source_target_pairs={{0,1},{1,2},{2,3},{3,4},{4,5},{5,6},{6,7},{7,0},{8,9},{9,10},{10,1... | collective-permute-start | bytes 786440 | tf_op jit(solution)/shard_map/ppermute | solution.py:211
  18.9 15.9 %collective-permute-start.5 = (bf16[1024,128]{1,0:T(8,128)(2,1)S(1)}, bf16[1024,128]{1,0:T(8,128)(2,1)S(1)}, u32[]{:S(2)}, u32[]{:S(2)}) collective-permute-start(bf16[1024,128]{1,0:T(8,128)(2,1)S(1)} %shard_map.86.refs_0_), channel_id=1, source_target_pairs={{2,0},{10,8},{18,16},{26,24}} | collective-permute-start | bytes 786440 | tf_op jit(solution)/shard_map/ppermute | solution.py:211
  20.2 16.2 %collective-permute-start.6 = (bf16[1024,128]{1,0:T(8,128)(2,1)S(1)}, bf16[1024,128]{1,0:T(8,128)(2,1)S(1)}, u32[]{:S(2)}, u32[]{:S(2)}) collective-permute-start(bf16[1024,128]{1,0:T(8,128)(2,1)S(1)} %shard_map.86.refs_0_), channel_id=1, source_target_pairs={{4,0},{12,8},{20,16},{28,24}} | collective-permute-start | bytes 786440 | tf_op jit(solution)/shard_map/ppermute | solution.py:211
  22.8 22.3 %collective-permute-start.7 = (bf16[1024,128]{1,0:T(8,128)(2,1)S(1)}, bf16[1024,128]{1,0:T(8,128)(2,1)}, u32[]{:S(2)}, u32[]{:S(2)}) collective-permute-start(bf16[1024,128]{1,0:T(8,128)(2,1)S(1)} %shard_map.86.refs_0_), channel_id=1, source_target_pairs={{6,0},{14,8},{22,16},{30,24}} | collective-permute-start | bytes 786440 | tf_op jit(solution)/shard_map/ppermute | solution.py:211
  26.6 20.9 %collective-permute-start.11 = (bf16[256,128]{1,0:T(8,128)(2,1)}, bf16[256,128]{1,0:T(8,128)(2,1)S(1)}, u32[]{:S(2)}, u32[]{:S(2)}) collective-permute-start(bf16[256,128]{1,0:T(8,128)(2,1)} %get-tuple-element.38), channel_id=1, source_target_pairs={{0,8},{8,0},{16,24},{24,16},{1,9},{9,1},{17,25},{25,17},{2,10},{10... | collective-permute-start | bytes 196616 | tf_op jit(solution)/shard_map/ppermute | solution.py:224
  34.9 14.1 %collective-permute-start.12 = (bf16[256,128]{1,0:T(8,128)(2,1)}, bf16[256,128]{1,0:T(8,128)(2,1)}, u32[]{:S(2)}, u32[]{:S(2)}) collective-permute-start(bf16[256,128]{1,0:T(8,128)(2,1)} %get-tuple-element.39), channel_id=1, source_target_pairs={{0,16},{8,24},{16,0},{24,8},{1,17},{9,25},{17,1},{25,9},{2,18},{10... | collective-permute-start | bytes 196616 | tf_op jit(solution)/shard_map/ppermute | solution.py:224
  37.1 13.3 %collective-permute-start.13 = (bf16[256,128]{1,0:T(8,128)(2,1)}, bf16[256,128]{1,0:T(8,128)(2,1)}, u32[]{:S(2)}, u32[]{:S(2)}) collective-permute-start(bf16[256,128]{1,0:T(8,128)(2,1)} %get-tuple-element.40), channel_id=1, source_target_pairs={{0,24},{8,16},{16,8},{24,0},{1,25},{9,17},{17,9},{25,1},{2,26},{10... | collective-permute-start | bytes 196616 | tf_op jit(solution)/shard_map/ppermute | solution.py:224
  52.6 8.4 %collective-permute-start.10 = (bf16[1024,128]{1,0:T(8,128)(2,1)S(1)}, bf16[1024,128]{1,0:T(8,128)(2,1)S(1)}, u32[]{:S(2)}, u32[]{:S(2)}) collective-permute-start(bf16[1024,128]{1,0:T(8,128)(2,1)S(1)} %get-tuple-element.36.refs_0_), channel_id=1, source_target_pairs={{0,2},{2,4},{4,6},{8,10},{10,12},{12,14},{16,18},{18,20},{20,22},{... | collective-permute-start | bytes 786440 | tf_op jit(solution)/shard_map/ppermute | solution.py:211
  55.0 8.8 %collective-permute-start.21 = (bf16[1024,128]{1,0:T(8,128)(2,1)S(1)}, bf16[1024,128]{1,0:T(8,128)(2,1)S(1)}, u32[]{:S(2)}, u32[]{:S(2)}) collective-permute-start(bf16[1024,128]{1,0:T(8,128)(2,1)S(1)} %get-tuple-element.36.refs_0_), channel_id=1, source_target_pairs={{0,1},{1,0},{2,3},{3,2},{4,5},{5,4},{6,7},{7,6},{8,9},{9,8},{10,11... | collective-permute-start | bytes 786440 | tf_op jit(solution)/shard_map/ppermute | solution.py:211
  59.7 13.9 %collective-permute-start.15 = (bf16[1024,128]{1,0:T(8,128)(2,1)S(1)}, bf16[1024,128]{1,0:T(8,128)(2,1)S(1)}, u32[]{:S(2)}, u32[]{:S(2)}) collective-permute-start(bf16[1024,128]{1,0:T(8,128)(2,1)S(1)} %shard_map.90.refs_0_), channel_id=1, source_target_pairs={{2,0},{10,8},{18,16},{26,24}} | collective-permute-start | bytes 786440 | tf_op jit(solution)/shard_map/ppermute | solution.py:211
  61.0 12.6 %collective-permute-start.16 = (bf16[1024,128]{1,0:T(8,128)(2,1)S(1)}, bf16[1024,128]{1,0:T(8,128)(2,1)S(1)}, u32[]{:S(2)}, u32[]{:S(2)}) collective-permute-start(bf16[1024,128]{1,0:T(8,128)(2,1)S(1)} %shard_map.90.refs_0_), channel_id=1, source_target_pairs={{4,0},{12,8},{20,16},{28,24}} | collective-permute-start | bytes 786440 | tf_op jit(solution)/shard_map/ppermute | solution.py:211
  62.4 11.3 %collective-permute-start.17 = (bf16[1024,128]{1,0:T(8,128)(2,1)S(1)}, bf16[1024,128]{1,0:T(8,128)(2,1)S(1)}, u32[]{:S(2)}, u32[]{:S(2)}) collective-permute-start(bf16[1024,128]{1,0:T(8,128)(2,1)S(1)} %shard_map.90.refs_0_), channel_id=1, source_target_pairs={{6,0},{14,8},{22,16},{30,24}} | collective-permute-start | bytes 786440 | tf_op jit(solution)/shard_map/ppermute | solution.py:211
  63.7 20.1 %collective-permute-start.25 = (bf16[1024,128]{1,0:T(8,128)(2,1)S(1)}, bf16[1024,128]{1,0:T(8,128)(2,1)S(1)}, u32[]{:S(2)}, u32[]{:S(2)}) collective-permute-start(bf16[1024,128]{1,0:T(8,128)(2,1)S(1)} %shard_map.94.refs_0_), channel_id=1, source_target_pairs={{2,0},{10,8},{18,16},{26,24}} | collective-permute-start | bytes 786440 | tf_op jit(solution)/shard_map/ppermute | solution.py:211
  80.1 12.0 %collective-permute-start.26 = (bf16[1024,128]{1,0:T(8,128)(2,1)S(1)}, bf16[1024,128]{1,0:T(8,128)(2,1)S(1)}, u32[]{:S(2)}, u32[]{:S(2)}) collective-permute-start(bf16[1024,128]{1,0:T(8,128)(2,1)S(1)} %shard_map.94.refs_0_), channel_id=1, source_target_pairs={{4,0},{12,8},{20,16},{28,24}} | collective-permute-start | bytes 786440 | tf_op jit(solution)/shard_map/ppermute | solution.py:211
  81.4 10.7 %collective-permute-start.27 = (bf16[1024,128]{1,0:T(8,128)(2,1)S(1)}, bf16[1024,128]{1,0:T(8,128)(2,1)S(1)}, u32[]{:S(2)}, u32[]{:S(2)}) collective-permute-start(bf16[1024,128]{1,0:T(8,128)(2,1)S(1)} %shard_map.94.refs_0_), channel_id=1, source_target_pairs={{6,0},{14,8},{22,16},{30,24}} | collective-permute-start | bytes 786440 | tf_op jit(solution)/shard_map/ppermute | solution.py:211
  83.8 8.3 %collective-permute-start.31 = (bf16[1024,128]{1,0:T(8,128)(2,1)S(1)}, bf16[1024,128]{1,0:T(8,128)(2,1)S(1)}, u32[]{:S(2)}, u32[]{:S(2)}) collective-permute-start(bf16[1024,128]{1,0:T(8,128)(2,1)S(1)} %get-tuple-element.53.first), channel_id=1, source_target_pairs={{0,1},{1,0},{2,3},{3,2},{4,5},{5,4},{6,7},{7,6},{8,9},{9,8},{10,11... | collective-permute-start | bytes 786440 | tf_op jit(solution)/shard_map/ppermute | solution.py:211
  83.9 13.3 %collective-permute-start.23 = (bf16[1024,128]{1,0:T(8,128)(2,1)S(1)}, bf16[1024,128]{1,0:T(8,128)(2,1)S(1)}, u32[]{:S(2)}, u32[]{:S(2)}) collective-permute-start(bf16[1024,128]{1,0:T(8,128)(2,1)S(1)} %shard_map.93), channel_id=1, source_target_pairs={{0,2},{2,4},{4,6},{8,10},{10,12},{12,14},{16,18},{18,20},{20,22},{... | collective-permute-start | bytes 786440 | tf_op jit(solution)/shard_map/ppermute | solution.py:211
  97.2 13.9 %collective-permute-start.38 = (bf16[1024,128]{1,0:T(8,128)(2,1)S(1)}, bf16[1024,128]{1,0:T(8,128)(2,1)S(1)}, u32[]{:S(2)}, u32[]{:S(2)}) collective-permute-start(bf16[1024,128]{1,0:T(8,128)(2,1)S(1)} %shard_map.99.refs_8_), channel_id=1, source_target_pairs={{2,0},{10,8},{18,16},{26,24}} | collective-permute-start | bytes 786440 | tf_op jit(solution)/shard_map/ppermute | solution.py:211
  98.5 12.6 %collective-permute-start.39 = (bf16[1024,128]{1,0:T(8,128)(2,1)S(1)}, bf16[1024,128]{1,0:T(8,128)(2,1)S(1)}, u32[]{:S(2)}, u32[]{:S(2)}) collective-permute-start(bf16[1024,128]{1,0:T(8,128)(2,1)S(1)} %shard_map.99.refs_8_), channel_id=1, source_target_pairs={{4,0},{12,8},{20,16},{28,24}} | collective-permute-start | bytes 786440 | tf_op jit(solution)/shard_map/ppermute | solution.py:211
  99.8 11.3 %collective-permute-start.40 = (bf16[1024,128]{1,0:T(8,128)(2,1)S(1)}, bf16[1024,128]{1,0:T(8,128)(2,1)S(1)}, u32[]{:S(2)}, u32[]{:S(2)}) collective-permute-start(bf16[1024,128]{1,0:T(8,128)(2,1)S(1)} %shard_map.99.refs_8_), channel_id=1, source_target_pairs={{6,0},{14,8},{22,16},{30,24}} | collective-permute-start | bytes 786440 | tf_op jit(solution)/shard_map/ppermute | solution.py:211
  101.1 13.4 %collective-permute-start.32 = (bf16[1024,128]{1,0:T(8,128)(2,1)S(1)}, bf16[1024,128]{1,0:T(8,128)(2,1)S(1)}, u32[]{:S(2)}, u32[]{:S(2)}) collective-permute-start(bf16[1024,128]{1,0:T(8,128)(2,1)S(1)} %shard_map.97), channel_id=1, source_target_pairs={{0,2},{2,4},{4,6},{8,10},{10,12},{12,14},{16,18},{18,20},{20,22},{... | collective-permute-start | bytes 786440 | tf_op jit(solution)/shard_map/ppermute | solution.py:211
  (32 other events, 172.8 us)

commit v9 on v8

--- a/solution.py
+++ b/solution.py
@@ -138,14 +138,14 @@
                 emit(groups, block, sends, 1, source, table)
 
 
-def carry_kernel(current, passed, carry):
+def carry_kernel(section, current, passed, carry):
     delay = lax.axis_index("delay")
 
-    @pl.when(delay == 0)
+    @pl.when(delay == section)
     def _():
         carry[...] = current[...]
 
-    @pl.when(delay != 0)
+    @pl.when(delay != section)
     def _():
         carry[...] = passed[...]
 
@@ -215,9 +215,6 @@
 
     def shift(array, by=1):
         return along(array, [(d, (d + by) % delays) for d in range(delays)])
-
-    def onward(array, by=1):
-        return along(array, [(d, d + by) for d in range(0, delays - by, by)])
 
     def exchange(sends):
         return [sends[0]] + [
@@ -272,11 +269,14 @@
         found.append(current)
         return sends
 
+    handed = []
+
     def pass_on():
-        array = found[-1]
+        handed.append(swap(found[-1]))
+        array = handed[-1]
         if slots:
-            array = call(carry_kernel, whole, (), (array, slots[-1]))
-        slots.append(onward(array, 2))
+            array = call(bind(carry_kernel, 1), whole, (), (array, slots[-1]))
+        slots.append(along(array, [(max(2 * z, 1), 2 * z + 2) for z in range(chips - 1)]))
 
     def near_of(blocks, first):
         return call(
@@ -285,11 +285,10 @@
 
     sends = stepped(0, fields, (earlier,), 1)
     blocks = exchange(sends)
-    handed = swap(found[0])
     pass_on()
     wide, narrow = near_of(blocks, 2)
     fields, _ = gathered(narrow)
-    sends = stepped(1, (*later, wide), (handed, slots[0], oldest), 2)
+    sends = stepped(1, (*later, wide), (handed[0], slots[0], oldest), 2)
     older = exchange(sends)
     pass_on()
     wide, narrow = near_of(older, 1)
@@ -303,7 +302,7 @@
             (*law, dense, aside, *blocks, *older, *later),
         )
     )
-    carry = call(carry_kernel, whole, (), (found[-1], slots[-1]))
+    carry = call(bind(carry_kernel, 0), whole, (), (found[-1], slots[-1]))
     reach = [STEPS - 1 - step for step in range(STEPS)]
     heads = [z for z in reach if z < chips]
     finals = []

time: 131 us -> 125 us (0.954)
  waiting for transfers between devices: 51.3 us -> 44.9 us
    ppermute x30 -> x32, waiting for transfers between devices: 48.5 us -> 33 us  [along(): return lax.ppermute(array, 'delay', pairs)]
    ppermute x15, waiting for transfers between devices: 2.78 us -> 11.9 us  [exchange(): lax.ppermute(sends[hop], 'group', [(g, peer_of(g, hop, groups)) for g in...]
    unnamed x23 -> x17, local copies, waits for them, and re-layouts: 6.77 us -> 6.06 us
    ppermute x30 -> x32, starting transfers between devices: 30.2 us -> 30.3 us  [along(): return lax.ppermute(array, 'delay', pairs)]
  transfers between devices with their start and end apart: 45 -> 47, of which waited for: 16 -> 19; matrix products, arithmetic and copies ran while one was open for 1% -> 1% of each run, Pallas kernels for 15% -> 16%
where the time goes in v9:
time: 125 us; the launch traced here: 124 us
  starting transfers between devices  51.1 us (41%)
  waiting for transfers between devices  44.9 us (36%)
  Pallas kernels  20.5 us (16%)
  local copies, waits for them, and re-layouts  6.29 us (5%)
    ppermute x32, waiting for transfers between devices, along(): return lax.ppermute(array, 'delay', pairs)  33 us
    ppermute x32, starting transfers between devices, along(): return lax.ppermute(array, 'delay', pairs)  30.3 us
    ppermute x15, starting transfers between devices, exchange(): lax.ppermute(sends[hop], 'group', [(g, peer_of(g, hop, groups)) for g in...  20.8 us
    pallas_call x21, Pallas kernels, call(): pl.pallas_call(kernel, out_shape=out_shape, in_specs=[SMEM] * len(scalars...  19.6 us
    ppermute x15, waiting for transfers between devices, exchange(): lax.ppermute(sends[hop], 'group', [(g, peer_of(g, hop, groups)) for g in...  11.9 us
    unnamed x17, local copies, waits for them, and re-layouts  6.06 us
  transfers between devices with their start and end apart: 47, of which 19 were waited for; matrix products, arithmetic and copies ran while one was open for 1% of the time, Pallas kernels for 16%

profile of v9, /device:TPU:0, one launch (start us, length us, event | category | flops | bytes accessed | tf_op | source)
XLA Modules:
  0.0 123.5 jit_solution(2623684548481173985)
XLA Ops:
  2.7 2.5 %collective-permute-start.1 = (bf16[256,128]{1,0:T(8,128)(2,1)S(1)}, bf16[256,128]{1,0:T(8,128)(2,1)S(1)}, u32[]{:S(2)}, u32[]{:S(2)}) collective-permute-start(bf16[256,128]{1,0:T(8,128)(2,1)S(1)} %get-tuple-element.33), channel_id=1, source_target_pairs={{0,8},{8,0},{16,24},{24,16},{1,9},{9,1},{17,25},{25,17},{2,10},{10... | collective-permute-start | bytes 196616 | tf_op jit(solution)/shard_map/ppermute | solution.py:221
  10.6 1.9 %collective-permute-done.3.refs_3_ = bf16[256,128]{1,0:T(8,128)(2,1)S(1)} collective-permute-done((bf16[256,128]{1,0:T(8,128)(2,1)S(1)}, bf16[256,128]{1,0:T(8,128)(2,1)S(1)}, u32[]{:S(2)}, u32[]{:S(2)}) %collective-permute-start.3) | collective-permute-done | bytes 65568 | tf_op jit(solution)/shard_map/ppermute | solution.py:221
  13.9 1.6 %collective-permute-start = (s32[1,4,4]{2,1,0:T(4,128)S(1)}, s32[1,4,4]{2,1,0:T(4,128)S(1)}, u32[]{:S(2)}, u32[]{:S(2)}) collective-permute-start(s32[1,4,4]{2,1,0:T(4,128)S(1)} %copy-done.5), channel_id=1, source_target_pairs={{0,1},{1,0},{2,3},{3,2},{4,5},{5,4},{6,7},{7,6},{8,9},{9,8},{10,11... | collective-permute-start | bytes 200 | tf_op jit(solution)/shard_map/ppermute | solution.py:211
  26.3 1.6 %copy-done.1 = bf16[1024,1024]{1,0:T(8,128)(2,1)S(1)} copy-done((bf16[1024,1024]{1,0:T(8,128)(2,1)S(1)}, bf16[1024,1024]{1,0:T(8,128)(2,1)}, u32[]{:S(2)}) %copy-start.1) | copy-done | bytes 2097176
  27.9 4.6 %shard_map.82.sheet = bf16[1024,1024]{1,0:T(8,128)(2,1)S(1)} custom-call(bf16[1024,1024]{1,0:T(8,128)(2,1)S(1)} %copy-done.1, f32[1024,1]{1,0:T(8,128)S(1)} %copy.10.column, f32[1,1024]{1,0:T(1,128)S(1)} %bitcast.9), custom_call_target="tpu_custom_call" | custom-call | tf_op jit(solution)/shard_map/pallas_call | solution.py:29
  32.5 2.2 %collective-permute-done.5.refs_1_ = bf16[1024,128]{1,0:T(8,128)(2,1)} collective-permute-done((bf16[1024,128]{1,0:T(8,128)(2,1)S(1)}, bf16[1024,128]{1,0:T(8,128)(2,1)}, u32[]{:S(2)}, u32[]{:S(2)}) %collective-permute-start.5) | collective-permute-done | bytes 262176 | tf_op jit(solution)/shard_map/ppermute | solution.py:211
  34.8 2.0 %shard_map.87 = (bf16[1024,128]{1,0:T(8,128)(2,1)S(1)}, bf16[256,128]{1,0:T(8,128)(2,1)S(1)}, bf16[256,128]{1,0:T(8,128)(2,1)S(1)}, bf16[256,128]{1,0:T(8,128)(2,1)S(1)}, bf16[256,128]{1,0:T(8,128)(2,1)S(1)}) custom-call(s32[1,4,4]{2,1,0:T(4,128)S(1)} %copy-done.5, s32[1,4,4]{2,1,0:T(4,128)S(1)} %collective-permute-done.other, ...), custom_call_target="tpu_custom_call" | custom-call | tf_op jit(solution)/shard_map/pallas_call | solution.py:29
  38.4 1.8 %collective-permute-start.20 = (bf16[256,128]{1,0:T(8,128)(2,1)S(1)}, bf16[256,128]{1,0:T(8,128)(2,1)S(1)}, u32[]{:S(2)}, u32[]{:S(2)}) collective-permute-start(bf16[256,128]{1,0:T(8,128)(2,1)S(1)} %get-tuple-element.43), channel_id=1, source_target_pairs={{0,16},{8,24},{16,0},{24,8},{1,17},{9,25},{17,1},{25,9},{2,18},{10... | collective-permute-start | bytes 196616 | tf_op jit(solution)/shard_map/ppermute | solution.py:221
  43.2 2.2 %collective-permute-start.21 = (bf16[256,128]{1,0:T(8,128)(2,1)S(1)}, bf16[256,128]{1,0:T(8,128)(2,1)S(1)}, u32[]{:S(2)}, u32[]{:S(2)}) collective-permute-start(bf16[256,128]{1,0:T(8,128)(2,1)S(1)} %get-tuple-element.44), channel_id=1, source_target_pairs={{0,24},{8,16},{16,8},{24,0},{1,25},{9,17},{17,9},{25,1},{2,26},{10... | collective-permute-start | bytes 196616 | tf_op jit(solution)/shard_map/ppermute | solution.py:221
  45.4 3.1 %collective-permute-done.21.refs_3_ = bf16[256,128]{1,0:T(8,128)(2,1)S(1)} collective-permute-done((bf16[256,128]{1,0:T(8,128)(2,1)S(1)}, bf16[256,128]{1,0:T(8,128)(2,1)S(1)}, u32[]{:S(2)}, u32[]{:S(2)}) %collective-permute-start.21) | collective-permute-done | bytes 65568 | tf_op jit(solution)/shard_map/ppermute | solution.py:221
  52.5 2.8 %collective-permute-start.25 = (bf16[1024,128]{1,0:T(8,128)(2,1)S(1)}, bf16[1024,128]{1,0:T(8,128)(2,1)S(1)}, u32[]{:S(2)}, u32[]{:S(2)}) collective-permute-start(bf16[1024,128]{1,0:T(8,128)(2,1)S(1)} %get-tuple-element.47.first), channel_id=1, source_target_pairs={{0,1},{1,0},{2,3},{3,2},{4,5},{5,4},{6,7},{7,6},{8,9},{9,8},{10,11... | collective-permute-start | bytes 786440 | tf_op jit(solution)/shard_map/ppermute | solution.py:211
  55.3 5.1 %collective-permute-done.17.refs_2_ = bf16[1024,128]{1,0:T(8,128)(2,1)S(1)} collective-permute-done((bf16[1024,128]{1,0:T(8,128)(2,1)S(1)}, bf16[1024,128]{1,0:T(8,128)(2,1)S(1)}, u32[]{:S(2)}, u32[]{:S(2)}) %collective-permute-start.17) | collective-permute-done | bytes 262176 | tf_op jit(solution)/shard_map/ppermute | solution.py:211
  62.7 2.0 %collective-permute-start.30 = (bf16[512,128]{1,0:T(8,128)(2,1)S(1)}, bf16[512,128]{1,0:T(8,128)(2,1)S(1)}, u32[]{:S(2)}, u32[]{:S(2)}) collective-permute-start(bf16[512,128]{1,0:T(8,128)(2,1)S(1)} %get-tuple-element.50), channel_id=1, source_target_pairs={{0,16},{8,24},{16,0},{24,8},{1,17},{9,25},{17,1},{25,9},{2,18},{10... | collective-permute-start | bytes 393224 | tf_op jit(solution)/shard_map/ppermute | solution.py:221
  65.6 2.8 %collective-permute-done.29.refs_1_.refs_5_ = bf16[512,128]{1,0:T(8,128)(2,1)S(1)} collective-permute-done((bf16[512,128]{1,0:T(8,128)(2,1)S(1)}, bf16[512,128]{1,0:T(8,128)(2,1)S(1)}, u32[]{:S(2)}, u32[]{:S(2)}) %collective-permute-start.29) | collective-permute-done | bytes 131104 | tf_op jit(solution)/shard_map/ppermute | solution.py:221
  74.0 2.6 %collective-permute-done.26.refs_1_ = bf16[1024,128]{1,0:T(8,128)(2,1)S(1)} collective-permute-done((bf16[1024,128]{1,0:T(8,128)(2,1)S(1)}, bf16[1024,128]{1,0:T(8,128)(2,1)S(1)}, u32[]{:S(2)}, u32[]{:S(2)}) %collective-permute-start.26) | collective-permute-done | bytes 262176 | tf_op jit(solution)/shard_map/ppermute | solution.py:211
  77.3 5.2 %collective-permute-done.27.refs_2_ = bf16[1024,128]{1,0:T(8,128)(2,1)S(1)} collective-permute-done((bf16[1024,128]{1,0:T(8,128)(2,1)S(1)}, bf16[1024,128]{1,0:T(8,128)(2,1)S(1)}, u32[]{:S(2)}, u32[]{:S(2)}) %collective-permute-start.27) | collective-permute-done | bytes 262176 | tf_op jit(solution)/shard_map/ppermute | solution.py:211
  84.8 2.5 %collective-permute-start.38 = (bf16[256,128]{1,0:T(8,128)(2,1)S(1)}, bf16[256,128]{1,0:T(8,128)(2,1)S(1)}, u32[]{:S(2)}, u32[]{:S(2)}) collective-permute-start(bf16[256,128]{1,0:T(8,128)(2,1)S(1)} %get-tuple-element.57), channel_id=1, source_target_pairs={{0,16},{8,24},{16,0},{24,8},{1,17},{9,25},{17,1},{25,9},{2,18},{10... | collective-permute-start | bytes 196616 | tf_op jit(solution)/shard_map/ppermute | solution.py:221
  88.6 2.5 %collective-permute-start.39 = (bf16[256,128]{1,0:T(8,128)(2,1)S(1)}, bf16[256,128]{1,0:T(8,128)(2,1)S(1)}, u32[]{:S(2)}, u32[]{:S(2)}) collective-permute-start(bf16[256,128]{1,0:T(8,128)(2,1)S(1)} %get-tuple-element.58), channel_id=1, source_target_pairs={{0,24},{8,16},{16,8},{24,0},{1,25},{9,17},{17,9},{25,1},{2,26},{10... | collective-permute-start | bytes 196616 | tf_op jit(solution)/shard_map/ppermute | solution.py:221
  96.0 9.0 %collective-permute-done.40.refs_9_ = bf16[1024,128]{1,0:T(8,128)(2,1)S(1)} collective-permute-done((bf16[1024,128]{1,0:T(8,128)(2,1)S(1)}, bf16[1024,128]{1,0:T(8,128)(2,1)S(1)}, u32[]{:S(2)}, u32[]{:S(2)}) %collective-permute-start.40) | collective-permute-done | bytes 262176 | tf_op jit(solution)/shard_map/ppermute | solution.py:211
  105.1 3.4 %shard_map.100.current.refs_2_ = bf16[1024,128]{1,0:T(8,128)(2,1)S(1)} custom-call(bf16[1024,1024]{1,0:T(8,128)(2,1)S(1)} %shard_map.82.sheet, f32[1024,1]{1,0:T(8,128)S(1)} %copy.10.column, bf16[4,1024,128]{2,1,0:T(8,128)(2,1)S(1)} %copy-done, bf16[1024,1024]{1,0:T(8,128)(2,1)S(1)} %shard_map.83.matrix, bf16[1024,1024]{1,0:T(8,128)(2,1)} %collective-permute-done.36.aside, ...), custom_call_target="tpu_custom_call" | custom-call | tf_op jit(solution)/shard_map/pallas_call | solution.py:29
  110.1 2.4 %collective-permute-start.44 = (bf16[1024,128]{1,0:T(8,128)(2,1)S(1)}, bf16[1024,128]{1,0:T(8,128)(2,1)S(1)}, u32[]{:S(2)}, u32[]{:S(2)}) collective-permute-start(bf16[1024,128]{1,0:T(8,128)(2,1)S(1)} %shard_map.101), channel_id=1, source_target_pairs={{2,6},{0,4},{10,14},{8,12},{18,22},{16,20},{26,30},{24,28}} | collective-permute-start | bytes 786440 | tf_op jit(solution)/shard_map/ppermute | solution.py:211
  113.9 2.9 %collective-permute-done.44.refs_6_ = bf16[1024,128]{1,0:T(8,128)(2,1)S(1)} collective-permute-done((bf16[1024,128]{1,0:T(8,128)(2,1)S(1)}, bf16[1024,128]{1,0:T(8,128)(2,1)S(1)}, u32[]{:S(2)}, u32[]{:S(2)}) %collective-permute-start.44) | collective-permute-done | bytes 262176 | tf_op jit(solution)/shard_map/ppermute | solution.py:211
  116.8 2.8 %collective-permute-done.45.refs_7_ = bf16[1024,128]{1,0:T(8,128)(2,1)S(1)} collective-permute-done((bf16[1024,128]{1,0:T(8,128)(2,1)S(1)}, bf16[1024,128]{1,0:T(8,128)(2,1)S(1)}, u32[]{:S(2)}, u32[]{:S(2)}) %collective-permute-start.45) | collective-permute-done | bytes 262176 | tf_op jit(solution)/shard_map/ppermute | solution.py:211
  120.3 2.0 %collective-permute-done.35.early_other = bf16[1024,128]{1,0:T(8,128)(2,1)S(1)} collective-permute-done((bf16[1024,128]{1,0:T(8,128)(2,1)S(1)}, bf16[1024,128]{1,0:T(8,128)(2,1)S(1)}, u32[]{:S(2)}, u32[]{:S(2)}) %collective-permute-start.35) | collective-permute-done | bytes 262176 | tf_op jit(solution)/shard_map/ppermute | solution.py:211
  (112 shorter events, 51.2 us)
Async XLA Ops:
  0.0 13.8 %collective-permute-start.8 = (bf16[1024,128]{1,0:T(8,128)(2,1)}, bf16[1024,128]{1,0:T(8,128)(2,1)}, u32[]{:S(2)}, u32[]{:S(2)}) collective-permute-start(bf16[1024,128]{1,0:T(8,128)(2,1)} %bitcast.6), channel_id=1, source_target_pairs={{0,1},{1,2},{2,3},{3,4},{4,5},{5,6},{6,7},{7,0},{8,9},{9,10},{10,1... | collective-permute-start | bytes 786440 | tf_op jit(solution)/shard_map/ppermute | solution.py:211
  13.4 91.7 %collective-permute-start.36 = (bf16[1024,1024]{1,0:T(8,128)(2,1)S(1)}, bf16[1024,1024]{1,0:T(8,128)(2,1)}, u32[]{:S(2)}, u32[]{:S(2)}) collective-permute-start(bf16[1024,1024]{1,0:T(8,128)(2,1)S(1)} %shard_map.83.matrix), channel_id=1, source_target_pairs={{0,1},{1,0},{2,3},{3,2},{4,5},{5,4},{6,7},{7,6},{8,9},{9,8},{10,11... | collective-permute-start | bytes 6291464 | tf_op jit(solution)/shard_map/ppermute | solution.py:211
  13.8 12.2 %collective-permute-start.9 = (bf16[1024,128]{1,0:T(8,128)(2,1)}, bf16[1024,128]{1,0:T(8,128)(2,1)S(1)}, u32[]{:S(2)}, u32[]{:S(2)}) collective-permute-start(bf16[1024,128]{1,0:T(8,128)(2,1)} %collective-permute-done.8.source), channel_id=1, source_target_pairs={{0,1},{1,2},{2,3},{3,4},{4,5},{5,6},{6,7},{7,0},{8,9},{9,10},{10,1... | collective-permute-start | bytes 786440 | tf_op jit(solution)/shard_map/ppermute | solution.py:211
  20.8 14.0 %collective-permute-start.5 = (bf16[1024,128]{1,0:T(8,128)(2,1)S(1)}, bf16[1024,128]{1,0:T(8,128)(2,1)}, u32[]{:S(2)}, u32[]{:S(2)}) collective-permute-start(bf16[1024,128]{1,0:T(8,128)(2,1)S(1)} %shard_map.86.refs_0_), channel_id=1, source_target_pairs={{2,0},{10,8},{18,16},{26,24}} | collective-permute-start | bytes 786440 | tf_op jit(solution)/shard_map/ppermute | solution.py:211
  22.3 12.5 %collective-permute-start.6 = (bf16[1024,128]{1,0:T(8,128)(2,1)S(1)}, bf16[1024,128]{1,0:T(8,128)(2,1)}, u32[]{:S(2)}, u32[]{:S(2)}) collective-permute-start(bf16[1024,128]{1,0:T(8,128)(2,1)S(1)} %shard_map.86.refs_0_), channel_id=1, source_target_pairs={{4,0},{12,8},{20,16},{28,24}} | collective-permute-start | bytes 786440 | tf_op jit(solution)/shard_map/ppermute | solution.py:211
  24.0 10.8 %collective-permute-start.7 = (bf16[1024,128]{1,0:T(8,128)(2,1)S(1)}, bf16[1024,128]{1,0:T(8,128)(2,1)}, u32[]{:S(2)}, u32[]{:S(2)}) collective-permute-start(bf16[1024,128]{1,0:T(8,128)(2,1)S(1)} %shard_map.86.refs_0_), channel_id=1, source_target_pairs={{6,0},{14,8},{22,16},{30,24}} | collective-permute-start | bytes 786440 | tf_op jit(solution)/shard_map/ppermute | solution.py:211
  26.0 12.4 %collective-permute-start.15 = (bf16[1024,128]{1,0:T(8,128)(2,1)S(1)}, bf16[1024,128]{1,0:T(8,128)(2,1)}, u32[]{:S(2)}, u32[]{:S(2)}) collective-permute-start(bf16[1024,128]{1,0:T(8,128)(2,1)S(1)} %shard_map.89.first), channel_id=1, source_target_pairs={{0,1},{1,0},{2,3},{3,2},{4,5},{5,4},{6,7},{7,6},{8,9},{9,8},{10,11... | collective-permute-start | bytes 786440 | tf_op jit(solution)/shard_map/ppermute | solution.py:211
  34.8 15.0 %collective-permute-start.22 = (bf16[1024,128]{1,0:T(8,128)(2,1)S(1)}, bf16[1024,128]{1,0:T(8,128)(2,1)S(1)}, u32[]{:S(2)}, u32[]{:S(2)}) collective-permute-start(bf16[1024,128]{1,0:T(8,128)(2,1)S(1)} %collective-permute-done.9.refs_4_), channel_id=1, source_target_pairs={{0,1},{1,2},{2,3},{3,4},{4,5},{5,6},{6,7},{7,0},{8,9},{9,10},{10,1... | collective-permute-start | bytes 786440 | tf_op jit(solution)/shard_map/ppermute | solution.py:211
  36.8 14.3 %collective-permute-start.10 = (bf16[1024,128]{1,0:T(8,128)(2,1)S(1)}, bf16[1024,128]{1,0:T(8,128)(2,1)S(1)}, u32[]{:S(2)}, u32[]{:S(2)}) collective-permute-start(bf16[1024,128]{1,0:T(8,128)(2,1)S(1)} %get-tuple-element.36.refs_0_), channel_id=1, source_target_pairs={{0,1},{1,0},{2,3},{3,2},{4,5},{5,4},{6,7},{7,6},{8,9},{9,8},{10,11... | collective-permute-start | bytes 786440 | tf_op jit(solution)/shard_map/ppermute | solution.py:211
  41.9 10.5 %collective-permute-start.16 = (bf16[1024,128]{1,0:T(8,128)(2,1)S(1)}, bf16[1024,128]{1,0:T(8,128)(2,1)S(1)}, u32[]{:S(2)}, u32[]{:S(2)}) collective-permute-start(bf16[1024,128]{1,0:T(8,128)(2,1)S(1)} %shard_map.90.refs_0_), channel_id=1, source_target_pairs={{2,0},{10,8},{18,16},{26,24}} | collective-permute-start | bytes 786440 | tf_op jit(solution)/shard_map/ppermute | solution.py:211
  48.5 12.0 %collective-permute-start.17 = (bf16[1024,128]{1,0:T(8,128)(2,1)S(1)}, bf16[1024,128]{1,0:T(8,128)(2,1)S(1)}, u32[]{:S(2)}, u32[]{:S(2)}) collective-permute-start(bf16[1024,128]{1,0:T(8,128)(2,1)S(1)} %shard_map.90.refs_0_), channel_id=1, source_target_pairs={{4,0},{12,8},{20,16},{28,24}} | collective-permute-start | bytes 786440 | tf_op jit(solution)/shard_map/ppermute | solution.py:211
  49.8 10.7 %collective-permute-start.18 = (bf16[1024,128]{1,0:T(8,128)(2,1)S(1)}, bf16[1024,128]{1,0:T(8,128)(2,1)S(1)}, u32[]{:S(2)}, u32[]{:S(2)}) collective-permute-start(bf16[1024,128]{1,0:T(8,128)(2,1)S(1)} %shard_map.90.refs_0_), channel_id=1, source_target_pairs={{6,0},{14,8},{22,16},{30,24}} | collective-permute-start | bytes 786440 | tf_op jit(solution)/shard_map/ppermute | solution.py:211
  51.1 9.4 %collective-permute-start.11 = (bf16[1024,128]{1,0:T(8,128)(2,1)S(1)}, bf16[1024,128]{1,0:T(8,128)(2,1)S(1)}, u32[]{:S(2)}, u32[]{:S(2)}) collective-permute-start(bf16[1024,128]{1,0:T(8,128)(2,1)S(1)} %collective-permute-done.10.refs_5_), channel_id=1, source_target_pairs={{1,2},{2,4},{4,6},{9,10},{10,12},{12,14},{17,18},{18,20},{20,22},{... | collective-permute-start | bytes 786440 | tf_op jit(solution)/shard_map/ppermute | solution.py:211
  52.5 12.2 %collective-permute-start.25 = (bf16[1024,128]{1,0:T(8,128)(2,1)S(1)}, bf16[1024,128]{1,0:T(8,128)(2,1)S(1)}, u32[]{:S(2)}, u32[]{:S(2)}) collective-permute-start(bf16[1024,128]{1,0:T(8,128)(2,1)S(1)} %get-tuple-element.47.first), channel_id=1, source_target_pairs={{0,1},{1,0},{2,3},{3,2},{4,5},{5,4},{6,7},{7,6},{8,9},{9,8},{10,11... | collective-permute-start | bytes 786440 | tf_op jit(solution)/shard_map/ppermute | solution.py:211
  61.9 12.0 %collective-permute-start.23 = (bf16[1024,128]{1,0:T(8,128)(2,1)S(1)}, bf16[1024,128]{1,0:T(8,128)(2,1)S(1)}, u32[]{:S(2)}, u32[]{:S(2)}) collective-permute-start(bf16[1024,128]{1,0:T(8,128)(2,1)S(1)} %get-tuple-element.46.refs_0_), channel_id=1, source_target_pairs={{0,1},{1,0},{2,3},{3,2},{4,5},{5,4},{6,7},{7,6},{8,9},{9,8},{10,11... | collective-permute-start | bytes 786440 | tf_op jit(solution)/shard_map/ppermute | solution.py:211
  70.6 12.0 %collective-permute-start.27 = (bf16[1024,128]{1,0:T(8,128)(2,1)S(1)}, bf16[1024,128]{1,0:T(8,128)(2,1)S(1)}, u32[]{:S(2)}, u32[]{:S(2)}) collective-permute-start(bf16[1024,128]{1,0:T(8,128)(2,1)S(1)} %shard_map.94.refs_0_), channel_id=1, source_target_pairs={{4,0},{12,8},{20,16},{28,24}} | collective-permute-start | bytes 786440 | tf_op jit(solution)/shard_map/ppermute | solution.py:211
  71.9 10.7 %collective-permute-start.28 = (bf16[1024,128]{1,0:T(8,128)(2,1)S(1)}, bf16[1024,128]{1,0:T(8,128)(2,1)S(1)}, u32[]{:S(2)}, u32[]{:S(2)}) collective-permute-start(bf16[1024,128]{1,0:T(8,128)(2,1)S(1)} %shard_map.94.refs_0_), channel_id=1, source_target_pairs={{6,0},{14,8},{22,16},{30,24}} | collective-permute-start | bytes 786440 | tf_op jit(solution)/shard_map/ppermute | solution.py:211
  73.9 8.6 %collective-permute-start.32 = (bf16[1024,128]{1,0:T(8,128)(2,1)S(1)}, bf16[1024,128]{1,0:T(8,128)(2,1)S(1)}, u32[]{:S(2)}, u32[]{:S(2)}) collective-permute-start(bf16[1024,128]{1,0:T(8,128)(2,1)S(1)} %get-tuple-element.53.first), channel_id=1, source_target_pairs={{0,1},{1,0},{2,3},{3,2},{4,5},{5,4},{6,7},{7,6},{8,9},{9,8},{10,11... | collective-permute-start | bytes 786440 | tf_op jit(solution)/shard_map/ppermute | solution.py:211
  76.7 15.8 %collective-permute-start.24 = (bf16[1024,128]{1,0:T(8,128)(2,1)S(1)}, bf16[1024,128]{1,0:T(8,128)(2,1)S(1)}, u32[]{:S(2)}, u32[]{:S(2)}) collective-permute-start(bf16[1024,128]{1,0:T(8,128)(2,1)S(1)} %shard_map.93), channel_id=1, source_target_pairs={{1,2},{2,4},{4,6},{9,10},{10,12},{12,14},{17,18},{18,20},{20,22},{... | collective-permute-start | bytes 786440 | tf_op jit(solution)/shard_map/ppermute | solution.py:211
  84.0 9.8 %collective-permute-start.33 = (bf16[1024,128]{1,0:T(8,128)(2,1)S(1)}, bf16[1024,128]{1,0:T(8,128)(2,1)S(1)}, u32[]{:S(2)}, u32[]{:S(2)}) collective-permute-start(bf16[1024,128]{1,0:T(8,128)(2,1)S(1)} %get-tuple-element.54.refs_1_), channel_id=1, source_target_pairs={{0,1},{1,0},{2,3},{3,2},{4,5},{5,4},{6,7},{7,6},{8,9},{9,8},{10,11... | collective-permute-start | bytes 786440 | tf_op jit(solution)/shard_map/ppermute | solution.py:211
  91.2 13.9 %collective-permute-start.40 = (bf16[1024,128]{1,0:T(8,128)(2,1)S(1)}, bf16[1024,128]{1,0:T(8,128)(2,1)S(1)}, u32[]{:S(2)}, u32[]{:S(2)}) collective-permute-start(bf16[1024,128]{1,0:T(8,128)(2,1)S(1)} %shard_map.99.refs_8_), channel_id=1, source_target_pairs={{2,0},{10,8},{18,16},{26,24}} | collective-permute-start | bytes 786440 | tf_op jit(solution)/shard_map/ppermute | solution.py:211
  92.5 12.6 %collective-permute-start.41 = (bf16[1024,128]{1,0:T(8,128)(2,1)S(1)}, bf16[1024,128]{1,0:T(8,128)(2,1)S(1)}, u32[]{:S(2)}, u32[]{:S(2)}) collective-permute-start(bf16[1024,128]{1,0:T(8,128)(2,1)S(1)} %shard_map.99.refs_8_), channel_id=1, source_target_pairs={{4,0},{12,8},{20,16},{28,24}} | collective-permute-start | bytes 786440 | tf_op jit(solution)/shard_map/ppermute | solution.py:211
  93.8 11.3 %collective-permute-start.42 = (bf16[1024,128]{1,0:T(8,128)(2,1)S(1)}, bf16[1024,128]{1,0:T(8,128)(2,1)S(1)}, u32[]{:S(2)}, u32[]{:S(2)}) collective-permute-start(bf16[1024,128]{1,0:T(8,128)(2,1)S(1)} %shard_map.99.refs_8_), channel_id=1, source_target_pairs={{6,0},{14,8},{22,16},{30,24}} | collective-permute-start | bytes 786440 | tf_op jit(solution)/shard_map/ppermute | solution.py:211
  95.3 13.2 %collective-permute-start.34 = (bf16[1024,128]{1,0:T(8,128)(2,1)S(1)}, bf16[1024,128]{1,0:T(8,128)(2,1)S(1)}, u32[]{:S(2)}, u32[]{:S(2)}) collective-permute-start(bf16[1024,128]{1,0:T(8,128)(2,1)S(1)} %shard_map.97), channel_id=1, source_target_pairs={{1,2},{2,4},{4,6},{9,10},{10,12},{12,14},{17,18},{18,20},{20,22},{... | collective-permute-start | bytes 786440 | tf_op jit(solution)/shard_map/ppermute | solution.py:211
  (31 other events, 156.9 us)

commit v10 on v9

--- a/solution.py
+++ b/solution.py
@@ -222,13 +222,22 @@
             for hop in range(1, groups)
         ]
 
-    def gathered(term, first=0):
+    def gathered(term, name, first=0):
         other = swap(term)
         chip = call(bind(plus_kernel, first), whole, (), (term, other))
-        fields = [chip]
-        for z in range(1, chips):
-            fields.append(along(chip, [(2 * z, 0)]))
-        return fields, other
+        if name == "3":
+            fields = [chip]
+            for z in range(1, chips):
+                fields.append(along(chip, [(2 * z, 0)]))
+            return fields, other
+        stride, stage = 1, 1
+        while stride < chips:
+            if stage > 1:
+                chip = call(bind(plus_kernel, 0), whole, (), (chip, came))
+            pairs = [(2 * z, 2 * (z - stride)) for z in range(stride, chips, 2 * stride)]
+            came = along(chip, pairs)
+            stride, stage = 2 * stride, stage + 1
+        return [chip, came], other
 
     earlier = shift(history[0])
     listed = jnp.clip(block_row, 0, rows // block - 1)
@@ -245,14 +254,14 @@
         bind(dense_kernel, groups, block, depth),
         shape((rows, groups * block), BF16), (listed, block_count), (weights,),
     )
-    fields, _ = gathered(term_of(blocks, 0))
+    fields, _ = gathered(term_of(blocks, 0), "0")
     sends = picked(earlier)
     blocks = exchange(sends)
     earlier = shift(earlier)
     inverse = 1.0 / sheet_diag
     column, row = inverse[:, None], inverse[None, :]
     sheet = call(sheet_kernel, shape((rows, rows), BF16), (), (self_block, column, row), 20)
-    later, _ = gathered(term_of(blocks, 1))
+    later, _ = gathered(term_of(blocks, 1), "1")
     other = swap(send_pick)
     oldest = shift(earlier)
     aside = swap(dense)
@@ -287,12 +296,12 @@
     blocks = exchange(sends)
     pass_on()
     wide, narrow = near_of(blocks, 2)
-    fields, _ = gathered(narrow)
+    fields, _ = gathered(narrow, "2")
     sends = stepped(1, (*later, wide), (handed[0], slots[0], oldest), 2)
     older = exchange(sends)
     pass_on()
     wide, narrow = near_of(older, 1)
-    later, partner = gathered(narrow, 2)
+    later, partner = gathered(narrow, "3", 2)
     sends = stepped(2, (*fields, wide, partner), (), 1)
     blocks = exchange(sends)
     pass_on()

time: 125 us -> 119 us (0.952)
  starting transfers between devices: 51.1 us -> 39 us
  waiting for transfers between devices: 44.9 us -> 50 us
    ppermute x32 -> x29, starting transfers between devices: 30.3 us -> 20.3 us  [along(): return lax.ppermute(array, 'delay', pairs)]
    ppermute x32 -> x29, waiting for transfers between devices: 33 us -> 37.1 us  [along(): return lax.ppermute(array, 'delay', pairs)]
    ppermute x15, starting transfers between devices: 20.8 us -> 18.7 us  [exchange(): lax.ppermute(sends[hop], 'group', [(g, peer_of(g, hop, groups)) for g in...]
    pallas_call x21 -> x24, Pallas kernels: 19.6 us -> 19.5 us  [call(): pl.pallas_call(kernel, out_shape=out_shape, in_specs=[SMEM] * len(scalars...]
    unnamed x17 -> x19, local copies, waits for them, and re-layouts: 6.06 us -> 6.07 us
  transfers between devices with their start and end apart: 47 -> 44, of which waited for: 19 -> 18; matrix products, arithmetic and copies ran while one was open for 1% -> 1% of each run, Pallas kernels for 16% -> 16%
where the time goes in v10:
time: 119 us; the launch traced here: 116 us
  waiting for transfers between devices  50 us (42%)
  starting transfers between devices  39 us (33%)
  Pallas kernels  20.5 us (17%)
  local copies, waits for them, and re-layouts  6.3 us (5%)
    ppermute x29, waiting for transfers between devices, along(): return lax.ppermute(array, 'delay', pairs)  37.1 us
    ppermute x29, starting transfers between devices, along(): return lax.ppermute(array, 'delay', pairs)  20.3 us
    pallas_call x24, Pallas kernels, call(): pl.pallas_call(kernel, out_shape=out_shape, in_specs=[SMEM] * len(scalars...  19.5 us
    ppermute x15, starting transfers between devices, exchange(): lax.ppermute(sends[hop], 'group', [(g, peer_of(g, hop, groups)) for g in...  18.7 us
    ppermute x15, waiting for transfers between devices, exchange(): lax.ppermute(sends[hop], 'group', [(g, peer_of(g, hop, groups)) for g in...  12.9 us
    unnamed x19, local copies, waits for them, and re-layouts  6.07 us
  transfers between devices with their start and end apart: 44, of which 18 were waited for; matrix products, arithmetic and copies ran while one was open for 1% of the time, Pallas kernels for 16%

profile of v10, /device:TPU:0, one launch (start us, length us, event | category | flops | bytes accessed | tf_op | source)
XLA Modules:
  0.0 116.3 jit_solution(10292586342523724536)
XLA Ops:
  2.2 3.0 %collective-permute-start.1 = (bf16[256,128]{1,0:T(8,128)(2,1)S(1)}, bf16[256,128]{1,0:T(8,128)(2,1)S(1)}, u32[]{:S(2)}, u32[]{:S(2)}) collective-permute-start(bf16[256,128]{1,0:T(8,128)(2,1)S(1)} %get-tuple-element.33), channel_id=1, source_target_pairs={{0,8},{8,0},{16,24},{24,16},{1,9},{9,1},{17,25},{25,17},{2,10},{10... | collective-permute-start | bytes 196616 | tf_op jit(solution)/shard_map/ppermute | solution.py:221
  5.3 1.5 %collective-permute-start.2 = (bf16[256,128]{1,0:T(8,128)(2,1)S(1)}, bf16[256,128]{1,0:T(8,128)(2,1)S(1)}, u32[]{:S(2)}, u32[]{:S(2)}) collective-permute-start(bf16[256,128]{1,0:T(8,128)(2,1)S(1)} %get-tuple-element.34), channel_id=1, source_target_pairs={{0,16},{8,24},{16,0},{24,8},{1,17},{9,25},{17,1},{25,9},{2,18},{10... | collective-permute-start | bytes 196616 | tf_op jit(solution)/shard_map/ppermute | solution.py:221
  15.6 5.4 %collective-permute-done.7.source = bf16[1024,128]{1,0:T(8,128)(2,1)} collective-permute-done((bf16[1024,128]{1,0:T(8,128)(2,1)S(1)}, bf16[1024,128]{1,0:T(8,128)(2,1)}, u32[]{:S(2)}, u32[]{:S(2)}) %collective-permute-start.7) | collective-permute-done | bytes 262176 | tf_op jit(solution)/shard_map/ppermute | solution.py:211
  22.7 1.5 %collective-permute-start.12 = (bf16[256,128]{1,0:T(8,128)(2,1)S(1)}, bf16[256,128]{1,0:T(8,128)(2,1)S(1)}, u32[]{:S(2)}, u32[]{:S(2)}) collective-permute-start(bf16[256,128]{1,0:T(8,128)(2,1)S(1)} %get-tuple-element.39), channel_id=1, source_target_pairs={{0,16},{8,24},{16,0},{24,8},{1,17},{9,25},{17,1},{25,9},{2,18},{10... | collective-permute-start | bytes 196616 | tf_op jit(solution)/shard_map/ppermute | solution.py:221
  27.7 1.7 %collective-permute-done.13.refs_3_ = bf16[256,128]{1,0:T(8,128)(2,1)S(1)} collective-permute-done((bf16[256,128]{1,0:T(8,128)(2,1)S(1)}, bf16[256,128]{1,0:T(8,128)(2,1)S(1)}, u32[]{:S(2)}, u32[]{:S(2)}) %collective-permute-start.13) | collective-permute-done | bytes 65568 | tf_op jit(solution)/shard_map/ppermute | solution.py:221
  30.9 1.6 %copy-done.1 = bf16[1024,1024]{1,0:T(8,128)(2,1)S(1)} copy-done((bf16[1024,1024]{1,0:T(8,128)(2,1)S(1)}, bf16[1024,1024]{1,0:T(8,128)(2,1)}, u32[]{:S(2)}) %copy-start.1) | copy-done | bytes 2097176
  32.5 4.6 %shard_map.82.sheet = bf16[1024,1024]{1,0:T(8,128)(2,1)S(1)} custom-call(bf16[1024,1024]{1,0:T(8,128)(2,1)S(1)} %copy-done.1, f32[1024,1]{1,0:T(8,128)S(1)} %copy.10.column, f32[1,1024]{1,0:T(1,128)S(1)} %bitcast.9), custom_call_target="tpu_custom_call" | custom-call | tf_op jit(solution)/shard_map/pallas_call | solution.py:29
  37.2 1.7 %shard_map.88 = (bf16[1024,128]{1,0:T(8,128)(2,1)S(1)}, bf16[256,128]{1,0:T(8,128)(2,1)S(1)}, bf16[256,128]{1,0:T(8,128)(2,1)S(1)}, bf16[256,128]{1,0:T(8,128)(2,1)S(1)}, bf16[256,128]{1,0:T(8,128)(2,1)S(1)}) custom-call(s32[1,4,4]{2,1,0:T(4,128)S(1)} %copy-done.6, s32[1,4,4]{2,1,0:T(4,128)S(1)} %collective-permute-done.other, ...), custom_call_target="tpu_custom_call" | custom-call | tf_op jit(solution)/shard_map/pallas_call | solution.py:29
  41.9 1.5 %collective-permute-start.18 = (bf16[256,128]{1,0:T(8,128)(2,1)S(1)}, bf16[256,128]{1,0:T(8,128)(2,1)S(1)}, u32[]{:S(2)}, u32[]{:S(2)}) collective-permute-start(bf16[256,128]{1,0:T(8,128)(2,1)S(1)} %get-tuple-element.43), channel_id=1, source_target_pairs={{0,16},{8,24},{16,0},{24,8},{1,17},{9,25},{17,1},{25,9},{2,18},{10... | collective-permute-start | bytes 196616 | tf_op jit(solution)/shard_map/ppermute | solution.py:221
  43.4 1.5 %collective-permute-start.19 = (bf16[256,128]{1,0:T(8,128)(2,1)S(1)}, bf16[256,128]{1,0:T(8,128)(2,1)S(1)}, u32[]{:S(2)}, u32[]{:S(2)}) collective-permute-start(bf16[256,128]{1,0:T(8,128)(2,1)S(1)} %get-tuple-element.44), channel_id=1, source_target_pairs={{0,24},{8,16},{16,8},{24,0},{1,25},{9,17},{17,9},{25,1},{2,26},{10... | collective-permute-start | bytes 196616 | tf_op jit(solution)/shard_map/ppermute | solution.py:221
  44.9 1.5 %collective-permute-done.18.refs_2_ = bf16[256,128]{1,0:T(8,128)(2,1)S(1)} collective-permute-done((bf16[256,128]{1,0:T(8,128)(2,1)S(1)}, bf16[256,128]{1,0:T(8,128)(2,1)S(1)}, u32[]{:S(2)}, u32[]{:S(2)}) %collective-permute-start.18) | collective-permute-done | bytes 65568 | tf_op jit(solution)/shard_map/ppermute | solution.py:221
  46.4 2.2 %collective-permute-done.19.refs_3_ = bf16[256,128]{1,0:T(8,128)(2,1)S(1)} collective-permute-done((bf16[256,128]{1,0:T(8,128)(2,1)S(1)}, bf16[256,128]{1,0:T(8,128)(2,1)S(1)}, u32[]{:S(2)}, u32[]{:S(2)}) %collective-permute-start.19) | collective-permute-done | bytes 65568 | tf_op jit(solution)/shard_map/ppermute | solution.py:221
  53.3 5.1 %collective-permute-done.20.refs_5_ = bf16[1024,128]{1,0:T(8,128)(2,1)S(1)} collective-permute-done((bf16[1024,128]{1,0:T(8,128)(2,1)S(1)}, bf16[1024,128]{1,0:T(8,128)(2,1)S(1)}, u32[]{:S(2)}, u32[]{:S(2)}) %collective-permute-start.20) | collective-permute-done | bytes 262176 | tf_op jit(solution)/shard_map/ppermute | solution.py:211
  58.4 2.8 %collective-permute-done.16.refs_1_ = bf16[1024,128]{1,0:T(8,128)(2,1)S(1)} collective-permute-done((bf16[1024,128]{1,0:T(8,128)(2,1)S(1)}, bf16[1024,128]{1,0:T(8,128)(2,1)S(1)}, u32[]{:S(2)}, u32[]{:S(2)}) %collective-permute-start.16) | collective-permute-done | bytes 262176 | tf_op jit(solution)/shard_map/ppermute | solution.py:211
  64.7 1.5 %collective-permute-start.28 = (bf16[512,128]{1,0:T(8,128)(2,1)S(1)}, bf16[512,128]{1,0:T(8,128)(2,1)S(1)}, u32[]{:S(2)}, u32[]{:S(2)}) collective-permute-start(bf16[512,128]{1,0:T(8,128)(2,1)S(1)} %get-tuple-element.51), channel_id=1, source_target_pairs={{0,24},{8,16},{16,8},{24,0},{1,25},{9,17},{17,9},{25,1},{2,26},{10... | collective-permute-start | bytes 393224 | tf_op jit(solution)/shard_map/ppermute | solution.py:221
  69.0 1.6 %collective-permute-done.28.refs_3_.refs_7_ = bf16[512,128]{1,0:T(8,128)(2,1)S(1)} collective-permute-done((bf16[512,128]{1,0:T(8,128)(2,1)S(1)}, bf16[512,128]{1,0:T(8,128)(2,1)S(1)}, u32[]{:S(2)}, u32[]{:S(2)}) %collective-permute-start.28) | collective-permute-done | bytes 131104 | tf_op jit(solution)/shard_map/ppermute | solution.py:221
  72.1 4.8 %collective-permute-done.25.refs_1_ = bf16[1024,128]{1,0:T(8,128)(2,1)S(1)} collective-permute-done((bf16[1024,128]{1,0:T(8,128)(2,1)S(1)}, bf16[1024,128]{1,0:T(8,128)(2,1)S(1)}, u32[]{:S(2)}, u32[]{:S(2)}) %collective-permute-start.25) | collective-permute-done | bytes 262176 | tf_op jit(solution)/shard_map/ppermute | solution.py:211
  80.3 2.5 %collective-permute-done.34.refs_1_ = bf16[256,128]{1,0:T(8,128)(2,1)S(1)} collective-permute-done((bf16[256,128]{1,0:T(8,128)(2,1)S(1)}, bf16[256,128]{1,0:T(8,128)(2,1)S(1)}, u32[]{:S(2)}, u32[]{:S(2)}) %collective-permute-start.34) | collective-permute-done | bytes 65568 | tf_op jit(solution)/shard_map/ppermute | solution.py:221
  89.0 9.2 %collective-permute-done.37.refs_9_ = bf16[1024,128]{1,0:T(8,128)(2,1)S(1)} collective-permute-done((bf16[1024,128]{1,0:T(8,128)(2,1)S(1)}, bf16[1024,128]{1,0:T(8,128)(2,1)S(1)}, u32[]{:S(2)}, u32[]{:S(2)}) %collective-permute-start.37) | collective-permute-done | bytes 262176 | tf_op jit(solution)/shard_map/ppermute | solution.py:211
  98.2 3.4 %shard_map.103.current.refs_2_ = bf16[1024,128]{1,0:T(8,128)(2,1)S(1)} custom-call(bf16[1024,1024]{1,0:T(8,128)(2,1)S(1)} %shard_map.82.sheet, f32[1024,1]{1,0:T(8,128)S(1)} %copy.10.column, bf16[4,1024,128]{2,1,0:T(8,128)(2,1)S(1)} %copy-done, bf16[1024,1024]{1,0:T(8,128)(2,1)S(1)} %shard_map.83.matrix, bf16[1024,1024]{1,0:T(8,128)(2,1)} %collective-permute-done.33.aside, ...), custom_call_target="tpu_custom_call" | custom-call | tf_op jit(solution)/shard_map/pallas_call | solution.py:29
  104.3 1.4 %collective-permute-start.41 = (bf16[1024,128]{1,0:T(8,128)(2,1)S(1)}, bf16[1024,128]{1,0:T(8,128)(2,1)S(1)}, u32[]{:S(2)}, u32[]{:S(2)}) collective-permute-start(bf16[1024,128]{1,0:T(8,128)(2,1)S(1)} %shard_map.104), channel_id=1, source_target_pairs={{2,6},{0,4},{10,14},{8,12},{18,22},{16,20},{26,30},{24,28}} | collective-permute-start | bytes 786440 | tf_op jit(solution)/shard_map/ppermute | solution.py:211
  106.8 2.8 %collective-permute-done.40.refs_5_ = bf16[1024,128]{1,0:T(8,128)(2,1)S(1)} collective-permute-done((bf16[1024,128]{1,0:T(8,128)(2,1)S(1)}, bf16[1024,128]{1,0:T(8,128)(2,1)S(1)}, u32[]{:S(2)}, u32[]{:S(2)}) %collective-permute-start.40) | collective-permute-done | bytes 262176 | tf_op jit(solution)/shard_map/ppermute | solution.py:211
  109.6 2.9 %collective-permute-done.41.refs_6_ = bf16[1024,128]{1,0:T(8,128)(2,1)S(1)} collective-permute-done((bf16[1024,128]{1,0:T(8,128)(2,1)S(1)}, bf16[1024,128]{1,0:T(8,128)(2,1)S(1)}, u32[]{:S(2)}, u32[]{:S(2)}) %collective-permute-start.41) | collective-permute-done | bytes 262176 | tf_op jit(solution)/shard_map/ppermute | solution.py:211
  113.2 2.0 %collective-permute-done.32.early_other = bf16[1024,128]{1,0:T(8,128)(2,1)S(1)} collective-permute-done((bf16[1024,128]{1,0:T(8,128)(2,1)S(1)}, bf16[1024,128]{1,0:T(8,128)(2,1)S(1)}, u32[]{:S(2)}, u32[]{:S(2)}) %collective-permute-start.32) | collective-permute-done | bytes 262176 | tf_op jit(solution)/shard_map/ppermute | solution.py:211
  (111 shorter events, 48.0 us)
Async XLA Ops:
  2.2 8.3 %collective-permute-start.1 = (bf16[256,128]{1,0:T(8,128)(2,1)S(1)}, bf16[256,128]{1,0:T(8,128)(2,1)S(1)}, u32[]{:S(2)}, u32[]{:S(2)}) collective-permute-start(bf16[256,128]{1,0:T(8,128)(2,1)S(1)} %get-tuple-element.33), channel_id=1, source_target_pairs={{0,8},{8,0},{16,24},{24,16},{1,9},{9,1},{17,25},{25,17},{2,10},{10... | collective-permute-start | bytes 196616 | tf_op jit(solution)/shard_map/ppermute | solution.py:221
  12.8 85.4 %collective-permute-start.33 = (bf16[1024,1024]{1,0:T(8,128)(2,1)S(1)}, bf16[1024,1024]{1,0:T(8,128)(2,1)}, u32[]{:S(2)}, u32[]{:S(2)}) collective-permute-start(bf16[1024,1024]{1,0:T(8,128)(2,1)S(1)} %shard_map.83.matrix), channel_id=1, source_target_pairs={{0,1},{1,0},{2,3},{3,2},{4,5},{5,4},{6,7},{7,6},{8,9},{9,8},{10,11... | collective-permute-start | bytes 6291464 | tf_op jit(solution)/shard_map/ppermute | solution.py:211
  13.3 7.8 %collective-permute-start.7 = (bf16[1024,128]{1,0:T(8,128)(2,1)S(1)}, bf16[1024,128]{1,0:T(8,128)(2,1)}, u32[]{:S(2)}, u32[]{:S(2)}) collective-permute-start(bf16[1024,128]{1,0:T(8,128)(2,1)S(1)} %bitcast.7), channel_id=1, source_target_pairs={{0,1},{1,2},{2,3},{3,4},{4,5},{5,6},{6,7},{7,0},{8,9},{9,10},{10,1... | collective-permute-start | bytes 786440 | tf_op jit(solution)/shard_map/ppermute | solution.py:211
  14.3 11.3 %collective-permute-start.5 = (bf16[1024,128]{1,0:T(8,128)(2,1)S(1)}, bf16[1024,128]{1,0:T(8,128)(2,1)S(1)}, u32[]{:S(2)}, u32[]{:S(2)}) collective-permute-start(bf16[1024,128]{1,0:T(8,128)(2,1)S(1)} %shard_map.86.first), channel_id=1, source_target_pairs={{2,0},{6,4},{10,8},{14,12},{18,16},{22,20},{26,24},{30,28}} | collective-permute-start | bytes 786440 | tf_op jit(solution)/shard_map/ppermute | solution.py:211
  25.6 11.5 %collective-permute-start.8 = (bf16[1024,128]{1,0:T(8,128)(2,1)}, bf16[1024,128]{1,0:T(8,128)(2,1)S(1)}, u32[]{:S(2)}, u32[]{:S(2)}) collective-permute-start(bf16[1024,128]{1,0:T(8,128)(2,1)} %collective-permute-done.7.source), channel_id=1, source_target_pairs={{0,1},{1,2},{2,3},{3,4},{4,5},{5,6},{6,7},{7,0},{8,9},{9,10},{10,1... | collective-permute-start | bytes 786440 | tf_op jit(solution)/shard_map/ppermute | solution.py:211
  26.4 10.8 %collective-permute-start.6 = (bf16[1024,128]{1,0:T(8,128)(2,1)S(1)}, bf16[1024,128]{1,0:T(8,128)(2,1)}, u32[]{:S(2)}, u32[]{:S(2)}) collective-permute-start(bf16[1024,128]{1,0:T(8,128)(2,1)S(1)} %shard_map.87.refs_0_), channel_id=1, source_target_pairs={{4,0},{12,8},{20,16},{28,24}} | collective-permute-start | bytes 786440 | tf_op jit(solution)/shard_map/ppermute | solution.py:211
  30.1 9.4 %collective-permute-start.14 = (bf16[1024,128]{1,0:T(8,128)(2,1)S(1)}, bf16[1024,128]{1,0:T(8,128)(2,1)}, u32[]{:S(2)}, u32[]{:S(2)}) collective-permute-start(bf16[1024,128]{1,0:T(8,128)(2,1)S(1)} %shard_map.90.first), channel_id=1, source_target_pairs={{0,1},{1,0},{2,3},{3,2},{4,5},{5,4},{6,7},{7,6},{8,9},{9,8},{10,11... | collective-permute-start | bytes 786440 | tf_op jit(solution)/shard_map/ppermute | solution.py:211
  30.2 7.0 %collective-permute-start = (s32[1,4,4]{2,1,0:T(4,128)S(1)}, s32[1,4,4]{2,1,0:T(4,128)S(1)}, u32[]{:S(2)}, u32[]{:S(2)}) collective-permute-start(s32[1,4,4]{2,1,0:T(4,128)S(1)} %copy-done.6), channel_id=1, source_target_pairs={{0,1},{1,0},{2,3},{3,2},{4,5},{5,4},{6,7},{7,6},{8,9},{9,8},{10,11... | collective-permute-start | bytes 200 | tf_op jit(solution)/shard_map/ppermute | solution.py:211
  40.5 9.3 %collective-permute-start.15 = (bf16[1024,128]{1,0:T(8,128)(2,1)S(1)}, bf16[1024,128]{1,0:T(8,128)(2,1)S(1)}, u32[]{:S(2)}, u32[]{:S(2)}) collective-permute-start(bf16[1024,128]{1,0:T(8,128)(2,1)S(1)} %shard_map.91.first), channel_id=1, source_target_pairs={{2,0},{6,4},{10,8},{14,12},{18,16},{22,20},{26,24},{30,28}} | collective-permute-start | bytes 786440 | tf_op jit(solution)/shard_map/ppermute | solution.py:211
  41.8 9.4 %collective-permute-start.9 = (bf16[1024,128]{1,0:T(8,128)(2,1)S(1)}, bf16[1024,128]{1,0:T(8,128)(2,1)S(1)}, u32[]{:S(2)}, u32[]{:S(2)}) collective-permute-start(bf16[1024,128]{1,0:T(8,128)(2,1)S(1)} %get-tuple-element.36.refs_0_), channel_id=1, source_target_pairs={{0,1},{1,0},{2,3},{3,2},{4,5},{5,4},{6,7},{7,6},{8,9},{9,8},{10,11... | collective-permute-start | bytes 786440 | tf_op jit(solution)/shard_map/ppermute | solution.py:211
  49.4 9.0 %collective-permute-start.20 = (bf16[1024,128]{1,0:T(8,128)(2,1)S(1)}, bf16[1024,128]{1,0:T(8,128)(2,1)S(1)}, u32[]{:S(2)}, u32[]{:S(2)}) collective-permute-start(bf16[1024,128]{1,0:T(8,128)(2,1)S(1)} %collective-permute-done.8.refs_2_), channel_id=1, source_target_pairs={{0,1},{1,2},{2,3},{3,4},{4,5},{5,6},{6,7},{7,0},{8,9},{9,10},{10,1... | collective-permute-start | bytes 786440 | tf_op jit(solution)/shard_map/ppermute | solution.py:211
  50.0 11.3 %collective-permute-start.16 = (bf16[1024,128]{1,0:T(8,128)(2,1)S(1)}, bf16[1024,128]{1,0:T(8,128)(2,1)S(1)}, u32[]{:S(2)}, u32[]{:S(2)}) collective-permute-start(bf16[1024,128]{1,0:T(8,128)(2,1)S(1)} %shard_map.92.refs_0_), channel_id=1, source_target_pairs={{4,0},{12,8},{20,16},{28,24}} | collective-permute-start | bytes 786440 | tf_op jit(solution)/shard_map/ppermute | solution.py:211
  51.3 10.0 %collective-permute-start.10 = (bf16[1024,128]{1,0:T(8,128)(2,1)S(1)}, bf16[1024,128]{1,0:T(8,128)(2,1)S(1)}, u32[]{:S(2)}, u32[]{:S(2)}) collective-permute-start(bf16[1024,128]{1,0:T(8,128)(2,1)S(1)} %collective-permute-done.9.refs_3_), channel_id=1, source_target_pairs={{1,2},{2,4},{4,6},{9,10},{10,12},{12,14},{17,18},{18,20},{20,22},{... | collective-permute-start | bytes 786440 | tf_op jit(solution)/shard_map/ppermute | solution.py:211
  52.0 14.2 %collective-permute-start.24 = (bf16[1024,128]{1,0:T(8,128)(2,1)S(1)}, bf16[1024,128]{1,0:T(8,128)(2,1)S(1)}, u32[]{:S(2)}, u32[]{:S(2)}) collective-permute-start(bf16[1024,128]{1,0:T(8,128)(2,1)S(1)} %shard_map.96.first), channel_id=1, source_target_pairs={{2,0},{6,4},{10,8},{14,12},{18,16},{22,20},{26,24},{30,28}} | collective-permute-start | bytes 786440 | tf_op jit(solution)/shard_map/ppermute | solution.py:211
  64.7 5.9 %collective-permute-start.28 = (bf16[512,128]{1,0:T(8,128)(2,1)S(1)}, bf16[512,128]{1,0:T(8,128)(2,1)S(1)}, u32[]{:S(2)}, u32[]{:S(2)}) collective-permute-start(bf16[512,128]{1,0:T(8,128)(2,1)S(1)} %get-tuple-element.51), channel_id=1, source_target_pairs={{0,24},{8,16},{16,8},{24,0},{1,25},{9,17},{17,9},{25,1},{2,26},{10... | collective-permute-start | bytes 393224 | tf_op jit(solution)/shard_map/ppermute | solution.py:221
  67.7 9.2 %collective-permute-start.25 = (bf16[1024,128]{1,0:T(8,128)(2,1)S(1)}, bf16[1024,128]{1,0:T(8,128)(2,1)S(1)}, u32[]{:S(2)}, u32[]{:S(2)}) collective-permute-start(bf16[1024,128]{1,0:T(8,128)(2,1)S(1)} %shard_map.97.refs_0_), channel_id=1, source_target_pairs={{4,0},{12,8},{20,16},{28,24}} | collective-permute-start | bytes 786440 | tf_op jit(solution)/shard_map/ppermute | solution.py:211
  71.4 14.2 %collective-permute-start.22 = (bf16[1024,128]{1,0:T(8,128)(2,1)S(1)}, bf16[1024,128]{1,0:T(8,128)(2,1)S(1)}, u32[]{:S(2)}, u32[]{:S(2)}) collective-permute-start(bf16[1024,128]{1,0:T(8,128)(2,1)S(1)} %shard_map.95), channel_id=1, source_target_pairs={{1,2},{2,4},{4,6},{9,10},{10,12},{12,14},{17,18},{18,20},{20,22},{... | collective-permute-start | bytes 786440 | tf_op jit(solution)/shard_map/ppermute | solution.py:211
  78.2 8.7 %collective-permute-start.30 = (bf16[1024,128]{1,0:T(8,128)(2,1)S(1)}, bf16[1024,128]{1,0:T(8,128)(2,1)S(1)}, u32[]{:S(2)}, u32[]{:S(2)}) collective-permute-start(bf16[1024,128]{1,0:T(8,128)(2,1)S(1)} %get-tuple-element.54.refs_1_), channel_id=1, source_target_pairs={{0,1},{1,0},{2,3},{3,2},{4,5},{5,4},{6,7},{7,6},{8,9},{9,8},{10,11... | collective-permute-start | bytes 786440 | tf_op jit(solution)/shard_map/ppermute | solution.py:211
  84.3 13.9 %collective-permute-start.37 = (bf16[1024,128]{1,0:T(8,128)(2,1)S(1)}, bf16[1024,128]{1,0:T(8,128)(2,1)S(1)}, u32[]{:S(2)}, u32[]{:S(2)}) collective-permute-start(bf16[1024,128]{1,0:T(8,128)(2,1)S(1)} %shard_map.102.refs_8_), channel_id=1, source_target_pairs={{2,0},{10,8},{18,16},{26,24}} | collective-permute-start | bytes 786440 | tf_op jit(solution)/shard_map/ppermute | solution.py:211
  85.6 12.6 %collective-permute-start.38 = (bf16[1024,128]{1,0:T(8,128)(2,1)S(1)}, bf16[1024,128]{1,0:T(8,128)(2,1)S(1)}, u32[]{:S(2)}, u32[]{:S(2)}) collective-permute-start(bf16[1024,128]{1,0:T(8,128)(2,1)S(1)} %shard_map.102.refs_8_), channel_id=1, source_target_pairs={{4,0},{12,8},{20,16},{28,24}} | collective-permute-start | bytes 786440 | tf_op jit(solution)/shard_map/ppermute | solution.py:211
  86.9 11.3 %collective-permute-start.39 = (bf16[1024,128]{1,0:T(8,128)(2,1)S(1)}, bf16[1024,128]{1,0:T(8,128)(2,1)S(1)}, u32[]{:S(2)}, u32[]{:S(2)}) collective-permute-start(bf16[1024,128]{1,0:T(8,128)(2,1)S(1)} %shard_map.102.refs_8_), channel_id=1, source_target_pairs={{6,0},{14,8},{22,16},{30,24}} | collective-permute-start | bytes 786440 | tf_op jit(solution)/shard_map/ppermute | solution.py:211
  88.3 14.7 %collective-permute-start.31 = (bf16[1024,128]{1,0:T(8,128)(2,1)S(1)}, bf16[1024,128]{1,0:T(8,128)(2,1)S(1)}, u32[]{:S(2)}, u32[]{:S(2)}) collective-permute-start(bf16[1024,128]{1,0:T(8,128)(2,1)S(1)} %shard_map.100), channel_id=1, source_target_pairs={{1,2},{2,4},{4,6},{9,10},{10,12},{12,14},{17,18},{18,20},{20,22},{... | collective-permute-start | bytes 786440 | tf_op jit(solution)/shard_map/ppermute | solution.py:211
  103.0 6.7 %collective-permute-start.40 = (bf16[1024,128]{1,0:T(8,128)(2,1)S(1)}, bf16[1024,128]{1,0:T(8,128)(2,1)S(1)}, u32[]{:S(2)}, u32[]{:S(2)}) collective-permute-start(bf16[1024,128]{1,0:T(8,128)(2,1)S(1)} %shard_map.104), channel_id=1, source_target_pairs={{4,6},{2,4},{0,2},{12,14},{10,12},{8,10},{20,22},{18,20},{16,18},{... | collective-permute-start | bytes 786440 | tf_op jit(solution)/shard_map/ppermute | solution.py:211
  104.3 8.2 %collective-permute-start.41 = (bf16[1024,128]{1,0:T(8,128)(2,1)S(1)}, bf16[1024,128]{1,0:T(8,128)(2,1)S(1)}, u32[]{:S(2)}, u32[]{:S(2)}) collective-permute-start(bf16[1024,128]{1,0:T(8,128)(2,1)S(1)} %shard_map.104), channel_id=1, source_target_pairs={{2,6},{0,4},{10,14},{8,12},{18,22},{16,20},{26,30},{24,28}} | collective-permute-start | bytes 786440 | tf_op jit(solution)/shard_map/ppermute | solution.py:211
  (29 other events, 131.6 us)

commit v11 on v9

--- a/solution.py
+++ b/solution.py
@@ -76,23 +76,27 @@
         out[part * block : (part + 1) * block, :] = source[pl.ds(start, block), :]
 
 
-def pick_kernel(groups, block, table, source, *sends):
-    emit(groups, block, sends, 0, source, table)
-
-
-def term_kernel(groups, block, first, matrix, *refs):
+def pick_kernel(groups, block, parts, table, *refs):
+    sources, sends = refs[:parts], refs[parts:]
+    for part, source in enumerate(sources):
+        emit(groups, block, sends, part, source, table)
+
+
+def term_kernel(groups, block, firsts, matrix, *refs):
     blocks, out = refs[:groups], refs[groups]
-    total = product(matrix, blocks, 0, block)
-    if first > 0:
-        total = jnp.where(lax.axis_index("delay") >= first, total, 0.0)
-    out[...] = total.astype(BF16)
-
-
-def plus_kernel(start, first, second, out):
-    total = first[...].astype(F32) + second[...].astype(F32)
-    if start > 0:
-        total = jnp.where(lax.axis_index("delay") >= start, total, 0.0)
-    out[...] = total.astype(BF16)
+    rows = matrix.shape[0]
+    for part, first in enumerate(firsts):
+        total = product(matrix, blocks, part, block)
+        if first > 0:
+            total = jnp.where(lax.axis_index("delay") >= first, total, 0.0)
+        out[part * rows : (part + 1) * rows, :] = total.astype(BF16)
+
+
+def plus_kernel(first, second, *outs):
+    rows = outs[0].shape[0]
+    for part, out in enumerate(outs):
+        here = slice(part * rows, (part + 1) * rows)
+        out[...] = (first[here, :].astype(F32) + second[here, :].astype(F32)).astype(BF16)
 
 
 def near_kernel(groups, block, first, matrix, *refs):
@@ -203,8 +207,8 @@
     rows, columns = history.shape[1:]
     shape = jax.ShapeDtypeStruct
     piece = lambda parts=1: shape((parts * block, columns), BF16)
-    whole = shape((rows, columns), BF16)
-    wide_whole = shape((rows, columns), F32)
+    many = lambda count: shape((count * rows, columns), BF16)
+    whole, wide_whole = many(1), shape((rows, columns), F32)
     bind = functools.partial
 
     def along(array, pairs):
@@ -213,8 +217,8 @@
     def swap(array):
         return along(array, [(d, d ^ 1) for d in range(delays)])
 
-    def shift(array, by=1):
-        return along(array, [(d, (d + by) % delays) for d in range(delays)])
+    def shift(array):
+        return along(array, [(d, (d + 1) % delays) for d in range(delays)])
 
     def exchange(sends):
         return [sends[0]] + [
@@ -222,87 +226,87 @@
             for hop in range(1, groups)
         ]
 
-    def gathered(term, first=0):
-        other = swap(term)
-        chip = call(bind(plus_kernel, first), whole, (), (term, other))
-        fields = [chip]
-        for z in range(1, chips):
-            fields.append(along(chip, [(2 * z, 0)]))
-        return fields, other
-
-    earlier = shift(history[0])
+    def run(kernel, out_shape, scalars, arrays, spare=2):
+        return call(kernel, out_shape, scalars, arrays, spare)
+
+    def staged(chip):
+        stride, came = 1, None
+        while stride < chips:
+            if came is not None:
+                (chip,) = run(plus_kernel, [whole], (), (chip, came))
+            pairs = [(2 * z, 2 * (z - stride)) for z in range(stride, chips, 2 * stride)]
+            came = along(chip, pairs)
+            stride *= 2
+        return [chip, came]
+
+    h1 = shift(history[0])
     listed = jnp.clip(block_row, 0, rows // block - 1)
-
-    def picked(array):
-        return call(bind(pick_kernel, groups, block), [piece()] * groups, (send_pick,), (array,))
-
-    def term_of(blocks, first):
-        return call(bind(term_kernel, groups, block, first), whole, (), (dense, *blocks))
-
-    sends = picked(history[0])
-    blocks = exchange(sends)
-    dense = call(
+    pick = lambda arrays: run(
+        bind(pick_kernel, groups, block, len(arrays)), [piece(len(arrays))] * groups, (send_pick,), arrays
+    )
+    term = lambda firsts, blocks: run(bind(term_kernel, groups, block, firsts), many(len(firsts)), (), (dense, *blocks))
+
+    blocks = exchange(pick((history[0],)))
+    dense = run(
         bind(dense_kernel, groups, block, depth),
         shape((rows, groups * block), BF16), (listed, block_count), (weights,),
     )
-    fields, _ = gathered(term_of(blocks, 0))
-    sends = picked(earlier)
-    blocks = exchange(sends)
-    earlier = shift(earlier)
+    h2 = shift(h1)
+    mine = term((0,), blocks)
+    (chip,) = run(plus_kernel, [whole], (), (mine, swap(mine)))
+    field0 = staged(chip)
+    blocks = exchange(pick((h1, h2)))
+    h3 = shift(h2)
     inverse = 1.0 / sheet_diag
     column, row = inverse[:, None], inverse[None, :]
-    sheet = call(sheet_kernel, shape((rows, rows), BF16), (), (self_block, column, row), 20)
-    later, _ = gathered(term_of(blocks, 1))
+    sheet = run(sheet_kernel, shape((rows, rows), BF16), (), (self_block, column, row), 20)
+    mine = term((1, 2), blocks)
+    chip1, chip2 = run(plus_kernel, [whole, whole], (), (mine, swap(mine)))
+    field1, field2 = staged(chip1), staged(chip2)
     other = swap(send_pick)
-    oldest = shift(earlier)
     aside = swap(dense)
 
     law = (sheet, column, incident)
-    tables = (send_pick, other)
     found, slots = [], []
 
     def stepped(step, fields, extra, parts):
-        current, *sends = call(
+        current, *sends = run(
             bind(step_kernel, groups, block, step, len(fields)),
-            [whole] + [piece(parts)] * groups, tables, (*law, *fields, *extra),
+            [whole] + [piece(parts)] * groups, (send_pick, other), (*law, *fields, *extra),
         )
         found.append(current)
         return sends
 
-    handed = []
-
     def pass_on():
-        handed.append(swap(found[-1]))
-        array = handed[-1]
+        handed = array = swap(found[-1])
         if slots:
-            array = call(bind(carry_kernel, 1), whole, (), (array, slots[-1]))
-        slots.append(along(array, [(max(2 * z, 1), 2 * z + 2) for z in range(chips - 1)]))
+            array = run(bind(carry_kernel, 1), whole, (), (array, slots[-1]))
+        pairs = [(max(2 * z, 1), 2 * z + 2) for z in range(chips - 1)]
+        slots.append(along(array, pairs))
+        return handed
 
     def near_of(blocks, first):
-        return call(
-            bind(near_kernel, groups, block, first), [wide_whole, whole], (), (dense, *blocks)
-        )
-
-    sends = stepped(0, fields, (earlier,), 1)
-    blocks = exchange(sends)
-    pass_on()
-    wide, narrow = near_of(blocks, 2)
-    fields, _ = gathered(narrow)
-    sends = stepped(1, (*later, wide), (handed[0], slots[0], oldest), 2)
-    older = exchange(sends)
+        return run(bind(near_kernel, groups, block, first), [wide_whole, whole], (), (dense, *blocks))
+
+    blocks = exchange(stepped(0, field0, (h3,), 1))
+    handed = pass_on()
+    wide, narrow = near_of(blocks, 3)
+    (chip,) = run(plus_kernel, [whole], (), (narrow, swap(narrow)))
+    field3 = staged(chip)
+    older = exchange(stepped(1, (*field1, wide), (handed, slots[0]), 2))
     pass_on()
     wide, narrow = near_of(older, 1)
-    later, partner = gathered(narrow, 2)
-    sends = stepped(2, (*fields, wide, partner), (), 1)
-    blocks = exchange(sends)
+    partner = swap(narrow)
+    second = along(narrow, [(2, 0)])
+    blocks = exchange(stepped(2, (*field2, wide, partner), (), 1))
     pass_on()
     found.append(
-        call(
+        run(
             bind(last_kernel, groups, block, 3), whole, (),
-            (*law, dense, aside, *blocks, *older, *later),
+            (*law, dense, aside, *blocks, *older, *field3, second),
         )
     )
-    carry = call(bind(carry_kernel, 0), whole, (), (found[-1], slots[-1]))
+    carry = run(bind(carry_kernel, 0), whole, (), (found[-1], slots[-1]))
     reach = [STEPS - 1 - step for step in range(STEPS)]
     heads = [z for z in reach if z < chips]
     finals = []
@@ -326,9 +330,7 @@
                 if not known:
                     sources.append(array)
                 plan[-1].append(known[0] if known else len(sources) - 1)
-        return call(
-            bind(choose_kernel, plan), shape((len(steps) * rows, columns), BF16), (), sources
-        )
+        return run(bind(choose_kernel, plan), many(len(steps)), (), sources)
 
     ready = [s for s in range(STEPS) if chips - 1 <= reach[s]] or [0]
     early = chosen(ready)
@@ -337,7 +339,7 @@
     late_other = swap(late)
     out = pl.pallas_call(
         out_kernel,
-        out_shape=shape((STEPS * rows, columns), BF16),
+        out_shape=many(STEPS),
         in_specs=[VMEM] * 4,
         out_specs=pl.BlockSpec(memory_space=pl.ANY),
         scratch_shapes=[pltpu.SemaphoreType.DMA((2,))],

time: 125 us -> 124 us (level)
  starting transfers between devices: 51.1 us -> 43.1 us
  waiting for transfers between devices: 44.9 us -> 50.7 us
    ppermute x32 -> x29, starting transfers between devices: 30.3 us -> 22.3 us  [along(): return lax.ppermute(array, 'delay', pairs)]
    ppermute x15, waiting for transfers between devices: 11.9 us -> 19.7 us  [exchange(): lax.ppermute(sends[hop], 'group', [(g, peer_of(g, hop, groups)) for g in...]
    ppermute x32 -> x29, waiting for transfers between devices: 33 us -> 31 us  [along(): return lax.ppermute(array, 'delay', pairs)]
    pallas_call x21 -> x24, Pallas kernels: 19.6 us -> 20.4 us  [call(): pl.pallas_call(kernel, out_shape=out_shape, in_specs=[SMEM] * len(scalars...]
  transfers between devices with their start and end apart: 47 -> 44, of which waited for: 19 -> 24; matrix products, arithmetic and copies ran while one was open for 1% -> 1% of each run, Pallas kernels for 16% -> 17%
where the time goes in v11:
time: 124 us; the launch traced here: 122 us
  waiting for transfers between devices  50.7 us (41%)
  starting transfers between devices  43.1 us (35%)
  Pallas kernels  21.4 us (17%)
  local copies, waits for them, and re-layouts  6.29 us (5%)
    ppermute x29, waiting for transfers between devices, along(): return lax.ppermute(array, 'delay', pairs)  31 us
    ppermute x29, starting transfers between devices, along(): return lax.ppermute(array, 'delay', pairs)  22.3 us
    ppermute x15, starting transfers between devices, exchange(): lax.ppermute(sends[hop], 'group', [(g, peer_of(g, hop, groups)) for g in...  20.7 us
    pallas_call x24, Pallas kernels, call(): pl.pallas_call(kernel, out_shape=out_shape, in_specs=[SMEM] * len(scalars...  20.4 us
    ppermute x15, waiting for transfers between devices, exchange(): lax.ppermute(sends[hop], 'group', [(g, peer_of(g, hop, groups)) for g in...  19.7 us
    unnamed x17, local copies, waits for them, and re-layouts  6.06 us
  transfers between devices with their start and end apart: 44, of which 24 were waited for; matrix products, arithmetic and copies ran while one was open for 1% of the time, Pallas kernels for 17%

profile of v11, /device:TPU:0, one launch (start us, length us, event | category | flops | bytes accessed | tf_op | source)
XLA Modules:
  0.0 122.1 jit_solution(14805752032474705576)
XLA Ops:
  2.7 2.5 %collective-permute-start.1 = (bf16[256,128]{1,0:T(8,128)(2,1)S(1)}, bf16[256,128]{1,0:T(8,128)(2,1)S(1)}, u32[]{:S(2)}, u32[]{:S(2)}) collective-permute-start(bf16[256,128]{1,0:T(8,128)(2,1)S(1)} %get-tuple-element.35), channel_id=1, source_target_pairs={{0,8},{8,0},{16,24},{24,16},{1,9},{9,1},{17,25},{25,17},{2,10},{10... | collective-permute-start | bytes 196616 | tf_op jit(solution)/shard_map/ppermute | solution.py:225
  13.5 3.0 %collective-permute-done.8.refs_1_ = bf16[1024,128]{1,0:T(8,128)(2,1)} collective-permute-done((bf16[1024,128]{1,0:T(8,128)(2,1)S(1)}, bf16[1024,128]{1,0:T(8,128)(2,1)}, u32[]{:S(2)}, u32[]{:S(2)}) %collective-permute-start.8) | collective-permute-done | bytes 262176 | tf_op jit(solution)/shard_map/ppermute | solution.py:215
  17.5 2.1 %collective-permute-start.12 = (bf16[512,128]{1,0:T(8,128)(2,1)S(1)}, bf16[512,128]{1,0:T(8,128)(2,1)S(1)}, u32[]{:S(2)}, u32[]{:S(2)}) collective-permute-start(bf16[512,128]{1,0:T(8,128)(2,1)S(1)} %get-tuple-element.40), channel_id=1, source_target_pairs={{0,8},{8,0},{16,24},{24,16},{1,9},{9,1},{17,25},{25,17},{2,10},{10... | collective-permute-start | bytes 393224 | tf_op jit(solution)/shard_map/ppermute | solution.py:225
  22.5 2.0 %collective-permute-done.13.refs_2_ = bf16[512,128]{1,0:T(8,128)(2,1)S(1)} collective-permute-done((bf16[512,128]{1,0:T(8,128)(2,1)S(1)}, bf16[512,128]{1,0:T(8,128)(2,1)S(1)}, u32[]{:S(2)}, u32[]{:S(2)}) %collective-permute-start.13) | collective-permute-done | bytes 131104 | tf_op jit(solution)/shard_map/ppermute | solution.py:225
  24.5 2.4 %collective-permute-done.14.refs_3_ = bf16[512,128]{1,0:T(8,128)(2,1)S(1)} collective-permute-done((bf16[512,128]{1,0:T(8,128)(2,1)S(1)}, bf16[512,128]{1,0:T(8,128)(2,1)S(1)}, u32[]{:S(2)}, u32[]{:S(2)}) %collective-permute-start.14) | collective-permute-done | bytes 131104 | tf_op jit(solution)/shard_map/ppermute | solution.py:225
  32.8 4.6 %shard_map.82.sheet = bf16[1024,1024]{1,0:T(8,128)(2,1)S(1)} custom-call(bf16[1024,1024]{1,0:T(8,128)(2,1)S(1)} %copy-done.1, f32[1024,1]{1,0:T(8,128)S(1)} %copy.10.column, f32[1,1024]{1,0:T(1,128)S(1)} %bitcast.9), custom_call_target="tpu_custom_call" | custom-call | tf_op jit(solution)/shard_map/pallas_call | solution.py:29
  39.1 1.8 %shard_map.88 = (bf16[1024,128]{1,0:T(8,128)(2,1)S(1)}, bf16[256,128]{1,0:T(8,128)(2,1)S(1)}, bf16[256,128]{1,0:T(8,128)(2,1)S(1)}, bf16[256,128]{1,0:T(8,128)(2,1)S(1)}, bf16[256,128]{1,0:T(8,128)(2,1)S(1)}) custom-call(s32[1,4,4]{2,1,0:T(4,128)S(1)} %copy-done.5, s32[1,4,4]{2,1,0:T(4,128)S(1)} %collective-permute-done.other, ...), custom_call_target="tpu_custom_call" | custom-call | tf_op jit(solution)/shard_map/pallas_call | solution.py:29
  44.1 6.3 %collective-permute-done.16.second = bf16[1024,128]{1,0:T(8,128)(2,1)S(1)} collective-permute-done((bf16[1024,128]{1,0:T(8,128)(2,1)S(1)}, bf16[1024,128]{1,0:T(8,128)(2,1)S(1)}, u32[]{:S(2)}, u32[]{:S(2)}) %collective-permute-start.16) | collective-permute-done | bytes 262176 | tf_op jit(solution)/shard_map/ppermute | solution.py:215
  51.8 1.8 %collective-permute-start.18 = (bf16[256,128]{1,0:T(8,128)(2,1)S(1)}, bf16[256,128]{1,0:T(8,128)(2,1)S(1)}, u32[]{:S(2)}, u32[]{:S(2)}) collective-permute-start(bf16[256,128]{1,0:T(8,128)(2,1)S(1)} %get-tuple-element.45), channel_id=1, source_target_pairs={{0,8},{8,0},{16,24},{24,16},{1,9},{9,1},{17,25},{25,17},{2,10},{10... | collective-permute-start | bytes 196616 | tf_op jit(solution)/shard_map/ppermute | solution.py:225
  56.1 1.7 %collective-permute-start.19 = (bf16[256,128]{1,0:T(8,128)(2,1)S(1)}, bf16[256,128]{1,0:T(8,128)(2,1)S(1)}, u32[]{:S(2)}, u32[]{:S(2)}) collective-permute-start(bf16[256,128]{1,0:T(8,128)(2,1)S(1)} %get-tuple-element.46), channel_id=1, source_target_pairs={{0,16},{8,24},{16,0},{24,8},{1,17},{9,25},{17,1},{25,9},{2,18},{10... | collective-permute-start | bytes 196616 | tf_op jit(solution)/shard_map/ppermute | solution.py:225
  57.8 2.5 %collective-permute-done.19.refs_2_ = bf16[256,128]{1,0:T(8,128)(2,1)S(1)} collective-permute-done((bf16[256,128]{1,0:T(8,128)(2,1)S(1)}, bf16[256,128]{1,0:T(8,128)(2,1)S(1)}, u32[]{:S(2)}, u32[]{:S(2)}) %collective-permute-start.19) | collective-permute-done | bytes 65568 | tf_op jit(solution)/shard_map/ppermute | solution.py:225
  60.4 2.6 %collective-permute-start.20 = (bf16[256,128]{1,0:T(8,128)(2,1)S(1)}, bf16[256,128]{1,0:T(8,128)(2,1)S(1)}, u32[]{:S(2)}, u32[]{:S(2)}) collective-permute-start(bf16[256,128]{1,0:T(8,128)(2,1)S(1)} %get-tuple-element.47), channel_id=1, source_target_pairs={{0,24},{8,16},{16,8},{24,0},{1,25},{9,17},{17,9},{25,1},{2,26},{10... | collective-permute-start | bytes 196616 | tf_op jit(solution)/shard_map/ppermute | solution.py:225
  63.0 2.6 %collective-permute-done.20.refs_3_ = bf16[256,128]{1,0:T(8,128)(2,1)S(1)} collective-permute-done((bf16[256,128]{1,0:T(8,128)(2,1)S(1)}, bf16[256,128]{1,0:T(8,128)(2,1)S(1)}, u32[]{:S(2)}, u32[]{:S(2)}) %collective-permute-start.20) | collective-permute-done | bytes 65568 | tf_op jit(solution)/shard_map/ppermute | solution.py:225
  67.7 2.0 %collective-permute-start.25 = (bf16[512,128]{1,0:T(8,128)(2,1)S(1)}, bf16[512,128]{1,0:T(8,128)(2,1)S(1)}, u32[]{:S(2)}, u32[]{:S(2)}) collective-permute-start(bf16[512,128]{1,0:T(8,128)(2,1)S(1)} %get-tuple-element.52), channel_id=1, source_target_pairs={{0,8},{8,0},{16,24},{24,16},{1,9},{9,1},{17,25},{25,17},{2,10},{10... | collective-permute-start | bytes 393224 | tf_op jit(solution)/shard_map/ppermute | solution.py:225
  69.7 2.0 %collective-permute-start.26 = (bf16[512,128]{1,0:T(8,128)(2,1)S(1)}, bf16[512,128]{1,0:T(8,128)(2,1)S(1)}, u32[]{:S(2)}, u32[]{:S(2)}) collective-permute-start(bf16[512,128]{1,0:T(8,128)(2,1)S(1)} %get-tuple-element.53), channel_id=1, source_target_pairs={{0,16},{8,24},{16,0},{24,8},{1,17},{9,25},{17,1},{25,9},{2,18},{10... | collective-permute-start | bytes 393224 | tf_op jit(solution)/shard_map/ppermute | solution.py:225
  75.6 1.9 %collective-permute-done.27.refs_3_.refs_7_ = bf16[512,128]{1,0:T(8,128)(2,1)S(1)} collective-permute-done((bf16[512,128]{1,0:T(8,128)(2,1)S(1)}, bf16[512,128]{1,0:T(8,128)(2,1)S(1)}, u32[]{:S(2)}, u32[]{:S(2)}) %collective-permute-start.27) | collective-permute-done | bytes 131104 | tf_op jit(solution)/shard_map/ppermute | solution.py:225
  83.5 2.4 %collective-permute-start.29 = (bf16[1024,128]{1,0:T(8,128)(2,1)S(1)}, bf16[1024,128]{1,0:T(8,128)(2,1)S(1)}, u32[]{:S(2)}, u32[]{:S(2)}) collective-permute-start(bf16[1024,128]{1,0:T(8,128)(2,1)S(1)} %get-tuple-element.57.refs_1_), channel_id=1, source_target_pairs={{0,1},{1,0},{2,3},{3,2},{4,5},{5,4},{6,7},{7,6},{8,9},{9,8},{10,11... | collective-permute-start | bytes 786440 | tf_op jit(solution)/shard_map/ppermute | solution.py:215
  90.9 5.1 %collective-permute-done.38.refs_9_ = bf16[1024,128]{1,0:T(8,128)(2,1)S(1)} collective-permute-done((bf16[1024,128]{1,0:T(8,128)(2,1)S(1)}, bf16[1024,128]{1,0:T(8,128)(2,1)S(1)}, u32[]{:S(2)}, u32[]{:S(2)}) %collective-permute-start.38) | collective-permute-done | bytes 262176 | tf_op jit(solution)/shard_map/ppermute | solution.py:215
  97.0 1.7 %collective-permute-done.39.refs_10_ = bf16[1024,128]{1,0:T(8,128)(2,1)S(1)} collective-permute-done((bf16[1024,128]{1,0:T(8,128)(2,1)S(1)}, bf16[1024,128]{1,0:T(8,128)(2,1)S(1)}, u32[]{:S(2)}, u32[]{:S(2)}) %collective-permute-start.39) | collective-permute-done | bytes 262176 | tf_op jit(solution)/shard_map/ppermute | solution.py:215
  100.6 3.3 %collective-permute-done.35.refs_3_ = bf16[256,128]{1,0:T(8,128)(2,1)S(1)} collective-permute-done((bf16[256,128]{1,0:T(8,128)(2,1)S(1)}, bf16[256,128]{1,0:T(8,128)(2,1)S(1)}, u32[]{:S(2)}, u32[]{:S(2)}) %collective-permute-start.35) | collective-permute-done | bytes 65568 | tf_op jit(solution)/shard_map/ppermute | solution.py:225
  103.9 3.4 %shard_map.103.current.refs_2_ = bf16[1024,128]{1,0:T(8,128)(2,1)S(1)} custom-call(bf16[1024,1024]{1,0:T(8,128)(2,1)S(1)} %shard_map.82.sheet, f32[1024,1]{1,0:T(8,128)S(1)} %copy.10.column, bf16[4,1024,128]{2,1,0:T(8,128)(2,1)S(1)} %copy-done, bf16[1024,1024]{1,0:T(8,128)(2,1)S(1)} %shard_map.83.matrix, bf16[1024,1024]{1,0:T(8,128)(2,1)} %collective-permute-done.32.aside, ...), custom_call_target="tpu_custom_call" | custom-call | tf_op jit(solution)/shard_map/pallas_call | solution.py:29
  112.5 2.8 %collective-permute-done.40.refs_5_ = bf16[1024,128]{1,0:T(8,128)(2,1)S(1)} collective-permute-done((bf16[1024,128]{1,0:T(8,128)(2,1)S(1)}, bf16[1024,128]{1,0:T(8,128)(2,1)S(1)}, u32[]{:S(2)}, u32[]{:S(2)}) %collective-permute-start.40) | collective-permute-done | bytes 262176 | tf_op jit(solution)/shard_map/ppermute | solution.py:215
  115.3 2.9 %collective-permute-done.41.refs_6_ = bf16[1024,128]{1,0:T(8,128)(2,1)S(1)} collective-permute-done((bf16[1024,128]{1,0:T(8,128)(2,1)S(1)}, bf16[1024,128]{1,0:T(8,128)(2,1)S(1)}, u32[]{:S(2)}, u32[]{:S(2)}) %collective-permute-start.41) | collective-permute-done | bytes 262176 | tf_op jit(solution)/shard_map/ppermute | solution.py:215
  118.9 2.0 %collective-permute-done.31.early_other = bf16[1024,128]{1,0:T(8,128)(2,1)S(1)} collective-permute-done((bf16[1024,128]{1,0:T(8,128)(2,1)S(1)}, bf16[1024,128]{1,0:T(8,128)(2,1)S(1)}, u32[]{:S(2)}, u32[]{:S(2)}) %collective-permute-start.31) | collective-permute-done | bytes 262176 | tf_op jit(solution)/shard_map/ppermute | solution.py:215
  (109 shorter events, 56.0 us)
Async XLA Ops:
  0.0 8.8 %collective-permute-start.7 = (bf16[1024,128]{1,0:T(8,128)(2,1)}, bf16[1024,128]{1,0:T(8,128)(2,1)S(1)}, u32[]{:S(2)}, u32[]{:S(2)}) collective-permute-start(bf16[1024,128]{1,0:T(8,128)(2,1)} %bitcast.6), channel_id=1, source_target_pairs={{0,1},{1,2},{2,3},{3,4},{4,5},{5,6},{6,7},{7,0},{8,9},{9,10},{10,1... | collective-permute-start | bytes 786440 | tf_op jit(solution)/shard_map/ppermute | solution.py:215
  2.7 9.1 %collective-permute-start.1 = (bf16[256,128]{1,0:T(8,128)(2,1)S(1)}, bf16[256,128]{1,0:T(8,128)(2,1)S(1)}, u32[]{:S(2)}, u32[]{:S(2)}) collective-permute-start(bf16[256,128]{1,0:T(8,128)(2,1)S(1)} %get-tuple-element.35), channel_id=1, source_target_pairs={{0,8},{8,0},{16,24},{24,16},{1,9},{9,1},{17,25},{25,17},{2,10},{10... | collective-permute-start | bytes 196616 | tf_op jit(solution)/shard_map/ppermute | solution.py:225
  5.3 6.6 %collective-permute-start.2 = (bf16[256,128]{1,0:T(8,128)(2,1)S(1)}, bf16[256,128]{1,0:T(8,128)(2,1)S(1)}, u32[]{:S(2)}, u32[]{:S(2)}) collective-permute-start(bf16[256,128]{1,0:T(8,128)(2,1)S(1)} %get-tuple-element.36), channel_id=1, source_target_pairs={{0,16},{8,24},{16,0},{24,8},{1,17},{9,25},{17,1},{25,9},{2,18},{10... | collective-permute-start | bytes 196616 | tf_op jit(solution)/shard_map/ppermute | solution.py:225
  8.8 7.7 %collective-permute-start.8 = (bf16[1024,128]{1,0:T(8,128)(2,1)S(1)}, bf16[1024,128]{1,0:T(8,128)(2,1)}, u32[]{:S(2)}, u32[]{:S(2)}) collective-permute-start(bf16[1024,128]{1,0:T(8,128)(2,1)S(1)} %collective-permute-done.7.refs_0_), channel_id=1, source_target_pairs={{0,1},{1,2},{2,3},{3,4},{4,5},{5,6},{6,7},{7,0},{8,9},{9,10},{10,1... | collective-permute-start | bytes 786440 | tf_op jit(solution)/shard_map/ppermute | solution.py:215
  13.2 7.9 %collective-permute-start.4 = (bf16[1024,128]{1,0:T(8,128)(2,1)S(1)}, bf16[1024,128]{1,0:T(8,128)(2,1)S(1)}, u32[]{:S(2)}, u32[]{:S(2)}) collective-permute-start(bf16[1024,128]{1,0:T(8,128)(2,1)S(1)} %shard_map.85.first), channel_id=1, source_target_pairs={{0,1},{1,0},{2,3},{3,2},{4,5},{5,4},{6,7},{7,6},{8,9},{9,8},{10,11... | collective-permute-start | bytes 786440 | tf_op jit(solution)/shard_map/ppermute | solution.py:215
  21.1 79.0 %collective-permute-start.32 = (bf16[1024,1024]{1,0:T(8,128)(2,1)S(1)}, bf16[1024,1024]{1,0:T(8,128)(2,1)}, u32[]{:S(2)}, u32[]{:S(2)}) collective-permute-start(bf16[1024,1024]{1,0:T(8,128)(2,1)S(1)} %shard_map.83.matrix), channel_id=1, source_target_pairs={{0,1},{1,0},{2,3},{3,2},{4,5},{5,4},{6,7},{7,6},{8,9},{9,8},{10,11... | collective-permute-start | bytes 6291464 | tf_op jit(solution)/shard_map/ppermute | solution.py:215
  21.2 8.3 %collective-permute-start.5 = (bf16[1024,128]{1,0:T(8,128)(2,1)S(1)}, bf16[1024,128]{1,0:T(8,128)(2,1)S(1)}, u32[]{:S(2)}, u32[]{:S(2)}) collective-permute-start(bf16[1024,128]{1,0:T(8,128)(2,1)S(1)} %shard_map.86.first), channel_id=1, source_target_pairs={{2,0},{6,4},{10,8},{14,12},{18,16},{22,20},{26,24},{30,28}} | collective-permute-start | bytes 786440 | tf_op jit(solution)/shard_map/ppermute | solution.py:215
  28.2 12.8 %collective-permute-start.15 = (bf16[2048,128]{1,0:T(8,128)(2,1)S(1)}, bf16[2048,128]{1,0:T(8,128)(2,1)}, u32[]{:S(2)}, u32[]{:S(2)}) collective-permute-start(bf16[2048,128]{1,0:T(8,128)(2,1)S(1)} %shard_map.90.first), channel_id=1, source_target_pairs={{0,1},{1,0},{2,3},{3,2},{4,5},{5,4},{6,7},{7,6},{8,9},{9,8},{10,11... | collective-permute-start | bytes 1572872 | tf_op jit(solution)/shard_map/ppermute | solution.py:215
  28.3 9.1 %collective-permute-start.9 = (bf16[1024,128]{1,0:T(8,128)(2,1)}, bf16[1024,128]{1,0:T(8,128)(2,1)}, u32[]{:S(2)}, u32[]{:S(2)}) collective-permute-start(bf16[1024,128]{1,0:T(8,128)(2,1)} %collective-permute-done.8.refs_1_), channel_id=1, source_target_pairs={{0,1},{1,2},{2,3},{3,4},{4,5},{5,6},{6,7},{7,0},{8,9},{9,10},{10,1... | collective-permute-start | bytes 786440 | tf_op jit(solution)/shard_map/ppermute | solution.py:215
  29.5 9.5 %collective-permute-start.6 = (bf16[1024,128]{1,0:T(8,128)(2,1)S(1)}, bf16[1024,128]{1,0:T(8,128)(2,1)}, u32[]{:S(2)}, u32[]{:S(2)}) collective-permute-start(bf16[1024,128]{1,0:T(8,128)(2,1)S(1)} %shard_map.87.refs_0_), channel_id=1, source_target_pairs={{4,0},{12,8},{20,16},{28,24}} | collective-permute-start | bytes 786440 | tf_op jit(solution)/shard_map/ppermute | solution.py:215
  42.1 8.3 %collective-permute-start.16 = (bf16[1024,128]{1,0:T(8,128)(2,1)S(1)}, bf16[1024,128]{1,0:T(8,128)(2,1)S(1)}, u32[]{:S(2)}, u32[]{:S(2)}) collective-permute-start(bf16[1024,128]{1,0:T(8,128)(2,1)S(1)} %get-tuple-element.43.first), channel_id=1, source_target_pairs={{2,0},{6,4},{10,8},{14,12},{18,16},{22,20},{26,24},{30,28}} | collective-permute-start | bytes 786440 | tf_op jit(solution)/shard_map/ppermute | solution.py:215
  43.4 22.9 %collective-permute-start.11 = (bf16[1024,128]{1,0:T(8,128)(2,1)S(1)}, bf16[1024,128]{1,0:T(8,128)(2,1)S(1)}, u32[]{:S(2)}, u32[]{:S(2)}) collective-permute-start(bf16[1024,128]{1,0:T(8,128)(2,1)S(1)} %collective-permute-done.10.refs_3_), channel_id=1, source_target_pairs={{1,2},{2,4},{4,6},{9,10},{10,12},{12,14},{17,18},{18,20},{20,22},{... | collective-permute-start | bytes 786440 | tf_op jit(solution)/shard_map/ppermute | solution.py:215
  50.5 15.8 %collective-permute-start.17 = (bf16[1024,128]{1,0:T(8,128)(2,1)S(1)}, bf16[1024,128]{1,0:T(8,128)(2,1)S(1)}, u32[]{:S(2)}, u32[]{:S(2)}) collective-permute-start(bf16[1024,128]{1,0:T(8,128)(2,1)S(1)} %shard_map.92.refs_0_), channel_id=1, source_target_pairs={{4,0},{12,8},{20,16},{28,24}} | collective-permute-start | bytes 786440 | tf_op jit(solution)/shard_map/ppermute | solution.py:215
  53.5 18.1 %collective-permute-start.23 = (bf16[1024,128]{1,0:T(8,128)(2,1)S(1)}, bf16[1024,128]{1,0:T(8,128)(2,1)S(1)}, u32[]{:S(2)}, u32[]{:S(2)}) collective-permute-start(bf16[1024,128]{1,0:T(8,128)(2,1)S(1)} %get-tuple-element.50.first), channel_id=1, source_target_pairs={{2,0},{6,4},{10,8},{14,12},{18,16},{22,20},{26,24},{30,28}} | collective-permute-start | bytes 786440 | tf_op jit(solution)/shard_map/ppermute | solution.py:215
  71.7 6.7 %collective-permute-start.36 = (bf16[1024,128]{1,0:T(8,128)(2,1)S(1)}, bf16[1024,128]{1,0:T(8,128)(2,1)S(1)}, u32[]{:S(2)}, u32[]{:S(2)}) collective-permute-start(bf16[1024,128]{1,0:T(8,128)(2,1)S(1)} %get-tuple-element.62.first), channel_id=1, source_target_pairs={{0,1},{1,0},{2,3},{3,2},{4,5},{5,4},{6,7},{7,6},{8,9},{9,8},{10,11... | collective-permute-start | bytes 786440 | tf_op jit(solution)/shard_map/ppermute | solution.py:215
  72.8 9.3 %collective-permute-start.24 = (bf16[1024,128]{1,0:T(8,128)(2,1)S(1)}, bf16[1024,128]{1,0:T(8,128)(2,1)S(1)}, u32[]{:S(2)}, u32[]{:S(2)}) collective-permute-start(bf16[1024,128]{1,0:T(8,128)(2,1)S(1)} %shard_map.96.refs_0_), channel_id=1, source_target_pairs={{4,0},{12,8},{20,16},{28,24}} | collective-permute-start | bytes 786440 | tf_op jit(solution)/shard_map/ppermute | solution.py:215
  78.4 8.3 %collective-permute-start.37 = (bf16[1024,128]{1,0:T(8,128)(2,1)S(1)}, bf16[1024,128]{1,0:T(8,128)(2,1)S(1)}, u32[]{:S(2)}, u32[]{:S(2)}) collective-permute-start(bf16[1024,128]{1,0:T(8,128)(2,1)S(1)} %shard_map.101.first), channel_id=1, source_target_pairs={{2,0},{6,4},{10,8},{14,12},{18,16},{22,20},{26,24},{30,28}} | collective-permute-start | bytes 786440 | tf_op jit(solution)/shard_map/ppermute | solution.py:215
  79.7 9.6 %collective-permute-start.22 = (bf16[1024,128]{1,0:T(8,128)(2,1)S(1)}, bf16[1024,128]{1,0:T(8,128)(2,1)S(1)}, u32[]{:S(2)}, u32[]{:S(2)}) collective-permute-start(bf16[1024,128]{1,0:T(8,128)(2,1)S(1)} %shard_map.95), channel_id=1, source_target_pairs={{1,2},{2,4},{4,6},{9,10},{10,12},{12,14},{17,18},{18,20},{20,22},{... | collective-permute-start | bytes 786440 | tf_op jit(solution)/shard_map/ppermute | solution.py:215
  86.7 9.3 %collective-permute-start.38 = (bf16[1024,128]{1,0:T(8,128)(2,1)S(1)}, bf16[1024,128]{1,0:T(8,128)(2,1)S(1)}, u32[]{:S(2)}, u32[]{:S(2)}) collective-permute-start(bf16[1024,128]{1,0:T(8,128)(2,1)S(1)} %shard_map.102.refs_8_), channel_id=1, source_target_pairs={{4,0},{12,8},{20,16},{28,24}} | collective-permute-start | bytes 786440 | tf_op jit(solution)/shard_map/ppermute | solution.py:215
  88.0 10.7 %collective-permute-start.39 = (bf16[1024,128]{1,0:T(8,128)(2,1)S(1)}, bf16[1024,128]{1,0:T(8,128)(2,1)S(1)}, u32[]{:S(2)}, u32[]{:S(2)}) collective-permute-start(bf16[1024,128]{1,0:T(8,128)(2,1)S(1)} %get-tuple-element.56), channel_id=1, source_target_pairs={{2,0},{10,8},{18,16},{26,24}} | collective-permute-start | bytes 786440 | tf_op jit(solution)/shard_map/ppermute | solution.py:215
  89.6 19.0 %collective-permute-start.30 = (bf16[1024,128]{1,0:T(8,128)(2,1)S(1)}, bf16[1024,128]{1,0:T(8,128)(2,1)S(1)}, u32[]{:S(2)}, u32[]{:S(2)}) collective-permute-start(bf16[1024,128]{1,0:T(8,128)(2,1)S(1)} %shard_map.99), channel_id=1, source_target_pairs={{1,2},{2,4},{4,6},{9,10},{10,12},{12,14},{17,18},{18,20},{20,22},{... | collective-permute-start | bytes 786440 | tf_op jit(solution)/shard_map/ppermute | solution.py:215
  90.2 9.8 %collective-permute-start.33 = (bf16[256,128]{1,0:T(8,128)(2,1)S(1)}, bf16[256,128]{1,0:T(8,128)(2,1)S(1)}, u32[]{:S(2)}, u32[]{:S(2)}) collective-permute-start(bf16[256,128]{1,0:T(8,128)(2,1)S(1)} %get-tuple-element.59), channel_id=1, source_target_pairs={{0,8},{8,0},{16,24},{24,16},{1,9},{9,1},{17,25},{25,17},{2,10},{10... | collective-permute-start | bytes 196616 | tf_op jit(solution)/shard_map/ppermute | solution.py:225
  108.6 6.7 %collective-permute-start.40 = (bf16[1024,128]{1,0:T(8,128)(2,1)S(1)}, bf16[1024,128]{1,0:T(8,128)(2,1)S(1)}, u32[]{:S(2)}, u32[]{:S(2)}) collective-permute-start(bf16[1024,128]{1,0:T(8,128)(2,1)S(1)} %shard_map.104), channel_id=1, source_target_pairs={{4,6},{2,4},{0,2},{12,14},{10,12},{8,10},{20,22},{18,20},{16,18},{... | collective-permute-start | bytes 786440 | tf_op jit(solution)/shard_map/ppermute | solution.py:215
  109.9 8.2 %collective-permute-start.41 = (bf16[1024,128]{1,0:T(8,128)(2,1)S(1)}, bf16[1024,128]{1,0:T(8,128)(2,1)S(1)}, u32[]{:S(2)}, u32[]{:S(2)}) collective-permute-start(bf16[1024,128]{1,0:T(8,128)(2,1)S(1)} %shard_map.104), channel_id=1, source_target_pairs={{2,6},{0,4},{10,14},{8,12},{18,22},{16,20},{26,30},{24,28}} | collective-permute-start | bytes 786440 | tf_op jit(solution)/shard_map/ppermute | solution.py:215
  (28 other events, 121.3 us)

commit v12 on v11

--- a/solution.py
+++ b/solution.py
@@ -238,6 +238,9 @@
             came = along(chip, pairs)
             stride *= 2
         return [chip, came]
+
+    def direct(chip):
+        return [chip] + [along(chip, [(2 * z, 0)]) for z in range(1, chips)]
 
     h1 = shift(history[0])
     listed = jnp.clip(block_row, 0, rows // block - 1)
@@ -262,7 +265,7 @@
     sheet = run(sheet_kernel, shape((rows, rows), BF16), (), (self_block, column, row), 20)
     mine = term((1, 2), blocks)
     chip1, chip2 = run(plus_kernel, [whole, whole], (), (mine, swap(mine)))
-    field1, field2 = staged(chip1), staged(chip2)
+    field1, field2 = direct(chip1), staged(chip2)
     other = swap(send_pick)
     aside = swap(dense)
 
@@ -277,11 +280,11 @@
         found.append(current)
         return sends
 
-    def pass_on():
-        handed = array = swap(found[-1])
+    def pass_on(core=1):
+        handed = array = swap(found[-1]) if core else found[-1]
         if slots:
-            array = run(bind(carry_kernel, 1), whole, (), (array, slots[-1]))
-        pairs = [(max(2 * z, 1), 2 * z + 2) for z in range(chips - 1)]
+            array = run(bind(carry_kernel, core), whole, (), (array, slots[-1]))
+        pairs = [(max(2 * z, core), 2 * z + 2) for z in range(chips - 1)]
         slots.append(along(array, pairs))
         return handed
 
@@ -299,7 +302,7 @@
     partner = swap(narrow)
     second = along(narrow, [(2, 0)])
     blocks = exchange(stepped(2, (*field2, wide, partner), (), 1))
-    pass_on()
+    pass_on(0)
     found.append(
         run(
             bind(last_kernel, groups, block, 3), whole, (),

time: 124 us -> 122 us (0.984)
  waiting for transfers between devices: 50.7 us -> 48.9 us
    ppermute x15, starting transfers between devices: 20.7 us -> 15.7 us  [exchange(): lax.ppermute(sends[hop], 'group', [(g, peer_of(g, hop, groups)) for g in...]
    ppermute x29, starting transfers between devices: 22.3 us -> 26.6 us  [along(): return lax.ppermute(array, 'delay', pairs)]
    pallas_call x24 -> x23, Pallas kernels: 20.4 us -> 20.4 us  [call(): pl.pallas_call(kernel, out_shape=out_shape, in_specs=[SMEM] * len(scalars...]
  transfers between devices with their start and end apart: 44 -> 44, of which waited for: 24 -> 19; matrix products, arithmetic and copies ran while one was open for 1% -> 1% of each run, Pallas kernels for 17% -> 17%
where the time goes in v12:
time: 122 us; the launch traced here: 120 us
  waiting for transfers between devices  48.9 us (40%)
  starting transfers between devices  42.3 us (35%)
  Pallas kernels  21.4 us (18%)
  local copies, waits for them, and re-layouts  6.29 us (5%)
    ppermute x29, waiting for transfers between devices, along(): return lax.ppermute(array, 'delay', pairs)  30.2 us
    ppermute x29, starting transfers between devices, along(): return lax.ppermute(array, 'delay', pairs)  26.6 us
    pallas_call x23, Pallas kernels, call(): pl.pallas_call(kernel, out_shape=out_shape, in_specs=[SMEM] * len(scalars...  20.4 us
    ppermute x15, waiting for transfers between devices, exchange(): lax.ppermute(sends[hop], 'group', [(g, peer_of(g, hop, groups)) for g in...  18.7 us
    ppermute x15, starting transfers between devices, exchange(): lax.ppermute(sends[hop], 'group', [(g, peer_of(g, hop, groups)) for g in...  15.7 us
    unnamed x17, local copies, waits for them, and re-layouts  6.06 us
  transfers between devices with their start and end apart: 44, of which 19 were waited for; matrix products, arithmetic and copies ran while one was open for 1% of the time, Pallas kernels for 17%

profile of v12, /device:TPU:0, one launch (start us, length us, event | category | flops | bytes accessed | tf_op | source)
XLA Modules:
  0.0 119.6 jit_solution(18045885688757119726)
XLA Ops:
  2.7 2.5 %collective-permute-start.1 = (bf16[256,128]{1,0:T(8,128)(2,1)S(1)}, bf16[256,128]{1,0:T(8,128)(2,1)S(1)}, u32[]{:S(2)}, u32[]{:S(2)}) collective-permute-start(bf16[256,128]{1,0:T(8,128)(2,1)S(1)} %get-tuple-element.35), channel_id=1, source_target_pairs={{0,8},{8,0},{16,24},{24,16},{1,9},{9,1},{17,25},{25,17},{2,10},{10... | collective-permute-start | bytes 196616 | tf_op jit(solution)/shard_map/ppermute | solution.py:225
  5.3 1.5 %collective-permute-start.2 = (bf16[256,128]{1,0:T(8,128)(2,1)S(1)}, bf16[256,128]{1,0:T(8,128)(2,1)S(1)}, u32[]{:S(2)}, u32[]{:S(2)}) collective-permute-start(bf16[256,128]{1,0:T(8,128)(2,1)S(1)} %get-tuple-element.36), channel_id=1, source_target_pairs={{0,16},{8,24},{16,0},{24,8},{1,17},{9,25},{17,1},{25,9},{2,18},{10... | collective-permute-start | bytes 196616 | tf_op jit(solution)/shard_map/ppermute | solution.py:225
  10.6 1.9 %collective-permute-done.3.refs_3_ = bf16[256,128]{1,0:T(8,128)(2,1)S(1)} collective-permute-done((bf16[256,128]{1,0:T(8,128)(2,1)S(1)}, bf16[256,128]{1,0:T(8,128)(2,1)S(1)}, u32[]{:S(2)}, u32[]{:S(2)}) %collective-permute-start.3) | collective-permute-done | bytes 65568 | tf_op jit(solution)/shard_map/ppermute | solution.py:225
  16.4 4.7 %collective-permute-done.8.refs_1_ = bf16[1024,128]{1,0:T(8,128)(2,1)} collective-permute-done((bf16[1024,128]{1,0:T(8,128)(2,1)S(1)}, bf16[1024,128]{1,0:T(8,128)(2,1)}, u32[]{:S(2)}, u32[]{:S(2)}) %collective-permute-start.8) | collective-permute-done | bytes 262176 | tf_op jit(solution)/shard_map/ppermute | solution.py:215
  23.0 1.5 %collective-permute-start.13 = (bf16[512,128]{1,0:T(8,128)(2,1)S(1)}, bf16[512,128]{1,0:T(8,128)(2,1)S(1)}, u32[]{:S(2)}, u32[]{:S(2)}) collective-permute-start(bf16[512,128]{1,0:T(8,128)(2,1)S(1)} %get-tuple-element.41), channel_id=1, source_target_pairs={{0,16},{8,24},{16,0},{24,8},{1,17},{9,25},{17,1},{25,9},{2,18},{10... | collective-permute-start | bytes 393224 | tf_op jit(solution)/shard_map/ppermute | solution.py:225
  28.5 1.9 %collective-permute-done.14.refs_3_ = bf16[512,128]{1,0:T(8,128)(2,1)S(1)} collective-permute-done((bf16[512,128]{1,0:T(8,128)(2,1)S(1)}, bf16[512,128]{1,0:T(8,128)(2,1)S(1)}, u32[]{:S(2)}, u32[]{:S(2)}) %collective-permute-start.14) | collective-permute-done | bytes 131104 | tf_op jit(solution)/shard_map/ppermute | solution.py:225
  32.0 1.6 %copy-done.1 = bf16[1024,1024]{1,0:T(8,128)(2,1)S(1)} copy-done((bf16[1024,1024]{1,0:T(8,128)(2,1)S(1)}, bf16[1024,1024]{1,0:T(8,128)(2,1)}, u32[]{:S(2)}) %copy-start.1) | copy-done | bytes 2097176
  33.6 4.6 %shard_map.82.sheet = bf16[1024,1024]{1,0:T(8,128)(2,1)S(1)} custom-call(bf16[1024,1024]{1,0:T(8,128)(2,1)S(1)} %copy-done.1, f32[1024,1]{1,0:T(8,128)S(1)} %copy.10.column, f32[1,1024]{1,0:T(1,128)S(1)} %bitcast.9), custom_call_target="tpu_custom_call" | custom-call | tf_op jit(solution)/shard_map/pallas_call | solution.py:29
  38.2 1.8 %shard_map.88 = (bf16[1024,128]{1,0:T(8,128)(2,1)S(1)}, bf16[256,128]{1,0:T(8,128)(2,1)S(1)}, bf16[256,128]{1,0:T(8,128)(2,1)S(1)}, bf16[256,128]{1,0:T(8,128)(2,1)S(1)}, bf16[256,128]{1,0:T(8,128)(2,1)S(1)}) custom-call(s32[1,4,4]{2,1,0:T(4,128)S(1)} %copy-done.5, s32[1,4,4]{2,1,0:T(4,128)S(1)} %collective-permute-done.other, ...), custom_call_target="tpu_custom_call" | custom-call | tf_op jit(solution)/shard_map/pallas_call | solution.py:29
  46.7 3.0 %collective-permute-done.19.refs_1_ = bf16[256,128]{1,0:T(8,128)(2,1)S(1)} collective-permute-done((bf16[256,128]{1,0:T(8,128)(2,1)S(1)}, bf16[256,128]{1,0:T(8,128)(2,1)S(1)}, u32[]{:S(2)}, u32[]{:S(2)}) %collective-permute-start.19) | collective-permute-done | bytes 65568 | tf_op jit(solution)/shard_map/ppermute | solution.py:225
  52.0 3.0 %collective-permute-done.21.refs_3_ = bf16[256,128]{1,0:T(8,128)(2,1)S(1)} collective-permute-done((bf16[256,128]{1,0:T(8,128)(2,1)S(1)}, bf16[256,128]{1,0:T(8,128)(2,1)S(1)}, u32[]{:S(2)}, u32[]{:S(2)}) %collective-permute-start.21) | collective-permute-done | bytes 65568 | tf_op jit(solution)/shard_map/ppermute | solution.py:225
  58.4 1.6 %collective-permute-done.17.refs_2_ = bf16[1024,128]{1,0:T(8,128)(2,1)S(1)} collective-permute-done((bf16[1024,128]{1,0:T(8,128)(2,1)S(1)}, bf16[1024,128]{1,0:T(8,128)(2,1)S(1)}, u32[]{:S(2)}, u32[]{:S(2)}) %collective-permute-start.17) | collective-permute-done | bytes 262176 | tf_op jit(solution)/shard_map/ppermute | solution.py:215
  60.0 5.2 %collective-permute-done.18.refs_3_ = bf16[1024,128]{1,0:T(8,128)(2,1)S(1)} collective-permute-done((bf16[1024,128]{1,0:T(8,128)(2,1)S(1)}, bf16[1024,128]{1,0:T(8,128)(2,1)S(1)}, u32[]{:S(2)}, u32[]{:S(2)}) %collective-permute-start.18) | collective-permute-done | bytes 262176 | tf_op jit(solution)/shard_map/ppermute | solution.py:215
  65.1 1.4 %shard_map.93 = (bf16[1024,128]{1,0:T(8,128)(2,1)S(1)}, bf16[512,128]{1,0:T(8,128)(2,1)S(1)}, bf16[512,128]{1,0:T(8,128)(2,1)S(1)}, bf16[512,128]{1,0:T(8,128)(2,1)S(1)}, bf16[512,128]{1,0:T(8,128)(2,1)S(1)}) custom-call(s32[1,4,4]{2,1,0:T(4,128)S(1)} %copy-done.5, s32[1,4,4]{2,1,0:T(4,128)S(1)} %collective-permute-done.other, ...), custom_call_target="tpu_custom_call" | custom-call | tf_op jit(solution)/shard_map/pallas_call | solution.py:29
  68.4 1.8 %collective-permute-start.28 = (bf16[512,128]{1,0:T(8,128)(2,1)S(1)}, bf16[512,128]{1,0:T(8,128)(2,1)S(1)}, u32[]{:S(2)}, u32[]{:S(2)}) collective-permute-start(bf16[512,128]{1,0:T(8,128)(2,1)S(1)} %get-tuple-element.54), channel_id=1, source_target_pairs={{0,24},{8,16},{16,8},{24,0},{1,25},{9,17},{17,9},{25,1},{2,26},{10... | collective-permute-start | bytes 393224 | tf_op jit(solution)/shard_map/ppermute | solution.py:225
  70.3 2.8 %collective-permute-done.26.refs_1_.refs_5_ = bf16[512,128]{1,0:T(8,128)(2,1)S(1)} collective-permute-done((bf16[512,128]{1,0:T(8,128)(2,1)S(1)}, bf16[512,128]{1,0:T(8,128)(2,1)S(1)}, u32[]{:S(2)}, u32[]{:S(2)}) %collective-permute-start.26) | collective-permute-done | bytes 131104 | tf_op jit(solution)/shard_map/ppermute | solution.py:225
  77.3 6.9 %collective-permute-done.37.second = bf16[1024,128]{1,0:T(8,128)(2,1)S(1)} collective-permute-done((bf16[1024,128]{1,0:T(8,128)(2,1)S(1)}, bf16[1024,128]{1,0:T(8,128)(2,1)S(1)}, u32[]{:S(2)}, u32[]{:S(2)}) %collective-permute-start.37) | collective-permute-done | bytes 262176 | tf_op jit(solution)/shard_map/ppermute | solution.py:215
  88.5 4.6 %collective-permute-start.30 = (bf16[1024,128]{1,0:T(8,128)(2,1)S(1)}, bf16[1024,128]{1,0:T(8,128)(2,1)S(1)}, u32[]{:S(2)}, u32[]{:S(2)}) collective-permute-start(bf16[1024,128]{1,0:T(8,128)(2,1)S(1)} %shard_map.98), channel_id=1, source_target_pairs={{0,2},{2,4},{4,6},{8,10},{10,12},{12,14},{16,18},{18,20},{20,22},{... | collective-permute-start | bytes 786440 | tf_op jit(solution)/shard_map/ppermute | solution.py:215
  94.4 1.8 %collective-permute-done.39.refs_10_ = bf16[1024,128]{1,0:T(8,128)(2,1)S(1)} collective-permute-done((bf16[1024,128]{1,0:T(8,128)(2,1)S(1)}, bf16[1024,128]{1,0:T(8,128)(2,1)S(1)}, u32[]{:S(2)}, u32[]{:S(2)}) %collective-permute-start.39) | collective-permute-done | bytes 262176 | tf_op jit(solution)/shard_map/ppermute | solution.py:215
  98.1 3.2 %collective-permute-done.35.refs_3_ = bf16[256,128]{1,0:T(8,128)(2,1)S(1)} collective-permute-done((bf16[256,128]{1,0:T(8,128)(2,1)S(1)}, bf16[256,128]{1,0:T(8,128)(2,1)S(1)}, u32[]{:S(2)}, u32[]{:S(2)}) %collective-permute-start.35) | collective-permute-done | bytes 65568 | tf_op jit(solution)/shard_map/ppermute | solution.py:225
  101.4 3.4 %shard_map.102.current.refs_2_ = bf16[1024,128]{1,0:T(8,128)(2,1)S(1)} custom-call(bf16[1024,1024]{1,0:T(8,128)(2,1)S(1)} %shard_map.82.sheet, f32[1024,1]{1,0:T(8,128)S(1)} %copy.10.column, bf16[4,1024,128]{2,1,0:T(8,128)(2,1)S(1)} %copy-done, bf16[1024,1024]{1,0:T(8,128)(2,1)S(1)} %shard_map.83.matrix, bf16[1024,1024]{1,0:T(8,128)(2,1)} %collective-permute-done.32.aside, ...), custom_call_target="tpu_custom_call" | custom-call | tf_op jit(solution)/shard_map/pallas_call | solution.py:29
  110.0 2.8 %collective-permute-done.40.refs_5_ = bf16[1024,128]{1,0:T(8,128)(2,1)S(1)} collective-permute-done((bf16[1024,128]{1,0:T(8,128)(2,1)S(1)}, bf16[1024,128]{1,0:T(8,128)(2,1)S(1)}, u32[]{:S(2)}, u32[]{:S(2)}) %collective-permute-start.40) | collective-permute-done | bytes 262176 | tf_op jit(solution)/shard_map/ppermute | solution.py:215
  112.8 2.9 %collective-permute-done.41.refs_6_ = bf16[1024,128]{1,0:T(8,128)(2,1)S(1)} collective-permute-done((bf16[1024,128]{1,0:T(8,128)(2,1)S(1)}, bf16[1024,128]{1,0:T(8,128)(2,1)S(1)}, u32[]{:S(2)}, u32[]{:S(2)}) %collective-permute-start.41) | collective-permute-done | bytes 262176 | tf_op jit(solution)/shard_map/ppermute | solution.py:215
  116.4 2.0 %collective-permute-done.31.early_other = bf16[1024,128]{1,0:T(8,128)(2,1)S(1)} collective-permute-done((bf16[1024,128]{1,0:T(8,128)(2,1)S(1)}, bf16[1024,128]{1,0:T(8,128)(2,1)S(1)}, u32[]{:S(2)}, u32[]{:S(2)}) %collective-permute-start.31) | collective-permute-done | bytes 262176 | tf_op jit(solution)/shard_map/ppermute | solution.py:215
  (108 shorter events, 50.5 us)
Async XLA Ops:
  0.0 13.4 %collective-permute-start.7 = (bf16[1024,128]{1,0:T(8,128)(2,1)}, bf16[1024,128]{1,0:T(8,128)(2,1)S(1)}, u32[]{:S(2)}, u32[]{:S(2)}) collective-permute-start(bf16[1024,128]{1,0:T(8,128)(2,1)} %bitcast.6), channel_id=1, source_target_pairs={{0,1},{1,2},{2,3},{3,4},{4,5},{5,6},{6,7},{7,0},{8,9},{9,10},{10,1... | collective-permute-start | bytes 786440 | tf_op jit(solution)/shard_map/ppermute | solution.py:215
  2.7 7.8 %collective-permute-start.1 = (bf16[256,128]{1,0:T(8,128)(2,1)S(1)}, bf16[256,128]{1,0:T(8,128)(2,1)S(1)}, u32[]{:S(2)}, u32[]{:S(2)}) collective-permute-start(bf16[256,128]{1,0:T(8,128)(2,1)S(1)} %get-tuple-element.35), channel_id=1, source_target_pairs={{0,8},{8,0},{16,24},{24,16},{1,9},{9,1},{17,25},{25,17},{2,10},{10... | collective-permute-start | bytes 196616 | tf_op jit(solution)/shard_map/ppermute | solution.py:225
  13.4 7.7 %collective-permute-start.8 = (bf16[1024,128]{1,0:T(8,128)(2,1)S(1)}, bf16[1024,128]{1,0:T(8,128)(2,1)}, u32[]{:S(2)}, u32[]{:S(2)}) collective-permute-start(bf16[1024,128]{1,0:T(8,128)(2,1)S(1)} %collective-permute-done.7.refs_0_), channel_id=1, source_target_pairs={{0,1},{1,2},{2,3},{3,4},{4,5},{5,6},{6,7},{7,0},{8,9},{9,10},{10,1... | collective-permute-start | bytes 786440 | tf_op jit(solution)/shard_map/ppermute | solution.py:215
  13.8 87.6 %collective-permute-start.32 = (bf16[1024,1024]{1,0:T(8,128)(2,1)S(1)}, bf16[1024,1024]{1,0:T(8,128)(2,1)}, u32[]{:S(2)}, u32[]{:S(2)}) collective-permute-start(bf16[1024,1024]{1,0:T(8,128)(2,1)S(1)} %shard_map.83.matrix), channel_id=1, source_target_pairs={{0,1},{1,0},{2,3},{3,2},{4,5},{5,4},{6,7},{7,6},{8,9},{9,8},{10,11... | collective-permute-start | bytes 6291464 | tf_op jit(solution)/shard_map/ppermute | solution.py:215
  15.1 10.6 %collective-permute-start.5 = (bf16[1024,128]{1,0:T(8,128)(2,1)S(1)}, bf16[1024,128]{1,0:T(8,128)(2,1)S(1)}, u32[]{:S(2)}, u32[]{:S(2)}) collective-permute-start(bf16[1024,128]{1,0:T(8,128)(2,1)S(1)} %shard_map.86.first), channel_id=1, source_target_pairs={{2,0},{6,4},{10,8},{14,12},{18,16},{22,20},{26,24},{30,28}} | collective-permute-start | bytes 786440 | tf_op jit(solution)/shard_map/ppermute | solution.py:215
  25.7 12.5 %collective-permute-start.9 = (bf16[1024,128]{1,0:T(8,128)(2,1)}, bf16[1024,128]{1,0:T(8,128)(2,1)}, u32[]{:S(2)}, u32[]{:S(2)}) collective-permute-start(bf16[1024,128]{1,0:T(8,128)(2,1)} %collective-permute-done.8.refs_1_), channel_id=1, source_target_pairs={{0,1},{1,2},{2,3},{3,4},{4,5},{5,6},{6,7},{7,0},{8,9},{9,10},{10,1... | collective-permute-start | bytes 786440 | tf_op jit(solution)/shard_map/ppermute | solution.py:215
  27.2 11.1 %collective-permute-start.6 = (bf16[1024,128]{1,0:T(8,128)(2,1)S(1)}, bf16[1024,128]{1,0:T(8,128)(2,1)}, u32[]{:S(2)}, u32[]{:S(2)}) collective-permute-start(bf16[1024,128]{1,0:T(8,128)(2,1)S(1)} %shard_map.87.refs_0_), channel_id=1, source_target_pairs={{4,0},{12,8},{20,16},{28,24}} | collective-permute-start | bytes 786440 | tf_op jit(solution)/shard_map/ppermute | solution.py:215
  28.5 9.7 %collective-permute-start = (s32[1,4,4]{2,1,0:T(4,128)S(1)}, s32[1,4,4]{2,1,0:T(4,128)S(1)}, u32[]{:S(2)}, u32[]{:S(2)}) collective-permute-start(s32[1,4,4]{2,1,0:T(4,128)S(1)} %copy-done.5), channel_id=1, source_target_pairs={{0,1},{1,0},{2,3},{3,2},{4,5},{5,4},{6,7},{7,6},{8,9},{9,8},{10,11... | collective-permute-start | bytes 200 | tf_op jit(solution)/shard_map/ppermute | solution.py:215
  31.6 10.8 %collective-permute-start.15 = (bf16[2048,128]{1,0:T(8,128)(2,1)S(1)}, bf16[2048,128]{1,0:T(8,128)(2,1)}, u32[]{:S(2)}, u32[]{:S(2)}) collective-permute-start(bf16[2048,128]{1,0:T(8,128)(2,1)S(1)} %shard_map.90.first), channel_id=1, source_target_pairs={{0,1},{1,0},{2,3},{3,2},{4,5},{5,4},{6,7},{7,6},{8,9},{9,8},{10,11... | collective-permute-start | bytes 1572872 | tf_op jit(solution)/shard_map/ppermute | solution.py:215
  41.8 15.2 %collective-permute-start.11 = (bf16[1024,128]{1,0:T(8,128)(2,1)S(1)}, bf16[1024,128]{1,0:T(8,128)(2,1)S(1)}, u32[]{:S(2)}, u32[]{:S(2)}) collective-permute-start(bf16[1024,128]{1,0:T(8,128)(2,1)S(1)} %collective-permute-done.10.refs_5_), channel_id=1, source_target_pairs={{1,2},{2,4},{4,6},{9,10},{10,12},{12,14},{17,18},{18,20},{20,22},{... | collective-permute-start | bytes 786440 | tf_op jit(solution)/shard_map/ppermute | solution.py:215
  43.6 13.4 %collective-permute-start.16 = (bf16[1024,128]{1,0:T(8,128)(2,1)S(1)}, bf16[1024,128]{1,0:T(8,128)(2,1)S(1)}, u32[]{:S(2)}, u32[]{:S(2)}) collective-permute-start(bf16[1024,128]{1,0:T(8,128)(2,1)S(1)} %get-tuple-element.43.refs_0_), channel_id=1, source_target_pairs={{2,0},{10,8},{18,16},{26,24}} | collective-permute-start | bytes 786440 | tf_op jit(solution)/shard_map/ppermute | solution.py:215
  50.7 9.3 %collective-permute-start.17 = (bf16[1024,128]{1,0:T(8,128)(2,1)S(1)}, bf16[1024,128]{1,0:T(8,128)(2,1)S(1)}, u32[]{:S(2)}, u32[]{:S(2)}) collective-permute-start(bf16[1024,128]{1,0:T(8,128)(2,1)S(1)} %get-tuple-element.43.refs_0_), channel_id=1, source_target_pairs={{4,0},{12,8},{20,16},{28,24}} | collective-permute-start | bytes 786440 | tf_op jit(solution)/shard_map/ppermute | solution.py:215
  55.0 10.2 %collective-permute-start.18 = (bf16[1024,128]{1,0:T(8,128)(2,1)S(1)}, bf16[1024,128]{1,0:T(8,128)(2,1)S(1)}, u32[]{:S(2)}, u32[]{:S(2)}) collective-permute-start(bf16[1024,128]{1,0:T(8,128)(2,1)S(1)} %get-tuple-element.43.refs_0_), channel_id=1, source_target_pairs={{6,0},{14,8},{22,16},{30,24}} | collective-permute-start | bytes 786440 | tf_op jit(solution)/shard_map/ppermute | solution.py:215
  57.0 10.0 %collective-permute-start.36 = (bf16[1024,128]{1,0:T(8,128)(2,1)S(1)}, bf16[1024,128]{1,0:T(8,128)(2,1)S(1)}, u32[]{:S(2)}, u32[]{:S(2)}) collective-permute-start(bf16[1024,128]{1,0:T(8,128)(2,1)S(1)} %get-tuple-element.62.first), channel_id=1, source_target_pairs={{0,1},{1,0},{2,3},{3,2},{4,5},{5,4},{6,7},{7,6},{8,9},{9,8},{10,11... | collective-permute-start | bytes 786440 | tf_op jit(solution)/shard_map/ppermute | solution.py:215
  57.1 11.4 %collective-permute-start.24 = (bf16[1024,128]{1,0:T(8,128)(2,1)S(1)}, bf16[1024,128]{1,0:T(8,128)(2,1)S(1)}, u32[]{:S(2)}, u32[]{:S(2)}) collective-permute-start(bf16[1024,128]{1,0:T(8,128)(2,1)S(1)} %get-tuple-element.50.first), channel_id=1, source_target_pairs={{2,0},{6,4},{10,8},{14,12},{18,16},{22,20},{26,24},{30,28}} | collective-permute-start | bytes 786440 | tf_op jit(solution)/shard_map/ppermute | solution.py:215
  66.6 10.0 %collective-permute-start.22 = (bf16[1024,128]{1,0:T(8,128)(2,1)S(1)}, bf16[1024,128]{1,0:T(8,128)(2,1)S(1)}, u32[]{:S(2)}, u32[]{:S(2)}) collective-permute-start(bf16[1024,128]{1,0:T(8,128)(2,1)S(1)} %get-tuple-element.49.refs_0_), channel_id=1, source_target_pairs={{0,1},{1,0},{2,3},{3,2},{4,5},{5,4},{6,7},{7,6},{8,9},{9,8},{10,11... | collective-permute-start | bytes 786440 | tf_op jit(solution)/shard_map/ppermute | solution.py:215
  73.1 11.1 %collective-permute-start.37 = (bf16[1024,128]{1,0:T(8,128)(2,1)S(1)}, bf16[1024,128]{1,0:T(8,128)(2,1)S(1)}, u32[]{:S(2)}, u32[]{:S(2)}) collective-permute-start(bf16[1024,128]{1,0:T(8,128)(2,1)S(1)} %shard_map.100.first), channel_id=1, source_target_pairs={{2,0},{6,4},{10,8},{14,12},{18,16},{22,20},{26,24},{30,28}} | collective-permute-start | bytes 786440 | tf_op jit(solution)/shard_map/ppermute | solution.py:215
  74.5 11.1 %collective-permute-start.25 = (bf16[1024,128]{1,0:T(8,128)(2,1)S(1)}, bf16[1024,128]{1,0:T(8,128)(2,1)S(1)}, u32[]{:S(2)}, u32[]{:S(2)}) collective-permute-start(bf16[1024,128]{1,0:T(8,128)(2,1)S(1)} %shard_map.95.refs_0_), channel_id=1, source_target_pairs={{4,0},{12,8},{20,16},{28,24}} | collective-permute-start | bytes 786440 | tf_op jit(solution)/shard_map/ppermute | solution.py:215
  76.5 10.3 %collective-permute-start.29 = (bf16[1024,128]{1,0:T(8,128)(2,1)S(1)}, bf16[1024,128]{1,0:T(8,128)(2,1)S(1)}, u32[]{:S(2)}, u32[]{:S(2)}) collective-permute-start(bf16[1024,128]{1,0:T(8,128)(2,1)S(1)} %get-tuple-element.56), channel_id=1, source_target_pairs={{0,1},{1,0},{2,3},{3,2},{4,5},{5,4},{6,7},{7,6},{8,9},{9,8},{10,11... | collective-permute-start | bytes 786440 | tf_op jit(solution)/shard_map/ppermute | solution.py:215
  76.6 11.6 %collective-permute-start.23 = (bf16[1024,128]{1,0:T(8,128)(2,1)S(1)}, bf16[1024,128]{1,0:T(8,128)(2,1)S(1)}, u32[]{:S(2)}, u32[]{:S(2)}) collective-permute-start(bf16[1024,128]{1,0:T(8,128)(2,1)S(1)} %shard_map.94), channel_id=1, source_target_pairs={{1,2},{2,4},{4,6},{9,10},{10,12},{12,14},{17,18},{18,20},{20,22},{... | collective-permute-start | bytes 786440 | tf_op jit(solution)/shard_map/ppermute | solution.py:215
  84.2 9.6 %collective-permute-start.38 = (bf16[1024,128]{1,0:T(8,128)(2,1)S(1)}, bf16[1024,128]{1,0:T(8,128)(2,1)S(1)}, u32[]{:S(2)}, u32[]{:S(2)}) collective-permute-start(bf16[1024,128]{1,0:T(8,128)(2,1)S(1)} %shard_map.101.refs_8_), channel_id=1, source_target_pairs={{4,0},{12,8},{20,16},{28,24}} | collective-permute-start | bytes 786440 | tf_op jit(solution)/shard_map/ppermute | solution.py:215
  85.5 10.7 %collective-permute-start.39 = (bf16[1024,128]{1,0:T(8,128)(2,1)S(1)}, bf16[1024,128]{1,0:T(8,128)(2,1)S(1)}, u32[]{:S(2)}, u32[]{:S(2)}) collective-permute-start(bf16[1024,128]{1,0:T(8,128)(2,1)S(1)} %get-tuple-element.56), channel_id=1, source_target_pairs={{2,0},{10,8},{18,16},{26,24}} | collective-permute-start | bytes 786440 | tf_op jit(solution)/shard_map/ppermute | solution.py:215
  88.5 17.6 %collective-permute-start.30 = (bf16[1024,128]{1,0:T(8,128)(2,1)S(1)}, bf16[1024,128]{1,0:T(8,128)(2,1)S(1)}, u32[]{:S(2)}, u32[]{:S(2)}) collective-permute-start(bf16[1024,128]{1,0:T(8,128)(2,1)S(1)} %shard_map.98), channel_id=1, source_target_pairs={{0,2},{2,4},{4,6},{8,10},{10,12},{12,14},{16,18},{18,20},{20,22},{... | collective-permute-start | bytes 786440 | tf_op jit(solution)/shard_map/ppermute | solution.py:215
  107.5 8.2 %collective-permute-start.41 = (bf16[1024,128]{1,0:T(8,128)(2,1)S(1)}, bf16[1024,128]{1,0:T(8,128)(2,1)S(1)}, u32[]{:S(2)}, u32[]{:S(2)}) collective-permute-start(bf16[1024,128]{1,0:T(8,128)(2,1)S(1)} %shard_map.103), channel_id=1, source_target_pairs={{2,6},{0,4},{10,14},{8,12},{18,22},{16,20},{26,30},{24,28}} | collective-permute-start | bytes 786440 | tf_op jit(solution)/shard_map/ppermute | solution.py:215
  (28 other events, 128.3 us)

commit v13 on v12

--- a/solution.py
+++ b/solution.py
@@ -221,10 +221,11 @@
         return along(array, [(d, (d + 1) % delays) for d in range(delays)])
 
     def exchange(sends):
-        return [sends[0]] + [
-            lax.ppermute(sends[hop], "group", [(g, peer_of(g, hop, groups)) for g in range(groups)])
-            for hop in range(1, groups)
-        ]
+        got = [sends[0]]
+        for hop in range(1, groups):
+            pairs = [(g, peer_of(g, hop, groups)) for g in range(groups)]
+            got.append(lax.ppermute(sends[hop], "group", pairs))
+        return got
 
     def run(kernel, out_shape, scalars, arrays, spare=2):
         return call(kernel, out_shape, scalars, arrays, spare)

time: 122 us -> 122 us (level)
  no operation moved by 1% of the time
where the time goes in v13:
time: 122 us; the launch traced here: 120 us
  waiting for transfers between devices  48.9 us (40%)
  starting transfers between devices  42.3 us (35%)
  Pallas kernels  21.4 us (18%)
  local copies, waits for them, and re-layouts  6.29 us (5%)
    ppermute x29, waiting for transfers between devices, along(): return lax.ppermute(array, 'delay', pairs)  30.2 us
    ppermute x29, starting transfers between devices, along(): return lax.ppermute(array, 'delay', pairs)  26.6 us
    pallas_call x23, Pallas kernels, call(): pl.pallas_call(kernel, out_shape=out_shape, in_specs=[SMEM] * len(scalars...  20.4 us
    ppermute x15, waiting for transfers between devices, exchange(): got.append(lax.ppermute(sends[hop], 'group', pairs))  18.7 us
    ppermute x15, starting transfers between devices, exchange(): got.append(lax.ppermute(sends[hop], 'group', pairs))  15.7 us
    unnamed x17, local copies, waits for them, and re-layouts  6.06 us
  transfers between devices with their start and end apart: 44, of which 19 were waited for; matrix products, arithmetic and copies ran while one was open for 1% of the time, Pallas kernels for 17%

profile of v13, /device:TPU:0, one launch (start us, length us, event | category | flops | bytes accessed | tf_op | source)
XLA Modules:
  0.0 119.6 jit_solution(18045885688757119726)
XLA Ops:
  2.7 2.5 %collective-permute-start.1 = (bf16[256,128]{1,0:T(8,128)(2,1)S(1)}, bf16[256,128]{1,0:T(8,128)(2,1)S(1)}, u32[]{:S(2)}, u32[]{:S(2)}) collective-permute-start(bf16[256,128]{1,0:T(8,128)(2,1)S(1)} %get-tuple-element.35), channel_id=1, source_target_pairs={{0,8},{8,0},{16,24},{24,16},{1,9},{9,1},{17,25},{25,17},{2,10},{10... | collective-permute-start | bytes 196616 | tf_op jit(solution)/shard_map/ppermute | solution.py:227
  5.3 1.5 %collective-permute-start.2 = (bf16[256,128]{1,0:T(8,128)(2,1)S(1)}, bf16[256,128]{1,0:T(8,128)(2,1)S(1)}, u32[]{:S(2)}, u32[]{:S(2)}) collective-permute-start(bf16[256,128]{1,0:T(8,128)(2,1)S(1)} %get-tuple-element.36), channel_id=1, source_target_pairs={{0,16},{8,24},{16,0},{24,8},{1,17},{9,25},{17,1},{25,9},{2,18},{10... | collective-permute-start | bytes 196616 | tf_op jit(solution)/shard_map/ppermute | solution.py:227
  10.6 1.9 %collective-permute-done.3.refs_3_ = bf16[256,128]{1,0:T(8,128)(2,1)S(1)} collective-permute-done((bf16[256,128]{1,0:T(8,128)(2,1)S(1)}, bf16[256,128]{1,0:T(8,128)(2,1)S(1)}, u32[]{:S(2)}, u32[]{:S(2)}) %collective-permute-start.3) | collective-permute-done | bytes 65568 | tf_op jit(solution)/shard_map/ppermute | solution.py:227
  16.4 4.7 %collective-permute-done.8.refs_1_ = bf16[1024,128]{1,0:T(8,128)(2,1)} collective-permute-done((bf16[1024,128]{1,0:T(8,128)(2,1)S(1)}, bf16[1024,128]{1,0:T(8,128)(2,1)}, u32[]{:S(2)}, u32[]{:S(2)}) %collective-permute-start.8) | collective-permute-done | bytes 262176 | tf_op jit(solution)/shard_map/ppermute | solution.py:215
  23.0 1.5 %collective-permute-start.13 = (bf16[512,128]{1,0:T(8,128)(2,1)S(1)}, bf16[512,128]{1,0:T(8,128)(2,1)S(1)}, u32[]{:S(2)}, u32[]{:S(2)}) collective-permute-start(bf16[512,128]{1,0:T(8,128)(2,1)S(1)} %get-tuple-element.41), channel_id=1, source_target_pairs={{0,16},{8,24},{16,0},{24,8},{1,17},{9,25},{17,1},{25,9},{2,18},{10... | collective-permute-start | bytes 393224 | tf_op jit(solution)/shard_map/ppermute | solution.py:227
  28.5 1.9 %collective-permute-done.14.refs_3_ = bf16[512,128]{1,0:T(8,128)(2,1)S(1)} collective-permute-done((bf16[512,128]{1,0:T(8,128)(2,1)S(1)}, bf16[512,128]{1,0:T(8,128)(2,1)S(1)}, u32[]{:S(2)}, u32[]{:S(2)}) %collective-permute-start.14) | collective-permute-done | bytes 131104 | tf_op jit(solution)/shard_map/ppermute | solution.py:227
  32.0 1.6 %copy-done.1 = bf16[1024,1024]{1,0:T(8,128)(2,1)S(1)} copy-done((bf16[1024,1024]{1,0:T(8,128)(2,1)S(1)}, bf16[1024,1024]{1,0:T(8,128)(2,1)}, u32[]{:S(2)}) %copy-start.1) | copy-done | bytes 2097176
  33.6 4.6 %shard_map.82.sheet = bf16[1024,1024]{1,0:T(8,128)(2,1)S(1)} custom-call(bf16[1024,1024]{1,0:T(8,128)(2,1)S(1)} %copy-done.1, f32[1024,1]{1,0:T(8,128)S(1)} %copy.10.column, f32[1,1024]{1,0:T(1,128)S(1)} %bitcast.9), custom_call_target="tpu_custom_call" | custom-call | tf_op jit(solution)/shard_map/pallas_call | solution.py:29
  38.2 1.8 %shard_map.88 = (bf16[1024,128]{1,0:T(8,128)(2,1)S(1)}, bf16[256,128]{1,0:T(8,128)(2,1)S(1)}, bf16[256,128]{1,0:T(8,128)(2,1)S(1)}, bf16[256,128]{1,0:T(8,128)(2,1)S(1)}, bf16[256,128]{1,0:T(8,128)(2,1)S(1)}) custom-call(s32[1,4,4]{2,1,0:T(4,128)S(1)} %copy-done.5, s32[1,4,4]{2,1,0:T(4,128)S(1)} %collective-permute-done.other, ...), custom_call_target="tpu_custom_call" | custom-call | tf_op jit(solution)/shard_map/pallas_call | solution.py:29
  46.7 3.0 %collective-permute-done.19.refs_1_ = bf16[256,128]{1,0:T(8,128)(2,1)S(1)} collective-permute-done((bf16[256,128]{1,0:T(8,128)(2,1)S(1)}, bf16[256,128]{1,0:T(8,128)(2,1)S(1)}, u32[]{:S(2)}, u32[]{:S(2)}) %collective-permute-start.19) | collective-permute-done | bytes 65568 | tf_op jit(solution)/shard_map/ppermute | solution.py:227
  52.0 3.0 %collective-permute-done.21.refs_3_ = bf16[256,128]{1,0:T(8,128)(2,1)S(1)} collective-permute-done((bf16[256,128]{1,0:T(8,128)(2,1)S(1)}, bf16[256,128]{1,0:T(8,128)(2,1)S(1)}, u32[]{:S(2)}, u32[]{:S(2)}) %collective-permute-start.21) | collective-permute-done | bytes 65568 | tf_op jit(solution)/shard_map/ppermute | solution.py:227
  58.4 1.6 %collective-permute-done.17.refs_2_ = bf16[1024,128]{1,0:T(8,128)(2,1)S(1)} collective-permute-done((bf16[1024,128]{1,0:T(8,128)(2,1)S(1)}, bf16[1024,128]{1,0:T(8,128)(2,1)S(1)}, u32[]{:S(2)}, u32[]{:S(2)}) %collective-permute-start.17) | collective-permute-done | bytes 262176 | tf_op jit(solution)/shard_map/ppermute | solution.py:215
  60.0 5.2 %collective-permute-done.18.refs_3_ = bf16[1024,128]{1,0:T(8,128)(2,1)S(1)} collective-permute-done((bf16[1024,128]{1,0:T(8,128)(2,1)S(1)}, bf16[1024,128]{1,0:T(8,128)(2,1)S(1)}, u32[]{:S(2)}, u32[]{:S(2)}) %collective-permute-start.18) | collective-permute-done | bytes 262176 | tf_op jit(solution)/shard_map/ppermute | solution.py:215
  65.1 1.4 %shard_map.93 = (bf16[1024,128]{1,0:T(8,128)(2,1)S(1)}, bf16[512,128]{1,0:T(8,128)(2,1)S(1)}, bf16[512,128]{1,0:T(8,128)(2,1)S(1)}, bf16[512,128]{1,0:T(8,128)(2,1)S(1)}, bf16[512,128]{1,0:T(8,128)(2,1)S(1)}) custom-call(s32[1,4,4]{2,1,0:T(4,128)S(1)} %copy-done.5, s32[1,4,4]{2,1,0:T(4,128)S(1)} %collective-permute-done.other, ...), custom_call_target="tpu_custom_call" | custom-call | tf_op jit(solution)/shard_map/pallas_call | solution.py:29
  68.4 1.8 %collective-permute-start.28 = (bf16[512,128]{1,0:T(8,128)(2,1)S(1)}, bf16[512,128]{1,0:T(8,128)(2,1)S(1)}, u32[]{:S(2)}, u32[]{:S(2)}) collective-permute-start(bf16[512,128]{1,0:T(8,128)(2,1)S(1)} %get-tuple-element.54), channel_id=1, source_target_pairs={{0,24},{8,16},{16,8},{24,0},{1,25},{9,17},{17,9},{25,1},{2,26},{10... | collective-permute-start | bytes 393224 | tf_op jit(solution)/shard_map/ppermute | solution.py:227
  70.3 2.8 %collective-permute-done.26.refs_1_.refs_5_ = bf16[512,128]{1,0:T(8,128)(2,1)S(1)} collective-permute-done((bf16[512,128]{1,0:T(8,128)(2,1)S(1)}, bf16[512,128]{1,0:T(8,128)(2,1)S(1)}, u32[]{:S(2)}, u32[]{:S(2)}) %collective-permute-start.26) | collective-permute-done | bytes 131104 | tf_op jit(solution)/shard_map/ppermute | solution.py:227
  77.3 6.9 %collective-permute-done.37.second = bf16[1024,128]{1,0:T(8,128)(2,1)S(1)} collective-permute-done((bf16[1024,128]{1,0:T(8,128)(2,1)S(1)}, bf16[1024,128]{1,0:T(8,128)(2,1)S(1)}, u32[]{:S(2)}, u32[]{:S(2)}) %collective-permute-start.37) | collective-permute-done | bytes 262176 | tf_op jit(solution)/shard_map/ppermute | solution.py:215
  88.5 4.6 %collective-permute-start.30 = (bf16[1024,128]{1,0:T(8,128)(2,1)S(1)}, bf16[1024,128]{1,0:T(8,128)(2,1)S(1)}, u32[]{:S(2)}, u32[]{:S(2)}) collective-permute-start(bf16[1024,128]{1,0:T(8,128)(2,1)S(1)} %shard_map.98), channel_id=1, source_target_pairs={{0,2},{2,4},{4,6},{8,10},{10,12},{12,14},{16,18},{18,20},{20,22},{... | collective-permute-start | bytes 786440 | tf_op jit(solution)/shard_map/ppermute | solution.py:215
  94.4 1.8 %collective-permute-done.39.refs_10_ = bf16[1024,128]{1,0:T(8,128)(2,1)S(1)} collective-permute-done((bf16[1024,128]{1,0:T(8,128)(2,1)S(1)}, bf16[1024,128]{1,0:T(8,128)(2,1)S(1)}, u32[]{:S(2)}, u32[]{:S(2)}) %collective-permute-start.39) | collective-permute-done | bytes 262176 | tf_op jit(solution)/shard_map/ppermute | solution.py:215
  98.1 3.2 %collective-permute-done.35.refs_3_ = bf16[256,128]{1,0:T(8,128)(2,1)S(1)} collective-permute-done((bf16[256,128]{1,0:T(8,128)(2,1)S(1)}, bf16[256,128]{1,0:T(8,128)(2,1)S(1)}, u32[]{:S(2)}, u32[]{:S(2)}) %collective-permute-start.35) | collective-permute-done | bytes 65568 | tf_op jit(solution)/shard_map/ppermute | solution.py:227
  101.4 3.4 %shard_map.102.current.refs_2_ = bf16[1024,128]{1,0:T(8,128)(2,1)S(1)} custom-call(bf16[1024,1024]{1,0:T(8,128)(2,1)S(1)} %shard_map.82.sheet, f32[1024,1]{1,0:T(8,128)S(1)} %copy.10.column, bf16[4,1024,128]{2,1,0:T(8,128)(2,1)S(1)} %copy-done, bf16[1024,1024]{1,0:T(8,128)(2,1)S(1)} %shard_map.83.matrix, bf16[1024,1024]{1,0:T(8,128)(2,1)} %collective-permute-done.32.aside, ...), custom_call_target="tpu_custom_call" | custom-call | tf_op jit(solution)/shard_map/pallas_call | solution.py:29
  110.0 2.8 %collective-permute-done.40.refs_5_ = bf16[1024,128]{1,0:T(8,128)(2,1)S(1)} collective-permute-done((bf16[1024,128]{1,0:T(8,128)(2,1)S(1)}, bf16[1024,128]{1,0:T(8,128)(2,1)S(1)}, u32[]{:S(2)}, u32[]{:S(2)}) %collective-permute-start.40) | collective-permute-done | bytes 262176 | tf_op jit(solution)/shard_map/ppermute | solution.py:215
  112.8 2.9 %collective-permute-done.41.refs_6_ = bf16[1024,128]{1,0:T(8,128)(2,1)S(1)} collective-permute-done((bf16[1024,128]{1,0:T(8,128)(2,1)S(1)}, bf16[1024,128]{1,0:T(8,128)(2,1)S(1)}, u32[]{:S(2)}, u32[]{:S(2)}) %collective-permute-start.41) | collective-permute-done | bytes 262176 | tf_op jit(solution)/shard_map/ppermute | solution.py:215
  116.4 2.0 %collective-permute-done.31.early_other = bf16[1024,128]{1,0:T(8,128)(2,1)S(1)} collective-permute-done((bf16[1024,128]{1,0:T(8,128)(2,1)S(1)}, bf16[1024,128]{1,0:T(8,128)(2,1)S(1)}, u32[]{:S(2)}, u32[]{:S(2)}) %collective-permute-start.31) | collective-permute-done | bytes 262176 | tf_op jit(solution)/shard_map/ppermute | solution.py:215
  (108 shorter events, 50.5 us)
Async XLA Ops:
  0.0 13.4 %collective-permute-start.7 = (bf16[1024,128]{1,0:T(8,128)(2,1)}, bf16[1024,128]{1,0:T(8,128)(2,1)S(1)}, u32[]{:S(2)}, u32[]{:S(2)}) collective-permute-start(bf16[1024,128]{1,0:T(8,128)(2,1)} %bitcast.6), channel_id=1, source_target_pairs={{0,1},{1,2},{2,3},{3,4},{4,5},{5,6},{6,7},{7,0},{8,9},{9,10},{10,1... | collective-permute-start | bytes 786440 | tf_op jit(solution)/shard_map/ppermute | solution.py:215
  2.7 7.8 %collective-permute-start.1 = (bf16[256,128]{1,0:T(8,128)(2,1)S(1)}, bf16[256,128]{1,0:T(8,128)(2,1)S(1)}, u32[]{:S(2)}, u32[]{:S(2)}) collective-permute-start(bf16[256,128]{1,0:T(8,128)(2,1)S(1)} %get-tuple-element.35), channel_id=1, source_target_pairs={{0,8},{8,0},{16,24},{24,16},{1,9},{9,1},{17,25},{25,17},{2,10},{10... | collective-permute-start | bytes 196616 | tf_op jit(solution)/shard_map/ppermute | solution.py:227
  13.4 7.7 %collective-permute-start.8 = (bf16[1024,128]{1,0:T(8,128)(2,1)S(1)}, bf16[1024,128]{1,0:T(8,128)(2,1)}, u32[]{:S(2)}, u32[]{:S(2)}) collective-permute-start(bf16[1024,128]{1,0:T(8,128)(2,1)S(1)} %collective-permute-done.7.refs_0_), channel_id=1, source_target_pairs={{0,1},{1,2},{2,3},{3,4},{4,5},{5,6},{6,7},{7,0},{8,9},{9,10},{10,1... | collective-permute-start | bytes 786440 | tf_op jit(solution)/shard_map/ppermute | solution.py:215
  13.8 87.6 %collective-permute-start.32 = (bf16[1024,1024]{1,0:T(8,128)(2,1)S(1)}, bf16[1024,1024]{1,0:T(8,128)(2,1)}, u32[]{:S(2)}, u32[]{:S(2)}) collective-permute-start(bf16[1024,1024]{1,0:T(8,128)(2,1)S(1)} %shard_map.83.matrix), channel_id=1, source_target_pairs={{0,1},{1,0},{2,3},{3,2},{4,5},{5,4},{6,7},{7,6},{8,9},{9,8},{10,11... | collective-permute-start | bytes 6291464 | tf_op jit(solution)/shard_map/ppermute | solution.py:215
  15.1 10.6 %collective-permute-start.5 = (bf16[1024,128]{1,0:T(8,128)(2,1)S(1)}, bf16[1024,128]{1,0:T(8,128)(2,1)S(1)}, u32[]{:S(2)}, u32[]{:S(2)}) collective-permute-start(bf16[1024,128]{1,0:T(8,128)(2,1)S(1)} %shard_map.86.first), channel_id=1, source_target_pairs={{2,0},{6,4},{10,8},{14,12},{18,16},{22,20},{26,24},{30,28}} | collective-permute-start | bytes 786440 | tf_op jit(solution)/shard_map/ppermute | solution.py:215
  25.7 12.5 %collective-permute-start.9 = (bf16[1024,128]{1,0:T(8,128)(2,1)}, bf16[1024,128]{1,0:T(8,128)(2,1)}, u32[]{:S(2)}, u32[]{:S(2)}) collective-permute-start(bf16[1024,128]{1,0:T(8,128)(2,1)} %collective-permute-done.8.refs_1_), channel_id=1, source_target_pairs={{0,1},{1,2},{2,3},{3,4},{4,5},{5,6},{6,7},{7,0},{8,9},{9,10},{10,1... | collective-permute-start | bytes 786440 | tf_op jit(solution)/shard_map/ppermute | solution.py:215
  27.2 11.1 %collective-permute-start.6 = (bf16[1024,128]{1,0:T(8,128)(2,1)S(1)}, bf16[1024,128]{1,0:T(8,128)(2,1)}, u32[]{:S(2)}, u32[]{:S(2)}) collective-permute-start(bf16[1024,128]{1,0:T(8,128)(2,1)S(1)} %shard_map.87.refs_0_), channel_id=1, source_target_pairs={{4,0},{12,8},{20,16},{28,24}} | collective-permute-start | bytes 786440 | tf_op jit(solution)/shard_map/ppermute | solution.py:215
  28.5 9.7 %collective-permute-start = (s32[1,4,4]{2,1,0:T(4,128)S(1)}, s32[1,4,4]{2,1,0:T(4,128)S(1)}, u32[]{:S(2)}, u32[]{:S(2)}) collective-permute-start(s32[1,4,4]{2,1,0:T(4,128)S(1)} %copy-done.5), channel_id=1, source_target_pairs={{0,1},{1,0},{2,3},{3,2},{4,5},{5,4},{6,7},{7,6},{8,9},{9,8},{10,11... | collective-permute-start | bytes 200 | tf_op jit(solution)/shard_map/ppermute | solution.py:215
  31.6 10.8 %collective-permute-start.15 = (bf16[2048,128]{1,0:T(8,128)(2,1)S(1)}, bf16[2048,128]{1,0:T(8,128)(2,1)}, u32[]{:S(2)}, u32[]{:S(2)}) collective-permute-start(bf16[2048,128]{1,0:T(8,128)(2,1)S(1)} %shard_map.90.first), channel_id=1, source_target_pairs={{0,1},{1,0},{2,3},{3,2},{4,5},{5,4},{6,7},{7,6},{8,9},{9,8},{10,11... | collective-permute-start | bytes 1572872 | tf_op jit(solution)/shard_map/ppermute | solution.py:215
  41.8 15.2 %collective-permute-start.11 = (bf16[1024,128]{1,0:T(8,128)(2,1)S(1)}, bf16[1024,128]{1,0:T(8,128)(2,1)S(1)}, u32[]{:S(2)}, u32[]{:S(2)}) collective-permute-start(bf16[1024,128]{1,0:T(8,128)(2,1)S(1)} %collective-permute-done.10.refs_5_), channel_id=1, source_target_pairs={{1,2},{2,4},{4,6},{9,10},{10,12},{12,14},{17,18},{18,20},{20,22},{... | collective-permute-start | bytes 786440 | tf_op jit(solution)/shard_map/ppermute | solution.py:215
  43.6 13.4 %collective-permute-start.16 = (bf16[1024,128]{1,0:T(8,128)(2,1)S(1)}, bf16[1024,128]{1,0:T(8,128)(2,1)S(1)}, u32[]{:S(2)}, u32[]{:S(2)}) collective-permute-start(bf16[1024,128]{1,0:T(8,128)(2,1)S(1)} %get-tuple-element.43.refs_0_), channel_id=1, source_target_pairs={{2,0},{10,8},{18,16},{26,24}} | collective-permute-start | bytes 786440 | tf_op jit(solution)/shard_map/ppermute | solution.py:215
  50.7 9.3 %collective-permute-start.17 = (bf16[1024,128]{1,0:T(8,128)(2,1)S(1)}, bf16[1024,128]{1,0:T(8,128)(2,1)S(1)}, u32[]{:S(2)}, u32[]{:S(2)}) collective-permute-start(bf16[1024,128]{1,0:T(8,128)(2,1)S(1)} %get-tuple-element.43.refs_0_), channel_id=1, source_target_pairs={{4,0},{12,8},{20,16},{28,24}} | collective-permute-start | bytes 786440 | tf_op jit(solution)/shard_map/ppermute | solution.py:215
  55.0 10.2 %collective-permute-start.18 = (bf16[1024,128]{1,0:T(8,128)(2,1)S(1)}, bf16[1024,128]{1,0:T(8,128)(2,1)S(1)}, u32[]{:S(2)}, u32[]{:S(2)}) collective-permute-start(bf16[1024,128]{1,0:T(8,128)(2,1)S(1)} %get-tuple-element.43.refs_0_), channel_id=1, source_target_pairs={{6,0},{14,8},{22,16},{30,24}} | collective-permute-start | bytes 786440 | tf_op jit(solution)/shard_map/ppermute | solution.py:215
  57.0 10.0 %collective-permute-start.36 = (bf16[1024,128]{1,0:T(8,128)(2,1)S(1)}, bf16[1024,128]{1,0:T(8,128)(2,1)S(1)}, u32[]{:S(2)}, u32[]{:S(2)}) collective-permute-start(bf16[1024,128]{1,0:T(8,128)(2,1)S(1)} %get-tuple-element.62.first), channel_id=1, source_target_pairs={{0,1},{1,0},{2,3},{3,2},{4,5},{5,4},{6,7},{7,6},{8,9},{9,8},{10,11... | collective-permute-start | bytes 786440 | tf_op jit(solution)/shard_map/ppermute | solution.py:215
  57.1 11.4 %collective-permute-start.24 = (bf16[1024,128]{1,0:T(8,128)(2,1)S(1)}, bf16[1024,128]{1,0:T(8,128)(2,1)S(1)}, u32[]{:S(2)}, u32[]{:S(2)}) collective-permute-start(bf16[1024,128]{1,0:T(8,128)(2,1)S(1)} %get-tuple-element.50.first), channel_id=1, source_target_pairs={{2,0},{6,4},{10,8},{14,12},{18,16},{22,20},{26,24},{30,28}} | collective-permute-start | bytes 786440 | tf_op jit(solution)/shard_map/ppermute | solution.py:215
  66.6 10.0 %collective-permute-start.22 = (bf16[1024,128]{1,0:T(8,128)(2,1)S(1)}, bf16[1024,128]{1,0:T(8,128)(2,1)S(1)}, u32[]{:S(2)}, u32[]{:S(2)}) collective-permute-start(bf16[1024,128]{1,0:T(8,128)(2,1)S(1)} %get-tuple-element.49.refs_0_), channel_id=1, source_target_pairs={{0,1},{1,0},{2,3},{3,2},{4,5},{5,4},{6,7},{7,6},{8,9},{9,8},{10,11... | collective-permute-start | bytes 786440 | tf_op jit(solution)/shard_map/ppermute | solution.py:215
  73.1 11.1 %collective-permute-start.37 = (bf16[1024,128]{1,0:T(8,128)(2,1)S(1)}, bf16[1024,128]{1,0:T(8,128)(2,1)S(1)}, u32[]{:S(2)}, u32[]{:S(2)}) collective-permute-start(bf16[1024,128]{1,0:T(8,128)(2,1)S(1)} %shard_map.100.first), channel_id=1, source_target_pairs={{2,0},{6,4},{10,8},{14,12},{18,16},{22,20},{26,24},{30,28}} | collective-permute-start | bytes 786440 | tf_op jit(solution)/shard_map/ppermute | solution.py:215
  74.5 11.1 %collective-permute-start.25 = (bf16[1024,128]{1,0:T(8,128)(2,1)S(1)}, bf16[1024,128]{1,0:T(8,128)(2,1)S(1)}, u32[]{:S(2)}, u32[]{:S(2)}) collective-permute-start(bf16[1024,128]{1,0:T(8,128)(2,1)S(1)} %shard_map.95.refs_0_), channel_id=1, source_target_pairs={{4,0},{12,8},{20,16},{28,24}} | collective-permute-start | bytes 786440 | tf_op jit(solution)/shard_map/ppermute | solution.py:215
  76.5 10.3 %collective-permute-start.29 = (bf16[1024,128]{1,0:T(8,128)(2,1)S(1)}, bf16[1024,128]{1,0:T(8,128)(2,1)S(1)}, u32[]{:S(2)}, u32[]{:S(2)}) collective-permute-start(bf16[1024,128]{1,0:T(8,128)(2,1)S(1)} %get-tuple-element.56), channel_id=1, source_target_pairs={{0,1},{1,0},{2,3},{3,2},{4,5},{5,4},{6,7},{7,6},{8,9},{9,8},{10,11... | collective-permute-start | bytes 786440 | tf_op jit(solution)/shard_map/ppermute | solution.py:215
  76.6 11.6 %collective-permute-start.23 = (bf16[1024,128]{1,0:T(8,128)(2,1)S(1)}, bf16[1024,128]{1,0:T(8,128)(2,1)S(1)}, u32[]{:S(2)}, u32[]{:S(2)}) collective-permute-start(bf16[1024,128]{1,0:T(8,128)(2,1)S(1)} %shard_map.94), channel_id=1, source_target_pairs={{1,2},{2,4},{4,6},{9,10},{10,12},{12,14},{17,18},{18,20},{20,22},{... | collective-permute-start | bytes 786440 | tf_op jit(solution)/shard_map/ppermute | solution.py:215
  84.2 9.6 %collective-permute-start.38 = (bf16[1024,128]{1,0:T(8,128)(2,1)S(1)}, bf16[1024,128]{1,0:T(8,128)(2,1)S(1)}, u32[]{:S(2)}, u32[]{:S(2)}) collective-permute-start(bf16[1024,128]{1,0:T(8,128)(2,1)S(1)} %shard_map.101.refs_8_), channel_id=1, source_target_pairs={{4,0},{12,8},{20,16},{28,24}} | collective-permute-start | bytes 786440 | tf_op jit(solution)/shard_map/ppermute | solution.py:215
  85.5 10.7 %collective-permute-start.39 = (bf16[1024,128]{1,0:T(8,128)(2,1)S(1)}, bf16[1024,128]{1,0:T(8,128)(2,1)S(1)}, u32[]{:S(2)}, u32[]{:S(2)}) collective-permute-start(bf16[1024,128]{1,0:T(8,128)(2,1)S(1)} %get-tuple-element.56), channel_id=1, source_target_pairs={{2,0},{10,8},{18,16},{26,24}} | collective-permute-start | bytes 786440 | tf_op jit(solution)/shard_map/ppermute | solution.py:215
  88.5 17.6 %collective-permute-start.30 = (bf16[1024,128]{1,0:T(8,128)(2,1)S(1)}, bf16[1024,128]{1,0:T(8,128)(2,1)S(1)}, u32[]{:S(2)}, u32[]{:S(2)}) collective-permute-start(bf16[1024,128]{1,0:T(8,128)(2,1)S(1)} %shard_map.98), channel_id=1, source_target_pairs={{0,2},{2,4},{4,6},{8,10},{10,12},{12,14},{16,18},{18,20},{20,22},{... | collective-permute-start | bytes 786440 | tf_op jit(solution)/shard_map/ppermute | solution.py:215
  107.5 8.2 %collective-permute-start.41 = (bf16[1024,128]{1,0:T(8,128)(2,1)S(1)}, bf16[1024,128]{1,0:T(8,128)(2,1)S(1)}, u32[]{:S(2)}, u32[]{:S(2)}) collective-permute-start(bf16[1024,128]{1,0:T(8,128)(2,1)S(1)} %shard_map.103), channel_id=1, source_target_pairs={{2,6},{0,4},{10,14},{8,12},{18,22},{16,20},{26,30},{24,28}} | collective-permute-start | bytes 786440 | tf_op jit(solution)/shard_map/ppermute | solution.py:215
  (28 other events, 128.3 us)

commit v14 on v13

--- a/solution.py
+++ b/solution.py
@@ -52,13 +52,15 @@
                 dense[pl.ds(start, block), hop * block : (hop + 1) * block] = weights[source, entry]
 
 
-def sheet_kernel(self_block, column, row, sheet):
-    scaled = self_block[...].astype(F32) * column[...]
+def sheet_kernel(self_block, diagonal, sheet, column):
+    row = 1.0 / diagonal[...]
+    column[...] = jnp.broadcast_to(row, (column.shape[1], row.shape[1])).T
+    scaled = self_block[...].astype(F32) * column[:, :1]
     first = scaled.astype(BF16)
     second = dot(first, first)
     total = second - scaled
     third = dot(second.astype(BF16), first)
-    sheet[...] = ((total - third) * row[...]).astype(BF16)
+    sheet[...] = ((total - third) * row).astype(BF16)
 
 
 def product(matrix, blocks, part, block):
@@ -261,9 +263,9 @@
     field0 = staged(chip)
     blocks = exchange(pick((h1, h2)))
     h3 = shift(h2)
-    inverse = 1.0 / sheet_diag
-    column, row = inverse[:, None], inverse[None, :]
-    sheet = run(sheet_kernel, shape((rows, rows), BF16), (), (self_block, column, row), 20)
+    sheet, column = run(
+        sheet_kernel, [shape((rows, rows), BF16), wide_whole], (), (self_block, sheet_diag[None, :]), 20
+    )
     mine = term((1, 2), blocks)
     chip1, chip2 = run(plus_kernel, [whole, whole], (), (mine, swap(mine)))
     field1, field2 = direct(chip1), staged(chip2)

time: 122 us -> 116 us (0.951)
  the two profiles are of different devices: /device:TPU:0 before, /device:TPU:29 now
where the time goes in v14:
time: 116 us
  starting transfers between devices  74.1 us (64%)
  waiting for transfers between devices  18.2 us (16%)
  Pallas kernels  18 us (16%)
  local copies, waits for them, and re-layouts  4.52 us (4%)
    ppermute x29, starting transfers between devices, along(): return lax.ppermute(array, 'delay', pairs)  60.6 us
    pallas_call x23, Pallas kernels, call(): pl.pallas_call(kernel, out_shape=out_shape, in_specs=[SMEM] * len(scalars...  17 us
    ppermute x15, starting transfers between devices, exchange(): got.append(lax.ppermute(sends[hop], 'group', pairs))  13.5 us
    ppermute x15, waiting for transfers between devices, exchange(): got.append(lax.ppermute(sends[hop], 'group', pairs))  12.3 us
    ppermute x29, waiting for transfers between devices, along(): return lax.ppermute(array, 'delay', pairs)  5.94 us
    unnamed x17, local copies, waits for them, and re-layouts  4.52 us
  transfers between devices with their start and end apart: 44, of which 11 were waited for; matrix products, arithmetic and copies ran while one was open for 1% of the time, Pallas kernels for 15%

profile of v14, /device:TPU:29, one launch (start us, length us, event | category | flops | bytes accessed | tf_op | source)
XLA Modules:
  0.0 115.5 jit_solution(10135242369310947635)
XLA Ops:
  2.8 1.3 %collective-permute-start.1 = (bf16[256,128]{1,0:T(8,128)(2,1)S(1)}, bf16[256,128]{1,0:T(8,128)(2,1)S(1)}, u32[]{:S(2)}, u32[]{:S(2)}) collective-permute-start(bf16[256,128]{1,0:T(8,128)(2,1)S(1)} %get-tuple-element.39), channel_id=1, source_target_pairs={{0,8},{8,0},{16,24},{24,16},{1,9},{9,1},{17,25},{25,17},{2,10},{10... | collective-permute-start | bytes 196616 | tf_op jit(solution)/shard_map/ppermute | solution.py:229
  6.3 1.4 %copy-done.2 = bf16[1,4,3,256,256]{4,3,2,1,0:T(8,128)(2,1)S(1)} copy-done((bf16[1,4,3,256,256]{4,3,2,1,0:T(8,128)(2,1)S(1)}, bf16[1,4,3,256,256]{4,3,2,1,0:T(8,128)(2,1)}, u32[]{:S(2)}) %copy-start.2) | copy-done | bytes 1572888
  12.9 2.1 %collective-permute-done.8.refs_1_ = bf16[1024,128]{1,0:T(8,128)(2,1)S(1)} collective-permute-done((bf16[1024,128]{1,0:T(8,128)(2,1)S(1)}, bf16[1024,128]{1,0:T(8,128)(2,1)S(1)}, u32[]{:S(2)}, u32[]{:S(2)}) %collective-permute-start.8) | collective-permute-done | bytes 262176 | tf_op jit(solution)/shard_map/ppermute | solution.py:217
  15.7 1.2 %collective-permute-start.12 = (bf16[512,128]{1,0:T(8,128)(2,1)S(1)}, bf16[512,128]{1,0:T(8,128)(2,1)S(1)}, u32[]{:S(2)}, u32[]{:S(2)}) collective-permute-start(bf16[512,128]{1,0:T(8,128)(2,1)S(1)} %get-tuple-element.44), channel_id=1, source_target_pairs={{0,8},{8,0},{16,24},{24,16},{1,9},{9,1},{17,25},{25,17},{2,10},{10... | collective-permute-start | bytes 393224 | tf_op jit(solution)/shard_map/ppermute | solution.py:229
  17.2 1.2 %collective-permute-start.14 = (bf16[512,128]{1,0:T(8,128)(2,1)S(1)}, bf16[512,128]{1,0:T(8,128)(2,1)S(1)}, u32[]{:S(2)}, u32[]{:S(2)}) collective-permute-start(bf16[512,128]{1,0:T(8,128)(2,1)S(1)} %get-tuple-element.46), channel_id=1, source_target_pairs={{0,24},{8,16},{16,8},{24,0},{1,25},{9,17},{17,9},{25,1},{2,26},{10... | collective-permute-start | bytes 393224 | tf_op jit(solution)/shard_map/ppermute | solution.py:229
  18.4 5.2 %collective-permute-start.9 = (bf16[1024,128]{1,0:T(8,128)(2,1)S(1)}, bf16[1024,128]{1,0:T(8,128)(2,1)S(1)}, u32[]{:S(2)}, u32[]{:S(2)}) collective-permute-start(bf16[1024,128]{1,0:T(8,128)(2,1)S(1)} %collective-permute-done.8.refs_1_), channel_id=1, source_target_pairs={{0,1},{1,2},{2,3},{3,4},{4,5},{5,6},{6,7},{7,0},{8,9},{9,10},{10,1... | collective-permute-start | bytes 786440 | tf_op jit(solution)/shard_map/ppermute | solution.py:217
  24.4 1.2 %shard_map.90.first = bf16[2048,128]{1,0:T(8,128)(2,1)S(1)} custom-call(bf16[1024,1024]{1,0:T(8,128)(2,1)S(1)} %shard_map.83.matrix, bf16[512,128]{1,0:T(8,128)(2,1)S(1)} %get-tuple-element.43.refs_0_, bf16[512,128]{1,0:T(8,128)(2,1)S(1)} %collective-permute-done.12.refs_1_, bf16[512,128]{1,0:T(8,128)(2,1)S(1)} %collective-permute-done.13.refs_2_, ...), custom_call_target="tpu_custom_call" | custom-call | tf_op jit(solution)/shard_map/pallas_call | solution.py:29
  25.6 1.4 %collective-permute-start.15 = (bf16[2048,128]{1,0:T(8,128)(2,1)S(1)}, bf16[2048,128]{1,0:T(8,128)(2,1)S(1)}, u32[]{:S(2)}, u32[]{:S(2)}) collective-permute-start(bf16[2048,128]{1,0:T(8,128)(2,1)S(1)} %shard_map.90.first), channel_id=1, source_target_pairs={{0,1},{1,0},{2,3},{3,2},{4,5},{5,4},{6,7},{7,6},{8,9},{9,8},{10,11... | collective-permute-start | bytes 1572872 | tf_op jit(solution)/shard_map/ppermute | solution.py:217
  27.1 4.9 %shard_map.82 = (bf16[1024,1024]{1,0:T(8,128)(2,1)S(1)}, f32[1024,128]{1,0:T(8,128)S(1)}) custom-call(bf16[1024,1024]{1,0:T(8,128)(2,1)S(1)} %copy-done.1, f32[1,1024]{1,0:T(1,128)S(1)} %bitcast.7), custom_call_target="tpu_custom_call" | custom-call | tf_op jit(solution)/shard_map/pallas_call | solution.py:29
  32.1 1.4 %shard_map.88 = (bf16[1024,128]{1,0:T(8,128)(2,1)S(1)}, bf16[256,128]{1,0:T(8,128)(2,1)S(1)}, bf16[256,128]{1,0:T(8,128)(2,1)S(1)}, bf16[256,128]{1,0:T(8,128)(2,1)S(1)}, bf16[256,128]{1,0:T(8,128)(2,1)S(1)}) custom-call(s32[1,4,4]{2,1,0:T(4,128)S(1)} %copy-done.5, s32[1,4,4]{2,1,0:T(4,128)S(1)} %collective-permute-done.other, ...), custom_call_target="tpu_custom_call" | custom-call | tf_op jit(solution)/shard_map/pallas_call | solution.py:29
  38.1 1.7 %collective-permute-done.19.refs_1_ = bf16[256,128]{1,0:T(8,128)(2,1)S(1)} collective-permute-done((bf16[256,128]{1,0:T(8,128)(2,1)S(1)}, bf16[256,128]{1,0:T(8,128)(2,1)S(1)}, u32[]{:S(2)}, u32[]{:S(2)}) %collective-permute-start.19) | collective-permute-done | bytes 65568 | tf_op jit(solution)/shard_map/ppermute | solution.py:229
  41.7 2.1 %collective-permute-done.21.refs_3_ = bf16[256,128]{1,0:T(8,128)(2,1)S(1)} collective-permute-done((bf16[256,128]{1,0:T(8,128)(2,1)S(1)}, bf16[256,128]{1,0:T(8,128)(2,1)S(1)}, u32[]{:S(2)}, u32[]{:S(2)}) %collective-permute-start.21) | collective-permute-done | bytes 65568 | tf_op jit(solution)/shard_map/ppermute | solution.py:229
  45.2 7.7 %collective-permute-start.36 = (bf16[1024,128]{1,0:T(8,128)(2,1)S(1)}, bf16[1024,128]{1,0:T(8,128)(2,1)S(1)}, u32[]{:S(2)}, u32[]{:S(2)}) collective-permute-start(bf16[1024,128]{1,0:T(8,128)(2,1)S(1)} %get-tuple-element.66.first), channel_id=1, source_target_pairs={{0,1},{1,0},{2,3},{3,2},{4,5},{5,4},{6,7},{7,6},{8,9},{9,8},{10,11... | collective-permute-start | bytes 786440 | tf_op jit(solution)/shard_map/ppermute | solution.py:217
  53.7 1.4 %shard_map.93 = (bf16[1024,128]{1,0:T(8,128)(2,1)S(1)}, bf16[512,128]{1,0:T(8,128)(2,1)S(1)}, bf16[512,128]{1,0:T(8,128)(2,1)S(1)}, bf16[512,128]{1,0:T(8,128)(2,1)S(1)}, bf16[512,128]{1,0:T(8,128)(2,1)S(1)}) custom-call(s32[1,4,4]{2,1,0:T(4,128)S(1)} %copy-done.5, s32[1,4,4]{2,1,0:T(4,128)S(1)} %collective-permute-done.other, ...), custom_call_target="tpu_custom_call" | custom-call | tf_op jit(solution)/shard_map/pallas_call | solution.py:29
  55.1 2.4 %collective-permute-start.22 = (bf16[1024,128]{1,0:T(8,128)(2,1)S(1)}, bf16[1024,128]{1,0:T(8,128)(2,1)S(1)}, u32[]{:S(2)}, u32[]{:S(2)}) collective-permute-start(bf16[1024,128]{1,0:T(8,128)(2,1)S(1)} %get-tuple-element.53.refs_0_), channel_id=1, source_target_pairs={{0,1},{1,0},{2,3},{3,2},{4,5},{5,4},{6,7},{7,6},{8,9},{9,8},{10,11... | collective-permute-start | bytes 786440 | tf_op jit(solution)/shard_map/ppermute | solution.py:217
  60.3 2.3 %collective-permute-done.26.refs_1_.refs_5_ = bf16[512,128]{1,0:T(8,128)(2,1)S(1)} collective-permute-done((bf16[512,128]{1,0:T(8,128)(2,1)S(1)}, bf16[512,128]{1,0:T(8,128)(2,1)S(1)}, u32[]{:S(2)}, u32[]{:S(2)}) %collective-permute-start.26) | collective-permute-done | bytes 131104 | tf_op jit(solution)/shard_map/ppermute | solution.py:229
  64.0 2.4 %collective-permute-done.28.refs_3_.refs_7_ = bf16[512,128]{1,0:T(8,128)(2,1)S(1)} collective-permute-done((bf16[512,128]{1,0:T(8,128)(2,1)S(1)}, bf16[512,128]{1,0:T(8,128)(2,1)S(1)}, u32[]{:S(2)}, u32[]{:S(2)}) %collective-permute-start.28) | collective-permute-done | bytes 131104 | tf_op jit(solution)/shard_map/ppermute | solution.py:229
  70.2 1.4 %shard_map.97 = (bf16[1024,128]{1,0:T(8,128)(2,1)S(1)}, bf16[256,128]{1,0:T(8,128)(2,1)S(1)}, bf16[256,128]{1,0:T(8,128)(2,1)S(1)}, bf16[256,128]{1,0:T(8,128)(2,1)S(1)}, bf16[256,128]{1,0:T(8,128)(2,1)S(1)}) custom-call(s32[1,4,4]{2,1,0:T(4,128)S(1)} %copy-done.5, s32[1,4,4]{2,1,0:T(4,128)S(1)} %collective-permute-done.other, ...), custom_call_target="tpu_custom_call" | custom-call | tf_op jit(solution)/shard_map/pallas_call | solution.py:29
  73.8 1.3 %collective-permute-start.34 = (bf16[256,128]{1,0:T(8,128)(2,1)S(1)}, bf16[256,128]{1,0:T(8,128)(2,1)S(1)}, u32[]{:S(2)}, u32[]{:S(2)}) collective-permute-start(bf16[256,128]{1,0:T(8,128)(2,1)S(1)} %get-tuple-element.64), channel_id=1, source_target_pairs={{0,16},{8,24},{16,0},{24,8},{1,17},{9,25},{17,1},{25,9},{2,18},{10... | collective-permute-start | bytes 196616 | tf_op jit(solution)/shard_map/ppermute | solution.py:229
  75.7 1.5 %collective-permute-done.34.refs_2_ = bf16[256,128]{1,0:T(8,128)(2,1)S(1)} collective-permute-done((bf16[256,128]{1,0:T(8,128)(2,1)S(1)}, bf16[256,128]{1,0:T(8,128)(2,1)S(1)}, u32[]{:S(2)}, u32[]{:S(2)}) %collective-permute-start.34) | collective-permute-done | bytes 65568 | tf_op jit(solution)/shard_map/ppermute | solution.py:229
  77.2 1.9 %collective-permute-done.35.refs_3_ = bf16[256,128]{1,0:T(8,128)(2,1)S(1)} collective-permute-done((bf16[256,128]{1,0:T(8,128)(2,1)S(1)}, bf16[256,128]{1,0:T(8,128)(2,1)S(1)}, u32[]{:S(2)}, u32[]{:S(2)}) %collective-permute-start.35) | collective-permute-done | bytes 65568 | tf_op jit(solution)/shard_map/ppermute | solution.py:229
  79.1 1.8 %shard_map.102.current.refs_2_ = bf16[1024,128]{1,0:T(8,128)(2,1)S(1)} custom-call(bf16[1024,1024]{1,0:T(8,128)(2,1)S(1)} %get-tuple-element.36.sheet, f32[1024,128]{1,0:T(8,128)S(1)} %get-tuple-element.37.column, bf16[4,1024,128]{2,1,0:T(8,128)(2,1)S(1)} %copy-done, bf16[1024,1024]{1,0:T(8,128)(2,1)S(1)} %shard_map.83.matrix, ...), custom_call_target="tpu_custom_call" | custom-call | tf_op jit(solution)/shard_map/pallas_call | solution.py:29
  83.1 29.0 %collective-permute-start.43 = (bf16[3072,128]{1,0:T(8,128)(2,1)S(1)}, bf16[3072,128]{1,0:T(8,128)(2,1)S(1)}, u32[]{:S(2)}, u32[]{:S(2)}) collective-permute-start(bf16[3072,128]{1,0:T(8,128)(2,1)S(1)} %shard_map.104.late), channel_id=1, source_target_pairs={{0,1},{1,0},{2,3},{3,2},{4,5},{5,4},{6,7},{7,6},{8,9},{9,8},{10,11... | collective-permute-start | bytes 2359304 | tf_op jit(solution)/shard_map/ppermute | solution.py:217
  112.2 2.2 %collective-permute-done.31.early_other = bf16[1024,128]{1,0:T(8,128)(2,1)S(1)} collective-permute-done((bf16[1024,128]{1,0:T(8,128)(2,1)S(1)}, bf16[1024,128]{1,0:T(8,128)(2,1)S(1)}, u32[]{:S(2)}, u32[]{:S(2)}) %collective-permute-start.31) | collective-permute-done | bytes 262176 | tf_op jit(solution)/shard_map/ppermute | solution.py:217
  (106 shorter events, 34.5 us)
Async XLA Ops:
  0.0 11.0 %collective-permute-start.7 = (bf16[1024,128]{1,0:T(8,128)(2,1)}, bf16[1024,128]{1,0:T(8,128)(2,1)S(1)}, u32[]{:S(2)}, u32[]{:S(2)}) collective-permute-start(bf16[1024,128]{1,0:T(8,128)(2,1)} %bitcast.5), channel_id=1, source_target_pairs={{0,1},{1,2},{2,3},{3,4},{4,5},{5,6},{6,7},{7,0},{8,9},{9,10},{10,1... | collective-permute-start | bytes 786440 | tf_op jit(solution)/shard_map/ppermute | solution.py:217
  2.8 6.5 %collective-permute-start.1 = (bf16[256,128]{1,0:T(8,128)(2,1)S(1)}, bf16[256,128]{1,0:T(8,128)(2,1)S(1)}, u32[]{:S(2)}, u32[]{:S(2)}) collective-permute-start(bf16[256,128]{1,0:T(8,128)(2,1)S(1)} %get-tuple-element.39), channel_id=1, source_target_pairs={{0,8},{8,0},{16,24},{24,16},{1,9},{9,1},{17,25},{25,17},{2,10},{10... | collective-permute-start | bytes 196616 | tf_op jit(solution)/shard_map/ppermute | solution.py:229
  4.1 5.2 %collective-permute-start.2 = (bf16[256,128]{1,0:T(8,128)(2,1)S(1)}, bf16[256,128]{1,0:T(8,128)(2,1)S(1)}, u32[]{:S(2)}, u32[]{:S(2)}) collective-permute-start(bf16[256,128]{1,0:T(8,128)(2,1)S(1)} %get-tuple-element.40), channel_id=1, source_target_pairs={{0,16},{8,24},{16,0},{24,8},{1,17},{9,25},{17,1},{25,9},{2,18},{10... | collective-permute-start | bytes 196616 | tf_op jit(solution)/shard_map/ppermute | solution.py:229
  11.7 67.3 %collective-permute-start.32 = (bf16[1024,1024]{1,0:T(8,128)(2,1)S(1)}, bf16[1024,1024]{1,0:T(8,128)(2,1)S(1)}, u32[]{:S(2)}, u32[]{:S(2)}) collective-permute-start(bf16[1024,1024]{1,0:T(8,128)(2,1)S(1)} %shard_map.83.matrix), channel_id=1, source_target_pairs={{0,1},{1,0},{2,3},{3,2},{4,5},{5,4},{6,7},{7,6},{8,9},{9,8},{10,11... | collective-permute-start | bytes 6291464 | tf_op jit(solution)/shard_map/ppermute | solution.py:217
  12.2 6.2 %collective-permute-start.5 = (bf16[1024,128]{1,0:T(8,128)(2,1)S(1)}, bf16[1024,128]{1,0:T(8,128)(2,1)S(1)}, u32[]{:S(2)}, u32[]{:S(2)}) collective-permute-start(bf16[1024,128]{1,0:T(8,128)(2,1)S(1)} %shard_map.86.first), channel_id=1, source_target_pairs={{2,0},{6,4},{10,8},{14,12},{18,16},{22,20},{26,24},{30,28}} | collective-permute-start | bytes 786440 | tf_op jit(solution)/shard_map/ppermute | solution.py:217
  15.7 7.9 %collective-permute-start.12 = (bf16[512,128]{1,0:T(8,128)(2,1)S(1)}, bf16[512,128]{1,0:T(8,128)(2,1)S(1)}, u32[]{:S(2)}, u32[]{:S(2)}) collective-permute-start(bf16[512,128]{1,0:T(8,128)(2,1)S(1)} %get-tuple-element.44), channel_id=1, source_target_pairs={{0,8},{8,0},{16,24},{24,16},{1,9},{9,1},{17,25},{25,17},{2,10},{10... | collective-permute-start | bytes 393224 | tf_op jit(solution)/shard_map/ppermute | solution.py:229
  17.0 7.4 %collective-permute-start.13 = (bf16[512,128]{1,0:T(8,128)(2,1)S(1)}, bf16[512,128]{1,0:T(8,128)(2,1)S(1)}, u32[]{:S(2)}, u32[]{:S(2)}) collective-permute-start(bf16[512,128]{1,0:T(8,128)(2,1)S(1)} %get-tuple-element.45), channel_id=1, source_target_pairs={{0,16},{8,24},{16,0},{24,8},{1,17},{9,25},{17,1},{25,9},{2,18},{10... | collective-permute-start | bytes 393224 | tf_op jit(solution)/shard_map/ppermute | solution.py:229
  17.2 7.2 %collective-permute-start.14 = (bf16[512,128]{1,0:T(8,128)(2,1)S(1)}, bf16[512,128]{1,0:T(8,128)(2,1)S(1)}, u32[]{:S(2)}, u32[]{:S(2)}) collective-permute-start(bf16[512,128]{1,0:T(8,128)(2,1)S(1)} %get-tuple-element.46), channel_id=1, source_target_pairs={{0,24},{8,16},{16,8},{24,0},{1,25},{9,17},{17,9},{25,1},{2,26},{10... | collective-permute-start | bytes 393224 | tf_op jit(solution)/shard_map/ppermute | solution.py:229
  18.4 13.6 %collective-permute-start.9 = (bf16[1024,128]{1,0:T(8,128)(2,1)S(1)}, bf16[1024,128]{1,0:T(8,128)(2,1)S(1)}, u32[]{:S(2)}, u32[]{:S(2)}) collective-permute-start(bf16[1024,128]{1,0:T(8,128)(2,1)S(1)} %collective-permute-done.8.refs_1_), channel_id=1, source_target_pairs={{0,1},{1,2},{2,3},{3,4},{4,5},{5,6},{6,7},{7,0},{8,9},{9,10},{10,1... | collective-permute-start | bytes 786440 | tf_op jit(solution)/shard_map/ppermute | solution.py:217
  23.7 8.4 %collective-permute-start.6 = (bf16[1024,128]{1,0:T(8,128)(2,1)S(1)}, bf16[1024,128]{1,0:T(8,128)(2,1)S(1)}, u32[]{:S(2)}, u32[]{:S(2)}) collective-permute-start(bf16[1024,128]{1,0:T(8,128)(2,1)S(1)} %shard_map.87.refs_0_), channel_id=1, source_target_pairs={{4,0},{12,8},{20,16},{28,24}} | collective-permute-start | bytes 786440 | tf_op jit(solution)/shard_map/ppermute | solution.py:217
  25.6 10.2 %collective-permute-start.15 = (bf16[2048,128]{1,0:T(8,128)(2,1)S(1)}, bf16[2048,128]{1,0:T(8,128)(2,1)S(1)}, u32[]{:S(2)}, u32[]{:S(2)}) collective-permute-start(bf16[2048,128]{1,0:T(8,128)(2,1)S(1)} %shard_map.90.first), channel_id=1, source_target_pairs={{0,1},{1,0},{2,3},{3,2},{4,5},{5,4},{6,7},{7,6},{8,9},{9,8},{10,11... | collective-permute-start | bytes 1572872 | tf_op jit(solution)/shard_map/ppermute | solution.py:217
  35.1 10.1 %collective-permute-start.11 = (bf16[1024,128]{1,0:T(8,128)(2,1)S(1)}, bf16[1024,128]{1,0:T(8,128)(2,1)S(1)}, u32[]{:S(2)}, u32[]{:S(2)}) collective-permute-start(bf16[1024,128]{1,0:T(8,128)(2,1)S(1)} %collective-permute-done.10.refs_5_), channel_id=1, source_target_pairs={{1,2},{2,4},{4,6},{9,10},{10,12},{12,14},{17,18},{18,20},{20,22},{... | collective-permute-start | bytes 786440 | tf_op jit(solution)/shard_map/ppermute | solution.py:217
  36.0 17.0 %collective-permute-start.16 = (bf16[1024,128]{1,0:T(8,128)(2,1)S(1)}, bf16[1024,128]{1,0:T(8,128)(2,1)S(1)}, u32[]{:S(2)}, u32[]{:S(2)}) collective-permute-start(bf16[1024,128]{1,0:T(8,128)(2,1)S(1)} %get-tuple-element.47.refs_0_), channel_id=1, source_target_pairs={{2,0},{10,8},{18,16},{26,24}} | collective-permute-start | bytes 786440 | tf_op jit(solution)/shard_map/ppermute | solution.py:217
  41.0 12.6 %collective-permute-start.17 = (bf16[1024,128]{1,0:T(8,128)(2,1)S(1)}, bf16[1024,128]{1,0:T(8,128)(2,1)S(1)}, u32[]{:S(2)}, u32[]{:S(2)}) collective-permute-start(bf16[1024,128]{1,0:T(8,128)(2,1)S(1)} %get-tuple-element.47.refs_0_), channel_id=1, source_target_pairs={{4,0},{12,8},{20,16},{28,24}} | collective-permute-start | bytes 786440 | tf_op jit(solution)/shard_map/ppermute | solution.py:217
  43.8 9.8 %collective-permute-start.18 = (bf16[1024,128]{1,0:T(8,128)(2,1)S(1)}, bf16[1024,128]{1,0:T(8,128)(2,1)S(1)}, u32[]{:S(2)}, u32[]{:S(2)}) collective-permute-start(bf16[1024,128]{1,0:T(8,128)(2,1)S(1)} %get-tuple-element.47.refs_0_), channel_id=1, source_target_pairs={{6,0},{14,8},{22,16},{30,24}} | collective-permute-start | bytes 786440 | tf_op jit(solution)/shard_map/ppermute | solution.py:217
  45.2 13.3 %collective-permute-start.36 = (bf16[1024,128]{1,0:T(8,128)(2,1)S(1)}, bf16[1024,128]{1,0:T(8,128)(2,1)S(1)}, u32[]{:S(2)}, u32[]{:S(2)}) collective-permute-start(bf16[1024,128]{1,0:T(8,128)(2,1)S(1)} %get-tuple-element.66.first), channel_id=1, source_target_pairs={{0,1},{1,0},{2,3},{3,2},{4,5},{5,4},{6,7},{7,6},{8,9},{9,8},{10,11... | collective-permute-start | bytes 786440 | tf_op jit(solution)/shard_map/ppermute | solution.py:217
  53.0 6.1 %collective-permute-start.24 = (bf16[1024,128]{1,0:T(8,128)(2,1)S(1)}, bf16[1024,128]{1,0:T(8,128)(2,1)S(1)}, u32[]{:S(2)}, u32[]{:S(2)}) collective-permute-start(bf16[1024,128]{1,0:T(8,128)(2,1)S(1)} %get-tuple-element.54.first), channel_id=1, source_target_pairs={{2,0},{6,4},{10,8},{14,12},{18,16},{22,20},{26,24},{30,28}} | collective-permute-start | bytes 786440 | tf_op jit(solution)/shard_map/ppermute | solution.py:217
  55.1 12.9 %collective-permute-start.22 = (bf16[1024,128]{1,0:T(8,128)(2,1)S(1)}, bf16[1024,128]{1,0:T(8,128)(2,1)S(1)}, u32[]{:S(2)}, u32[]{:S(2)}) collective-permute-start(bf16[1024,128]{1,0:T(8,128)(2,1)S(1)} %get-tuple-element.53.refs_0_), channel_id=1, source_target_pairs={{0,1},{1,0},{2,3},{3,2},{4,5},{5,4},{6,7},{7,6},{8,9},{9,8},{10,11... | collective-permute-start | bytes 786440 | tf_op jit(solution)/shard_map/ppermute | solution.py:217
  59.1 7.2 %collective-permute-start.28 = (bf16[512,128]{1,0:T(8,128)(2,1)S(1)}, bf16[512,128]{1,0:T(8,128)(2,1)S(1)}, u32[]{:S(2)}, u32[]{:S(2)}) collective-permute-start(bf16[512,128]{1,0:T(8,128)(2,1)S(1)} %get-tuple-element.58), channel_id=1, source_target_pairs={{0,24},{8,16},{16,8},{24,0},{1,25},{9,17},{17,9},{25,1},{2,26},{10... | collective-permute-start | bytes 393224 | tf_op jit(solution)/shard_map/ppermute | solution.py:229
  62.5 6.2 %collective-permute-start.37 = (bf16[1024,128]{1,0:T(8,128)(2,1)S(1)}, bf16[1024,128]{1,0:T(8,128)(2,1)S(1)}, u32[]{:S(2)}, u32[]{:S(2)}) collective-permute-start(bf16[1024,128]{1,0:T(8,128)(2,1)S(1)} %shard_map.100.first), channel_id=1, source_target_pairs={{2,0},{6,4},{10,8},{14,12},{18,16},{22,20},{26,24},{30,28}} | collective-permute-start | bytes 786440 | tf_op jit(solution)/shard_map/ppermute | solution.py:217
  63.3 6.2 %collective-permute-start.25 = (bf16[1024,128]{1,0:T(8,128)(2,1)S(1)}, bf16[1024,128]{1,0:T(8,128)(2,1)S(1)}, u32[]{:S(2)}, u32[]{:S(2)}) collective-permute-start(bf16[1024,128]{1,0:T(8,128)(2,1)S(1)} %shard_map.95.refs_0_), channel_id=1, source_target_pairs={{4,0},{12,8},{20,16},{28,24}} | collective-permute-start | bytes 786440 | tf_op jit(solution)/shard_map/ppermute | solution.py:217
  69.5 5.5 %collective-permute-start.39 = (bf16[1024,128]{1,0:T(8,128)(2,1)S(1)}, bf16[1024,128]{1,0:T(8,128)(2,1)S(1)}, u32[]{:S(2)}, u32[]{:S(2)}) collective-permute-start(bf16[1024,128]{1,0:T(8,128)(2,1)S(1)} %get-tuple-element.60), channel_id=1, source_target_pairs={{2,0},{10,8},{18,16},{26,24}} | collective-permute-start | bytes 786440 | tf_op jit(solution)/shard_map/ppermute | solution.py:217
  71.7 9.9 %collective-permute-start.30 = (bf16[1024,128]{1,0:T(8,128)(2,1)S(1)}, bf16[1024,128]{1,0:T(8,128)(2,1)S(1)}, u32[]{:S(2)}, u32[]{:S(2)}) collective-permute-start(bf16[1024,128]{1,0:T(8,128)(2,1)S(1)} %shard_map.98), channel_id=1, source_target_pairs={{0,2},{2,4},{4,6},{8,10},{10,12},{12,14},{16,18},{18,20},{20,22},{... | collective-permute-start | bytes 786440 | tf_op jit(solution)/shard_map/ppermute | solution.py:217
  83.1 31.3 %collective-permute-start.43 = (bf16[3072,128]{1,0:T(8,128)(2,1)S(1)}, bf16[3072,128]{1,0:T(8,128)(2,1)S(1)}, u32[]{:S(2)}, u32[]{:S(2)}) collective-permute-start(bf16[3072,128]{1,0:T(8,128)(2,1)S(1)} %shard_map.104.late), channel_id=1, source_target_pairs={{0,1},{1,0},{2,3},{3,2},{4,5},{5,4},{6,7},{7,6},{8,9},{9,8},{10,11... | collective-permute-start | bytes 2359304 | tf_op jit(solution)/shard_map/ppermute | solution.py:217
  (28 other events, 107.2 us)
